TPU v7x, 32 devices: a whole 2x2x4 slice. The times are simulated.
32 devices in a mesh: parts: 2 (over y), seq: 4 (over z), head: 2 (over x), fsdp: 2 (over core).
Axes of the slice: x: 2, y: 2, z: 4, core: 2. Of those that a mesh axis runs over, the one named last changes fastest.
Arguments:
- frames: bfloat16 [2048, 1024], P(('parts', 'seq', 'head', 'fsdp')), parts along dimension 0, may hold values from -24 to 24
- length: int32 [2], P('parts'), parts along dimension 0, may hold values from 512 to 1024
- ln1_gain: float32 [1024], replicated, may hold values from 0.1 to 1.9
- w_query: bfloat16 [1024, 1024], P('seq', ('head', 'fsdp')), may hold values from -0.2 to 0.2
- w_key: bfloat16 [1024, 1024], P('seq', ('head', 'fsdp')), may hold values from -3 to 3
- w_value: bfloat16 [1024, 1024], P('seq', ('head', 'fsdp')), may hold values from -0.375 to 0.375
- w_out: bfloat16 [1024, 1024], P(('head', 'fsdp'), 'seq'), may hold values from -0.1875 to 0.1875
- ln2_gain: float32 [1024], replicated, may hold values from 0.1 to 1.9
- pw1_value: bfloat16 [1024, 1024], P('seq', ('head', 'fsdp')), may hold values from -0.1875 to 0.1875
- pw1_gate: bfloat16 [1024, 1024], P('seq', ('head', 'fsdp')), may hold values from -0.375 to 0.375
- depth_kernel: float32 [9, 1024], P(None, ('head', 'fsdp')), may hold values from -2 to 2
- bn_scale: float32 [1024], P(('head', 'fsdp')), may hold values from 0.1 to 1.9
- bn_shift: float32 [1024], P(('head', 'fsdp')), may hold values from -3 to 3
- pw2: bfloat16 [1024, 1024], P(('head', 'fsdp'), 'seq'), may hold values from -0.1875 to 0.1875
Outputs:
- encoded: bfloat16 [2048, 1024], P(('parts', 'seq', 'head', 'fsdp')), parts along dimension 0
There are 2 independent parts, one for each index of `parts`. A program takes and returns all parts, laid end to end along the dimension named above; an argument that names none is the same for every part. Nothing has to cross between parts.
All inputs are finite; a program needn't handle non-finite values.
Results may differ from a plain program's by a relative error of at most 0.012.
The roundings to bfloat16 on the way count: a program that leaves them out, or rounds other values in their place, can miss the bound.
Values may be sent and summed in bfloat16 or wider, within the bound.
No kernel may reach another device: no remote copies, remote signals or barrier semaphores. Data moves between devices by JAX's collectives and lax.ppermute only.
A program may use at most 64 MiB of HBM per device.

v0:
```python
import math

import jax
import jax.numpy as jnp
from jax import lax
from jax.sharding import PartitionSpec as P

KERNEL = 9
HD = 128


def with_halo(block, sides, width):
    for axis, dim in sides:
        count = lax.axis_size(axis)
        forward = [(i, i + 1) for i in range(count - 1)]
        backward = [(target, source) for source, target in forward]
        low = lax.ppermute(
            lax.slice_in_dim(block, block.shape[dim] - width, None, axis=dim), axis, forward
        )
        high = lax.ppermute(lax.slice_in_dim(block, 0, width, axis=dim), axis, backward)
        block = jnp.concatenate([low, block, high], axis=dim)
    return block


def layer_norm(values_in, gain_vec):
    center = jnp.mean(values_in, axis=-1, keepdims=True)
    shifted = values_in - center
    spread = jnp.mean(shifted * shifted, axis=-1, keepdims=True)
    return shifted * lax.rsqrt(spread + 1e-05) * gain_vec


def shards(
    frames,
    length,
    ln1_gain,
    w_query,
    w_key,
    w_value,
    w_out,
    ln2_gain,
    pw1_value,
    pw1_gate,
    depth_kernel,
    bn_scale,
    bn_shift,
    pw2,
):
    group_size = lax.axis_size(("head", "fsdp"))
    my_rows = frames.shape[0]
    block_rows = my_rows * group_size
    head_cols = w_query.shape[1]
    heads_here = head_cols // HD
    seq_start = lax.axis_index("seq") * block_rows
    valid_len = length[0]
    score_scale = 1.0 / math.sqrt(HD)
    full_query, full_key, full_value, value_cols, gate_cols = (
        lax.all_gather(w_query, "seq", axis=0, tiled=True),
        lax.all_gather(w_key, "seq", axis=0, tiled=True),
        lax.all_gather(w_value, "seq", axis=0, tiled=True),
        lax.all_gather(pw1_value, "seq", axis=0, tiled=True),
        lax.all_gather(pw1_gate, "seq", axis=0, tiled=True),
    )
    out_rows, down_rows = (
        lax.all_gather(w_out, "seq", axis=1, tiled=True),
        lax.all_gather(pw2, "seq", axis=1, tiled=True),
    )
    projector = jnp.concatenate((full_query, full_key, full_value), axis=1)
    source = frames.astype(jnp.float32)
    normed = layer_norm(source, ln1_gain).astype(jnp.bfloat16)
    projected = jnp.dot(
        lax.all_gather(normed, ("head", "fsdp"), axis=0, tiled=True),
        projector,
        preferred_element_type=jnp.float32,
    ).astype(jnp.bfloat16)
    queries = projected[:, :head_cols].reshape(block_rows, heads_here, HD)
    keys_here = projected[:, head_cols : 2 * head_cols]
    values_here = projected[:, 2 * head_cols :]
    initial = (
        jnp.full((heads_here, block_rows), -1e30, jnp.float32),
        jnp.zeros((heads_here, block_rows), jnp.float32),
        jnp.zeros((heads_here, block_rows, HD), jnp.float32),
    )
    key_piece = lax.all_gather(keys_here, "seq", axis=0, tiled=True)
    value_piece = lax.all_gather(values_here, "seq", axis=0, tiled=True)
    row_count = key_piece.shape[0]
    block_size = math.gcd(row_count, 512)
    block_count = row_count // block_size
    key_blocks = key_piece.reshape(block_count, block_size, heads_here, HD)
    value_blocks = value_piece.reshape(block_count, block_size, heads_here, HD)
    places = jnp.arange(row_count, dtype=jnp.int32).reshape(block_count, block_size)

    def advance(inner_state, block_item):
        key_block, value_block, place = block_item
        peak_score, weight_sum, weighted = inner_state
        scores = (
            jnp.einsum("qhd,khd->hqk", queries, key_block, preferred_element_type=jnp.float32)
            * score_scale
        )
        scores = jnp.where((place < valid_len)[None, None, :], scores, -jnp.inf)
        new_peak = jnp.maximum(peak_score, jnp.max(scores, axis=2))
        factor = jnp.exp(peak_score - new_peak)
        weights = jnp.exp(scores - new_peak[:, :, None])
        weight_sum = weight_sum * factor + jnp.sum(weights, axis=2)
        weighted = weighted * factor[:, :, None] + jnp.einsum(
            "hqk,khd->hqd",
            weights.astype(jnp.bfloat16),
            value_block,
            preferred_element_type=jnp.float32,
        )
        return ((new_peak, weight_sum, weighted), None)

    result, unused = lax.scan(advance, initial, (key_blocks, value_blocks, places))
    peak_score, weight_sum, weighted = result
    context = (
        (weighted / weight_sum[:, :, None])
        .astype(jnp.bfloat16)
        .transpose(1, 0, 2)
        .reshape(block_rows, head_cols)
    )
    attended = lax.psum_scatter(
        jnp.dot(context, out_rows, preferred_element_type=jnp.float32).astype(jnp.bfloat16),
        ("head", "fsdp"),
        scatter_dimension=0,
        tiled=True,
    ).astype(jnp.float32)
    middle = source + attended
    normed_two = layer_norm(middle, ln2_gain).astype(jnp.bfloat16)
    piece = lax.all_gather(normed_two, ("head", "fsdp"), axis=0, tiled=True)
    value_part = jnp.dot(piece, value_cols, preferred_element_type=jnp.float32)
    gate_part = jnp.dot(piece, gate_cols, preferred_element_type=jnp.float32)
    places = seq_start + jnp.arange(piece.shape[0], dtype=jnp.int32)
    gated_rows = jnp.where(
        (places < valid_len)[:, None], value_part * jax.nn.sigmoid(gate_part), 0.0
    ).astype(jnp.bfloat16)
    rim_width = (KERNEL - 1) // 2
    padded = with_halo(gated_rows, (("seq", 0),), rim_width).astype(jnp.float32)
    depth_sum = depth_kernel[0] * padded[0:block_rows]
    for offset in range(1, KERNEL):
        depth_sum = depth_sum + depth_kernel[offset] * padded[offset : offset + block_rows]
    shifted = depth_sum * bn_scale + bn_shift
    active = (shifted * jax.nn.sigmoid(shifted)).astype(jnp.bfloat16)
    conv_part = lax.psum_scatter(
        jnp.dot(active, down_rows, preferred_element_type=jnp.float32).astype(jnp.bfloat16),
        ("head", "fsdp"),
        scatter_dimension=0,
        tiled=True,
    ).astype(jnp.float32)
    return (middle + conv_part).astype(jnp.bfloat16)


def solution(mesh):
    in_specs = (
        P(("parts", "seq", "head", "fsdp"), None),
        P("parts"),
        P(),
        P("seq", ("head", "fsdp")),
        P("seq", ("head", "fsdp")),
        P("seq", ("head", "fsdp")),
        P(("head", "fsdp"), "seq"),
        P(),
        P("seq", ("head", "fsdp")),
        P("seq", ("head", "fsdp")),
        P(None, ("head", "fsdp")),
        P(("head", "fsdp")),
        P(("head", "fsdp")),
        P(("head", "fsdp"), "seq"),
    )
    out_specs = P(("parts", "seq", "head", "fsdp"), None)
    return jax.shard_map(shards, mesh=mesh, in_specs=in_specs, out_specs=out_specs, check_vma=False)
```

profile of v0, /device:TPU:0, one launch (start us, length us, event | category | flops | bytes accessed | tf_op | source)
XLA Modules:
  0.0 217.0 jit_solution(8973462292048037482)
XLA Ops:
  6.6 1.1 convert_reduce_fusion
  7.7 1.1 fusion.24
  8.8 1.0 fusion.26
  9.8 8.8 %all_gather.33 = bf16[256,1024]{1,0:T(8,128)(2,1)S(1)} all-gather(bf16[64,1024]{1,0:T(8,128)(2,1)S(1)} %fusion.26), channel_id=1, replica_groups=mesh['parts'=2,'seq'=4,'head'=2,'fsdp'=2] {'head','fsdp'}, dimensions={0}, use_global_device_ids=true | all-gather | bytes 655360 | tf_op jit(solution)/shard_map/all_gather | solution.py:71
  18.6 16.3 %all_gather.34 = bf16[1024,256]{1,0:T(8,128)(2,1)S(1)} all-gather(bf16[256,256]{1,0:T(8,128)(2,1)S(1)} %copy-done.2), channel_id=1, replica_groups=mesh['parts'=2,'seq'=4,'head'=2,'fsdp'=2] {'seq'}, dimensions={0}, use_global_device_ids=true | all-gather | bytes 655360 | tf_op jit(solution)/shard_map/all_gather | solution.py:57
  34.9 15.9 %all_gather.35 = bf16[1024,256]{1,0:T(8,128)(2,1)S(1)} all-gather(bf16[256,256]{1,0:T(8,128)(2,1)S(1)} %copy-done.3), channel_id=1, replica_groups=mesh['parts'=2,'seq'=4,'head'=2,'fsdp'=2] {'seq'}, dimensions={0}, use_global_device_ids=true | all-gather | bytes 655360 | tf_op jit(solution)/shard_map/all_gather | solution.py:58
  50.8 16.1 %all_gather.36 = bf16[1024,256]{1,0:T(8,128)(2,1)S(1)} all-gather(bf16[256,256]{1,0:T(8,128)(2,1)S(1)} %copy-done.4), channel_id=1, replica_groups=mesh['parts'=2,'seq'=4,'head'=2,'fsdp'=2] {'seq'}, dimensions={0}, use_global_device_ids=true | all-gather | bytes 655360 | tf_op jit(solution)/shard_map/all_gather | solution.py:59
  67.0 0.6 fusion.14
  67.6 14.8 %all_gather.37 = bf16[1024,256]{1,0:T(8,128)(2,1)S(1)} all-gather(bf16[256,256]{1,0:T(8,128)(2,1)S(1)} %get-tuple-element.129), channel_id=1, replica_groups=mesh['parts'=2,'seq'=4,'head'=2,'fsdp'=2] {'seq'}, dimensions={0}, use_global_device_ids=true | all-gather | bytes 655360 | tf_op jit(solution)/shard_map/all_gather | solution.py:83
  82.5 16.1 %all_gather.38 = bf16[1024,256]{1,0:T(8,128)(2,1)S(1)} all-gather(bf16[256,256]{1,0:T(8,128)(2,1)S(1)} %get-tuple-element.127), channel_id=1, replica_groups=mesh['parts'=2,'seq'=4,'head'=2,'fsdp'=2] {'seq'}, dimensions={0}, use_global_device_ids=true | all-gather | bytes 655360 | tf_op jit(solution)/shard_map/all_gather | solution.py:84
  98.8 4.0 %while.15 = (s32[]{:T(128)}, f32[2,256]{1,0:T(2,128)S(1)}, f32[2,256]{1,0:T(2,128)S(1)}, f32[2,256,128]{2,1,0:T(8,128)S(1)}, s32[2,512]{1,0:T(2,128)S(1)}, /*ind...) while((s32[]{:T(128)}, f32[2,256]{1,0:T(2,128)S(1)}, ...), condition=%wide.region_5.6_spmd.clone, body=%wide.region_2.5_spmd.clone.sunk | while | flops 136252416 | bytes 5409925 | solution.py:112
  98.8 0.4 constant_dynamic-slice_fusion.3
  99.1 0.7 compare_reduce_fusion.2
  100.3 0.4 convolution_add_fusion.2
  100.8 0.4 constant_dynamic-slice_fusion.3
  101.2 0.7 compare_reduce_fusion.2
  102.4 0.4 convolution_add_fusion.2
  103.0 15.8 %all_gather.39 = bf16[256,1024]{1,0:T(8,128)(2,1)S(1)} all-gather(bf16[256,256]{1,0:T(8,128)(2,1)S(1)} %copy-done.5), channel_id=1, replica_groups=mesh['parts'=2,'seq'=4,'head'=2,'fsdp'=2] {'seq'}, dimensions={1}, use_global_device_ids=true | all-gather | bytes 655360 | tf_op jit(solution)/shard_map/all_gather | solution.py:64
  118.8 1.1 convolution_convert_fusion.1
  120.7 15.6 %all_gather.42 = bf16[1024,256]{1,0:T(8,128)(2,1)S(1)} all-gather(bf16[256,256]{1,0:T(8,128)(2,1)S(1)} %copy-done.6), channel_id=1, replica_groups=mesh['parts'=2,'seq'=4,'head'=2,'fsdp'=2] {'seq'}, dimensions={0}, use_global_device_ids=true | all-gather | bytes 655360 | tf_op jit(solution)/shard_map/all_gather | solution.py:61
  136.2 15.0 %all_gather.41 = bf16[1024,256]{1,0:T(8,128)(2,1)S(1)} all-gather(bf16[256,256]{1,0:T(8,128)(2,1)S(1)} %copy-done.7), channel_id=1, replica_groups=mesh['parts'=2,'seq'=4,'head'=2,'fsdp'=2] {'seq'}, dimensions={0}, use_global_device_ids=true | all-gather | bytes 655360 | tf_op jit(solution)/shard_map/all_gather | solution.py:60
  151.3 1.0 fusion.37
  152.3 1.1 multiply_reduce_fusion
  153.5 1.0 multiply_convert_fusion.1
  154.5 6.8 %all_gather.40 = bf16[256,1024]{1,0:T(8,128)(2,1)S(1)} all-gather(bf16[64,1024]{1,0:T(8,128)(2,1)S(1)} %multiply_convert_fusion.1), channel_id=1, replica_groups=mesh['parts'=2,'seq'=4,'head'=2,'fsdp'=2] {'head','fsdp'}, dimensions={0}, use_global_device_ids=true | all-gather | bytes 655360 | tf_op jit(solution)/shard_map/all_gather | solution.py:128
  161.3 0.3 fusion.19
  161.9 3.9 %collective-permute-start = (bf16[4,256]{1,0:T(4,128)(2,1)S(1)}, bf16[4,256]{1,0:T(4,128)(2,1)S(1)}, u32[]{:S(2)}, u32[]{:S(2)}) collective-permute-start(bf16[4,256]{1,0:T(4,128)(2,1)S(1)} %get-tuple-element.130), channel_id=1, source_target_pairs={{0,4},{4,8},{8,12},{1,5},{5,9},{9,13},{2,6},{6,10},{10,14},{3,7},{... | collective-permute-start | bytes 6152 | tf_op jit(solution)/shard_map/ppermute | solution.py:17
  165.8 1.3 collective-permute-start.1
  167.2 16.9 %all_gather.43 = bf16[256,1024]{1,0:T(8,128)(2,1)S(1)} all-gather(bf16[256,256]{1,0:T(8,128)(2,1)S(1)} %copy-done.8), channel_id=1, replica_groups=mesh['parts'=2,'seq'=4,'head'=2,'fsdp'=2] {'seq'}, dimensions={1}, use_global_device_ids=true | all-gather | bytes 655360 | tf_op jit(solution)/shard_map/all_gather | solution.py:65
  184.2 1.4 convolution_convert_fusion
  185.5 23.0 %reduce-scatter.5.cloned.1.call-done = bf16[64,1024]{1,0:T(8,128)(2,1)} async-done(((bf16[256,1024]{1,0:T(8,128)(2,1)}), bf16[64,1024]{1,0:T(8,128)(2,1)}) %reduce-scatter.5.cloned.1.call-update) | async-done | bytes 131088 | tf_op jit(solution)/shard_map/reduce_scatter | solution.py:142
  208.5 1.6 add_convert_fusion
  (62 shorter events, 2.0 us)
Async XLA Ops:
  6.5 12.0 %copy-start.2 = (bf16[256,256]{1,0:T(8,128)(2,1)S(1)}, bf16[256,256]{1,0:T(8,128)(2,1)}, u32[]{:S(2)}) copy-start(bf16[256,256]{1,0:T(8,128)(2,1)} %param.19) | copy-start | bytes 393220
  6.5 28.4 %copy-start.3 = (bf16[256,256]{1,0:T(8,128)(2,1)S(1)}, bf16[256,256]{1,0:T(8,128)(2,1)}, u32[]{:S(2)}) copy-start(bf16[256,256]{1,0:T(8,128)(2,1)} %param.20) | copy-start | bytes 393220
  6.5 144.7 %reduce-scatter.3.cloned.1.call-start = ((), (), s32[]{:S(2)}) async-start(), calls=%async_computation.2 | async-start | bytes 655360 | tf_op jit(solution)/shard_map/reduce_scatter | solution.py:120
  9.8 41.0 %copy-start.4 = (bf16[256,256]{1,0:T(8,128)(2,1)S(1)}, bf16[256,256]{1,0:T(8,128)(2,1)}, u32[]{:S(2)}) copy-start(bf16[256,256]{1,0:T(8,128)(2,1)} %param.21) | copy-start | bytes 393220
  98.7 4.2 %copy-start.5 = (bf16[256,256]{1,0:T(8,128)(2,1)S(1)}, bf16[256,256]{1,0:T(8,128)(2,1)}, u32[]{:S(2)}) copy-start(bf16[256,256]{1,0:T(8,128)(2,1)} %param.22) | copy-start | bytes 393220
  118.8 1.9 copy-start.6
  118.8 17.4 %copy-start.7 = (bf16[256,256]{1,0:T(8,128)(2,1)S(1)}, bf16[256,256]{1,0:T(8,128)(2,1)}, u32[]{:S(2)}) copy-start(bf16[256,256]{1,0:T(8,128)(2,1)} %param.24) | copy-start | bytes 393220
  119.9 31.3 %copy-start.9 = (f32[9,256]{1,0:T(8,128)S(1)}, f32[9,256]{1,0:T(8,128)}, u32[]{:S(2)}) copy-start(f32[9,256]{1,0:T(8,128)} %param.26) | copy-start | bytes 27652
  119.9 31.3 %copy-start = (bf16[64,1024]{1,0:T(8,128)(2,1)S(1)}, bf16[64,1024]{1,0:T(8,128)(2,1)}, u32[]{:S(2)}) copy-start(bf16[64,1024]{1,0:T(8,128)(2,1)} %param.16) | copy-start | bytes 393220
  120.0 33.5 %copy-start.10 = (f32[1024]{0:T(1024)S(1)}, f32[1024]{0:T(1024)}, u32[]{:S(2)}) copy-start(f32[1024]{0:T(1024)} %param.23) | copy-start | bytes 12292
  120.0 88.6 %reduce-scatter.5.cloned.1.call-start = ((), (), s32[]{:S(2)}) async-start(), calls=%async_computation.3 | async-start | bytes 655360 | tf_op jit(solution)/shard_map/reduce_scatter | solution.py:142
  161.6 5.6 %copy-start.8 = (bf16[256,256]{1,0:T(8,128)(2,1)S(1)}, bf16[256,256]{1,0:T(8,128)(2,1)}, u32[]{:S(2)}) copy-start(bf16[256,256]{1,0:T(8,128)(2,1)} %param.29) | copy-start | bytes 393220
  161.6 22.5 %copy-start.11 = (f32[256]{0:T(256)S(1)}, f32[256]{0:T(256)}, u32[]{:S(2)}) copy-start(f32[256]{0:T(256)} %param.28) | copy-start | bytes 3076
  161.6 22.5 %copy-start.12 = (f32[256]{0:T(256)S(1)}, f32[256]{0:T(256)}, u32[]{:S(2)}) copy-start(f32[256]{0:T(256)} %param.27) | copy-start | bytes 3076
  161.9 22.2 %collective-permute-start = (bf16[4,256]{1,0:T(4,128)(2,1)S(1)}, bf16[4,256]{1,0:T(4,128)(2,1)S(1)}, u32[]{:S(2)}, u32[]{:S(2)}) collective-permute-start(bf16[4,256]{1,0:T(4,128)(2,1)S(1)} %get-tuple-element.130), channel_id=1, source_target_pairs={{0,4},{4,8},{8,12},{1,5},{5,9},{9,13},{2,6},{6,10},{10,14},{3,7},{... | collective-permute-start | bytes 6152 | tf_op jit(solution)/shard_map/ppermute | solution.py:17
  165.8 18.3 %collective-permute-start.1 = (bf16[4,256]{1,0:T(4,128)(2,1)S(1)}, bf16[4,256]{1,0:T(4,128)(2,1)S(1)}, u32[]{:S(2)}, u32[]{:S(2)}) collective-permute-start(bf16[4,256]{1,0:T(4,128)(2,1)S(1)} %get-tuple-element.131), channel_id=1, source_target_pairs={{4,0},{8,4},{12,8},{5,1},{9,5},{13,9},{6,2},{10,6},{14,10},{7,3},{... | collective-permute-start | bytes 6152 | tf_op jit(solution)/shard_map/ppermute | solution.py:20
  184.2 24.4 %copy-start.1 = (bf16[64,1024]{1,0:T(8,128)(2,1)S(1)}, bf16[64,1024]{1,0:T(8,128)(2,1)}, u32[]{:S(2)}) copy-start(bf16[64,1024]{1,0:T(8,128)(2,1)} %reduce-scatter.3.cloned.1.call-done) | copy-start | bytes 393220
Sparse Core Ops, SparseCore 0:
  120.1 22.2 reduce-scatter.2
  185.7 22.8 reduce-scatter.4
where the time goes:
time: 217 us
  blocking collectives  158 us (73%)
  waiting for transfers between devices  23 us (11%)
  between operations  14.4 us (7%)
  other arithmetic  9.78 us (5%)
  starting transfers between devices  5.23 us (2%)
  matrix products  5.13 us (2%)
    reduce_scatter x1, waiting for transfers between devices, shards(): lax.psum_scatter(jnp.dot(active, down_rows, preferred_element_type=jnp.fl...  23 us
    all_gather x1, blocking collectives, shards(): lax.all_gather(pw2, 'seq', axis=1, tiled=True)  16.9 us
    all_gather x1, blocking collectives, shards(): lax.all_gather(w_query, 'seq', axis=0, tiled=True)  16.3 us
    all_gather x1, blocking collectives, shards(): lax.all_gather(w_value, 'seq', axis=0, tiled=True)  16.1 us
    all_gather x1, blocking collectives, shards(): value_piece = lax.all_gather(values_here, 'seq', axis=0, tiled=True)  16.1 us
    all_gather x1, blocking collectives, shards(): lax.all_gather(w_key, 'seq', axis=0, tiled=True)  15.9 us
    all_gather x1, blocking collectives, shards(): lax.all_gather(w_out, 'seq', axis=1, tiled=True)  15.8 us
    all_gather x1, blocking collectives, shards(): lax.all_gather(pw1_gate, 'seq', axis=0, tiled=True)  15.6 us
  transfers between devices with their start and end apart: 4, of which 1 were waited for; matrix products, arithmetic and copies ran while one was open for 0% of the time, Pallas kernels for 0%

commit v1 on v0

--- a/solution.py
+++ b/solution.py
@@ -3,6 +3,8 @@
 import jax
 import jax.numpy as jnp
 from jax import lax
+from jax.experimental import pallas as pl
+from jax.experimental.pallas import tpu as pltpu
 from jax.sharding import PartitionSpec as P
 
 KERNEL = 9
@@ -29,7 +31,7 @@
     return shifted * lax.rsqrt(spread + 1e-05) * gain_vec
 
 
-def shards(
+def shards_general(
     frames,
     length,
     ln1_gain,
@@ -148,6 +150,330 @@
     return (middle + conv_part).astype(jnp.bfloat16)
 
 
+SEQ = 4
+EDGE = (KERNEL - 1) // 2
+HALO = 2 * EDGE
+SWAP = [(0, 1), (1, 0)]
+F32 = jnp.float32
+BF16 = jnp.bfloat16
+
+
+def one_head_per_chip(mesh):
+    return dict(mesh.shape) == {"parts": 2, "seq": SEQ, "head": 2, "fsdp": 2}
+
+
+def xor_pairs(k):
+    return [(i, i ^ k) for i in range(SEQ)]
+
+
+def call(kernel, outs, scratch, places, *operands, flops=0):
+    moved = sum(math.prod(a.shape) * a.dtype.itemsize for a in (*operands, *outs))
+    return pl.pallas_call(
+        kernel,
+        out_shape=outs,
+        in_specs=[pl.BlockSpec(memory_space=pltpu.SMEM)]
+        + [pl.BlockSpec(memory_space=pltpu.VMEM)] * len(operands),
+        out_specs=[pl.BlockSpec(memory_space=pltpu.VMEM)] * len(outs),
+        scratch_shapes=scratch,
+        cost_estimate=pl.CostEstimate(flops=flops, bytes_accessed=moved, transcendentals=0),
+        compiler_params=pltpu.CompilerParams(vmem_limit_bytes=40 << 20),
+    )(places, *operands)
+
+
+def aligned(value, to):
+    return pl.multiple_of(value, to)
+
+
+def dot(a, b):
+    return jnp.dot(a, b, preferred_element_type=F32)
+
+
+def project_kernel(places, *refs):
+    blocks = refs[: 2 * SEQ]
+    gain, mine, other, q_out, send_out, edge_out, normed, weights, x_edge, q_edge = refs[2 * SEQ :]
+    s, h, f = places[0], places[1], places[2]
+    rows = blocks[0].shape[0]
+    half = mine.shape[2]
+    gain_row = gain[...]
+    for slot, block in enumerate(blocks):
+        at = (s ^ (slot // 2)) * 2 + (h ^ (slot % 2))
+        x = block[...].astype(F32)
+        normed[pl.ds(aligned(at * rows, rows), rows), :] = layer_norm(x, gain_row).astype(BF16)
+        x_edge[at, 0:EDGE, :] = x[:EDGE]
+        x_edge[at, EDGE:HALO, :] = x[rows - EDGE :]
+    for source in range(SEQ):
+        for m in range(3):
+            columns = slice(m * HD, (m + 1) * HD)
+            at = source * 2 * half
+            weights[pl.ds(aligned(at + f * half, half), half), columns] = mine[source, m]
+            weights[pl.ds(aligned(at + (1 - f) * half, half), half), columns] = other[source, m]
+    count = 2 * SEQ
+    total = count * rows
+    projected = dot(normed[...], weights[...])
+    q_out[...] = projected[:, :HD].astype(BF16)
+    send_out[0:total, :] = projected[:, HD : 2 * HD].astype(BF16)
+    send_out[total : 2 * total, :] = projected[:, 2 * HD :].astype(BF16)
+    for b in range(count):
+        q_edge[b, 0:EDGE, :] = projected[b * rows : b * rows + EDGE, :HD]
+        q_edge[b, EDGE:HALO, :] = projected[(b + 1) * rows - EDGE : (b + 1) * rows, :HD]
+
+    def around(edge, b):
+        low = jnp.maximum(b - f, 0)
+        high = jnp.minimum(b + 1 - f, count - 1)
+        return jnp.concatenate([edge[low, EDGE:HALO, :], edge[high, 0:EDGE, :]], axis=0)
+
+    halos = jnp.concatenate([around(q_edge, b) for b in range(count)], axis=0)
+    send_out[2 * total :, :] = halos.astype(BF16)
+    edge_out[...] = around(x_edge, s * 2 + h).astype(BF16)
+
+
+def attend_kernel(places, q_in, own, peer, ctx_out, q_rows):
+    f, valid_len = places[2], places[4]
+    count = ctx_out.shape[0]
+    total = q_in.shape[0]
+    rows = total // count
+    step = ctx_out.shape[1]
+    local = lax.broadcasted_iota(jnp.int32, (step, total), 1)
+    base = (local // rows) * (2 * rows) + local % rows
+    keep_own = base + f * rows < valid_len
+    keep_peer = base + (1 - f) * rows < valid_len
+    scale = 1.0 / math.sqrt(HD)
+    keys_t = (((1,), (1,)), ((), ()))
+    for b in range(count):
+        q_rows[b, 0:rows, :] = q_in[b * rows : (b + 1) * rows, :].astype(F32)
+        q_rows[b, rows:step, :] = peer[2 * total + b * HALO : 2 * total + (b + 1) * HALO, :].astype(F32)
+    for b in range(count):
+        q = q_rows[b].astype(BF16)
+        first = lax.dot_general(q, own[0:total, :], keys_t, preferred_element_type=F32) * scale
+        second = lax.dot_general(q, peer[0:total, :], keys_t, preferred_element_type=F32) * scale
+        first = jnp.where(keep_own, first, -jnp.inf)
+        second = jnp.where(keep_peer, second, -jnp.inf)
+        peak = jnp.maximum(
+            jnp.max(first, axis=1, keepdims=True), jnp.max(second, axis=1, keepdims=True)
+        )
+        first = jnp.exp(first - peak)
+        second = jnp.exp(second - peak)
+        weight_sum = jnp.sum(first, axis=1, keepdims=True) + jnp.sum(second, axis=1, keepdims=True)
+        weighted = dot(first.astype(BF16), own[total : 2 * total, :]) + dot(
+            second.astype(BF16), peer[total : 2 * total, :]
+        )
+        ctx_out[b] = (weighted / weight_sum).astype(BF16)
+
+
+def middle_kernel(places, *refs):
+    gathered = refs[: 4 * SEQ]
+    far_mine, far_other, ctx, own_x, halo_x, gain, middle_out, norm_out, context, weights, mid = refs[4 * SEQ :]
+    s, h, f, p = places[0], places[1], places[2], places[3]
+    rows = own_x.shape[0]
+    step = ctx.shape[1]
+    half = far_mine.shape[1]
+
+    def put(k, y, core, side, value):
+        at = (2 * (h ^ side) + (f ^ core)) * 2 * half + (p ^ y) * half
+        weights[s ^ k, pl.ds(aligned(at, half), half), :] = value
+
+    for k in range(SEQ):
+        for y in range(2):
+            for core in range(2):
+                put(k, y, core, 0, gathered[(k * 2 + y) * 2 + core][0])
+            put(k, y, 0, 1, far_mine[k * 2 + y])
+            put(k, y, 1, 1, far_other[k * 2 + y])
+    for g in range(2 * SEQ):
+        head = (g % 2) * SEQ + g // 2
+        context[:, head * HD : (head + 1) * HD] = ctx[g]
+    columns = weights.shape[2]
+    mid[0:rows, :] = own_x[...].astype(F32)
+    mid[rows:step, :] = halo_x[...].astype(F32)
+    for j in range(SEQ):
+        at = slice(j * columns, (j + 1) * columns)
+        mid[:, at] = mid[:, at] + dot(context[...], weights[j])
+    middle = mid[...]
+    middle_out[...] = middle[:rows]
+    norm_out[...] = layer_norm(middle, gain[...]).astype(BF16)
+
+
+def convolve_kernel(places, *refs):
+    gathered = refs[: 4 * SEQ]
+    own_n, peer_n, own_c, peer_c, middle, base_out, share_out = refs[4 * SEQ : 4 * SEQ + 7]
+    normed, w_value, w_gate, w_down, channel, padded, active = refs[4 * SEQ + 7 :]
+    s, h, f, p, valid_len = places[0], places[1], places[2], places[3], places[4]
+    half, columns = gathered[0].shape[1:]
+    step = own_n.shape[0]
+    rows = step - HALO
+    for k in range(SEQ):
+        for y in range(2):
+            for core in range(2):
+                stack = gathered[(k * 2 + y) * 2 + core]
+                at = pl.ds(aligned((s ^ k) * 2 * half + (p ^ y) * half, half), half)
+                w_value[f ^ core, at, :] = stack[1]
+                w_gate[f ^ core, at, :] = stack[2]
+                at = pl.ds(aligned((f ^ core) * 2 * half + (p ^ y) * half, half), half)
+                w_down[s ^ k, at, :] = stack[3]
+    channel[f] = own_c[...]
+    channel[1 - f] = peer_c[...]
+    normed[0:step, :] = own_n[...]
+    normed[step : 2 * step, :] = peer_n[...]
+    place = lax.broadcasted_iota(jnp.int32, (step, columns), 0)
+    offset = jnp.where(place < rows, place, jnp.where(place < rows + EDGE, place - rows - EDGE, place - EDGE))
+    for c in range(2):
+        x = normed[...]
+        value_part = dot(x, w_value[c])
+        gate_part = dot(x, w_gate[c])
+        gated = value_part * jax.nn.sigmoid(gate_part)
+        for b in range(2):
+            start = (4 * s + 2 * (h ^ b) + f) * rows
+            t = offset + start
+            kept = jnp.where((t >= 0) & (t < valid_len), gated[b * step : (b + 1) * step], 0.0)
+            kept = kept.astype(BF16).astype(F32)
+            padded[b, 8 : 8 + rows, :] = kept[:rows]
+            padded[b, 8 - EDGE : 8, :] = kept[rows : rows + EDGE]
+            padded[b, 8 + rows : 8 + rows + EDGE, :] = kept[rows + EDGE :]
+            depth_sum = channel[c, 0:1, :] * padded[b, 8 - EDGE : 8 - EDGE + rows, :]
+            for j in range(1, KERNEL):
+                low = 8 - EDGE + j
+                depth_sum = depth_sum + channel[c, j : j + 1, :] * padded[b, low : low + rows, :]
+            shifted = depth_sum * channel[c, KERNEL : KERNEL + 1, :] + channel[c, KERNEL + 1 : KERNEL + 2, :]
+            active[b * rows : (b + 1) * rows, c * columns : (c + 1) * columns] = (
+                shifted * jax.nn.sigmoid(shifted)
+            ).astype(BF16)
+    for j in range(SEQ):
+        at = slice(j * columns, (j + 1) * columns)
+        share = dot(active[...], w_down[j])
+        base_out[:, at] = middle[:, at] + share[:rows]
+        share_out[:, at] = share[rows:].astype(BF16)
+
+
+def shards_chip_per_head(
+    frames,
+    length,
+    ln1_gain,
+    w_query,
+    w_key,
+    w_value,
+    w_out,
+    ln2_gain,
+    pw1_value,
+    pw1_gate,
+    depth_kernel,
+    bn_scale,
+    bn_shift,
+    pw2,
+):
+    rows, width = frames.shape
+    count = 2 * SEQ
+    step = rows + HALO
+    s, h, f, p = (lax.axis_index(a) for a in ("seq", "head", "fsdp", "parts"))
+    places = jnp.stack([s, h, f, p, length[0]]).astype(jnp.int32)
+    half = w_query.shape[0] // 2
+    columns = w_query.shape[1]
+
+    def other_core(x):
+        return lax.ppermute(x, "fsdp", SWAP)
+
+    def other_side(x):
+        return lax.ppermute(x, "head", SWAP)
+
+    projectors = jnp.stack([w_query, w_key, w_value])
+    keep = lax.dynamic_slice_in_dim(projectors, f * half, half, axis=1)
+    give = lax.dynamic_slice_in_dim(projectors, (1 - f) * half, half, axis=1)
+    got = other_core(give)
+    low = jnp.where(f == 0, keep, got)
+    high = jnp.where(f == 0, got, keep)
+    by_head = jnp.stack([low[:, :, :HD], low[:, :, HD:], high[:, :, :HD], high[:, :, HD:]])
+    w_mine = lax.all_to_all(by_head, "seq", 0, 0, tiled=True)
+    w_other = other_core(w_mine)
+    blocks = []
+    for k in range(SEQ):
+        block = frames if k == 0 else lax.ppermute(frames, "seq", xor_pairs(k))
+        blocks += [block, other_side(block)]
+    stack = jnp.stack([w_out, pw1_value, pw1_gate, pw2])
+    stack = lax.dynamic_slice_in_dim(stack, p * half, half, axis=1)
+    gathered = []
+    for k in range(SEQ):
+        near = stack if k == 0 else lax.ppermute(stack, "seq", xor_pairs(k))
+        for part in (near, lax.ppermute(near, "parts", SWAP)):
+            gathered += [part, other_core(part)]
+    far_mine = other_side(jnp.stack([a[0] for a in gathered[::2]]))
+    far_other = other_core(far_mine)
+    channels = jnp.concatenate([depth_kernel, bn_scale[None], bn_shift[None], jnp.zeros((5, columns), F32)])
+    channels_peer = other_core(channels)
+
+    shape = jax.ShapeDtypeStruct
+    queries, send, edges = call(
+        project_kernel,
+        [
+            shape((count * rows, HD), BF16),
+            shape((2 * count * rows + count * HALO, HD), BF16),
+            shape((HALO, width), BF16),
+        ],
+        [
+            pltpu.VMEM((count * rows, width), BF16),
+            pltpu.VMEM((width, 3 * HD), BF16),
+            pltpu.VMEM((count, HALO, width), F32),
+            pltpu.VMEM((count, HALO, HD), F32),
+        ],
+        places,
+        *blocks,
+        ln1_gain[None],
+        w_mine,
+        w_other,
+        flops=6 * count * rows * width * HD,
+    )
+    received = other_core(send)
+    halo_x = other_core(edges)
+    (ctx,) = call(
+        attend_kernel,
+        [shape((count, step, HD), BF16)],
+        [pltpu.VMEM((count, step, HD), F32)],
+        places,
+        queries,
+        send,
+        received,
+        flops=8 * count * step * count * rows * HD,
+    )
+    ctx = lax.all_to_all(ctx, ("seq", "head"), 0, 0, tiled=True)
+    middle, normed = call(
+        middle_kernel,
+        [shape((rows, width), F32), shape((step, width), BF16)],
+        [
+            pltpu.VMEM((step, width), BF16),
+            pltpu.VMEM((SEQ, width, columns), BF16),
+            pltpu.VMEM((step, width), F32),
+        ],
+        places,
+        *gathered,
+        far_mine,
+        far_other,
+        ctx,
+        frames,
+        halo_x,
+        ln2_gain[None],
+        flops=2 * step * width * width,
+    )
+    base, share = call(
+        convolve_kernel,
+        [shape((rows, width), F32), shape((rows, width), BF16)],
+        [
+            pltpu.VMEM((2 * step, width), BF16),
+            pltpu.VMEM((2, width, columns), BF16),
+            pltpu.VMEM((2, width, columns), BF16),
+            pltpu.VMEM((SEQ, 2 * columns, columns), BF16),
+            pltpu.VMEM((2, 16, columns), F32),
+            pltpu.VMEM((2, 16 + rows, columns), F32),
+            pltpu.VMEM((2 * rows, 2 * columns), BF16),
+        ],
+        places,
+        *gathered,
+        normed,
+        other_side(normed),
+        channels,
+        channels_peer,
+        middle,
+        flops=6 * step * width * width,
+    )
+    return (base + other_side(share).astype(F32)).astype(BF16)
+
+
 def solution(mesh):
     in_specs = (
         P(("parts", "seq", "head", "fsdp"), None),
@@ -166,4 +492,5 @@
         P(("head", "fsdp"), "seq"),
     )
     out_specs = P(("parts", "seq", "head", "fsdp"), None)
-    return jax.shard_map(shards, mesh=mesh, in_specs=in_specs, out_specs=out_specs, check_vma=False)
+    body = shards_chip_per_head if one_head_per_chip(mesh) else shards_general
+    return jax.shard_map(body, mesh=mesh, in_specs=in_specs, out_specs=out_specs, check_vma=False)

time: 217 us -> 110 us (0.51)
  blocking collectives: 158 us -> 0 us
  starting transfers between devices: 5.23 us -> 34.2 us
  waiting for transfers between devices: 23 us -> 49.2 us
  between operations: 14.4 us -> 0.85 us
  local copies, waits for them, and re-layouts: 1.24 us -> 12.3 us
  Pallas kernels: 0 us -> 10.6 us
  other arithmetic: 9.78 us -> 2.74 us
  matrix products: 5.13 us -> 0 us
    all_gather x11 -> x0, blocking collectives: 158 us -> none  [the longest x1 16.9 us: shards(): lax.all_gather(pw2, 'seq', axis=1, tiled=True)]
    ppermute x2 -> x31, waiting for transfers between devices: 0.01 us -> 43.1 us  [the longest x7 14.1 us: other_side(): return lax.ppermute(x, 'head', SWAP)]
    reduce_scatter x2 -> x0, waiting for transfers between devices: 23 us -> none  [the longest x1 23 us: shards(): lax.psum_scatter(jnp.dot(active, down_rows, preferred_element_type=jnp.fl...]
    ppermute x2 -> x31, starting transfers between devices: 5.19 us -> 24.6 us  [the longest x3 6.97 us: shards_chip_per_head(): block = frames if k == 0 else lax.ppermute(frames, 'seq', xor_pairs(k))]
    unnamed x26 -> x45, local copies, waits for them, and re-layouts: 0.07 us -> 10.8 us
    pallas_call x0 -> x4, Pallas kernels: none -> 10.6 us  [call(): pl.pallas_call(kernel, out_shape=outs, in_specs=[pl.BlockSpec(memory_spac...]
    all_to_all x0 -> x2, starting transfers between devices: none -> 9.65 us  [the longest x1 4.87 us: shards_chip_per_head(): w_mine = lax.all_to_all(by_head, 'seq', 0, 0, tiled=True)]
    all_to_all x0 -> x2, waiting for transfers between devices: none -> 6.17 us  [the longest x1 6.17 us: shards_chip_per_head(): ctx = lax.all_to_all(ctx, ('seq', 'head'), 0, 0, tiled=True)]
  transfers between devices with their start and end apart: 4 -> 33, of which waited for: 1 -> 18; matrix products, arithmetic and copies ran while one was open for 0% -> 6% of each run, Pallas kernels for 0% -> 5%
where the time goes in v1:
time: 110 us
  waiting for transfers between devices  49.2 us (45%)
  starting transfers between devices  34.2 us (31%)
  local copies, waits for them, and re-layouts  12.3 us (11%)
  Pallas kernels  10.6 us (10%)
  other arithmetic  2.74 us (2%)
    ppermute x7, waiting for transfers between devices, other_side(): return lax.ppermute(x, 'head', SWAP)  14.1 us
    ppermute x3, waiting for transfers between devices, shards_chip_per_head(): near = stack if k == 0 else lax.ppermute(stack, 'seq', xor_pairs(k))  13.9 us
    unnamed x45, local copies, waits for them, and re-layouts  10.8 us
    pallas_call x4, Pallas kernels, call(): pl.pallas_call(kernel, out_shape=outs, in_specs=[pl.BlockSpec(memory_spac...  10.6 us
    ppermute x3, waiting for transfers between devices, shards_chip_per_head(): block = frames if k == 0 else lax.ppermute(frames, 'seq', xor_pairs(k))  7.33 us
    ppermute x3, starting transfers between devices, shards_chip_per_head(): block = frames if k == 0 else lax.ppermute(frames, 'seq', xor_pairs(k))  6.97 us
    all_to_all x1, waiting for transfers between devices, shards_chip_per_head(): ctx = lax.all_to_all(ctx, ('seq', 'head'), 0, 0, tiled=True)  6.17 us
    ppermute x7, starting transfers between devices, other_side(): return lax.ppermute(x, 'head', SWAP)  5.73 us
  transfers between devices with their start and end apart: 33, of which 18 were waited for; matrix products, arithmetic and copies ran while one was open for 6% of the time, Pallas kernels for 5%

profile of v1, /device:TPU:0, one launch (start us, length us, event | category | flops | bytes accessed | tf_op | source)
XLA Modules:
  0.0 110.0 jit_solution(350426972770374813)
XLA Ops:
  0.0 1.0 fusion.2.refs_0_
  1.0 3.0 %collective-permute-start.1 = (bf16[4,128,256]{2,1,0:T(8,128)(2,1)S(1)}, bf16[4,128,256]{2,1,0:T(8,128)(2,1)S(1)}, u32[]{:S(2)}, u32[]{:S(2)}) collective-permute-start(bf16[4,128,256]{2,1,0:T(8,128)(2,1)S(1)} %fusion.2.refs_0_), channel_id=1, source_target_pairs={{0,16},{16,0},{1,17},{17,1},{2,18},{18,2},{3,19},{19,3},{4,20},{20... | collective-permute-start | bytes 786440 | tf_op jit(solution)/shard_map/ppermute | solution.py:394
  4.1 1.6 %collective-permute-start.3 = (bf16[4,128,256]{2,1,0:T(8,128)(2,1)S(1)}, bf16[4,128,256]{2,1,0:T(8,128)(2,1)S(1)}, u32[]{:S(2)}, u32[]{:S(2)}) collective-permute-start(bf16[4,128,256]{2,1,0:T(8,128)(2,1)S(1)} %fusion.2.refs_0_), channel_id=1, source_target_pairs={{0,4},{4,0},{8,12},{12,8},{1,5},{5,1},{9,13},{13,9},{2,6},{6,2},{1... | collective-permute-start | bytes 786440 | tf_op jit(solution)/shard_map/ppermute | solution.py:393
  5.6 2.6 %collective-permute-start.7 = (bf16[4,128,256]{2,1,0:T(8,128)(2,1)S(1)}, bf16[4,128,256]{2,1,0:T(8,128)(2,1)S(1)}, u32[]{:S(2)}, u32[]{:S(2)}) collective-permute-start(bf16[4,128,256]{2,1,0:T(8,128)(2,1)S(1)} %fusion.2.refs_0_), channel_id=1, source_target_pairs={{0,8},{4,12},{8,0},{12,4},{1,9},{5,13},{9,1},{13,5},{2,10},{6,14},... | collective-permute-start | bytes 786440 | tf_op jit(solution)/shard_map/ppermute | solution.py:393
  11.1 4.9 %all-to-all-start = ((bf16[4,3,128,128]{3,2,1,0:T(8,128)(2,1)}), bf16[4,3,128,128]{3,2,1,0:T(8,128)(2,1)S(1)}, u32[]{:S(2)}, u32[]{:S(2)}) async-start(bf16[4,3,128,128]{3,2,1,0:T(8,128)(2,1)} %pad_maximum_fusion.1), calls=%async_computation | async-start | bytes 786432 | tf_op jit(solution)/shard_map/all_to_all | solution.py:383
  16.9 13.3 %collective-permute-done.7.refs_8_ = bf16[4,128,256]{2,1,0:T(8,128)(2,1)S(1)} collective-permute-done((bf16[4,128,256]{2,1,0:T(8,128)(2,1)S(1)}, bf16[4,128,256]{2,1,0:T(8,128)(2,1)S(1)}, u32[]{:S(2)}, u32[]{:S(2)}) %collective-permute-start.7) | collective-permute-done | bytes 262176 | tf_op jit(solution)/shard_map/ppermute | solution.py:393
  30.7 1.5 %collective-permute-start.13 = (bf16[4,128,256]{2,1,0:T(8,128)(2,1)S(1)}, bf16[4,128,256]{2,1,0:T(8,128)(2,1)S(1)}, u32[]{:S(2)}, u32[]{:S(2)}) collective-permute-start(bf16[4,128,256]{2,1,0:T(8,128)(2,1)S(1)} %collective-permute-done.11.refs_12_), channel_id=1, source_target_pairs={{0,16},{16,0},{1,17},{17,1},{2,18},{18,2},{3,19},{19,3},{4,20},{20... | collective-permute-start | bytes 786440 | tf_op jit(solution)/shard_map/ppermute | solution.py:394
  34.8 1.8 %collective-permute-done.9.refs_10_ = bf16[4,128,256]{2,1,0:T(8,128)(2,1)S(1)} collective-permute-done((bf16[4,128,256]{2,1,0:T(8,128)(2,1)S(1)}, bf16[4,128,256]{2,1,0:T(8,128)(2,1)S(1)}, u32[]{:S(2)}, u32[]{:S(2)}) %collective-permute-start.9) | collective-permute-done | bytes 262176 | tf_op jit(solution)/shard_map/ppermute | solution.py:394
  37.9 1.5 %collective-permute-done.13.refs_14_ = bf16[4,128,256]{2,1,0:T(8,128)(2,1)S(1)} collective-permute-done((bf16[4,128,256]{2,1,0:T(8,128)(2,1)S(1)}, bf16[4,128,256]{2,1,0:T(8,128)(2,1)S(1)}, u32[]{:S(2)}, u32[]{:S(2)}) %collective-permute-start.13) | collective-permute-done | bytes 262176 | tf_op jit(solution)/shard_map/ppermute | solution.py:394
  40.0 1.5 %collective-permute-start.15 = (bf16[8,128,256]{2,1,0:T(8,128)(2,1)}, bf16[8,128,256]{2,1,0:T(8,128)(2,1)}, u32[]{:S(2)}, u32[]{:S(2)}) collective-permute-start(bf16[8,128,256]{2,1,0:T(8,128)(2,1)} %slice_dynamic-update-slice_fusion), channel_id=1, source_target_pairs={{0,2},{2,0},{1,3},{3,1},{4,6},{6,4},{5,7},{7,5},{8,10},{10,8},{9,1... | collective-permute-start | bytes 1572872 | tf_op jit(solution)/shard_map/ppermute | solution.py:374
  41.5 4.4 %collective-permute-start.18 = (bf16[64,1024]{1,0:T(8,128)(2,1)S(1)}, bf16[64,1024]{1,0:T(8,128)(2,1)S(1)}, u32[]{:S(2)}, u32[]{:S(2)}) collective-permute-start(bf16[64,1024]{1,0:T(8,128)(2,1)S(1)} %copy-done), channel_id=1, source_target_pairs={{0,4},{4,0},{8,12},{12,8},{1,5},{5,1},{9,13},{13,9},{2,6},{6,2},{1... | collective-permute-start | bytes 393224 | tf_op jit(solution)/shard_map/ppermute | solution.py:387
  46.0 1.0 collective-permute-start.20
  47.0 1.5 %collective-permute-start.22 = (bf16[64,1024]{1,0:T(8,128)(2,1)S(1)}, bf16[64,1024]{1,0:T(8,128)(2,1)}, u32[]{:S(2)}, u32[]{:S(2)}) collective-permute-start(bf16[64,1024]{1,0:T(8,128)(2,1)S(1)} %copy-done), channel_id=1, source_target_pairs={{0,12},{4,8},{8,4},{12,0},{1,13},{5,9},{9,5},{13,1},{2,14},{6,10},... | collective-permute-start | bytes 393224 | tf_op jit(solution)/shard_map/ppermute | solution.py:387
  49.7 6.6 %collective-permute-done.20.refs_4_ = bf16[64,1024]{1,0:T(8,128)(2,1)S(1)} collective-permute-done((bf16[64,1024]{1,0:T(8,128)(2,1)S(1)}, bf16[64,1024]{1,0:T(8,128)(2,1)S(1)}, u32[]{:S(2)}, u32[]{:S(2)}) %collective-permute-start.20) | collective-permute-done | bytes 131104 | tf_op jit(solution)/shard_map/ppermute | solution.py:387
  57.6 1.5 %collective-permute-start.21 = (bf16[64,1024]{1,0:T(8,128)(2,1)S(1)}, bf16[64,1024]{1,0:T(8,128)(2,1)}, u32[]{:S(2)}, u32[]{:S(2)}) collective-permute-start(bf16[64,1024]{1,0:T(8,128)(2,1)S(1)} %collective-permute-done.20.refs_4_), channel_id=1, source_target_pairs={{0,2},{2,0},{1,3},{3,1},{4,6},{6,4},{5,7},{7,5},{8,10},{10,8},{9,1... | collective-permute-start | bytes 393224 | tf_op jit(solution)/shard_map/ppermute | solution.py:374
  59.1 3.0 %collective-permute-done.19.refs_3_ = bf16[64,1024]{1,0:T(8,128)(2,1)S(1)} collective-permute-done((bf16[64,1024]{1,0:T(8,128)(2,1)S(1)}, bf16[64,1024]{1,0:T(8,128)(2,1)S(1)}, u32[]{:S(2)}, u32[]{:S(2)}) %collective-permute-start.19) | collective-permute-done | bytes 131104 | tf_op jit(solution)/shard_map/ppermute | solution.py:374
  63.4 1.5 %collective-permute-done.21.refs_5_ = bf16[64,1024]{1,0:T(8,128)(2,1)} collective-permute-done((bf16[64,1024]{1,0:T(8,128)(2,1)S(1)}, bf16[64,1024]{1,0:T(8,128)(2,1)}, u32[]{:S(2)}, u32[]{:S(2)}) %collective-permute-start.21) | collective-permute-done | bytes 131104 | tf_op jit(solution)/shard_map/ppermute | solution.py:374
  65.0 3.0 %collective-permute-done.23.refs_7_ = bf16[64,1024]{1,0:T(8,128)(2,1)} collective-permute-done((bf16[64,1024]{1,0:T(8,128)(2,1)}, bf16[64,1024]{1,0:T(8,128)(2,1)}, u32[]{:S(2)}, u32[]{:S(2)}) %collective-permute-start.23) | collective-permute-done | bytes 131104 | tf_op jit(solution)/shard_map/ppermute | solution.py:374
  68.0 0.9 copy-done.4
  68.9 0.9 copy-done.6
  69.8 2.6 %shard_map.136 = (bf16[512,128]{1,0:T(8,128)(2,1)S(1)}, bf16[1088,128]{1,0:T(8,128)(2,1)S(1)}, bf16[8,1024]{1,0:T(8,128)(2,1)S(1)}) custom-call(s32[5]{0:T(128)S(1)} %stack.64.places, bf16[64,1024]{1,0:T(8,128)(2,1)S(1)} %copy-done, bf16[64,1024]{1,0:T(8,128)(2,1)S(1)} %copy-done.4, bf16[64,1024]{1,0:T(8,128)(2,1)S(1)} %collective-permute-done.18.refs_2_, ...), custom_call_target="tpu_custom_call" | custom-call | flops 402653184 | bytes 2265088 | tf_op jit(solution)/shard_map/pallas_call | solution.py:171
  74.1 0.8 collective-permute-done.12.refs_13_
  76.6 3.4 %shard_map.137 = bf16[8,72,128]{2,1,0:T(8,128)(2,1)S(1)} custom-call(s32[5]{0:T(128)S(1)} %stack.64.places, bf16[512,128]{1,0:T(8,128)(2,1)S(1)} %get-tuple-element.12.q_in, bf16[1088,128]{1,0:T(8,128)(2,1)S(1)} %get-tuple-element.13.own, bf16[1088,128]{1,0:T(8,128)(2,1)S(1)} %collective-permute-done.26.peer), custom_call_target="tpu_custom_call" | custom-call | flops 301989888 | bytes 835584 | tf_op jit(solution)/shard_map/pallas_call | solution.py:171
  80.6 4.8 %all-to-all-start.1 = ((bf16[8,72,128]{2,1,0:T(8,128)(2,1)}), bf16[8,72,128]{2,1,0:T(8,128)(2,1)}, u32[]{:S(2)}, u32[]{:S(2)}) async-start(bf16[8,72,128]{2,1,0:T(8,128)(2,1)} %copy-done.2), calls=%async_computation.1 | async-start | bytes 294912 | tf_op jit(solution)/shard_map/all_to_all | solution.py:434
  86.9 6.2 %all-to-all-done.1.refs_18_ = bf16[8,72,128]{2,1,0:T(8,128)(2,1)} async-done(((bf16[8,72,128]{2,1,0:T(8,128)(2,1)}), bf16[8,72,128]{2,1,0:T(8,128)(2,1)}, u32[]{:S(2)}, u32[]{:S(2)}) %all-to-all-start.1) | async-done | bytes 147488 | tf_op jit(solution)/shard_map/all_to_all | solution.py:434
  94.4 2.3 %shard_map.138 = (f32[64,1024]{1,0:T(8,128)S(1)}, bf16[72,1024]{1,0:T(8,128)(2,1)S(1)}) custom-call(s32[5]{0:T(128)S(1)} %copy-done.8, bf16[4,128,256]{2,1,0:T(8,128)(2,1)S(1)} %fusion.2.refs_0_, bf16[4,128,256]{2,1,0:T(8,128)(2,1)S(1)} %collective-permute-done.refs_1_, bf16[4,128,256]{2,1,0:T(8,128)(2,1)S(1)} %collective-permute-done.1.refs_2_, ...), custom_call_target="tpu_custom_call" | custom-call | flops 150994944 | bytes 5951488 | tf_op jit(solution)/shard_map/pallas_call | solution.py:171
  96.7 0.8 collective-permute-start.28
  98.4 1.2 %collective-permute-done.29.refs_19_ = f32[16,256]{1,0:T(8,128)S(1)} collective-permute-done((f32[16,256]{1,0:T(8,128)S(1)}, f32[16,256]{1,0:T(8,128)S(1)}, u32[]{:S(2)}, u32[]{:S(2)}) %collective-permute-start.29) | collective-permute-done | bytes 16416 | tf_op jit(solution)/shard_map/ppermute | solution.py:371
  99.5 2.4 %collective-permute-done.28.refs_17_ = bf16[72,1024]{1,0:T(8,128)(2,1)S(1)} collective-permute-done((bf16[72,1024]{1,0:T(8,128)(2,1)S(1)}, bf16[72,1024]{1,0:T(8,128)(2,1)S(1)}, u32[]{:S(2)}, u32[]{:S(2)}) %collective-permute-start.28) | collective-permute-done | bytes 147488 | tf_op jit(solution)/shard_map/ppermute | solution.py:374
  102.0 2.3 %shard_map.139 = (f32[64,1024]{1,0:T(8,128)S(1)}, bf16[64,1024]{1,0:T(8,128)(2,1)S(1)}) custom-call(s32[5]{0:T(128)S(1)} %copy-done.8, bf16[4,128,256]{2,1,0:T(8,128)(2,1)S(1)} %fusion.2.refs_0_, bf16[4,128,256]{2,1,0:T(8,128)(2,1)S(1)} %collective-permute-done.refs_1_, bf16[4,128,256]{2,1,0:T(8,128)(2,1)S(1)} %collective-permute-done.1.refs_2_, ...), custom_call_target="tpu_custom_call" | custom-call | flops 452984832 | bytes 5177344 | tf_op jit(solution)/shard_map/pallas_call | solution.py:171
  104.3 0.8 collective-permute-start.30
  105.1 4.2 %collective-permute-done.30 = bf16[64,1024]{1,0:T(8,128)(2,1)S(1)} collective-permute-done((bf16[64,1024]{1,0:T(8,128)(2,1)S(1)}, bf16[64,1024]{1,0:T(8,128)(2,1)S(1)}, u32[]{:S(2)}, u32[]{:S(2)}) %collective-permute-start.30) | collective-permute-done | bytes 131104 | tf_op jit(solution)/shard_map/ppermute | solution.py:374
  (95 shorter events, 20.1 us)
Async XLA Ops:
  1.0 31.2 %collective-permute-start.1 = (bf16[4,128,256]{2,1,0:T(8,128)(2,1)S(1)}, bf16[4,128,256]{2,1,0:T(8,128)(2,1)S(1)}, u32[]{:S(2)}, u32[]{:S(2)}) collective-permute-start(bf16[4,128,256]{2,1,0:T(8,128)(2,1)S(1)} %fusion.2.refs_0_), channel_id=1, source_target_pairs={{0,16},{16,0},{1,17},{17,1},{2,18},{18,2},{3,19},{19,3},{4,20},{20... | collective-permute-start | bytes 786440 | tf_op jit(solution)/shard_map/ppermute | solution.py:394
  4.1 12.5 %collective-permute-start.3 = (bf16[4,128,256]{2,1,0:T(8,128)(2,1)S(1)}, bf16[4,128,256]{2,1,0:T(8,128)(2,1)S(1)}, u32[]{:S(2)}, u32[]{:S(2)}) collective-permute-start(bf16[4,128,256]{2,1,0:T(8,128)(2,1)S(1)} %fusion.2.refs_0_), channel_id=1, source_target_pairs={{0,4},{4,0},{8,12},{12,8},{1,5},{5,1},{9,13},{13,9},{2,6},{6,2},{1... | collective-permute-start | bytes 786440 | tf_op jit(solution)/shard_map/ppermute | solution.py:393
  5.6 24.6 %collective-permute-start.7 = (bf16[4,128,256]{2,1,0:T(8,128)(2,1)S(1)}, bf16[4,128,256]{2,1,0:T(8,128)(2,1)S(1)}, u32[]{:S(2)}, u32[]{:S(2)}) collective-permute-start(bf16[4,128,256]{2,1,0:T(8,128)(2,1)S(1)} %fusion.2.refs_0_), channel_id=1, source_target_pairs={{0,8},{4,12},{8,0},{12,4},{1,9},{5,13},{9,1},{13,5},{2,10},{6,14},... | collective-permute-start | bytes 786440 | tf_op jit(solution)/shard_map/ppermute | solution.py:393
  8.2 22.5 %collective-permute-start.11 = (bf16[4,128,256]{2,1,0:T(8,128)(2,1)S(1)}, bf16[4,128,256]{2,1,0:T(8,128)(2,1)S(1)}, u32[]{:S(2)}, u32[]{:S(2)}) collective-permute-start(bf16[4,128,256]{2,1,0:T(8,128)(2,1)S(1)} %fusion.2.refs_0_), channel_id=1, source_target_pairs={{0,12},{4,8},{8,4},{12,0},{1,13},{5,9},{9,5},{13,1},{2,14},{6,10},... | collective-permute-start | bytes 786440 | tf_op jit(solution)/shard_map/ppermute | solution.py:393
  8.5 1.5 %collective-permute-start.24 = (bf16[3,128,256]{2,1,0:T(8,128)(2,1)S(1)}, bf16[3,128,256]{2,1,0:T(8,128)(2,1)S(1)}, u32[]{:S(2)}, u32[]{:S(2)}) collective-permute-start(bf16[3,128,256]{2,1,0:T(8,128)(2,1)S(1)} %constant_dynamic-slice_fusion), channel_id=1, source_target_pairs={{0,1},{1,0},{2,3},{3,2},{4,5},{5,4},{6,7},{7,6},{8,9},{9,8},{10,11... | collective-permute-start | bytes 589832 | tf_op jit(solution)/shard_map/ppermute | solution.py:371
  11.1 35.9 %all-to-all-start = ((bf16[4,3,128,128]{3,2,1,0:T(8,128)(2,1)}), bf16[4,3,128,128]{3,2,1,0:T(8,128)(2,1)S(1)}, u32[]{:S(2)}, u32[]{:S(2)}) async-start(bf16[4,3,128,128]{3,2,1,0:T(8,128)(2,1)} %pad_maximum_fusion.1), calls=%async_computation | async-start | bytes 786432 | tf_op jit(solution)/shard_map/all_to_all | solution.py:383
  16.5 17.0 %collective-permute-start.5 = (bf16[4,128,256]{2,1,0:T(8,128)(2,1)S(1)}, bf16[4,128,256]{2,1,0:T(8,128)(2,1)S(1)}, u32[]{:S(2)}, u32[]{:S(2)}) collective-permute-start(bf16[4,128,256]{2,1,0:T(8,128)(2,1)S(1)} %collective-permute-done.3.refs_4_), channel_id=1, source_target_pairs={{0,16},{16,0},{1,17},{17,1},{2,18},{18,2},{3,19},{19,3},{4,20},{20... | collective-permute-start | bytes 786440 | tf_op jit(solution)/shard_map/ppermute | solution.py:394
  30.2 6.4 %collective-permute-start.9 = (bf16[4,128,256]{2,1,0:T(8,128)(2,1)S(1)}, bf16[4,128,256]{2,1,0:T(8,128)(2,1)S(1)}, u32[]{:S(2)}, u32[]{:S(2)}) collective-permute-start(bf16[4,128,256]{2,1,0:T(8,128)(2,1)S(1)} %collective-permute-done.7.refs_8_), channel_id=1, source_target_pairs={{0,16},{16,0},{1,17},{17,1},{2,18},{18,2},{3,19},{19,3},{4,20},{20... | collective-permute-start | bytes 786440 | tf_op jit(solution)/shard_map/ppermute | solution.py:394
  30.7 8.7 %collective-permute-start.13 = (bf16[4,128,256]{2,1,0:T(8,128)(2,1)S(1)}, bf16[4,128,256]{2,1,0:T(8,128)(2,1)S(1)}, u32[]{:S(2)}, u32[]{:S(2)}) collective-permute-start(bf16[4,128,256]{2,1,0:T(8,128)(2,1)S(1)} %collective-permute-done.11.refs_12_), channel_id=1, source_target_pairs={{0,16},{16,0},{1,17},{17,1},{2,18},{18,2},{3,19},{19,3},{4,20},{20... | collective-permute-start | bytes 786440 | tf_op jit(solution)/shard_map/ppermute | solution.py:394
  40.0 34.0 %collective-permute-start.15 = (bf16[8,128,256]{2,1,0:T(8,128)(2,1)}, bf16[8,128,256]{2,1,0:T(8,128)(2,1)}, u32[]{:S(2)}, u32[]{:S(2)}) collective-permute-start(bf16[8,128,256]{2,1,0:T(8,128)(2,1)} %slice_dynamic-update-slice_fusion), channel_id=1, source_target_pairs={{0,2},{2,0},{1,3},{3,1},{4,6},{6,4},{5,7},{7,5},{8,10},{10,8},{9,1... | collective-permute-start | bytes 1572872 | tf_op jit(solution)/shard_map/ppermute | solution.py:374
  41.5 7.7 %collective-permute-start.18 = (bf16[64,1024]{1,0:T(8,128)(2,1)S(1)}, bf16[64,1024]{1,0:T(8,128)(2,1)S(1)}, u32[]{:S(2)}, u32[]{:S(2)}) collective-permute-start(bf16[64,1024]{1,0:T(8,128)(2,1)S(1)} %copy-done), channel_id=1, source_target_pairs={{0,4},{4,0},{8,12},{12,8},{1,5},{5,1},{9,13},{13,9},{2,6},{6,2},{1... | collective-permute-start | bytes 393224 | tf_op jit(solution)/shard_map/ppermute | solution.py:387
  46.0 10.4 %collective-permute-start.20 = (bf16[64,1024]{1,0:T(8,128)(2,1)S(1)}, bf16[64,1024]{1,0:T(8,128)(2,1)S(1)}, u32[]{:S(2)}, u32[]{:S(2)}) collective-permute-start(bf16[64,1024]{1,0:T(8,128)(2,1)S(1)} %copy-done), channel_id=1, source_target_pairs={{0,8},{4,12},{8,0},{12,4},{1,9},{5,13},{9,1},{13,5},{2,10},{6,14},... | collective-permute-start | bytes 393224 | tf_op jit(solution)/shard_map/ppermute | solution.py:387
  47.0 21.0 %collective-permute-start.25 = (bf16[4,3,128,128]{3,2,1,0:T(8,128)(2,1)S(1)}, bf16[4,3,128,128]{3,2,1,0:T(8,128)(2,1)S(1)}, u32[]{:S(2)}, u32[]{:S(2)}) collective-permute-start(bf16[4,3,128,128]{3,2,1,0:T(8,128)(2,1)S(1)} %all-to-all-done.refs_9_), channel_id=1, source_target_pairs={{0,1},{1,0},{2,3},{3,2},{4,5},{5,4},{6,7},{7,6},{8,9},{9,8},{10,11... | collective-permute-start | bytes 1179656 | tf_op jit(solution)/shard_map/ppermute | solution.py:371
  47.0 9.9 %collective-permute-start.22 = (bf16[64,1024]{1,0:T(8,128)(2,1)S(1)}, bf16[64,1024]{1,0:T(8,128)(2,1)}, u32[]{:S(2)}, u32[]{:S(2)}) collective-permute-start(bf16[64,1024]{1,0:T(8,128)(2,1)S(1)} %copy-done), channel_id=1, source_target_pairs={{0,12},{4,8},{8,4},{12,0},{1,13},{5,9},{9,5},{13,1},{2,14},{6,10},... | collective-permute-start | bytes 393224 | tf_op jit(solution)/shard_map/ppermute | solution.py:387
  49.2 7.7 %collective-permute-start.17 = (bf16[64,1024]{1,0:T(8,128)(2,1)S(1)}, bf16[64,1024]{1,0:T(8,128)(2,1)S(1)}, u32[]{:S(2)}, u32[]{:S(2)}) collective-permute-start(bf16[64,1024]{1,0:T(8,128)(2,1)S(1)} %copy-done), channel_id=1, source_target_pairs={{0,2},{2,0},{1,3},{3,1},{4,6},{6,4},{5,7},{7,5},{8,10},{10,8},{9,1... | collective-permute-start | bytes 393224 | tf_op jit(solution)/shard_map/ppermute | solution.py:374
  56.4 5.7 %collective-permute-start.19 = (bf16[64,1024]{1,0:T(8,128)(2,1)S(1)}, bf16[64,1024]{1,0:T(8,128)(2,1)S(1)}, u32[]{:S(2)}, u32[]{:S(2)}) collective-permute-start(bf16[64,1024]{1,0:T(8,128)(2,1)S(1)} %collective-permute-done.18.refs_2_), channel_id=1, source_target_pairs={{0,2},{2,0},{1,3},{3,1},{4,6},{6,4},{5,7},{7,5},{8,10},{10,8},{9,1... | collective-permute-start | bytes 393224 | tf_op jit(solution)/shard_map/ppermute | solution.py:374
  56.9 16.7 %collective-permute-start = (bf16[4,128,256]{2,1,0:T(8,128)(2,1)S(1)}, bf16[4,128,256]{2,1,0:T(8,128)(2,1)S(1)}, u32[]{:S(2)}, u32[]{:S(2)}) collective-permute-start(bf16[4,128,256]{2,1,0:T(8,128)(2,1)S(1)} %fusion.2.refs_0_), channel_id=1, source_target_pairs={{0,1},{1,0},{2,3},{3,2},{4,5},{5,4},{6,7},{7,6},{8,9},{9,8},{10,11... | collective-permute-start | bytes 786440 | tf_op jit(solution)/shard_map/ppermute | solution.py:371
  57.6 7.4 %collective-permute-start.21 = (bf16[64,1024]{1,0:T(8,128)(2,1)S(1)}, bf16[64,1024]{1,0:T(8,128)(2,1)}, u32[]{:S(2)}, u32[]{:S(2)}) collective-permute-start(bf16[64,1024]{1,0:T(8,128)(2,1)S(1)} %collective-permute-done.20.refs_4_), channel_id=1, source_target_pairs={{0,2},{2,0},{1,3},{3,1},{4,6},{6,4},{5,7},{7,5},{8,10},{10,8},{9,1... | collective-permute-start | bytes 393224 | tf_op jit(solution)/shard_map/ppermute | solution.py:374
  62.7 5.3 %collective-permute-start.23 = (bf16[64,1024]{1,0:T(8,128)(2,1)}, bf16[64,1024]{1,0:T(8,128)(2,1)}, u32[]{:S(2)}, u32[]{:S(2)}) collective-permute-start(bf16[64,1024]{1,0:T(8,128)(2,1)} %collective-permute-done.22.refs_6_), channel_id=1, source_target_pairs={{0,2},{2,0},{1,3},{3,1},{4,6},{6,4},{5,7},{7,5},{8,10},{10,8},{9,1... | collective-permute-start | bytes 393224 | tf_op jit(solution)/shard_map/ppermute | solution.py:374
  73.0 3.2 %collective-permute-start.26 = (bf16[1088,128]{1,0:T(8,128)(2,1)S(1)}, bf16[1088,128]{1,0:T(8,128)(2,1)S(1)}, u32[]{:S(2)}, u32[]{:S(2)}) collective-permute-start(bf16[1088,128]{1,0:T(8,128)(2,1)S(1)} %get-tuple-element.13.own), channel_id=1, source_target_pairs={{0,1},{1,0},{2,3},{3,2},{4,5},{5,4},{6,7},{7,6},{8,9},{9,8},{10,11... | collective-permute-start | bytes 835592 | tf_op jit(solution)/shard_map/ppermute | solution.py:371
  73.0 1.9 %collective-permute-start.12 = (bf16[4,128,256]{2,1,0:T(8,128)(2,1)S(1)}, bf16[4,128,256]{2,1,0:T(8,128)(2,1)S(1)}, u32[]{:S(2)}, u32[]{:S(2)}) collective-permute-start(bf16[4,128,256]{2,1,0:T(8,128)(2,1)S(1)} %collective-permute-done.11.refs_12_), channel_id=1, source_target_pairs={{0,1},{1,0},{2,3},{3,2},{4,5},{5,4},{6,7},{7,6},{8,9},{9,8},{10,11... | collective-permute-start | bytes 786440 | tf_op jit(solution)/shard_map/ppermute | solution.py:371
  73.6 1.8 %collective-permute-start.4 = (bf16[4,128,256]{2,1,0:T(8,128)(2,1)S(1)}, bf16[4,128,256]{2,1,0:T(8,128)(2,1)S(1)}, u32[]{:S(2)}, u32[]{:S(2)}) collective-permute-start(bf16[4,128,256]{2,1,0:T(8,128)(2,1)S(1)} %collective-permute-done.3.refs_4_), channel_id=1, source_target_pairs={{0,1},{1,0},{2,3},{3,2},{4,5},{5,4},{6,7},{7,6},{8,9},{9,8},{10,11... | collective-permute-start | bytes 786440 | tf_op jit(solution)/shard_map/ppermute | solution.py:371
  73.6 2.5 %collective-permute-start.8 = (bf16[4,128,256]{2,1,0:T(8,128)(2,1)S(1)}, bf16[4,128,256]{2,1,0:T(8,128)(2,1)S(1)}, u32[]{:S(2)}, u32[]{:S(2)}) collective-permute-start(bf16[4,128,256]{2,1,0:T(8,128)(2,1)S(1)} %collective-permute-done.7.refs_8_), channel_id=1, source_target_pairs={{0,1},{1,0},{2,3},{3,2},{4,5},{5,4},{6,7},{7,6},{8,9},{9,8},{10,11... | collective-permute-start | bytes 786440 | tf_op jit(solution)/shard_map/ppermute | solution.py:371
  74.1 12.8 %collective-permute-start.16 = (bf16[8,128,256]{2,1,0:T(8,128)(2,1)}, bf16[8,128,256]{2,1,0:T(8,128)(2,1)}, u32[]{:S(2)}, u32[]{:S(2)}) collective-permute-start(bf16[8,128,256]{2,1,0:T(8,128)(2,1)} %collective-permute-done.15.refs_16_), channel_id=1, source_target_pairs={{0,1},{1,0},{2,3},{3,2},{4,5},{5,4},{6,7},{7,6},{8,9},{9,8},{10,11... | collective-permute-start | bytes 1572872 | tf_op jit(solution)/shard_map/ppermute | solution.py:371
  75.0 10.4 %collective-permute-start.2 = (bf16[4,128,256]{2,1,0:T(8,128)(2,1)S(1)}, bf16[4,128,256]{2,1,0:T(8,128)(2,1)S(1)}, u32[]{:S(2)}, u32[]{:S(2)}) collective-permute-start(bf16[4,128,256]{2,1,0:T(8,128)(2,1)S(1)} %collective-permute-done.1.refs_2_), channel_id=1, source_target_pairs={{0,1},{1,0},{2,3},{3,2},{4,5},{5,4},{6,7},{7,6},{8,9},{9,8},{10,11... | collective-permute-start | bytes 786440 | tf_op jit(solution)/shard_map/ppermute | solution.py:371
  75.3 10.8 %collective-permute-start.10 = (bf16[4,128,256]{2,1,0:T(8,128)(2,1)S(1)}, bf16[4,128,256]{2,1,0:T(8,128)(2,1)}, u32[]{:S(2)}, u32[]{:S(2)}) collective-permute-start(bf16[4,128,256]{2,1,0:T(8,128)(2,1)S(1)} %collective-permute-done.9.refs_10_), channel_id=1, source_target_pairs={{0,1},{1,0},{2,3},{3,2},{4,5},{5,4},{6,7},{7,6},{8,9},{9,8},{10,11... | collective-permute-start | bytes 786440 | tf_op jit(solution)/shard_map/ppermute | solution.py:371
  76.1 10.1 %collective-permute-start.14 = (bf16[4,128,256]{2,1,0:T(8,128)(2,1)S(1)}, bf16[4,128,256]{2,1,0:T(8,128)(2,1)}, u32[]{:S(2)}, u32[]{:S(2)}) collective-permute-start(bf16[4,128,256]{2,1,0:T(8,128)(2,1)S(1)} %collective-permute-done.13.refs_14_), channel_id=1, source_target_pairs={{0,1},{1,0},{2,3},{3,2},{4,5},{5,4},{6,7},{7,6},{8,9},{9,8},{10,11... | collective-permute-start | bytes 786440 | tf_op jit(solution)/shard_map/ppermute | solution.py:371
  76.2 9.9 %collective-permute-start.6 = (bf16[4,128,256]{2,1,0:T(8,128)(2,1)S(1)}, bf16[4,128,256]{2,1,0:T(8,128)(2,1)}, u32[]{:S(2)}, u32[]{:S(2)}) collective-permute-start(bf16[4,128,256]{2,1,0:T(8,128)(2,1)S(1)} %collective-permute-done.5.refs_6_), channel_id=1, source_target_pairs={{0,1},{1,0},{2,3},{3,2},{4,5},{5,4},{6,7},{7,6},{8,9},{9,8},{10,11... | collective-permute-start | bytes 786440 | tf_op jit(solution)/shard_map/ppermute | solution.py:371
  80.6 12.4 %all-to-all-start.1 = ((bf16[8,72,128]{2,1,0:T(8,128)(2,1)}), bf16[8,72,128]{2,1,0:T(8,128)(2,1)}, u32[]{:S(2)}, u32[]{:S(2)}) async-start(bf16[8,72,128]{2,1,0:T(8,128)(2,1)} %copy-done.2), calls=%async_computation.1 | async-start | bytes 294912 | tf_op jit(solution)/shard_map/all_to_all | solution.py:434
  85.4 1.5 %collective-permute-start.27 = (bf16[8,1024]{1,0:T(8,128)(2,1)}, bf16[8,1024]{1,0:T(8,128)(2,1)S(1)}, u32[]{:S(2)}, u32[]{:S(2)}) collective-permute-start(bf16[8,1024]{1,0:T(8,128)(2,1)} %copy-done.11), channel_id=1, source_target_pairs={{0,1},{1,0},{2,3},{3,2},{4,5},{5,4},{6,7},{7,6},{8,9},{9,8},{10,11... | collective-permute-start | bytes 49160 | tf_op jit(solution)/shard_map/ppermute | solution.py:371
  96.7 5.2 %collective-permute-start.28 = (bf16[72,1024]{1,0:T(8,128)(2,1)S(1)}, bf16[72,1024]{1,0:T(8,128)(2,1)S(1)}, u32[]{:S(2)}, u32[]{:S(2)}) collective-permute-start(bf16[72,1024]{1,0:T(8,128)(2,1)S(1)} %get-tuple-element.15.refs_16_), channel_id=1, source_target_pairs={{0,2},{2,0},{1,3},{3,1},{4,6},{6,4},{5,7},{7,5},{8,10},{10,8},{9,1... | collective-permute-start | bytes 442376 | tf_op jit(solution)/shard_map/ppermute | solution.py:374
  104.3 5.0 %collective-permute-start.30 = (bf16[64,1024]{1,0:T(8,128)(2,1)S(1)}, bf16[64,1024]{1,0:T(8,128)(2,1)S(1)}, u32[]{:S(2)}, u32[]{:S(2)}) collective-permute-start(bf16[64,1024]{1,0:T(8,128)(2,1)S(1)} %get-tuple-element.18), channel_id=1, source_target_pairs={{0,2},{2,0},{1,3},{3,1},{4,6},{6,4},{5,7},{7,5},{8,10},{10,8},{9,1... | collective-permute-start | bytes 393224 | tf_op jit(solution)/shard_map/ppermute | solution.py:374
  (20 other events, 74.5 us)

commit v2 on v1

--- a/solution.py
+++ b/solution.py
@@ -166,7 +166,7 @@
     return [(i, i ^ k) for i in range(SEQ)]
 
 
-def call(kernel, outs, scratch, places, *operands, flops=0):
+def call(kernel, outs, scratch, length, *operands, flops=0, vmem=8):
     moved = sum(math.prod(a.shape) * a.dtype.itemsize for a in (*operands, *outs))
     return pl.pallas_call(
         kernel,
@@ -176,8 +176,8 @@
         out_specs=[pl.BlockSpec(memory_space=pltpu.VMEM)] * len(outs),
         scratch_shapes=scratch,
         cost_estimate=pl.CostEstimate(flops=flops, bytes_accessed=moved, transcendentals=0),
-        compiler_params=pltpu.CompilerParams(vmem_limit_bytes=40 << 20),
-    )(places, *operands)
+        compiler_params=pltpu.CompilerParams(vmem_limit_bytes=vmem << 20),
+    )(length, *operands)
 
 
 def aligned(value, to):
@@ -188,12 +188,17 @@
     return jnp.dot(a, b, preferred_element_type=F32)
 
 
-def project_kernel(places, *refs):
+def here():
+    return tuple(lax.axis_index(a) for a in ("seq", "head", "fsdp", "parts"))
+
+
+def project_kernel(length, *refs):
     blocks = refs[: 2 * SEQ]
-    gain, mine, other, q_out, send_out, edge_out, normed, weights, x_edge, q_edge = refs[2 * SEQ :]
-    s, h, f = places[0], places[1], places[2]
+    mine, other = refs[2 * SEQ : 3 * SEQ], refs[3 * SEQ : 4 * SEQ]
+    gain, q_out, send_out, edge_out, normed, weights, x_edge, q_edge = refs[4 * SEQ :]
+    s, h, f, _ = here()
     rows = blocks[0].shape[0]
-    half = mine.shape[2]
+    depth = mine[0].shape[1]
     gain_row = gain[...]
     for slot, block in enumerate(blocks):
         at = (s ^ (slot // 2)) * 2 + (h ^ (slot % 2))
@@ -201,12 +206,20 @@
         normed[pl.ds(aligned(at * rows, rows), rows), :] = layer_norm(x, gain_row).astype(BF16)
         x_edge[at, 0:EDGE, :] = x[:EDGE]
         x_edge[at, EDGE:HALO, :] = x[rows - EDGE :]
-    for source in range(SEQ):
-        for m in range(3):
-            columns = slice(m * HD, (m + 1) * HD)
-            at = source * 2 * half
-            weights[pl.ds(aligned(at + f * half, half), half), columns] = mine[source, m]
-            weights[pl.ds(aligned(at + (1 - f) * half, half), half), columns] = other[source, m]
+    def fill(pieces):
+        for k in range(SEQ):
+            at = pl.ds(aligned((s ^ k) * depth, depth), depth)
+            for m in range(3):
+                weights[at, m * HD : (m + 1) * HD] = pieces[k][m]
+
+    @pl.when(s // 2 == f)
+    def _():
+        fill(mine)
+
+    @pl.when(s // 2 != f)
+    def _():
+        fill(other)
+
     count = 2 * SEQ
     total = count * rows
     projected = dot(normed[...], weights[...])
@@ -224,15 +237,17 @@
 
     halos = jnp.concatenate([around(q_edge, b) for b in range(count)], axis=0)
     send_out[2 * total :, :] = halos.astype(BF16)
-    edge_out[...] = around(x_edge, s * 2 + h).astype(BF16)
-
-
-def attend_kernel(places, q_in, own, peer, ctx_out, q_rows):
-    f, valid_len = places[2], places[4]
-    count = ctx_out.shape[0]
+    edge_out[...] = jnp.concatenate([around(x_edge, s * 2 + b) for b in range(2)], axis=0).astype(BF16)
+
+
+def attend_kernel(length, q_in, own, peer, *refs):
+    ctx_outs, q_rows = refs[:SEQ], refs[SEQ]
+    s, _, f, _ = here()
+    valid_len = length[0]
+    count = q_rows.shape[0]
     total = q_in.shape[0]
     rows = total // count
-    step = ctx_out.shape[1]
+    step = q_rows.shape[1]
     local = lax.broadcasted_iota(jnp.int32, (step, total), 1)
     base = (local // rows) * (2 * rows) + local % rows
     keep_own = base + f * rows < valid_len
@@ -243,7 +258,8 @@
         q_rows[b, 0:rows, :] = q_in[b * rows : (b + 1) * rows, :].astype(F32)
         q_rows[b, rows:step, :] = peer[2 * total + b * HALO : 2 * total + (b + 1) * HALO, :].astype(F32)
     for b in range(count):
-        q = q_rows[b].astype(BF16)
+        k, side = b // 2, b % 2
+        q = q_rows[(s ^ k) * 2 + side].astype(BF16)
         first = lax.dot_general(q, own[0:total, :], keys_t, preferred_element_type=F32) * scale
         second = lax.dot_general(q, peer[0:total, :], keys_t, preferred_element_type=F32) * scale
         first = jnp.where(keep_own, first, -jnp.inf)
@@ -257,62 +273,55 @@
         weighted = dot(first.astype(BF16), own[total : 2 * total, :]) + dot(
             second.astype(BF16), peer[total : 2 * total, :]
         )
-        ctx_out[b] = (weighted / weight_sum).astype(BF16)
-
-
-def middle_kernel(places, *refs):
-    gathered = refs[: 4 * SEQ]
-    far_mine, far_other, ctx, own_x, halo_x, gain, middle_out, norm_out, context, weights, mid = refs[4 * SEQ :]
-    s, h, f, p = places[0], places[1], places[2], places[3]
-    rows = own_x.shape[0]
-    step = ctx.shape[1]
-    half = far_mine.shape[1]
-
-    def put(k, y, core, side, value):
-        at = (2 * (h ^ side) + (f ^ core)) * 2 * half + (p ^ y) * half
-        weights[s ^ k, pl.ds(aligned(at, half), half), :] = value
-
+        ctx_outs[k][side * step : (side + 1) * step, :] = (weighted / weight_sum).astype(BF16)
+
+
+def output_kernel(length, *refs):
+    pieces, ctx = refs[: 4 * SEQ], refs[4 * SEQ : 5 * SEQ]
+    share_out, send_out, context, weights = refs[5 * SEQ :]
+    s, h, f, p = here()
+    half, columns = pieces[0].shape
     for k in range(SEQ):
         for y in range(2):
             for core in range(2):
-                put(k, y, core, 0, gathered[(k * 2 + y) * 2 + core][0])
-            put(k, y, 0, 1, far_mine[k * 2 + y])
-            put(k, y, 1, 1, far_other[k * 2 + y])
-    for g in range(2 * SEQ):
-        head = (g % 2) * SEQ + g // 2
-        context[:, head * HD : (head + 1) * HD] = ctx[g]
-    columns = weights.shape[2]
-    mid[0:rows, :] = own_x[...].astype(F32)
-    mid[rows:step, :] = halo_x[...].astype(F32)
+                at = pl.ds(aligned((f ^ core) * 2 * half + (p ^ y) * half, half), half)
+                weights[s ^ k, at, :] = pieces[(k * 2 + y) * 2 + core][...]
+    for k in range(SEQ):
+        context[:, pl.ds(aligned((s ^ k) * HD, HD), HD)] = ctx[k][...]
     for j in range(SEQ):
         at = slice(j * columns, (j + 1) * columns)
-        mid[:, at] = mid[:, at] + dot(context[...], weights[j])
-    middle = mid[...]
-    middle_out[...] = middle[:rows]
-    norm_out[...] = layer_norm(middle, gain[...]).astype(BF16)
-
-
-def convolve_kernel(places, *refs):
-    gathered = refs[: 4 * SEQ]
-    own_n, peer_n, own_c, peer_c, middle, base_out, share_out = refs[4 * SEQ : 4 * SEQ + 7]
-    normed, w_value, w_gate, w_down, channel, padded, active = refs[4 * SEQ + 7 :]
-    s, h, f, p, valid_len = places[0], places[1], places[2], places[3], places[4]
-    half, columns = gathered[0].shape[1:]
-    step = own_n.shape[0]
-    rows = step - HALO
+        share = dot(context[...], weights[j])
+        share_out[:, at] = share
+        send_out[:, at] = share.astype(BF16)
+
+
+def convolve_kernel(length, *refs):
+    pieces = refs[: 4 * SEQ]
+    own_x, peer_x, halo_x, own_share, peer_share, gain, own_c, peer_c, base_out, share_out = refs[4 * SEQ : 4 * SEQ + 10]
+    mid, normed, w_value, w_gate, w_down, channel, padded, active, shares = refs[4 * SEQ + 10 :]
+    s, h, f, p = here()
+    valid_len = length[0]
+    half, columns = pieces[0].shape[1:]
+    rows = own_x.shape[0]
+    step = rows + HALO
     for k in range(SEQ):
         for y in range(2):
             for core in range(2):
-                stack = gathered[(k * 2 + y) * 2 + core]
+                stack = pieces[(k * 2 + y) * 2 + core]
                 at = pl.ds(aligned((s ^ k) * 2 * half + (p ^ y) * half, half), half)
-                w_value[f ^ core, at, :] = stack[1]
-                w_gate[f ^ core, at, :] = stack[2]
+                w_value[f ^ core, at, :] = stack[0]
+                w_gate[f ^ core, at, :] = stack[1]
                 at = pl.ds(aligned((f ^ core) * 2 * half + (p ^ y) * half, half), half)
-                w_down[s ^ k, at, :] = stack[3]
+                w_down[s ^ k, at, :] = stack[2]
     channel[f] = own_c[...]
     channel[1 - f] = peer_c[...]
-    normed[0:step, :] = own_n[...]
-    normed[step : 2 * step, :] = peer_n[...]
+    mid[pl.ds(aligned(h * step, 8), rows), :] = own_x[...].astype(F32)
+    mid[pl.ds(aligned((1 - h) * step, 8), rows), :] = peer_x[...].astype(F32)
+    for b in range(2):
+        mid[b * step + rows : (b + 1) * step, :] = halo_x[b * HALO : (b + 1) * HALO, :].astype(F32)
+    middle = mid[...] + (own_share[...] + peer_share[...].astype(F32))
+    mid[...] = middle
+    normed[...] = layer_norm(middle, gain[...]).astype(BF16)
     place = lax.broadcasted_iota(jnp.int32, (step, columns), 0)
     offset = jnp.where(place < rows, place, jnp.where(place < rows + EDGE, place - rows - EDGE, place - EDGE))
     for c in range(2):
@@ -321,8 +330,7 @@
         gate_part = dot(x, w_gate[c])
         gated = value_part * jax.nn.sigmoid(gate_part)
         for b in range(2):
-            start = (4 * s + 2 * (h ^ b) + f) * rows
-            t = offset + start
+            t = offset + (4 * s + 2 * b + f) * rows
             kept = jnp.where((t >= 0) & (t < valid_len), gated[b * step : (b + 1) * step], 0.0)
             kept = kept.astype(BF16).astype(F32)
             padded[b, 8 : 8 + rows, :] = kept[:rows]
@@ -337,10 +345,9 @@
                 shifted * jax.nn.sigmoid(shifted)
             ).astype(BF16)
     for j in range(SEQ):
-        at = slice(j * columns, (j + 1) * columns)
-        share = dot(active[...], w_down[j])
-        base_out[:, at] = middle[:, at] + share[:rows]
-        share_out[:, at] = share[rows:].astype(BF16)
+        shares[:, j * columns : (j + 1) * columns] = dot(active[...], w_down[j])
+    base_out[...] = mid[pl.ds(aligned(h * step, 8), rows), :] + shares[pl.ds(aligned(h * rows, rows), rows), :]
+    share_out[...] = shares[pl.ds(aligned((1 - h) * rows, rows), rows), :].astype(BF16)
 
 
 def shards_chip_per_head(
@@ -362,10 +369,10 @@
     rows, width = frames.shape
     count = 2 * SEQ
     step = rows + HALO
-    s, h, f, p = (lax.axis_index(a) for a in ("seq", "head", "fsdp", "parts"))
-    places = jnp.stack([s, h, f, p, length[0]]).astype(jnp.int32)
+    f, p = lax.axis_index("fsdp"), lax.axis_index("parts")
     half = w_query.shape[0] // 2
     columns = w_query.shape[1]
+    barrier = lax.optimization_barrier
 
     def other_core(x):
         return lax.ppermute(x, "fsdp", SWAP)
@@ -373,28 +380,46 @@
     def other_side(x):
         return lax.ppermute(x, "head", SWAP)
 
+    def other_part(x):
+        return lax.ppermute(x, "parts", SWAP)
+
+    def planes(x):
+        return [x] + [lax.ppermute(x, "seq", xor_pairs(k)) for k in range(1, SEQ)]
+
+    def part_half(x):
+        return lax.dynamic_slice_in_dim(x, p * half, half, axis=x.ndim - 2)
+
+    def spread(mine, others):
+        pieces = []
+        for near in (mine, *others):
+            for part in (near, other_part(near)):
+                pieces += [part, other_core(part)]
+        return pieces
+
+    near = planes(frames)
+    blocks = []
+    for block in near:
+        blocks += [block, other_side(block)]
+    s = lax.axis_index("seq")
     projectors = jnp.stack([w_query, w_key, w_value])
-    keep = lax.dynamic_slice_in_dim(projectors, f * half, half, axis=1)
-    give = lax.dynamic_slice_in_dim(projectors, (1 - f) * half, half, axis=1)
-    got = other_core(give)
-    low = jnp.where(f == 0, keep, got)
-    high = jnp.where(f == 0, got, keep)
-    by_head = jnp.stack([low[:, :, :HD], low[:, :, HD:], high[:, :, :HD], high[:, :, HD:]])
-    w_mine = lax.all_to_all(by_head, "seq", 0, 0, tiled=True)
-    w_other = other_core(w_mine)
-    blocks = []
-    for k in range(SEQ):
-        block = frames if k == 0 else lax.ppermute(frames, "seq", xor_pairs(k))
-        blocks += [block, other_side(block)]
-    stack = jnp.stack([w_out, pw1_value, pw1_gate, pw2])
-    stack = lax.dynamic_slice_in_dim(stack, p * half, half, axis=1)
-    gathered = []
-    for k in range(SEQ):
-        near = stack if k == 0 else lax.ppermute(stack, "seq", xor_pairs(k))
-        for part in (near, lax.ppermute(near, "parts", SWAP)):
-            gathered += [part, other_core(part)]
-    far_mine = other_side(jnp.stack([a[0] for a in gathered[::2]]))
-    far_other = other_core(far_mine)
+    even = lax.dynamic_slice_in_dim(projectors, (s % 2) * HD, HD, axis=2)
+    odd = lax.dynamic_slice_in_dim(projectors, (1 - s % 2) * HD, HD, axis=2)
+    w_mine = [even]
+    for k in range(1, SEQ):
+        pairs = [
+            (2 * i + core, 2 * (i ^ k) + core) for core in range(2) for i in range(SEQ) if (i ^ k) // 2 == core
+        ]
+        w_mine.append(lax.ppermute(odd if k % 2 else even, ("seq", "fsdp"), pairs))
+    to_other = [(2 * i + i // 2, 2 * i + 1 - i // 2) for i in range(SEQ)]
+    w_other = [lax.ppermute(w, ("seq", "fsdp"), to_other) for w in w_mine]
+
+    mine = part_half(w_out)
+    after, *_ = barrier((mine, *near[1:], *w_mine[1:]))
+    others = planes(after)[1:]
+    out_pieces = spread(mine, others)
+    mine = part_half(jnp.stack([pw1_value, pw1_gate, pw2]))
+    after, *_ = barrier((mine, *others))
+    pw_pieces = spread(mine, planes(after)[1:])
     channels = jnp.concatenate([depth_kernel, bn_scale[None], bn_shift[None], jnp.zeros((5, columns), F32)])
     channels_peer = other_core(channels)
 
@@ -404,7 +429,7 @@
         [
             shape((count * rows, HD), BF16),
             shape((2 * count * rows + count * HALO, HD), BF16),
-            shape((HALO, width), BF16),
+            shape((2 * HALO, width), BF16),
         ],
         [
             pltpu.VMEM((count * rows, width), BF16),
@@ -412,48 +437,43 @@
             pltpu.VMEM((count, HALO, width), F32),
             pltpu.VMEM((count, HALO, HD), F32),
         ],
-        places,
+        length,
         *blocks,
+        *w_mine,
+        *w_other,
         ln1_gain[None],
-        w_mine,
-        w_other,
         flops=6 * count * rows * width * HD,
     )
     received = other_core(send)
     halo_x = other_core(edges)
-    (ctx,) = call(
+    ctx = call(
         attend_kernel,
-        [shape((count, step, HD), BF16)],
+        [shape((2 * step, HD), BF16)] * SEQ,
         [pltpu.VMEM((count, step, HD), F32)],
-        places,
+        length,
         queries,
         send,
         received,
         flops=8 * count * step * count * rows * HD,
     )
-    ctx = lax.all_to_all(ctx, ("seq", "head"), 0, 0, tiled=True)
-    middle, normed = call(
-        middle_kernel,
-        [shape((rows, width), F32), shape((step, width), BF16)],
+    ctx = [ctx[0]] + [lax.ppermute(ctx[k], "seq", xor_pairs(k)) for k in range(1, SEQ)]
+    own_share, sent_share = call(
+        output_kernel,
+        [shape((2 * step, width), F32), shape((2 * step, width), BF16)],
         [
-            pltpu.VMEM((step, width), BF16),
-            pltpu.VMEM((SEQ, width, columns), BF16),
-            pltpu.VMEM((step, width), F32),
+            pltpu.VMEM((2 * step, SEQ * HD), BF16),
+            pltpu.VMEM((SEQ, 2 * columns, columns), BF16),
         ],
-        places,
-        *gathered,
-        far_mine,
-        far_other,
-        ctx,
-        frames,
-        halo_x,
-        ln2_gain[None],
+        length,
+        *out_pieces,
+        *ctx,
         flops=2 * step * width * width,
     )
     base, share = call(
         convolve_kernel,
         [shape((rows, width), F32), shape((rows, width), BF16)],
         [
+            pltpu.VMEM((2 * step, width), F32),
             pltpu.VMEM((2 * step, width), BF16),
             pltpu.VMEM((2, width, columns), BF16),
             pltpu.VMEM((2, width, columns), BF16),
@@ -461,15 +481,20 @@
             pltpu.VMEM((2, 16, columns), F32),
             pltpu.VMEM((2, 16 + rows, columns), F32),
             pltpu.VMEM((2 * rows, 2 * columns), BF16),
+            pltpu.VMEM((2 * rows, width), F32),
         ],
-        places,
-        *gathered,
-        normed,
-        other_side(normed),
+        length,
+        *pw_pieces,
+        frames,
+        blocks[1],
+        halo_x,
+        own_share,
+        other_side(sent_share),
+        ln2_gain[None],
         channels,
         channels_peer,
-        middle,
         flops=6 * step * width * width,
+        vmem=14,
     )
     return (base + other_side(share).astype(F32)).astype(BF16)
 

time: 110 us -> 95.5 us (0.87)
  starting transfers between devices: 34.2 us -> 50 us
  waiting for transfers between devices: 49.2 us -> 35.2 us
  local copies, waits for them, and re-layouts: 12.3 us -> 0.89 us
  Pallas kernels: 10.6 us -> 6.15 us
    ppermute x10 -> x27, starting transfers between devices: 16.8 us -> 39.8 us  [the longest x9 12.2 us: planes(): return [x] + [lax.ppermute(x, 'seq', xor_pairs(k)) for k in range(1, SEQ)]]
    unnamed x45 -> x22, local copies, waits for them, and re-layouts: 10.8 us -> 0.74 us
    all_to_all x2 -> x0, starting transfers between devices: 9.65 us -> none  [the longest x1 4.87 us: shards_chip_per_head(): w_mine = lax.all_to_all(by_head, 'seq', 0, 0, tiled=True)]
    ppermute x7 -> x6, waiting for transfers between devices: 14.1 us -> 6.2 us  [other_side(): return lax.ppermute(x, 'head', SWAP)]
    all_to_all x2 -> x0, waiting for transfers between devices: 6.17 us -> none  [the longest x1 6.17 us: shards_chip_per_head(): ctx = lax.all_to_all(ctx, ('seq', 'head'), 0, 0, tiled=True)]
    pallas_call x4, Pallas kernels: 10.6 us -> 6.15 us  [call(): pl.pallas_call(kernel, out_shape=outs, in_specs=[pl.BlockSpec(memory_spac...]
    another operation x2 -> x1, other arithmetic: 1.83 us -> 0.02 us  [shards_chip_per_head(): mine = part_half(jnp.stack([pw1_value, pw1_gate, pw2]))]
    ppermute x14 -> x19, starting transfers between devices: 2.04 us -> 3.32 us  [other_core(): return lax.ppermute(x, 'fsdp', SWAP)]
  transfers between devices with their start and end apart: 33 -> 52, of which waited for: 18 -> 20; matrix products, arithmetic and copies ran while one was open for 6% -> 1% of each run, Pallas kernels for 5% -> 5%
where the time goes in v2:
time: 95.5 us; the launch traced here: 95.2 us
  starting transfers between devices  50 us (52%)
  waiting for transfers between devices  35.2 us (37%)
  Pallas kernels  6.15 us (6%)
  other arithmetic  1.83 us (2%)
  between operations  1.05 us (1%)
    ppermute x9, waiting for transfers between devices, planes(): return [x] + [lax.ppermute(x, 'seq', xor_pairs(k)) for k in range(1, SEQ)]  14.8 us
    ppermute x9, starting transfers between devices, planes(): return [x] + [lax.ppermute(x, 'seq', xor_pairs(k)) for k in range(1, SEQ)]  12.2 us
    ppermute x4, starting transfers between devices, shards_chip_per_head(): w_other = [lax.ppermute(w, ('seq', 'fsdp'), to_other) for w in w_mine]  9.57 us
    ppermute x8, starting transfers between devices, other_part(): return lax.ppermute(x, 'parts', SWAP)  7.37 us
    ppermute x6, starting transfers between devices, other_side(): return lax.ppermute(x, 'head', SWAP)  6.85 us
    ppermute x6, waiting for transfers between devices, other_side(): return lax.ppermute(x, 'head', SWAP)  6.2 us
    pallas_call x4, Pallas kernels, call(): pl.pallas_call(kernel, out_shape=outs, in_specs=[pl.BlockSpec(memory_spac...  6.15 us
    ppermute x8, waiting for transfers between devices, other_part(): return lax.ppermute(x, 'parts', SWAP)  6.06 us
  transfers between devices with their start and end apart: 52, of which 20 were waited for; matrix products, arithmetic and copies ran while one was open for 1% of the time, Pallas kernels for 5%

profile of v2, /device:TPU:0, one launch (start us, length us, event | category | flops | bytes accessed | tf_op | source)
XLA Modules:
  0.0 95.2 jit_solution(3474620422305145292)
XLA Ops:
  0.0 3.0 %collective-permute-start.3 = (bf16[64,1024]{1,0:T(8,128)(2,1)}, bf16[64,1024]{1,0:T(8,128)(2,1)S(1)}, u32[]{:S(2)}, u32[]{:S(2)}) collective-permute-start(bf16[64,1024]{1,0:T(8,128)(2,1)} %refs_16_.1), channel_id=1, source_target_pairs={{0,4},{4,0},{8,12},{12,8},{1,5},{5,1},{9,13},{13,9},{2,6},{6,2},{1... | collective-permute-start | bytes 393224 | tf_op jit(solution)/shard_map/ppermute | solution.py:387
  3.0 2.6 %collective-permute-start.4 = (bf16[64,1024]{1,0:T(8,128)(2,1)}, bf16[64,1024]{1,0:T(8,128)(2,1)S(1)}, u32[]{:S(2)}, u32[]{:S(2)}) collective-permute-start(bf16[64,1024]{1,0:T(8,128)(2,1)} %refs_16_.1), channel_id=1, source_target_pairs={{0,8},{4,12},{8,0},{12,4},{1,9},{5,13},{9,1},{13,5},{2,10},{6,14},... | collective-permute-start | bytes 393224 | tf_op jit(solution)/shard_map/ppermute | solution.py:387
  5.6 1.8 %collective-permute-start.34 = (bf16[128,256]{1,0:T(8,128)(2,1)S(1)}, bf16[128,256]{1,0:T(8,128)(2,1)S(1)}, u32[]{:S(2)}, u32[]{:S(2)}) collective-permute-start(bf16[128,256]{1,0:T(8,128)(2,1)S(1)} %constant_dynamic-slice_fusion.2.refs_0_), channel_id=1, source_target_pairs={{0,16},{16,0},{1,17},{17,1},{2,18},{18,2},{3,19},{19,3},{4,20},{20... | collective-permute-start | bytes 196616 | tf_op jit(solution)/shard_map/ppermute | solution.py:384
  9.5 1.5 %collective-permute-start.24 = (bf16[64,1024]{1,0:T(8,128)(2,1)S(1)}, bf16[64,1024]{1,0:T(8,128)(2,1)S(1)}, u32[]{:S(2)}, u32[]{:S(2)}) collective-permute-start(bf16[64,1024]{1,0:T(8,128)(2,1)S(1)} %copy-done.1), channel_id=1, source_target_pairs={{0,2},{2,0},{1,3},{3,1},{4,6},{6,4},{5,7},{7,5},{8,10},{10,8},{9,1... | collective-permute-start | bytes 393224 | tf_op jit(solution)/shard_map/ppermute | solution.py:381
  12.3 2.6 %collective-permute-start.6 = (bf16[3,256,128]{2,1,0:T(8,128)(2,1)S(1)}, bf16[3,256,128]{2,1,0:T(8,128)(2,1)S(1)}, u32[]{:S(2)}, u32[]{:S(2)}) collective-permute-start(bf16[3,256,128]{2,1,0:T(8,128)(2,1)S(1)} %get-tuple-element.32), channel_id=1, source_target_pairs={{0,4},{4,0},{9,13},{13,9},{2,6},{6,2},{11,15},{15,11},{16,20},{20,... | collective-permute-start | bytes 589832 | tf_op jit(solution)/shard_map/ppermute | solution.py:412
  14.9 1.3 %collective-permute-start.7 = (bf16[3,256,128]{2,1,0:T(8,128)(2,1)S(1)}, bf16[3,256,128]{2,1,0:T(8,128)(2,1)S(1)}, u32[]{:S(2)}, u32[]{:S(2)}) collective-permute-start(bf16[3,256,128]{2,1,0:T(8,128)(2,1)S(1)} %get-tuple-element.31.refs_8_), channel_id=1, source_target_pairs={{8,0},{12,4},{1,9},{5,13},{10,2},{14,6},{3,11},{7,15},{24,16},{28,... | collective-permute-start | bytes 589832 | tf_op jit(solution)/shard_map/ppermute | solution.py:412
  17.5 5.7 %collective-permute-start.28 = (bf16[3,256,128]{2,1,0:T(8,128)(2,1)S(1)}, bf16[3,256,128]{2,1,0:T(8,128)(2,1)S(1)}, u32[]{:S(2)}, u32[]{:S(2)}) collective-permute-start(bf16[3,256,128]{2,1,0:T(8,128)(2,1)S(1)} %get-tuple-element.31.refs_8_), channel_id=1, source_target_pairs={{0,1},{4,5},{9,8},{13,12},{2,3},{6,7},{11,10},{15,14},{16,17},{20,... | collective-permute-start | bytes 589832 | tf_op jit(solution)/shard_map/ppermute | solution.py:414
  25.2 2.4 %collective-permute-done.7.refs_10_ = bf16[3,256,128]{2,1,0:T(8,128)(2,1)S(1)} collective-permute-done((bf16[3,256,128]{2,1,0:T(8,128)(2,1)S(1)}, bf16[3,256,128]{2,1,0:T(8,128)(2,1)S(1)}, u32[]{:S(2)}, u32[]{:S(2)}) %collective-permute-start.7) | collective-permute-done | bytes 196640 | tf_op jit(solution)/shard_map/ppermute | solution.py:412
  28.2 1.4 %collective-permute-start.26 = (bf16[64,1024]{1,0:T(8,128)(2,1)S(1)}, bf16[64,1024]{1,0:T(8,128)(2,1)S(1)}, u32[]{:S(2)}, u32[]{:S(2)}) collective-permute-start(bf16[64,1024]{1,0:T(8,128)(2,1)S(1)} %collective-permute-done.4.refs_4_), channel_id=1, source_target_pairs={{0,2},{2,0},{1,3},{3,1},{4,6},{6,4},{5,7},{7,5},{8,10},{10,8},{9,1... | collective-permute-start | bytes 393224 | tf_op jit(solution)/shard_map/ppermute | solution.py:381
  32.8 1.3 %collective-permute-start.30 = (bf16[3,256,128]{2,1,0:T(8,128)(2,1)S(1)}, bf16[3,256,128]{2,1,0:T(8,128)(2,1)S(1)}, u32[]{:S(2)}, u32[]{:S(2)}) collective-permute-start(bf16[3,256,128]{2,1,0:T(8,128)(2,1)S(1)} %collective-permute-done.7.refs_10_), channel_id=1, source_target_pairs={{0,1},{4,5},{9,8},{13,12},{2,3},{6,7},{11,10},{15,14},{16,17},{20,... | collective-permute-start | bytes 589832 | tf_op jit(solution)/shard_map/ppermute | solution.py:414
  34.1 1.3 %collective-permute-start.31 = (bf16[3,256,128]{2,1,0:T(8,128)(2,1)S(1)}, bf16[3,256,128]{2,1,0:T(8,128)(2,1)S(1)}, u32[]{:S(2)}, u32[]{:S(2)}) collective-permute-start(bf16[3,256,128]{2,1,0:T(8,128)(2,1)S(1)} %collective-permute-done.8.refs_11_), channel_id=1, source_target_pairs={{0,1},{4,5},{9,8},{13,12},{2,3},{6,7},{11,10},{15,14},{16,17},{20,... | collective-permute-start | bytes 589832 | tf_op jit(solution)/shard_map/ppermute | solution.py:414
  37.5 2.9 %collective-permute-done.9.refs_4_ = bf16[128,256]{1,0:T(8,128)(2,1)S(1)} collective-permute-done((bf16[128,256]{1,0:T(8,128)(2,1)S(1)}, bf16[128,256]{1,0:T(8,128)(2,1)S(1)}, u32[]{:S(2)}, u32[]{:S(2)}) %collective-permute-start.9) | collective-permute-done | bytes 65568 | tf_op jit(solution)/shard_map/ppermute | solution.py:387
  41.3 2.5 %collective-permute-done.10.refs_8_ = bf16[128,256]{1,0:T(8,128)(2,1)S(1)} collective-permute-done((bf16[128,256]{1,0:T(8,128)(2,1)S(1)}, bf16[128,256]{1,0:T(8,128)(2,1)S(1)}, u32[]{:S(2)}, u32[]{:S(2)}) %collective-permute-start.10) | collective-permute-done | bytes 65568 | tf_op jit(solution)/shard_map/ppermute | solution.py:387
  44.5 2.0 %collective-permute-done.11.refs_12_ = bf16[128,256]{1,0:T(8,128)(2,1)S(1)} collective-permute-done((bf16[128,256]{1,0:T(8,128)(2,1)S(1)}, bf16[128,256]{1,0:T(8,128)(2,1)S(1)}, u32[]{:S(2)}, u32[]{:S(2)}) %collective-permute-start.11) | collective-permute-done | bytes 65568 | tf_op jit(solution)/shard_map/ppermute | solution.py:387
  49.8 1.5 %shard_map.136 = (bf16[512,128]{1,0:T(8,128)(2,1)S(1)}, bf16[1088,128]{1,0:T(8,128)(2,1)S(1)}, bf16[16,1024]{1,0:T(8,128)(2,1)S(1)}) custom-call(s32[1]{0:T(128)S(6)} %copy.15.length, bf16[64,1024]{1,0:T(8,128)(2,1)S(1)} %copy-done.1, bf16[64,1024]{1,0:T(8,128)(2,1)S(1)} %collective-permute-done.24.refs_1_.refs_17_, ...), custom_call_target="tpu_custom_call" | custom-call | flops 402653184 | bytes 3067904 | tf_op jit(solution)/shard_map/pallas_call | solution.py:171
  51.9 1.3 %collective-permute-done.43.refs_14_ = bf16[128,256]{1,0:T(8,128)(2,1)S(1)} collective-permute-done((bf16[128,256]{1,0:T(8,128)(2,1)S(1)}, bf16[128,256]{1,0:T(8,128)(2,1)S(1)}, u32[]{:S(2)}, u32[]{:S(2)}) %collective-permute-start.43) | collective-permute-done | bytes 65568 | tf_op jit(solution)/shard_map/ppermute | solution.py:384
  54.6 2.6 %collective-permute-start.16 = (bf16[3,128,256]{2,1,0:T(8,128)(2,1)S(1)}, bf16[3,128,256]{2,1,0:T(8,128)(2,1)S(1)}, u32[]{:S(2)}, u32[]{:S(2)}) collective-permute-start(bf16[3,128,256]{2,1,0:T(8,128)(2,1)S(1)} %fusion.1.refs_0_), channel_id=1, source_target_pairs={{0,8},{4,12},{8,0},{12,4},{1,9},{5,13},{9,1},{13,5},{2,10},{6,14},... | collective-permute-start | bytes 589832 | tf_op jit(solution)/shard_map/ppermute | solution.py:387
  57.3 1.4 %collective-permute-start.20 = (bf16[3,128,256]{2,1,0:T(8,128)(2,1)S(1)}, bf16[3,128,256]{2,1,0:T(8,128)(2,1)S(1)}, u32[]{:S(2)}, u32[]{:S(2)}) collective-permute-start(bf16[3,128,256]{2,1,0:T(8,128)(2,1)S(1)} %fusion.1.refs_0_), channel_id=1, source_target_pairs={{0,12},{4,8},{8,4},{12,0},{1,13},{5,9},{9,5},{13,1},{2,14},{6,10},... | collective-permute-start | bytes 589832 | tf_op jit(solution)/shard_map/ppermute | solution.py:387
  58.6 4.9 %collective-permute-done.12.refs_4_ = bf16[3,128,256]{2,1,0:T(8,128)(2,1)S(1)} collective-permute-done((bf16[3,128,256]{2,1,0:T(8,128)(2,1)S(1)}, bf16[3,128,256]{2,1,0:T(8,128)(2,1)S(1)}, u32[]{:S(2)}, u32[]{:S(2)}) %collective-permute-start.12) | collective-permute-done | bytes 196640 | tf_op jit(solution)/shard_map/ppermute | solution.py:387
  63.7 2.8 %shard_map.137 = (bf16[144,128]{1,0:T(8,128)(2,1)S(1)}, bf16[144,128]{1,0:T(8,128)(2,1)S(1)}, bf16[144,128]{1,0:T(8,128)(2,1)S(1)}, bf16[144,128]{1,0:T(8,128)(2,1)S(1)}) custom-call(s32[1]{0:T(128)S(6)} %copy.15.length, bf16[512,128]{1,0:T(8,128)(2,1)S(1)} %get-tuple-element.21.q_in, bf16[1088,128]{1,0:T(8,128)(2,1)S(1)} %get-tuple-element.22.own, ...), custom_call_target="tpu_custom_call" | custom-call | flops 301989888 | bytes 835584 | tf_op jit(solution)/shard_map/pallas_call | solution.py:171
  66.6 2.6 %collective-permute-start.47 = (bf16[144,128]{1,0:T(8,128)(2,1)S(1)}, bf16[144,128]{1,0:T(8,128)(2,1)S(1)}, u32[]{:S(2)}, u32[]{:S(2)}) collective-permute-start(bf16[144,128]{1,0:T(8,128)(2,1)S(1)} %get-tuple-element.25), channel_id=1, source_target_pairs={{0,8},{4,12},{8,0},{12,4},{1,9},{5,13},{9,1},{13,5},{2,10},{6,14},... | collective-permute-start | bytes 110600 | tf_op jit(solution)/shard_map/ppermute | solution.py:459
  69.2 2.5 %collective-permute-done.16.refs_8_ = bf16[3,128,256]{2,1,0:T(8,128)(2,1)S(1)} collective-permute-done((bf16[3,128,256]{2,1,0:T(8,128)(2,1)S(1)}, bf16[3,128,256]{2,1,0:T(8,128)(2,1)S(1)}, u32[]{:S(2)}, u32[]{:S(2)}) %collective-permute-start.16) | collective-permute-done | bytes 196640 | tf_op jit(solution)/shard_map/ppermute | solution.py:387
  71.7 2.8 %collective-permute-start.48 = (bf16[144,128]{1,0:T(8,128)(2,1)S(1)}, bf16[144,128]{1,0:T(8,128)(2,1)S(1)}, u32[]{:S(2)}, u32[]{:S(2)}) collective-permute-start(bf16[144,128]{1,0:T(8,128)(2,1)S(1)} %get-tuple-element.26), channel_id=1, source_target_pairs={{0,12},{4,8},{8,4},{12,0},{1,13},{5,9},{9,5},{13,1},{2,14},{6,10},... | collective-permute-start | bytes 110600 | tf_op jit(solution)/shard_map/ppermute | solution.py:459
  74.6 2.0 %collective-permute-start.22 = (bf16[3,128,256]{2,1,0:T(8,128)(2,1)S(1)}, bf16[3,128,256]{2,1,0:T(8,128)(2,1)S(1)}, u32[]{:S(2)}, u32[]{:S(2)}) collective-permute-start(bf16[3,128,256]{2,1,0:T(8,128)(2,1)S(1)} %collective-permute-done.20.refs_12_), channel_id=1, source_target_pairs={{0,16},{16,0},{1,17},{17,1},{2,18},{18,2},{3,19},{19,3},{4,20},{20... | collective-permute-start | bytes 589832 | tf_op jit(solution)/shard_map/ppermute | solution.py:384
  76.6 1.5 %collective-permute-done.47.refs_18_ = bf16[144,128]{1,0:T(8,128)(2,1)S(1)} collective-permute-done((bf16[144,128]{1,0:T(8,128)(2,1)S(1)}, bf16[144,128]{1,0:T(8,128)(2,1)S(1)}, u32[]{:S(2)}, u32[]{:S(2)}) %collective-permute-start.47) | collective-permute-done | bytes 36896 | tf_op jit(solution)/shard_map/ppermute | solution.py:459
  79.1 1.3 %collective-permute-start.49 = (bf16[144,1024]{1,0:T(8,128)(2,1)S(1)}, bf16[144,1024]{1,0:T(8,128)(2,1)S(1)}, u32[]{:S(2)}, u32[]{:S(2)}) collective-permute-start(bf16[144,1024]{1,0:T(8,128)(2,1)S(1)} %get-tuple-element.28), channel_id=1, source_target_pairs={{0,2},{2,0},{1,3},{3,1},{4,6},{6,4},{5,7},{7,5},{8,10},{10,8},{9,1... | collective-permute-start | bytes 884744 | tf_op jit(solution)/shard_map/ppermute | solution.py:381
  80.4 1.4 %collective-permute-done.18.refs_10_ = bf16[3,128,256]{2,1,0:T(8,128)(2,1)S(1)} collective-permute-done((bf16[3,128,256]{2,1,0:T(8,128)(2,1)S(1)}, bf16[3,128,256]{2,1,0:T(8,128)(2,1)S(1)}, u32[]{:S(2)}, u32[]{:S(2)}) %collective-permute-start.18) | collective-permute-done | bytes 196640 | tf_op jit(solution)/shard_map/ppermute | solution.py:384
  81.8 2.1 %collective-permute-done.22.refs_14_ = bf16[3,128,256]{2,1,0:T(8,128)(2,1)S(1)} collective-permute-done((bf16[3,128,256]{2,1,0:T(8,128)(2,1)S(1)}, bf16[3,128,256]{2,1,0:T(8,128)(2,1)S(1)}, u32[]{:S(2)}, u32[]{:S(2)}) %collective-permute-start.22) | collective-permute-done | bytes 196640 | tf_op jit(solution)/shard_map/ppermute | solution.py:384
  85.9 2.2 %collective-permute-done.49.refs_20_ = bf16[144,1024]{1,0:T(8,128)(2,1)S(1)} collective-permute-done((bf16[144,1024]{1,0:T(8,128)(2,1)S(1)}, bf16[144,1024]{1,0:T(8,128)(2,1)S(1)}, u32[]{:S(2)}, u32[]{:S(2)}) %collective-permute-start.49) | collective-permute-done | bytes 294944 | tf_op jit(solution)/shard_map/ppermute | solution.py:381
  88.1 1.4 %shard_map.139 = (f32[64,1024]{1,0:T(8,128)S(1)}, bf16[64,1024]{1,0:T(8,128)(2,1)S(1)}) custom-call(s32[1]{0:T(128)S(6)} %copy.15.length, bf16[3,128,256]{2,1,0:T(8,128)(2,1)S(1)} %fusion.1.refs_0_, bf16[3,128,256]{2,1,0:T(8,128)(2,1)S(1)} %collective-permute-done.refs_1_, bf16[3,128,256]{2,1,0:T(8,128)(2,1)S(1)} %collective-permute-done.1.refs_2_, ...), custom_call_target="tpu_custom_call" | custom-call | flops 452984832 | bytes 4755456 | tf_op jit(solution)/shard_map/pallas_call | solution.py:171
  89.5 1.3 %collective-permute-start.51 = (bf16[64,1024]{1,0:T(8,128)(2,1)S(1)}, bf16[64,1024]{1,0:T(8,128)(2,1)S(1)}, u32[]{:S(2)}, u32[]{:S(2)}) collective-permute-start(bf16[64,1024]{1,0:T(8,128)(2,1)S(1)} %get-tuple-element.30), channel_id=1, source_target_pairs={{0,2},{2,0},{1,3},{3,1},{4,6},{6,4},{5,7},{7,5},{8,10},{10,8},{9,1... | collective-permute-start | bytes 393224 | tf_op jit(solution)/shard_map/ppermute | solution.py:381
  90.8 3.7 %collective-permute-done.51 = bf16[64,1024]{1,0:T(8,128)(2,1)S(1)} collective-permute-done((bf16[64,1024]{1,0:T(8,128)(2,1)S(1)}, bf16[64,1024]{1,0:T(8,128)(2,1)S(1)}, u32[]{:S(2)}, u32[]{:S(2)}) %collective-permute-start.51) | collective-permute-done | bytes 131104 | tf_op jit(solution)/shard_map/ppermute | solution.py:381
  (106 shorter events, 22.4 us)
Async XLA Ops:
  0.0 14.9 %collective-permute-start.3 = (bf16[64,1024]{1,0:T(8,128)(2,1)}, bf16[64,1024]{1,0:T(8,128)(2,1)S(1)}, u32[]{:S(2)}, u32[]{:S(2)}) collective-permute-start(bf16[64,1024]{1,0:T(8,128)(2,1)} %refs_16_.1), channel_id=1, source_target_pairs={{0,4},{4,0},{8,12},{12,8},{1,5},{5,1},{9,13},{13,9},{2,6},{6,2},{1... | collective-permute-start | bytes 393224 | tf_op jit(solution)/shard_map/ppermute | solution.py:387
  3.0 13.2 %collective-permute-start.4 = (bf16[64,1024]{1,0:T(8,128)(2,1)}, bf16[64,1024]{1,0:T(8,128)(2,1)S(1)}, u32[]{:S(2)}, u32[]{:S(2)}) collective-permute-start(bf16[64,1024]{1,0:T(8,128)(2,1)} %refs_16_.1), channel_id=1, source_target_pairs={{0,8},{4,12},{8,0},{12,4},{1,9},{5,13},{9,1},{13,5},{2,10},{6,14},... | collective-permute-start | bytes 393224 | tf_op jit(solution)/shard_map/ppermute | solution.py:387
  5.6 11.9 %collective-permute-start.5 = (bf16[64,1024]{1,0:T(8,128)(2,1)}, bf16[64,1024]{1,0:T(8,128)(2,1)S(1)}, u32[]{:S(2)}, u32[]{:S(2)}) collective-permute-start(bf16[64,1024]{1,0:T(8,128)(2,1)} %refs_16_.1), channel_id=1, source_target_pairs={{0,12},{4,8},{8,4},{12,0},{1,13},{5,9},{9,5},{13,1},{2,14},{6,10},... | collective-permute-start | bytes 393224 | tf_op jit(solution)/shard_map/ppermute | solution.py:387
  9.5 13.7 %collective-permute-start.24 = (bf16[64,1024]{1,0:T(8,128)(2,1)S(1)}, bf16[64,1024]{1,0:T(8,128)(2,1)S(1)}, u32[]{:S(2)}, u32[]{:S(2)}) collective-permute-start(bf16[64,1024]{1,0:T(8,128)(2,1)S(1)} %copy-done.1), channel_id=1, source_target_pairs={{0,2},{2,0},{1,3},{3,1},{4,6},{6,4},{5,7},{7,5},{8,10},{10,8},{9,1... | collective-permute-start | bytes 393224 | tf_op jit(solution)/shard_map/ppermute | solution.py:381
  12.3 12.9 %collective-permute-start.6 = (bf16[3,256,128]{2,1,0:T(8,128)(2,1)S(1)}, bf16[3,256,128]{2,1,0:T(8,128)(2,1)S(1)}, u32[]{:S(2)}, u32[]{:S(2)}) collective-permute-start(bf16[3,256,128]{2,1,0:T(8,128)(2,1)S(1)} %get-tuple-element.32), channel_id=1, source_target_pairs={{0,4},{4,0},{9,13},{13,9},{2,6},{6,2},{11,15},{15,11},{16,20},{20,... | collective-permute-start | bytes 589832 | tf_op jit(solution)/shard_map/ppermute | solution.py:412
  14.9 12.7 %collective-permute-start.7 = (bf16[3,256,128]{2,1,0:T(8,128)(2,1)S(1)}, bf16[3,256,128]{2,1,0:T(8,128)(2,1)S(1)}, u32[]{:S(2)}, u32[]{:S(2)}) collective-permute-start(bf16[3,256,128]{2,1,0:T(8,128)(2,1)S(1)} %get-tuple-element.31.refs_8_), channel_id=1, source_target_pairs={{8,0},{12,4},{1,9},{5,13},{10,2},{14,6},{3,11},{7,15},{24,16},{28,... | collective-permute-start | bytes 589832 | tf_op jit(solution)/shard_map/ppermute | solution.py:412
  16.2 12.0 %collective-permute-start.8 = (bf16[3,256,128]{2,1,0:T(8,128)(2,1)S(1)}, bf16[3,256,128]{2,1,0:T(8,128)(2,1)S(1)}, u32[]{:S(2)}, u32[]{:S(2)}) collective-permute-start(bf16[3,256,128]{2,1,0:T(8,128)(2,1)S(1)} %get-tuple-element.32), channel_id=1, source_target_pairs={{8,4},{12,0},{1,13},{5,9},{10,6},{14,2},{3,15},{7,11},{24,20},{28,... | collective-permute-start | bytes 589832 | tf_op jit(solution)/shard_map/ppermute | solution.py:412
  17.5 12.1 %collective-permute-start.28 = (bf16[3,256,128]{2,1,0:T(8,128)(2,1)S(1)}, bf16[3,256,128]{2,1,0:T(8,128)(2,1)S(1)}, u32[]{:S(2)}, u32[]{:S(2)}) collective-permute-start(bf16[3,256,128]{2,1,0:T(8,128)(2,1)S(1)} %get-tuple-element.31.refs_8_), channel_id=1, source_target_pairs={{0,1},{4,5},{9,8},{13,12},{2,3},{6,7},{11,10},{15,14},{16,17},{20,... | collective-permute-start | bytes 589832 | tf_op jit(solution)/shard_map/ppermute | solution.py:414
  24.5 7.0 %collective-permute-start.1 = (bf16[3,128,256]{2,1,0:T(8,128)(2,1)S(1)}, bf16[3,128,256]{2,1,0:T(8,128)(2,1)S(1)}, u32[]{:S(2)}, u32[]{:S(2)}) collective-permute-start(bf16[3,128,256]{2,1,0:T(8,128)(2,1)S(1)} %fusion.1.refs_0_), channel_id=1, source_target_pairs={{0,16},{16,0},{1,17},{17,1},{2,18},{18,2},{3,19},{19,3},{4,20},{20... | collective-permute-start | bytes 589832 | tf_op jit(solution)/shard_map/ppermute | solution.py:384
  25.2 7.6 %collective-permute-start = (bf16[3,128,256]{2,1,0:T(8,128)(2,1)S(1)}, bf16[3,128,256]{2,1,0:T(8,128)(2,1)S(1)}, u32[]{:S(2)}, u32[]{:S(2)}) collective-permute-start(bf16[3,128,256]{2,1,0:T(8,128)(2,1)S(1)} %fusion.1.refs_0_), channel_id=1, source_target_pairs={{0,1},{1,0},{2,3},{3,2},{4,5},{5,4},{6,7},{7,6},{8,9},{9,8},{10,11... | collective-permute-start | bytes 589832 | tf_op jit(solution)/shard_map/ppermute | solution.py:378
  27.5 6.6 %collective-permute-start.25 = (bf16[64,1024]{1,0:T(8,128)(2,1)S(1)}, bf16[64,1024]{1,0:T(8,128)(2,1)S(1)}, u32[]{:S(2)}, u32[]{:S(2)}) collective-permute-start(bf16[64,1024]{1,0:T(8,128)(2,1)S(1)} %collective-permute-done.3.refs_2_), channel_id=1, source_target_pairs={{0,2},{2,0},{1,3},{3,1},{4,6},{6,4},{5,7},{7,5},{8,10},{10,8},{9,1... | collective-permute-start | bytes 393224 | tf_op jit(solution)/shard_map/ppermute | solution.py:381
  28.2 7.2 %collective-permute-start.26 = (bf16[64,1024]{1,0:T(8,128)(2,1)S(1)}, bf16[64,1024]{1,0:T(8,128)(2,1)S(1)}, u32[]{:S(2)}, u32[]{:S(2)}) collective-permute-start(bf16[64,1024]{1,0:T(8,128)(2,1)S(1)} %collective-permute-done.4.refs_4_), channel_id=1, source_target_pairs={{0,2},{2,0},{1,3},{3,1},{4,6},{6,4},{5,7},{7,5},{8,10},{10,8},{9,1... | collective-permute-start | bytes 393224 | tf_op jit(solution)/shard_map/ppermute | solution.py:381
  29.6 7.1 %collective-permute-start.27 = (bf16[64,1024]{1,0:T(8,128)(2,1)S(1)}, bf16[64,1024]{1,0:T(8,128)(2,1)S(1)}, u32[]{:S(2)}, u32[]{:S(2)}) collective-permute-start(bf16[64,1024]{1,0:T(8,128)(2,1)S(1)} %collective-permute-done.5.refs_6_), channel_id=1, source_target_pairs={{0,2},{2,0},{1,3},{3,1},{4,6},{6,4},{5,7},{7,5},{8,10},{10,8},{9,1... | collective-permute-start | bytes 393224 | tf_op jit(solution)/shard_map/ppermute | solution.py:381
  31.5 16.9 %collective-permute-start.29 = (bf16[3,256,128]{2,1,0:T(8,128)(2,1)S(1)}, bf16[3,256,128]{2,1,0:T(8,128)(2,1)S(1)}, u32[]{:S(2)}, u32[]{:S(2)}) collective-permute-start(bf16[3,256,128]{2,1,0:T(8,128)(2,1)S(1)} %collective-permute-done.6.refs_9_), channel_id=1, source_target_pairs={{0,1},{4,5},{9,8},{13,12},{2,3},{6,7},{11,10},{15,14},{16,17},{20,... | collective-permute-start | bytes 589832 | tf_op jit(solution)/shard_map/ppermute | solution.py:414
  32.8 15.6 %collective-permute-start.30 = (bf16[3,256,128]{2,1,0:T(8,128)(2,1)S(1)}, bf16[3,256,128]{2,1,0:T(8,128)(2,1)S(1)}, u32[]{:S(2)}, u32[]{:S(2)}) collective-permute-start(bf16[3,256,128]{2,1,0:T(8,128)(2,1)S(1)} %collective-permute-done.7.refs_10_), channel_id=1, source_target_pairs={{0,1},{4,5},{9,8},{13,12},{2,3},{6,7},{11,10},{15,14},{16,17},{20,... | collective-permute-start | bytes 589832 | tf_op jit(solution)/shard_map/ppermute | solution.py:414
  34.1 14.8 %collective-permute-start.31 = (bf16[3,256,128]{2,1,0:T(8,128)(2,1)S(1)}, bf16[3,256,128]{2,1,0:T(8,128)(2,1)S(1)}, u32[]{:S(2)}, u32[]{:S(2)}) collective-permute-start(bf16[3,256,128]{2,1,0:T(8,128)(2,1)S(1)} %collective-permute-done.8.refs_11_), channel_id=1, source_target_pairs={{0,1},{4,5},{9,8},{13,12},{2,3},{6,7},{11,10},{15,14},{16,17},{20,... | collective-permute-start | bytes 589832 | tf_op jit(solution)/shard_map/ppermute | solution.py:414
  36.7 7.1 %collective-permute-start.10 = (bf16[128,256]{1,0:T(8,128)(2,1)S(1)}, bf16[128,256]{1,0:T(8,128)(2,1)S(1)}, u32[]{:S(2)}, u32[]{:S(2)}) collective-permute-start(bf16[128,256]{1,0:T(8,128)(2,1)S(1)} %constant_dynamic-slice_fusion.2.refs_0_), channel_id=1, source_target_pairs={{0,8},{4,12},{8,0},{12,4},{1,9},{5,13},{9,1},{13,5},{2,10},{6,14},... | collective-permute-start | bytes 196616 | tf_op jit(solution)/shard_map/ppermute | solution.py:387
  40.5 6.1 %collective-permute-start.11 = (bf16[128,256]{1,0:T(8,128)(2,1)S(1)}, bf16[128,256]{1,0:T(8,128)(2,1)S(1)}, u32[]{:S(2)}, u32[]{:S(2)}) collective-permute-start(bf16[128,256]{1,0:T(8,128)(2,1)S(1)} %constant_dynamic-slice_fusion.2.refs_0_), channel_id=1, source_target_pairs={{0,12},{4,8},{8,4},{12,0},{1,13},{5,9},{9,5},{13,1},{2,14},{6,10},... | collective-permute-start | bytes 196616 | tf_op jit(solution)/shard_map/ppermute | solution.py:387
  43.8 7.6 %collective-permute-start.37 = (bf16[128,256]{1,0:T(8,128)(2,1)S(1)}, bf16[128,256]{1,0:T(8,128)(2,1)S(1)}, u32[]{:S(2)}, u32[]{:S(2)}) collective-permute-start(bf16[128,256]{1,0:T(8,128)(2,1)S(1)} %collective-permute-done.9.refs_4_), channel_id=1, source_target_pairs={{0,16},{16,0},{1,17},{17,1},{2,18},{18,2},{3,19},{19,3},{4,20},{20... | collective-permute-start | bytes 196616 | tf_op jit(solution)/shard_map/ppermute | solution.py:384
  51.3 12.3 %collective-permute-start.45 = (bf16[1088,128]{1,0:T(8,128)(2,1)S(1)}, bf16[1088,128]{1,0:T(8,128)(2,1)S(1)}, u32[]{:S(2)}, u32[]{:S(2)}) collective-permute-start(bf16[1088,128]{1,0:T(8,128)(2,1)S(1)} %get-tuple-element.22.own), channel_id=1, source_target_pairs={{0,1},{1,0},{2,3},{3,2},{4,5},{5,4},{6,7},{7,6},{8,9},{9,8},{10,11... | collective-permute-start | bytes 835592 | tf_op jit(solution)/shard_map/ppermute | solution.py:378
  53.7 9.8 %collective-permute-start.12 = (bf16[3,128,256]{2,1,0:T(8,128)(2,1)S(1)}, bf16[3,128,256]{2,1,0:T(8,128)(2,1)S(1)}, u32[]{:S(2)}, u32[]{:S(2)}) collective-permute-start(bf16[3,128,256]{2,1,0:T(8,128)(2,1)S(1)} %fusion.1.refs_0_), channel_id=1, source_target_pairs={{0,4},{4,0},{8,12},{12,8},{1,5},{5,1},{9,13},{13,9},{2,6},{6,2},{1... | collective-permute-start | bytes 589832 | tf_op jit(solution)/shard_map/ppermute | solution.py:387
  54.5 12.1 %collective-permute-start.2 = (bf16[3,128,256]{2,1,0:T(8,128)(2,1)S(1)}, bf16[3,128,256]{2,1,0:T(8,128)(2,1)S(1)}, u32[]{:S(2)}, u32[]{:S(2)}) collective-permute-start(bf16[3,128,256]{2,1,0:T(8,128)(2,1)S(1)} %collective-permute-done.1.refs_2_), channel_id=1, source_target_pairs={{0,1},{1,0},{2,3},{3,2},{4,5},{5,4},{6,7},{7,6},{8,9},{9,8},{10,11... | collective-permute-start | bytes 589832 | tf_op jit(solution)/shard_map/ppermute | solution.py:378
  54.6 17.1 %collective-permute-start.16 = (bf16[3,128,256]{2,1,0:T(8,128)(2,1)S(1)}, bf16[3,128,256]{2,1,0:T(8,128)(2,1)S(1)}, u32[]{:S(2)}, u32[]{:S(2)}) collective-permute-start(bf16[3,128,256]{2,1,0:T(8,128)(2,1)S(1)} %fusion.1.refs_0_), channel_id=1, source_target_pairs={{0,8},{4,12},{8,0},{12,4},{1,9},{5,13},{9,1},{13,5},{2,10},{6,14},... | collective-permute-start | bytes 589832 | tf_op jit(solution)/shard_map/ppermute | solution.py:387
  57.3 17.3 %collective-permute-start.20 = (bf16[3,128,256]{2,1,0:T(8,128)(2,1)S(1)}, bf16[3,128,256]{2,1,0:T(8,128)(2,1)S(1)}, u32[]{:S(2)}, u32[]{:S(2)}) collective-permute-start(bf16[3,128,256]{2,1,0:T(8,128)(2,1)S(1)} %fusion.1.refs_0_), channel_id=1, source_target_pairs={{0,12},{4,8},{8,4},{12,0},{1,13},{5,9},{9,5},{13,1},{2,14},{6,10},... | collective-permute-start | bytes 589832 | tf_op jit(solution)/shard_map/ppermute | solution.py:387
  63.5 15.6 %collective-permute-start.14 = (bf16[3,128,256]{2,1,0:T(8,128)(2,1)S(1)}, bf16[3,128,256]{2,1,0:T(8,128)(2,1)S(1)}, u32[]{:S(2)}, u32[]{:S(2)}) collective-permute-start(bf16[3,128,256]{2,1,0:T(8,128)(2,1)S(1)} %collective-permute-done.12.refs_4_), channel_id=1, source_target_pairs={{0,16},{16,0},{1,17},{17,1},{2,18},{18,2},{3,19},{19,3},{4,20},{20... | collective-permute-start | bytes 589832 | tf_op jit(solution)/shard_map/ppermute | solution.py:384
  66.5 8.0 %collective-permute-start.46 = (bf16[144,128]{1,0:T(8,128)(2,1)S(1)}, bf16[144,128]{1,0:T(8,128)(2,1)S(1)}, u32[]{:S(2)}, u32[]{:S(2)}) collective-permute-start(bf16[144,128]{1,0:T(8,128)(2,1)S(1)} %get-tuple-element.24), channel_id=1, source_target_pairs={{0,4},{4,0},{8,12},{12,8},{1,5},{5,1},{9,13},{13,9},{2,6},{6,2},{1... | collective-permute-start | bytes 110600 | tf_op jit(solution)/shard_map/ppermute | solution.py:459
  66.6 11.5 %collective-permute-start.47 = (bf16[144,128]{1,0:T(8,128)(2,1)S(1)}, bf16[144,128]{1,0:T(8,128)(2,1)S(1)}, u32[]{:S(2)}, u32[]{:S(2)}) collective-permute-start(bf16[144,128]{1,0:T(8,128)(2,1)S(1)} %get-tuple-element.25), channel_id=1, source_target_pairs={{0,8},{4,12},{8,0},{12,4},{1,9},{5,13},{9,1},{13,5},{2,10},{6,14},... | collective-permute-start | bytes 110600 | tf_op jit(solution)/shard_map/ppermute | solution.py:459
  71.7 6.4 %collective-permute-start.48 = (bf16[144,128]{1,0:T(8,128)(2,1)S(1)}, bf16[144,128]{1,0:T(8,128)(2,1)S(1)}, u32[]{:S(2)}, u32[]{:S(2)}) collective-permute-start(bf16[144,128]{1,0:T(8,128)(2,1)S(1)} %get-tuple-element.26), channel_id=1, source_target_pairs={{0,12},{4,8},{8,4},{12,0},{1,13},{5,9},{9,5},{13,1},{2,14},{6,10},... | collective-permute-start | bytes 110600 | tf_op jit(solution)/shard_map/ppermute | solution.py:459
  74.6 7.2 %collective-permute-start.18 = (bf16[3,128,256]{2,1,0:T(8,128)(2,1)S(1)}, bf16[3,128,256]{2,1,0:T(8,128)(2,1)S(1)}, u32[]{:S(2)}, u32[]{:S(2)}) collective-permute-start(bf16[3,128,256]{2,1,0:T(8,128)(2,1)S(1)} %collective-permute-done.16.refs_8_), channel_id=1, source_target_pairs={{0,16},{16,0},{1,17},{17,1},{2,18},{18,2},{3,19},{19,3},{4,20},{20... | collective-permute-start | bytes 589832 | tf_op jit(solution)/shard_map/ppermute | solution.py:384
  74.6 9.3 %collective-permute-start.22 = (bf16[3,128,256]{2,1,0:T(8,128)(2,1)S(1)}, bf16[3,128,256]{2,1,0:T(8,128)(2,1)S(1)}, u32[]{:S(2)}, u32[]{:S(2)}) collective-permute-start(bf16[3,128,256]{2,1,0:T(8,128)(2,1)S(1)} %collective-permute-done.20.refs_12_), channel_id=1, source_target_pairs={{0,16},{16,0},{1,17},{17,1},{2,18},{18,2},{3,19},{19,3},{4,20},{20... | collective-permute-start | bytes 589832 | tf_op jit(solution)/shard_map/ppermute | solution.py:384
  78.1 6.3 %collective-permute-start.17 = (bf16[3,128,256]{2,1,0:T(8,128)(2,1)S(1)}, bf16[3,128,256]{2,1,0:T(8,128)(2,1)S(1)}, u32[]{:S(2)}, u32[]{:S(2)}) collective-permute-start(bf16[3,128,256]{2,1,0:T(8,128)(2,1)S(1)} %collective-permute-done.16.refs_8_), channel_id=1, source_target_pairs={{0,1},{1,0},{2,3},{3,2},{4,5},{5,4},{6,7},{7,6},{8,9},{9,8},{10,11... | collective-permute-start | bytes 589832 | tf_op jit(solution)/shard_map/ppermute | solution.py:378
  79.1 9.0 %collective-permute-start.49 = (bf16[144,1024]{1,0:T(8,128)(2,1)S(1)}, bf16[144,1024]{1,0:T(8,128)(2,1)S(1)}, u32[]{:S(2)}, u32[]{:S(2)}) collective-permute-start(bf16[144,1024]{1,0:T(8,128)(2,1)S(1)} %get-tuple-element.28), channel_id=1, source_target_pairs={{0,2},{2,0},{1,3},{3,1},{4,6},{6,4},{5,7},{7,5},{8,10},{10,8},{9,1... | collective-permute-start | bytes 884744 | tf_op jit(solution)/shard_map/ppermute | solution.py:381
  (31 other events, 158.5 us)

commit v3 on v2

--- a/solution.py
+++ b/solution.py
@@ -175,7 +175,7 @@
         + [pl.BlockSpec(memory_space=pltpu.VMEM)] * len(operands),
         out_specs=[pl.BlockSpec(memory_space=pltpu.VMEM)] * len(outs),
         scratch_shapes=scratch,
-        cost_estimate=pl.CostEstimate(flops=flops, bytes_accessed=moved, transcendentals=0),
+        cost_estimate=pl.CostEstimate(flops=0, bytes_accessed=0, transcendentals=0),
         compiler_params=pltpu.CompilerParams(vmem_limit_bytes=vmem << 20),
     )(length, *operands)
 
@@ -190,6 +190,32 @@
 
 def here():
     return tuple(lax.axis_index(a) for a in ("seq", "head", "fsdp", "parts"))
+
+
+def deal_kernel(length, *refs):
+    mine, other, outs = refs[:3], refs[3:6], refs[6:]
+    s, _, f, _ = here()
+    half = outs[0].shape[1]
+    rows = pl.ds(aligned(f * half, half), half)
+    for k in range(SEQ):
+        head = s ^ k
+        columns = pl.ds(aligned((head % 2) * HD, HD), HD)
+
+        @pl.when(head // 2 == f)
+        def _():
+            for m in range(3):
+                outs[k][m] = mine[m][rows, columns]
+
+        @pl.when(head // 2 != f)
+        def _():
+            for m in range(3):
+                outs[k][m] = other[m][rows, columns]
+
+
+def stack_kernel(length, *refs):
+    s = lax.axis_index("seq")
+    for k in range(SEQ):
+        refs[SEQ][s ^ k] = refs[k][...]
 
 
 def project_kernel(length, *refs):
@@ -198,7 +224,7 @@
     gain, q_out, send_out, edge_out, normed, weights, x_edge, q_edge = refs[4 * SEQ :]
     s, h, f, _ = here()
     rows = blocks[0].shape[0]
-    depth = mine[0].shape[1]
+    half = mine[0].shape[1]
     gain_row = gain[...]
     for slot, block in enumerate(blocks):
         at = (s ^ (slot // 2)) * 2 + (h ^ (slot % 2))
@@ -206,20 +232,11 @@
         normed[pl.ds(aligned(at * rows, rows), rows), :] = layer_norm(x, gain_row).astype(BF16)
         x_edge[at, 0:EDGE, :] = x[:EDGE]
         x_edge[at, EDGE:HALO, :] = x[rows - EDGE :]
-    def fill(pieces):
-        for k in range(SEQ):
-            at = pl.ds(aligned((s ^ k) * depth, depth), depth)
+    for k in range(SEQ):
+        for core, pieces in enumerate((mine, other)):
+            at = pl.ds(aligned((s ^ k) * 2 * half + (f ^ core) * half, half), half)
             for m in range(3):
                 weights[at, m * HD : (m + 1) * HD] = pieces[k][m]
-
-    @pl.when(s // 2 == f)
-    def _():
-        fill(mine)
-
-    @pl.when(s // 2 != f)
-    def _():
-        fill(other)
-
     count = 2 * SEQ
     total = count * rows
     projected = dot(normed[...], weights[...])
@@ -277,15 +294,15 @@
 
 
 def output_kernel(length, *refs):
-    pieces, ctx = refs[: 4 * SEQ], refs[4 * SEQ : 5 * SEQ]
-    share_out, send_out, context, weights = refs[5 * SEQ :]
+    pieces, ctx = refs[:4], refs[4 : 4 + SEQ]
+    share_out, send_out, context, weights = refs[4 + SEQ :]
     s, h, f, p = here()
-    half, columns = pieces[0].shape
-    for k in range(SEQ):
-        for y in range(2):
-            for core in range(2):
-                at = pl.ds(aligned((f ^ core) * 2 * half + (p ^ y) * half, half), half)
-                weights[s ^ k, at, :] = pieces[(k * 2 + y) * 2 + core][...]
+    half, columns = pieces[0].shape[1:]
+    for y in range(2):
+        for core in range(2):
+            at = pl.ds(aligned((f ^ core) * 2 * half + (p ^ y) * half, half), half)
+            for j in range(SEQ):
+                weights[j, at, :] = pieces[y * 2 + core][j]
     for k in range(SEQ):
         context[:, pl.ds(aligned((s ^ k) * HD, HD), HD)] = ctx[k][...]
     for j in range(SEQ):
@@ -389,41 +406,29 @@
     def part_half(x):
         return lax.dynamic_slice_in_dim(x, p * half, half, axis=x.ndim - 2)
 
-    def spread(mine, others):
-        pieces = []
-        for near in (mine, *others):
-            for part in (near, other_part(near)):
-                pieces += [part, other_core(part)]
-        return pieces
-
     near = planes(frames)
     blocks = []
     for block in near:
         blocks += [block, other_side(block)]
-    s = lax.axis_index("seq")
-    projectors = jnp.stack([w_query, w_key, w_value])
-    even = lax.dynamic_slice_in_dim(projectors, (s % 2) * HD, HD, axis=2)
-    odd = lax.dynamic_slice_in_dim(projectors, (1 - s % 2) * HD, HD, axis=2)
-    w_mine = [even]
-    for k in range(1, SEQ):
-        pairs = [
-            (2 * i + core, 2 * (i ^ k) + core) for core in range(2) for i in range(SEQ) if (i ^ k) // 2 == core
-        ]
-        w_mine.append(lax.ppermute(odd if k % 2 else even, ("seq", "fsdp"), pairs))
-    to_other = [(2 * i + i // 2, 2 * i + 1 - i // 2) for i in range(SEQ)]
-    w_other = [lax.ppermute(w, ("seq", "fsdp"), to_other) for w in w_mine]
-
-    mine = part_half(w_out)
-    after, *_ = barrier((mine, *near[1:], *w_mine[1:]))
-    others = planes(after)[1:]
-    out_pieces = spread(mine, others)
-    mine = part_half(jnp.stack([pw1_value, pw1_gate, pw2]))
-    after, *_ = barrier((mine, *others))
-    pw_pieces = spread(mine, planes(after)[1:])
-    channels = jnp.concatenate([depth_kernel, bn_scale[None], bn_shift[None], jnp.zeros((5, columns), F32)])
-    channels_peer = other_core(channels)
-
+    given = [w_query, w_key, w_value]
     shape = jax.ShapeDtypeStruct
+    dealt = call(
+        deal_kernel,
+        [shape((3, half, HD), BF16)] * SEQ,
+        [],
+        length,
+        *given,
+        *[other_core(w) for w in given],
+    )
+    w_mine = [dealt[0]] + [lax.ppermute(dealt[k], "seq", xor_pairs(k)) for k in range(1, SEQ)]
+    w_other = [other_core(w) for w in w_mine]
+
+    out_mine = part_half(w_out)
+    after, *_ = barrier((out_mine, *near[1:], *w_mine[1:]))
+    out_others = planes(after)[1:]
+    pw_mine = part_half(jnp.stack([pw1_value, pw1_gate, pw2]))
+    pw_first, *_ = barrier((pw_mine, *near[1:]))
+    pw_part = other_part(pw_first)
     queries, send, edges = call(
         project_kernel,
         [
@@ -445,6 +450,13 @@
         flops=6 * count * rows * width * HD,
     )
     received = other_core(send)
+    out_mine, _, *out_others = barrier((out_mine, received, *out_others))
+    (stack,) = call(stack_kernel, [shape((SEQ, half, columns), BF16)], [], length, out_mine, *out_others)
+    stack_part = other_part(stack)
+    out_pieces = [stack, other_core(stack), stack_part, other_core(stack_part)]
+    queries, _ = barrier((queries, stack))
+    after, *_ = barrier((pw_mine, send, *out_others))
+    pw_others = planes(after)[1:]
     halo_x = other_core(edges)
     ctx = call(
         attend_kernel,
@@ -456,6 +468,10 @@
         received,
         flops=8 * count * step * count * rows * HD,
     )
+    depth_kernel, pw_mine, pw_part, *_ = barrier((depth_kernel, pw_mine, pw_part, *ctx))
+    pw_pieces = [pw_mine, other_core(pw_mine), pw_part, other_core(pw_part)]
+    channels = jnp.concatenate([depth_kernel, bn_scale[None], bn_shift[None], jnp.zeros((5, columns), F32)])
+    channels_peer = other_core(channels)
     ctx = [ctx[0]] + [lax.ppermute(ctx[k], "seq", xor_pairs(k)) for k in range(1, SEQ)]
     own_share, sent_share = call(
         output_kernel,
@@ -469,6 +485,10 @@
         *ctx,
         flops=2 * step * width * width,
     )
+    *pw_others, own_share, sent_share = barrier((*pw_others, own_share, sent_share))
+    for near in pw_others:
+        part = other_part(near)
+        pw_pieces += [near, other_core(near), part, other_core(part)]
     base, share = call(
         convolve_kernel,
         [shape((rows, width), F32), shape((rows, width), BF16)],

time: 95.5 us -> 104 us (1.089)
  waiting for transfers between devices: 35.2 us -> 55.1 us
  starting transfers between devices: 50 us -> 36.6 us
  local copies, waits for them, and re-layouts: 0.89 us -> 3.55 us
  other arithmetic: 1.83 us -> 0.78 us
    ppermute x9, waiting for transfers between devices: 14.8 us -> 24.7 us  [planes(): return [x] + [lax.ppermute(x, 'seq', xor_pairs(k)) for k in range(1, SEQ)]]
    ppermute x7 -> x3, starting transfers between devices: 14.7 us -> 4.95 us  [shards_chip_per_head(): lax.ppermute(dealt[k], 'seq', xor_pairs(k))]
    ppermute x8 -> x5, waiting for transfers between devices: 6.06 us -> 15.2 us  [other_part(): return lax.ppermute(x, 'parts', SWAP)]
    unnamed x22 -> x26, local copies, waits for them, and re-layouts: 0.74 us -> 3.46 us
    ppermute x7 -> x3, waiting for transfers between devices: 2.41 us -> 4.55 us  [shards_chip_per_head(): lax.ppermute(dealt[k], 'seq', xor_pairs(k))]
    ppermute x19 -> x20, waiting for transfers between devices: 4.21 us -> 2.13 us  [other_core(): return lax.ppermute(x, 'fsdp', SWAP)]
    ppermute x8 -> x5, starting transfers between devices: 7.37 us -> 5.77 us  [other_part(): return lax.ppermute(x, 'parts', SWAP)]
    ppermute x6, starting transfers between devices: 6.85 us -> 5.35 us  [other_side(): return lax.ppermute(x, 'head', SWAP)]
  transfers between devices with their start and end apart: 52 -> 46, of which waited for: 20 -> 17; matrix products, arithmetic and copies ran while one was open for 1% -> 0% of each run, Pallas kernels for 5% -> 3%
where the time goes in v3:
time: 104 us; the launch traced here: 103 us
  waiting for transfers between devices  55.1 us (53%)
  starting transfers between devices  36.6 us (35%)
  Pallas kernels  6.39 us (6%)
  local copies, waits for them, and re-layouts  3.55 us (3%)
    ppermute x9, waiting for transfers between devices, planes(): return [x] + [lax.ppermute(x, 'seq', xor_pairs(k)) for k in range(1, SEQ)]  24.7 us
    ppermute x5, waiting for transfers between devices, other_part(): return lax.ppermute(x, 'parts', SWAP)  15.2 us
    ppermute x9, starting transfers between devices, planes(): return [x] + [lax.ppermute(x, 'seq', xor_pairs(k)) for k in range(1, SEQ)]  12.9 us
    ppermute x6, waiting for transfers between devices, other_side(): return lax.ppermute(x, 'head', SWAP)  7.46 us
    pallas_call x6, Pallas kernels, call(): pl.pallas_call(kernel, out_shape=outs, in_specs=[pl.BlockSpec(memory_spac...  6.39 us
    ppermute x5, starting transfers between devices, other_part(): return lax.ppermute(x, 'parts', SWAP)  5.77 us
    ppermute x6, starting transfers between devices, other_side(): return lax.ppermute(x, 'head', SWAP)  5.35 us
    ppermute x3, starting transfers between devices, shards_chip_per_head(): lax.ppermute(dealt[k], 'seq', xor_pairs(k))  4.95 us
  transfers between devices with their start and end apart: 46, of which 17 were waited for; matrix products, arithmetic and copies ran while one was open for 0% of the time, Pallas kernels for 3%

profile of v3, /device:TPU:0, one launch (start us, length us, event | category | flops | bytes accessed | tf_op | source)
XLA Modules:
  0.0 103.3 jit_solution(16915686814017102350)
XLA Ops:
  1.0 2.6 %collective-permute-start.4 = (bf16[64,1024]{1,0:T(8,128)(2,1)}, bf16[64,1024]{1,0:T(8,128)(2,1)S(1)}, u32[]{:S(2)}, u32[]{:S(2)}) collective-permute-start(bf16[64,1024]{1,0:T(8,128)(2,1)} %refs_16_.1), channel_id=1, source_target_pairs={{0,2},{2,0},{1,3},{3,1},{4,6},{6,4},{5,7},{7,5},{8,10},{10,8},{9,1... | collective-permute-start | bytes 393224 | tf_op jit(solution)/shard_map/ppermute | solution.py:398
  3.5 3.6 %collective-permute-start.2 = (bf16[64,1024]{1,0:T(8,128)(2,1)}, bf16[64,1024]{1,0:T(8,128)(2,1)S(1)}, u32[]{:S(2)}, u32[]{:S(2)}) collective-permute-start(bf16[64,1024]{1,0:T(8,128)(2,1)} %refs_16_.1), channel_id=1, source_target_pairs={{0,12},{4,8},{8,4},{12,0},{1,13},{5,9},{9,5},{13,1},{2,14},{6,10},... | collective-permute-start | bytes 393224 | tf_op jit(solution)/shard_map/ppermute | solution.py:404
  11.5 1.4 %collective-permute-start.11 = (bf16[3,128,128]{2,1,0:T(8,128)(2,1)S(1)}, bf16[3,128,128]{2,1,0:T(8,128)(2,1)S(1)}, u32[]{:S(2)}, u32[]{:S(2)}) collective-permute-start(bf16[3,128,128]{2,1,0:T(8,128)(2,1)S(1)} %get-tuple-element.38), channel_id=1, source_target_pairs={{0,4},{4,0},{8,12},{12,8},{1,5},{5,1},{9,13},{13,9},{2,6},{6,2},{1... | collective-permute-start | bytes 294920 | tf_op jit(solution)/shard_map/ppermute | solution.py:423
  12.9 2.9 %collective-permute-start.12 = (bf16[3,128,128]{2,1,0:T(8,128)(2,1)S(1)}, bf16[3,128,128]{2,1,0:T(8,128)(2,1)S(1)}, u32[]{:S(2)}, u32[]{:S(2)}) collective-permute-start(bf16[3,128,128]{2,1,0:T(8,128)(2,1)S(1)} %get-tuple-element.39), channel_id=1, source_target_pairs={{0,8},{4,12},{8,0},{12,4},{1,9},{5,13},{9,1},{13,5},{2,10},{6,14},... | collective-permute-start | bytes 294920 | tf_op jit(solution)/shard_map/ppermute | solution.py:423
  16.2 5.4 %collective-permute-done.1.refs_4_ = bf16[64,1024]{1,0:T(8,128)(2,1)S(1)} collective-permute-done((bf16[64,1024]{1,0:T(8,128)(2,1)}, bf16[64,1024]{1,0:T(8,128)(2,1)S(1)}, u32[]{:S(2)}, u32[]{:S(2)}) %collective-permute-start.1) | collective-permute-done | bytes 131104 | tf_op jit(solution)/shard_map/ppermute | solution.py:404
  23.0 1.8 %collective-permute-done.12.refs_10_ = bf16[3,128,128]{2,1,0:T(8,128)(2,1)S(1)} collective-permute-done((bf16[3,128,128]{2,1,0:T(8,128)(2,1)S(1)}, bf16[3,128,128]{2,1,0:T(8,128)(2,1)S(1)}, u32[]{:S(2)}, u32[]{:S(2)}) %collective-permute-start.12) | collective-permute-done | bytes 98336 | tf_op jit(solution)/shard_map/ppermute | solution.py:423
  25.4 2.7 %collective-permute-done.13.refs_11_ = bf16[3,128,128]{2,1,0:T(8,128)(2,1)S(1)} collective-permute-done((bf16[3,128,128]{2,1,0:T(8,128)(2,1)S(1)}, bf16[3,128,128]{2,1,0:T(8,128)(2,1)S(1)}, u32[]{:S(2)}, u32[]{:S(2)}) %collective-permute-start.13) | collective-permute-done | bytes 98336 | tf_op jit(solution)/shard_map/ppermute | solution.py:423
  28.8 2.3 %collective-permute-done.5.refs_3_ = bf16[64,1024]{1,0:T(8,128)(2,1)S(1)} collective-permute-done((bf16[64,1024]{1,0:T(8,128)(2,1)S(1)}, bf16[64,1024]{1,0:T(8,128)(2,1)S(1)}, u32[]{:S(2)}, u32[]{:S(2)}) %collective-permute-start.5) | collective-permute-done | bytes 131104 | tf_op jit(solution)/shard_map/ppermute | solution.py:398
  31.1 1.6 %shard_map.137 = (bf16[512,128]{1,0:T(8,128)(2,1)S(1)}, bf16[1088,128]{1,0:T(8,128)(2,1)S(1)}, bf16[16,1024]{1,0:T(8,128)(2,1)S(1)}) custom-call(s32[1]{0:T(128)S(6)} %copy.15.length, bf16[64,1024]{1,0:T(8,128)(2,1)S(1)} %copy-done.1, bf16[64,1024]{1,0:T(8,128)(2,1)S(1)} %collective-permute-done.4.refs_1_.refs_17_, ...), custom_call_target="tpu_custom_call" | custom-call | tf_op jit(solution)/shard_map/pallas_call | solution.py:171
  32.9 3.2 %collective-permute-start.21 = (bf16[128,256]{1,0:T(8,128)(2,1)S(1)}, bf16[128,256]{1,0:T(8,128)(2,1)S(1)}, u32[]{:S(2)}, u32[]{:S(2)}) collective-permute-start(bf16[128,256]{1,0:T(8,128)(2,1)S(1)} %constant_dynamic-slice_fusion.refs_0_), channel_id=1, source_target_pairs={{0,12},{4,8},{8,4},{12,0},{1,13},{5,9},{9,5},{13,1},{2,14},{6,10},... | collective-permute-start | bytes 196616 | tf_op jit(solution)/shard_map/ppermute | solution.py:404
  36.1 1.3 %collective-permute-start.19 = (bf16[128,256]{1,0:T(8,128)(2,1)S(1)}, bf16[128,256]{1,0:T(8,128)(2,1)S(1)}, u32[]{:S(2)}, u32[]{:S(2)}) collective-permute-start(bf16[128,256]{1,0:T(8,128)(2,1)S(1)} %constant_dynamic-slice_fusion.refs_0_), channel_id=1, source_target_pairs={{0,4},{4,0},{8,12},{12,8},{1,5},{5,1},{9,13},{13,9},{2,6},{6,2},{1... | collective-permute-start | bytes 196616 | tf_op jit(solution)/shard_map/ppermute | solution.py:404
  37.4 2.3 %collective-permute-done.21.refs_3_ = bf16[128,256]{1,0:T(8,128)(2,1)S(1)} collective-permute-done((bf16[128,256]{1,0:T(8,128)(2,1)S(1)}, bf16[128,256]{1,0:T(8,128)(2,1)S(1)}, u32[]{:S(2)}, u32[]{:S(2)}) %collective-permute-start.21) | collective-permute-done | bytes 65568 | tf_op jit(solution)/shard_map/ppermute | solution.py:404
  39.7 2.4 %collective-permute-done.20.refs_2_ = bf16[128,256]{1,0:T(8,128)(2,1)S(1)} collective-permute-done((bf16[128,256]{1,0:T(8,128)(2,1)S(1)}, bf16[128,256]{1,0:T(8,128)(2,1)S(1)}, u32[]{:S(2)}, u32[]{:S(2)}) %collective-permute-start.20) | collective-permute-done | bytes 65568 | tf_op jit(solution)/shard_map/ppermute | solution.py:404
  42.1 1.6 %collective-permute-start.28 = (bf16[4,128,256]{2,1,0:T(8,128)(2,1)S(1)}, bf16[4,128,256]{2,1,0:T(8,128)(2,1)S(1)}, u32[]{:S(2)}, u32[]{:S(2)}) collective-permute-start(bf16[4,128,256]{2,1,0:T(8,128)(2,1)S(1)} %shard_map.138.refs_0_), channel_id=1, source_target_pairs={{0,16},{16,0},{1,17},{17,1},{2,18},{18,2},{3,19},{19,3},{4,20},{20... | collective-permute-start | bytes 786440 | tf_op jit(solution)/shard_map/ppermute | solution.py:401
  44.3 7.0 %collective-permute-done.28.refs_2_ = bf16[4,128,256]{2,1,0:T(8,128)(2,1)S(1)} collective-permute-done((bf16[4,128,256]{2,1,0:T(8,128)(2,1)S(1)}, bf16[4,128,256]{2,1,0:T(8,128)(2,1)S(1)}, u32[]{:S(2)}, u32[]{:S(2)}) %collective-permute-start.28) | collective-permute-done | bytes 262176 | tf_op jit(solution)/shard_map/ppermute | solution.py:401
  51.4 2.8 %shard_map.139 = (bf16[144,128]{1,0:T(8,128)(2,1)S(1)}, bf16[144,128]{1,0:T(8,128)(2,1)S(1)}, bf16[144,128]{1,0:T(8,128)(2,1)S(1)}, bf16[144,128]{1,0:T(8,128)(2,1)S(1)}) custom-call(s32[1]{0:T(128)S(6)} %copy.15.length, bf16[512,128]{1,0:T(8,128)(2,1)S(1)} %get-tuple-element.48.q_in, bf16[1088,128]{1,0:T(8,128)(2,1)S(1)} %get-tuple-element.42.own, ...), custom_call_target="tpu_custom_call" | custom-call | tf_op jit(solution)/shard_map/pallas_call | solution.py:171
  54.2 1.4 %collective-permute-start.30 = (bf16[144,128]{1,0:T(8,128)(2,1)S(1)}, bf16[144,128]{1,0:T(8,128)(2,1)S(1)}, u32[]{:S(2)}, u32[]{:S(2)}) collective-permute-start(bf16[144,128]{1,0:T(8,128)(2,1)S(1)} %get-tuple-element.50), channel_id=1, source_target_pairs={{0,4},{4,0},{8,12},{12,8},{1,5},{5,1},{9,13},{13,9},{2,6},{6,2},{1... | collective-permute-start | bytes 110600 | tf_op jit(solution)/shard_map/ppermute | solution.py:475
  55.6 1.9 %collective-permute-start.31 = (bf16[144,128]{1,0:T(8,128)(2,1)S(1)}, bf16[144,128]{1,0:T(8,128)(2,1)S(1)}, u32[]{:S(2)}, u32[]{:S(2)}) collective-permute-start(bf16[144,128]{1,0:T(8,128)(2,1)S(1)} %get-tuple-element.51), channel_id=1, source_target_pairs={{0,8},{4,12},{8,0},{12,4},{1,9},{5,13},{9,1},{13,5},{2,10},{6,14},... | collective-permute-start | bytes 110600 | tf_op jit(solution)/shard_map/ppermute | solution.py:475
  57.5 1.1 %collective-permute-start.32 = (bf16[144,128]{1,0:T(8,128)(2,1)S(1)}, bf16[144,128]{1,0:T(8,128)(2,1)S(1)}, u32[]{:S(2)}, u32[]{:S(2)}) collective-permute-start(bf16[144,128]{1,0:T(8,128)(2,1)S(1)} %get-tuple-element.52), channel_id=1, source_target_pairs={{0,12},{4,8},{8,4},{12,0},{1,13},{5,9},{9,5},{13,1},{2,14},{6,10},... | collective-permute-start | bytes 110600 | tf_op jit(solution)/shard_map/ppermute | solution.py:475
  58.7 2.7 %collective-permute-start.26 = (bf16[3,128,256]{2,1,0:T(8,128)(2,1)S(1)}, bf16[3,128,256]{2,1,0:T(8,128)(2,1)S(1)}, u32[]{:S(2)}, u32[]{:S(2)}) collective-permute-start(bf16[3,128,256]{2,1,0:T(8,128)(2,1)S(1)} %fusion.1.refs_0_), channel_id=1, source_target_pairs={{0,12},{4,8},{8,4},{12,0},{1,13},{5,9},{9,5},{13,1},{2,14},{6,10},... | collective-permute-start | bytes 589832 | tf_op jit(solution)/shard_map/ppermute | solution.py:404
  61.4 1.4 %collective-permute-start.25 = (bf16[3,128,256]{2,1,0:T(8,128)(2,1)S(1)}, bf16[3,128,256]{2,1,0:T(8,128)(2,1)S(1)}, u32[]{:S(2)}, u32[]{:S(2)}) collective-permute-start(bf16[3,128,256]{2,1,0:T(8,128)(2,1)S(1)} %fusion.1.refs_0_), channel_id=1, source_target_pairs={{0,8},{4,12},{8,0},{12,4},{1,9},{5,13},{9,1},{13,5},{2,10},{6,14},... | collective-permute-start | bytes 589832 | tf_op jit(solution)/shard_map/ppermute | solution.py:404
  62.7 1.0 collective-permute-done.32.refs_7_
  64.8 3.6 %collective-permute-done.26.refs_12_ = bf16[3,128,256]{2,1,0:T(8,128)(2,1)S(1)} collective-permute-done((bf16[3,128,256]{2,1,0:T(8,128)(2,1)S(1)}, bf16[3,128,256]{2,1,0:T(8,128)(2,1)S(1)}, u32[]{:S(2)}, u32[]{:S(2)}) %collective-permute-start.26) | collective-permute-done | bytes 196640 | tf_op jit(solution)/shard_map/ppermute | solution.py:404
  68.3 11.0 %collective-permute-done.25.refs_8_ = bf16[3,128,256]{2,1,0:T(8,128)(2,1)S(1)} collective-permute-done((bf16[3,128,256]{2,1,0:T(8,128)(2,1)S(1)}, bf16[3,128,256]{2,1,0:T(8,128)(2,1)S(1)}, u32[]{:S(2)}, u32[]{:S(2)}) %collective-permute-start.25) | collective-permute-done | bytes 196640 | tf_op jit(solution)/shard_map/ppermute | solution.py:404
  79.4 1.5 %collective-permute-start.34 = (bf16[3,128,256]{2,1,0:T(8,128)(2,1)S(1)}, bf16[3,128,256]{2,1,0:T(8,128)(2,1)S(1)}, u32[]{:S(2)}, u32[]{:S(2)}) collective-permute-start(bf16[3,128,256]{2,1,0:T(8,128)(2,1)S(1)} %collective-permute-done.24.refs_4_), channel_id=1, source_target_pairs={{0,16},{16,0},{1,17},{17,1},{2,18},{18,2},{3,19},{19,3},{4,20},{20... | collective-permute-start | bytes 589832 | tf_op jit(solution)/shard_map/ppermute | solution.py:401
  83.4 1.6 %collective-permute-start.40 = (bf16[3,128,256]{2,1,0:T(8,128)(2,1)S(1)}, bf16[3,128,256]{2,1,0:T(8,128)(2,1)S(1)}, u32[]{:S(2)}, u32[]{:S(2)}) collective-permute-start(bf16[3,128,256]{2,1,0:T(8,128)(2,1)S(1)} %collective-permute-done.26.refs_12_), channel_id=1, source_target_pairs={{0,16},{16,0},{1,17},{17,1},{2,18},{18,2},{3,19},{19,3},{4,20},{20... | collective-permute-start | bytes 589832 | tf_op jit(solution)/shard_map/ppermute | solution.py:401
  85.0 1.0 collective-permute-done.34.refs_6_
  86.4 4.2 %collective-permute-done.37.refs_10_ = bf16[3,128,256]{2,1,0:T(8,128)(2,1)S(1)} collective-permute-done((bf16[3,128,256]{2,1,0:T(8,128)(2,1)S(1)}, bf16[3,128,256]{2,1,0:T(8,128)(2,1)S(1)}, u32[]{:S(2)}, u32[]{:S(2)}) %collective-permute-start.37) | collective-permute-done | bytes 196640 | tf_op jit(solution)/shard_map/ppermute | solution.py:401
  91.1 3.1 %collective-permute-done.40.refs_14_ = bf16[3,128,256]{2,1,0:T(8,128)(2,1)S(1)} collective-permute-done((bf16[3,128,256]{2,1,0:T(8,128)(2,1)S(1)}, bf16[3,128,256]{2,1,0:T(8,128)(2,1)S(1)}, u32[]{:S(2)}, u32[]{:S(2)}) %collective-permute-start.40) | collective-permute-done | bytes 196640 | tf_op jit(solution)/shard_map/ppermute | solution.py:401
  94.2 1.4 %collective-permute-done.41.refs_15_ = bf16[3,128,256]{2,1,0:T(8,128)(2,1)S(1)} collective-permute-done((bf16[3,128,256]{2,1,0:T(8,128)(2,1)S(1)}, bf16[3,128,256]{2,1,0:T(8,128)(2,1)S(1)}, u32[]{:S(2)}, u32[]{:S(2)}) %collective-permute-start.41) | collective-permute-done | bytes 196640 | tf_op jit(solution)/shard_map/ppermute | solution.py:395
  95.6 1.4 %shard_map.141 = (f32[64,1024]{1,0:T(8,128)S(1)}, bf16[64,1024]{1,0:T(8,128)(2,1)S(1)}) custom-call(s32[1]{0:T(128)S(6)} %copy.15.length, bf16[3,128,256]{2,1,0:T(8,128)(2,1)S(1)} %fusion.1.refs_0_, bf16[3,128,256]{2,1,0:T(8,128)(2,1)S(1)} %collective-permute-done.22.refs_1_, bf16[3,128,256]{2,1,0:T(8,128)(2,1)S(1)} %collective-permute-done.3.refs_2_, ...), custom_call_target="tpu_custom_call" | custom-call | tf_op jit(solution)/shard_map/pallas_call | solution.py:171
  97.6 5.0 %collective-permute-done.45 = bf16[64,1024]{1,0:T(8,128)(2,1)S(1)} collective-permute-done((bf16[64,1024]{1,0:T(8,128)(2,1)S(1)}, bf16[64,1024]{1,0:T(8,128)(2,1)S(1)}, u32[]{:S(2)}, u32[]{:S(2)}) %collective-permute-start.45) | collective-permute-done | bytes 131104 | tf_op jit(solution)/shard_map/ppermute | solution.py:398
  (98 shorter events, 14.2 us)
Async XLA Ops:
  0.0 7.1 %collective-permute-start.8 = (bf16[256,256]{1,0:T(8,128)(2,1)}, bf16[256,256]{1,0:T(8,128)(2,1)S(1)}, u32[]{:S(2)}, u32[]{:S(2)}) collective-permute-start(bf16[256,256]{1,0:T(8,128)(2,1)} %refs_0_.2), channel_id=1, source_target_pairs={{0,1},{1,0},{2,3},{3,2},{4,5},{5,4},{6,7},{7,6},{8,9},{9,8},{10,11... | collective-permute-start | bytes 393224 | tf_op jit(solution)/shard_map/ppermute | solution.py:395
  0.5 6.7 %collective-permute-start.9 = (bf16[256,256]{1,0:T(8,128)(2,1)}, bf16[256,256]{1,0:T(8,128)(2,1)S(1)}, u32[]{:S(2)}, u32[]{:S(2)}) collective-permute-start(bf16[256,256]{1,0:T(8,128)(2,1)} %refs_1_.1), channel_id=1, source_target_pairs={{0,1},{1,0},{2,3},{3,2},{4,5},{5,4},{6,7},{7,6},{8,9},{9,8},{10,11... | collective-permute-start | bytes 393224 | tf_op jit(solution)/shard_map/ppermute | solution.py:395
  0.5 8.1 %collective-permute-start.10 = (bf16[256,256]{1,0:T(8,128)(2,1)}, bf16[256,256]{1,0:T(8,128)(2,1)S(1)}, u32[]{:S(2)}, u32[]{:S(2)}) collective-permute-start(bf16[256,256]{1,0:T(8,128)(2,1)} %refs_2_.1), channel_id=1, source_target_pairs={{0,1},{1,0},{2,3},{3,2},{4,5},{5,4},{6,7},{7,6},{8,9},{9,8},{10,11... | collective-permute-start | bytes 393224 | tf_op jit(solution)/shard_map/ppermute | solution.py:395
  1.0 11.9 %collective-permute-start.4 = (bf16[64,1024]{1,0:T(8,128)(2,1)}, bf16[64,1024]{1,0:T(8,128)(2,1)S(1)}, u32[]{:S(2)}, u32[]{:S(2)}) collective-permute-start(bf16[64,1024]{1,0:T(8,128)(2,1)} %refs_16_.1), channel_id=1, source_target_pairs={{0,2},{2,0},{1,3},{3,1},{4,6},{6,4},{5,7},{7,5},{8,10},{10,8},{9,1... | collective-permute-start | bytes 393224 | tf_op jit(solution)/shard_map/ppermute | solution.py:398
  3.5 12.2 %collective-permute-start.2 = (bf16[64,1024]{1,0:T(8,128)(2,1)}, bf16[64,1024]{1,0:T(8,128)(2,1)S(1)}, u32[]{:S(2)}, u32[]{:S(2)}) collective-permute-start(bf16[64,1024]{1,0:T(8,128)(2,1)} %refs_16_.1), channel_id=1, source_target_pairs={{0,12},{4,8},{8,4},{12,0},{1,13},{5,9},{9,5},{13,1},{2,14},{6,10},... | collective-permute-start | bytes 393224 | tf_op jit(solution)/shard_map/ppermute | solution.py:404
  7.1 14.5 %collective-permute-start.1 = (bf16[64,1024]{1,0:T(8,128)(2,1)}, bf16[64,1024]{1,0:T(8,128)(2,1)S(1)}, u32[]{:S(2)}, u32[]{:S(2)}) collective-permute-start(bf16[64,1024]{1,0:T(8,128)(2,1)} %refs_16_.1), channel_id=1, source_target_pairs={{0,8},{4,12},{8,0},{12,4},{1,9},{5,13},{9,1},{13,5},{2,10},{6,14},... | collective-permute-start | bytes 393224 | tf_op jit(solution)/shard_map/ppermute | solution.py:404
  7.1 15.2 %collective-permute-start = (bf16[64,1024]{1,0:T(8,128)(2,1)}, bf16[64,1024]{1,0:T(8,128)(2,1)S(1)}, u32[]{:S(2)}, u32[]{:S(2)}) collective-permute-start(bf16[64,1024]{1,0:T(8,128)(2,1)} %refs_16_.1), channel_id=1, source_target_pairs={{0,4},{4,0},{8,12},{12,8},{1,5},{5,1},{9,13},{13,9},{2,6},{6,2},{1... | collective-permute-start | bytes 393224 | tf_op jit(solution)/shard_map/ppermute | solution.py:404
  11.5 10.9 %collective-permute-start.11 = (bf16[3,128,128]{2,1,0:T(8,128)(2,1)S(1)}, bf16[3,128,128]{2,1,0:T(8,128)(2,1)S(1)}, u32[]{:S(2)}, u32[]{:S(2)}) collective-permute-start(bf16[3,128,128]{2,1,0:T(8,128)(2,1)S(1)} %get-tuple-element.38), channel_id=1, source_target_pairs={{0,4},{4,0},{8,12},{12,8},{1,5},{5,1},{9,13},{13,9},{2,6},{6,2},{1... | collective-permute-start | bytes 294920 | tf_op jit(solution)/shard_map/ppermute | solution.py:423
  12.9 12.0 %collective-permute-start.12 = (bf16[3,128,128]{2,1,0:T(8,128)(2,1)S(1)}, bf16[3,128,128]{2,1,0:T(8,128)(2,1)S(1)}, u32[]{:S(2)}, u32[]{:S(2)}) collective-permute-start(bf16[3,128,128]{2,1,0:T(8,128)(2,1)S(1)} %get-tuple-element.39), channel_id=1, source_target_pairs={{0,8},{4,12},{8,0},{12,4},{1,9},{5,13},{9,1},{13,5},{2,10},{6,14},... | collective-permute-start | bytes 294920 | tf_op jit(solution)/shard_map/ppermute | solution.py:423
  15.7 12.9 %collective-permute-start.7 = (bf16[64,1024]{1,0:T(8,128)(2,1)S(1)}, bf16[64,1024]{1,0:T(8,128)(2,1)S(1)}, u32[]{:S(2)}, u32[]{:S(2)}) collective-permute-start(bf16[64,1024]{1,0:T(8,128)(2,1)S(1)} %collective-permute-done.2.refs_6_), channel_id=1, source_target_pairs={{0,2},{2,0},{1,3},{3,1},{4,6},{6,4},{5,7},{7,5},{8,10},{10,8},{9,1... | collective-permute-start | bytes 393224 | tf_op jit(solution)/shard_map/ppermute | solution.py:398
  21.7 6.4 %collective-permute-start.13 = (bf16[3,128,128]{2,1,0:T(8,128)(2,1)S(1)}, bf16[3,128,128]{2,1,0:T(8,128)(2,1)S(1)}, u32[]{:S(2)}, u32[]{:S(2)}) collective-permute-start(bf16[3,128,128]{2,1,0:T(8,128)(2,1)S(1)} %get-tuple-element.40), channel_id=1, source_target_pairs={{0,12},{4,8},{8,4},{12,0},{1,13},{5,9},{9,5},{13,1},{2,14},{6,10},... | collective-permute-start | bytes 294920 | tf_op jit(solution)/shard_map/ppermute | solution.py:423
  22.4 6.4 %collective-permute-start.6 = (bf16[64,1024]{1,0:T(8,128)(2,1)S(1)}, bf16[64,1024]{1,0:T(8,128)(2,1)S(1)}, u32[]{:S(2)}, u32[]{:S(2)}) collective-permute-start(bf16[64,1024]{1,0:T(8,128)(2,1)S(1)} %collective-permute-done.1.refs_4_), channel_id=1, source_target_pairs={{0,2},{2,0},{1,3},{3,1},{4,6},{6,4},{5,7},{7,5},{8,10},{10,8},{9,1... | collective-permute-start | bytes 393224 | tf_op jit(solution)/shard_map/ppermute | solution.py:398
  24.8 6.3 %collective-permute-start.5 = (bf16[64,1024]{1,0:T(8,128)(2,1)S(1)}, bf16[64,1024]{1,0:T(8,128)(2,1)S(1)}, u32[]{:S(2)}, u32[]{:S(2)}) collective-permute-start(bf16[64,1024]{1,0:T(8,128)(2,1)S(1)} %collective-permute-done.refs_2_), channel_id=1, source_target_pairs={{0,2},{2,0},{1,3},{3,1},{4,6},{6,4},{5,7},{7,5},{8,10},{10,8},{9,1... | collective-permute-start | bytes 393224 | tf_op jit(solution)/shard_map/ppermute | solution.py:398
  32.8 9.3 %collective-permute-start.18 = (bf16[1088,128]{1,0:T(8,128)(2,1)S(1)}, bf16[1088,128]{1,0:T(8,128)(2,1)S(1)}, u32[]{:S(2)}, u32[]{:S(2)}) collective-permute-start(bf16[1088,128]{1,0:T(8,128)(2,1)S(1)} %get-tuple-element.42.own), channel_id=1, source_target_pairs={{0,1},{1,0},{2,3},{3,2},{4,5},{5,4},{6,7},{7,6},{8,9},{9,8},{10,11... | collective-permute-start | bytes 835592 | tf_op jit(solution)/shard_map/ppermute | solution.py:395
  32.9 6.8 %collective-permute-start.21 = (bf16[128,256]{1,0:T(8,128)(2,1)S(1)}, bf16[128,256]{1,0:T(8,128)(2,1)S(1)}, u32[]{:S(2)}, u32[]{:S(2)}) collective-permute-start(bf16[128,256]{1,0:T(8,128)(2,1)S(1)} %constant_dynamic-slice_fusion.refs_0_), channel_id=1, source_target_pairs={{0,12},{4,8},{8,4},{12,0},{1,13},{5,9},{9,5},{13,1},{2,14},{6,10},... | collective-permute-start | bytes 196616 | tf_op jit(solution)/shard_map/ppermute | solution.py:404
  42.1 9.2 %collective-permute-start.28 = (bf16[4,128,256]{2,1,0:T(8,128)(2,1)S(1)}, bf16[4,128,256]{2,1,0:T(8,128)(2,1)S(1)}, u32[]{:S(2)}, u32[]{:S(2)}) collective-permute-start(bf16[4,128,256]{2,1,0:T(8,128)(2,1)S(1)} %shard_map.138.refs_0_), channel_id=1, source_target_pairs={{0,16},{16,0},{1,17},{17,1},{2,18},{18,2},{3,19},{19,3},{4,20},{20... | collective-permute-start | bytes 786440 | tf_op jit(solution)/shard_map/ppermute | solution.py:401
  43.8 13.8 %collective-permute-start.3 = (bf16[3,128,256]{2,1,0:T(8,128)(2,1)S(1)}, bf16[3,128,256]{2,1,0:T(8,128)(2,1)S(1)}, u32[]{:S(2)}, u32[]{:S(2)}) collective-permute-start(bf16[3,128,256]{2,1,0:T(8,128)(2,1)S(1)} %fusion.1.refs_0_), channel_id=1, source_target_pairs={{0,16},{16,0},{1,17},{17,1},{2,18},{18,2},{3,19},{19,3},{4,20},{20... | collective-permute-start | bytes 589832 | tf_op jit(solution)/shard_map/ppermute | solution.py:401
  44.3 19.5 %collective-permute-start.27 = (bf16[4,128,256]{2,1,0:T(8,128)(2,1)S(1)}, bf16[4,128,256]{2,1,0:T(8,128)(2,1)S(1)}, u32[]{:S(2)}, u32[]{:S(2)}) collective-permute-start(bf16[4,128,256]{2,1,0:T(8,128)(2,1)S(1)} %shard_map.138.refs_0_), channel_id=1, source_target_pairs={{0,1},{1,0},{2,3},{3,2},{4,5},{5,4},{6,7},{7,6},{8,9},{9,8},{10,11... | collective-permute-start | bytes 786440 | tf_op jit(solution)/shard_map/ppermute | solution.py:395
  51.4 12.5 %collective-permute-start.29 = (bf16[4,128,256]{2,1,0:T(8,128)(2,1)S(1)}, bf16[4,128,256]{2,1,0:T(8,128)(2,1)S(1)}, u32[]{:S(2)}, u32[]{:S(2)}) collective-permute-start(bf16[4,128,256]{2,1,0:T(8,128)(2,1)S(1)} %collective-permute-done.28.refs_2_), channel_id=1, source_target_pairs={{0,1},{1,0},{2,3},{3,2},{4,5},{5,4},{6,7},{7,6},{8,9},{9,8},{10,11... | collective-permute-start | bytes 786440 | tf_op jit(solution)/shard_map/ppermute | solution.py:395
  57.5 6.2 %collective-permute-start.32 = (bf16[144,128]{1,0:T(8,128)(2,1)S(1)}, bf16[144,128]{1,0:T(8,128)(2,1)S(1)}, u32[]{:S(2)}, u32[]{:S(2)}) collective-permute-start(bf16[144,128]{1,0:T(8,128)(2,1)S(1)} %get-tuple-element.52), channel_id=1, source_target_pairs={{0,12},{4,8},{8,4},{12,0},{1,13},{5,9},{9,5},{13,1},{2,14},{6,10},... | collective-permute-start | bytes 110600 | tf_op jit(solution)/shard_map/ppermute | solution.py:475
  58.7 9.7 %collective-permute-start.26 = (bf16[3,128,256]{2,1,0:T(8,128)(2,1)S(1)}, bf16[3,128,256]{2,1,0:T(8,128)(2,1)S(1)}, u32[]{:S(2)}, u32[]{:S(2)}) collective-permute-start(bf16[3,128,256]{2,1,0:T(8,128)(2,1)S(1)} %fusion.1.refs_0_), channel_id=1, source_target_pairs={{0,12},{4,8},{8,4},{12,0},{1,13},{5,9},{9,5},{13,1},{2,14},{6,10},... | collective-permute-start | bytes 589832 | tf_op jit(solution)/shard_map/ppermute | solution.py:404
  61.4 18.0 %collective-permute-start.25 = (bf16[3,128,256]{2,1,0:T(8,128)(2,1)S(1)}, bf16[3,128,256]{2,1,0:T(8,128)(2,1)S(1)}, u32[]{:S(2)}, u32[]{:S(2)}) collective-permute-start(bf16[3,128,256]{2,1,0:T(8,128)(2,1)S(1)} %fusion.1.refs_0_), channel_id=1, source_target_pairs={{0,8},{4,12},{8,0},{12,4},{1,9},{5,13},{9,1},{13,5},{2,10},{6,14},... | collective-permute-start | bytes 589832 | tf_op jit(solution)/shard_map/ppermute | solution.py:404
  63.7 15.6 %collective-permute-start.24 = (bf16[3,128,256]{2,1,0:T(8,128)(2,1)S(1)}, bf16[3,128,256]{2,1,0:T(8,128)(2,1)S(1)}, u32[]{:S(2)}, u32[]{:S(2)}) collective-permute-start(bf16[3,128,256]{2,1,0:T(8,128)(2,1)S(1)} %fusion.1.refs_0_), channel_id=1, source_target_pairs={{0,4},{4,0},{8,12},{12,8},{1,5},{5,1},{9,13},{13,9},{2,6},{6,2},{1... | collective-permute-start | bytes 589832 | tf_op jit(solution)/shard_map/ppermute | solution.py:404
  63.8 17.9 %collective-permute-start.42 = (bf16[16,1024]{1,0:T(8,128)(2,1)S(1)}, bf16[16,1024]{1,0:T(8,128)(2,1)S(1)}, u32[]{:S(2)}, u32[]{:S(2)}) collective-permute-start(bf16[16,1024]{1,0:T(8,128)(2,1)S(1)} %get-tuple-element.61), channel_id=1, source_target_pairs={{0,1},{1,0},{2,3},{3,2},{4,5},{5,4},{6,7},{7,6},{8,9},{9,8},{10,11... | collective-permute-start | bytes 98312 | tf_op jit(solution)/shard_map/ppermute | solution.py:395
  63.8 19.5 %collective-permute-start.22 = (bf16[3,128,256]{2,1,0:T(8,128)(2,1)S(1)}, bf16[3,128,256]{2,1,0:T(8,128)(2,1)S(1)}, u32[]{:S(2)}, u32[]{:S(2)}) collective-permute-start(bf16[3,128,256]{2,1,0:T(8,128)(2,1)S(1)} %fusion.1.refs_0_), channel_id=1, source_target_pairs={{0,1},{1,0},{2,3},{3,2},{4,5},{5,4},{6,7},{7,6},{8,9},{9,8},{10,11... | collective-permute-start | bytes 589832 | tf_op jit(solution)/shard_map/ppermute | solution.py:395
  68.3 15.0 %collective-permute-start.23 = (bf16[3,128,256]{2,1,0:T(8,128)(2,1)S(1)}, bf16[3,128,256]{2,1,0:T(8,128)(2,1)S(1)}, u32[]{:S(2)}, u32[]{:S(2)}) collective-permute-start(bf16[3,128,256]{2,1,0:T(8,128)(2,1)S(1)} %collective-permute-done.3.refs_2_), channel_id=1, source_target_pairs={{0,1},{1,0},{2,3},{3,2},{4,5},{5,4},{6,7},{7,6},{8,9},{9,8},{10,11... | collective-permute-start | bytes 589832 | tf_op jit(solution)/shard_map/ppermute | solution.py:395
  79.4 6.5 %collective-permute-start.34 = (bf16[3,128,256]{2,1,0:T(8,128)(2,1)S(1)}, bf16[3,128,256]{2,1,0:T(8,128)(2,1)S(1)}, u32[]{:S(2)}, u32[]{:S(2)}) collective-permute-start(bf16[3,128,256]{2,1,0:T(8,128)(2,1)S(1)} %collective-permute-done.24.refs_4_), channel_id=1, source_target_pairs={{0,16},{16,0},{1,17},{17,1},{2,18},{18,2},{3,19},{19,3},{4,20},{20... | collective-permute-start | bytes 589832 | tf_op jit(solution)/shard_map/ppermute | solution.py:401
  82.8 7.7 %collective-permute-start.37 = (bf16[3,128,256]{2,1,0:T(8,128)(2,1)S(1)}, bf16[3,128,256]{2,1,0:T(8,128)(2,1)S(1)}, u32[]{:S(2)}, u32[]{:S(2)}) collective-permute-start(bf16[3,128,256]{2,1,0:T(8,128)(2,1)S(1)} %collective-permute-done.25.refs_8_), channel_id=1, source_target_pairs={{0,16},{16,0},{1,17},{17,1},{2,18},{18,2},{3,19},{19,3},{4,20},{20... | collective-permute-start | bytes 589832 | tf_op jit(solution)/shard_map/ppermute | solution.py:401
  83.4 7.2 %collective-permute-start.36 = (bf16[3,128,256]{2,1,0:T(8,128)(2,1)S(1)}, bf16[3,128,256]{2,1,0:T(8,128)(2,1)S(1)}, u32[]{:S(2)}, u32[]{:S(2)}) collective-permute-start(bf16[3,128,256]{2,1,0:T(8,128)(2,1)S(1)} %collective-permute-done.25.refs_8_), channel_id=1, source_target_pairs={{0,1},{1,0},{2,3},{3,2},{4,5},{5,4},{6,7},{7,6},{8,9},{9,8},{10,11... | collective-permute-start | bytes 589832 | tf_op jit(solution)/shard_map/ppermute | solution.py:395
  83.4 10.8 %collective-permute-start.40 = (bf16[3,128,256]{2,1,0:T(8,128)(2,1)S(1)}, bf16[3,128,256]{2,1,0:T(8,128)(2,1)S(1)}, u32[]{:S(2)}, u32[]{:S(2)}) collective-permute-start(bf16[3,128,256]{2,1,0:T(8,128)(2,1)S(1)} %collective-permute-done.26.refs_12_), channel_id=1, source_target_pairs={{0,16},{16,0},{1,17},{17,1},{2,18},{18,2},{3,19},{19,3},{4,20},{20... | collective-permute-start | bytes 589832 | tf_op jit(solution)/shard_map/ppermute | solution.py:401
  85.9 8.3 %collective-permute-start.43 = (bf16[144,1024]{1,0:T(8,128)(2,1)S(1)}, bf16[144,1024]{1,0:T(8,128)(2,1)S(1)}, u32[]{:S(2)}, u32[]{:S(2)}) collective-permute-start(bf16[144,1024]{1,0:T(8,128)(2,1)S(1)} %get-tuple-element.63), channel_id=1, source_target_pairs={{0,2},{2,0},{1,3},{3,1},{4,6},{6,4},{5,7},{7,5},{8,10},{10,8},{9,1... | collective-permute-start | bytes 884744 | tf_op jit(solution)/shard_map/ppermute | solution.py:398
  86.4 7.8 %collective-permute-start.39 = (bf16[3,128,256]{2,1,0:T(8,128)(2,1)S(1)}, bf16[3,128,256]{2,1,0:T(8,128)(2,1)S(1)}, u32[]{:S(2)}, u32[]{:S(2)}) collective-permute-start(bf16[3,128,256]{2,1,0:T(8,128)(2,1)S(1)} %collective-permute-done.26.refs_12_), channel_id=1, source_target_pairs={{0,1},{1,0},{2,3},{3,2},{4,5},{5,4},{6,7},{7,6},{8,9},{9,8},{10,11... | collective-permute-start | bytes 589832 | tf_op jit(solution)/shard_map/ppermute | solution.py:395
  (27 other events, 214.8 us)

commit v4 on v3

--- a/solution.py
+++ b/solution.py
@@ -166,13 +166,13 @@
     return [(i, i ^ k) for i in range(SEQ)]
 
 
-def call(kernel, outs, scratch, length, *operands, flops=0, vmem=8):
-    moved = sum(math.prod(a.shape) * a.dtype.itemsize for a in (*operands, *outs))
+def call(kernel, outs, scratch, length, *operands, vmem=8, left=0):
     return pl.pallas_call(
         kernel,
         out_shape=outs,
         in_specs=[pl.BlockSpec(memory_space=pltpu.SMEM)]
-        + [pl.BlockSpec(memory_space=pltpu.VMEM)] * len(operands),
+        + [pl.BlockSpec(memory_space=pl.ANY)] * left
+        + [pl.BlockSpec(memory_space=pltpu.VMEM)] * (len(operands) - left),
         out_specs=[pl.BlockSpec(memory_space=pltpu.VMEM)] * len(outs),
         scratch_shapes=scratch,
         cost_estimate=pl.CostEstimate(flops=0, bytes_accessed=0, transcendentals=0),
@@ -193,8 +193,14 @@
 
 
 def deal_kernel(length, *refs):
-    mine, other, outs = refs[:3], refs[3:6], refs[6:]
-    s, _, f, _ = here()
+    sources, other, outs, (held, sems) = refs[:4], refs[4:7], refs[7:-2], refs[-2:]
+    copies = [pltpu.make_async_copy(w, held.at[i], sems.at[i]) for i, w in enumerate(sources)]
+    for copy in copies:
+        copy.start()
+    mine, w_out = [held.at[m] for m in range(3)], held.at[3]
+    s, _, f, p = here()
+    for copy in copies:
+        copy.wait()
     half = outs[0].shape[1]
     rows = pl.ds(aligned(f * half, half), half)
     for k in range(SEQ):
@@ -211,17 +217,14 @@
             for m in range(3):
                 outs[k][m] = other[m][rows, columns]
 
-
-def stack_kernel(length, *refs):
-    s = lax.axis_index("seq")
-    for k in range(SEQ):
-        refs[SEQ][s ^ k] = refs[k][...]
+        for m in range(w_out.shape[1] // HD):
+            outs[k][3 + m] = w_out[pl.ds(aligned(p * half, half), half), m * HD : (m + 1) * HD]
 
 
 def project_kernel(length, *refs):
     blocks = refs[: 2 * SEQ]
     mine, other = refs[2 * SEQ : 3 * SEQ], refs[3 * SEQ : 4 * SEQ]
-    gain, q_out, send_out, edge_out, normed, weights, x_edge, q_edge = refs[4 * SEQ :]
+    gain, q_out, send_out, edge_out, stack_out, normed, weights, x_edge, q_edge = refs[4 * SEQ :]
     s, h, f, _ = here()
     rows = blocks[0].shape[0]
     half = mine[0].shape[1]
@@ -237,6 +240,7 @@
             at = pl.ds(aligned((s ^ k) * 2 * half + (f ^ core) * half, half), half)
             for m in range(3):
                 weights[at, m * HD : (m + 1) * HD] = pieces[k][m]
+        stack_out[s ^ k] = mine[k][3:]
     count = 2 * SEQ
     total = count * rows
     projected = dot(normed[...], weights[...])
@@ -294,15 +298,20 @@
 
 
 def output_kernel(length, *refs):
-    pieces, ctx = refs[:4], refs[4 : 4 + SEQ]
-    share_out, send_out, context, weights = refs[4 + SEQ :]
+    near, far, ctx = refs[: 2 * SEQ], refs[2 * SEQ : 2 * SEQ + 2], refs[2 * SEQ + 2 : 3 * SEQ + 2]
+    share_out, send_out, context, weights = refs[3 * SEQ + 2 :]
     s, h, f, p = here()
-    half, columns = pieces[0].shape[1:]
-    for y in range(2):
-        for core in range(2):
-            at = pl.ds(aligned((f ^ core) * 2 * half + (p ^ y) * half, half), half)
-            for j in range(SEQ):
-                weights[j, at, :] = pieces[y * 2 + core][j]
+    half = near[0].shape[1]
+    columns = weights.shape[2]
+    for core in range(2):
+        first = (f ^ core) * 2 * half
+        here_at = pl.ds(aligned(first + p * half, half), half)
+        there_at = pl.ds(aligned(first + (1 - p) * half, half), half)
+        for m in range(columns // HD):
+            at = slice(m * HD, (m + 1) * HD)
+            for k in range(SEQ):
+                weights[s ^ k, here_at, at] = near[core * SEQ + k][3 + m]
+                weights[k, there_at, at] = far[core][k, m]
     for k in range(SEQ):
         context[:, pl.ds(aligned((s ^ k) * HD, HD), HD)] = ctx[k][...]
     for j in range(SEQ):
@@ -313,23 +322,22 @@
 
 
 def convolve_kernel(length, *refs):
-    pieces = refs[: 4 * SEQ]
-    own_x, peer_x, halo_x, own_share, peer_share, gain, own_c, peer_c, base_out, share_out = refs[4 * SEQ : 4 * SEQ + 10]
-    mid, normed, w_value, w_gate, w_down, channel, padded, active, shares = refs[4 * SEQ + 10 :]
+    pieces, own_x, peer_x, halo_x, own_share, peer_share, gain, own_c, peer_c, base_out, share_out = refs[:11]
+    mid, normed, w_value, w_gate, w_down, channel, padded, active, shares = refs[11:]
     s, h, f, p = here()
     valid_len = length[0]
-    half, columns = pieces[0].shape[1:]
+    half, columns = pieces.shape[1:]
     rows = own_x.shape[0]
     step = rows + HALO
-    for k in range(SEQ):
-        for y in range(2):
+    for part in range(2):
+        for plane in range(SEQ):
             for core in range(2):
-                stack = pieces[(k * 2 + y) * 2 + core]
-                at = pl.ds(aligned((s ^ k) * 2 * half + (p ^ y) * half, half), half)
-                w_value[f ^ core, at, :] = stack[0]
-                w_gate[f ^ core, at, :] = stack[1]
-                at = pl.ds(aligned((f ^ core) * 2 * half + (p ^ y) * half, half), half)
-                w_down[s ^ k, at, :] = stack[2]
+                first = ((part * SEQ + plane) * 2 + core) * 3
+                at = slice((2 * plane + part) * half, (2 * plane + part + 1) * half)
+                w_value[core, at, :] = pieces[first]
+                w_gate[core, at, :] = pieces[first + 1]
+                at = slice((2 * core + part) * half, (2 * core + part + 1) * half)
+                w_down[plane, at, :] = pieces[first + 2]
     channel[f] = own_c[...]
     channel[1 - f] = peer_c[...]
     mid[pl.ds(aligned(h * step, 8), rows), :] = own_x[...].astype(F32)
@@ -410,31 +418,29 @@
     blocks = []
     for block in near:
         blocks += [block, other_side(block)]
+    pw_mine = part_half(jnp.stack([pw1_value, pw1_gate, pw2]))
+    pw_all = lax.all_gather(pw_mine, ("parts", "seq", "fsdp"), axis=0, tiled=True)
     given = [w_query, w_key, w_value]
     shape = jax.ShapeDtypeStruct
     dealt = call(
         deal_kernel,
-        [shape((3, half, HD), BF16)] * SEQ,
-        [],
+        [shape((3 + columns // HD, half, HD), BF16)] * SEQ,
+        [pltpu.VMEM((4, 2 * half, columns), BF16), pltpu.SemaphoreType.DMA((4,))],
         length,
         *given,
+        w_out,
         *[other_core(w) for w in given],
+        left=4,
     )
     w_mine = [dealt[0]] + [lax.ppermute(dealt[k], "seq", xor_pairs(k)) for k in range(1, SEQ)]
     w_other = [other_core(w) for w in w_mine]
-
-    out_mine = part_half(w_out)
-    after, *_ = barrier((out_mine, *near[1:], *w_mine[1:]))
-    out_others = planes(after)[1:]
-    pw_mine = part_half(jnp.stack([pw1_value, pw1_gate, pw2]))
-    pw_first, *_ = barrier((pw_mine, *near[1:]))
-    pw_part = other_part(pw_first)
-    queries, send, edges = call(
+    queries, send, edges, stack = call(
         project_kernel,
         [
             shape((count * rows, HD), BF16),
             shape((2 * count * rows + count * HALO, HD), BF16),
             shape((2 * HALO, width), BF16),
+            shape((SEQ, columns // HD, half, HD), BF16),
         ],
         [
             pltpu.VMEM((count * rows, width), BF16),
@@ -447,16 +453,9 @@
         *w_mine,
         *w_other,
         ln1_gain[None],
-        flops=6 * count * rows * width * HD,
     )
     received = other_core(send)
-    out_mine, _, *out_others = barrier((out_mine, received, *out_others))
-    (stack,) = call(stack_kernel, [shape((SEQ, half, columns), BF16)], [], length, out_mine, *out_others)
     stack_part = other_part(stack)
-    out_pieces = [stack, other_core(stack), stack_part, other_core(stack_part)]
-    queries, _ = barrier((queries, stack))
-    after, *_ = barrier((pw_mine, send, *out_others))
-    pw_others = planes(after)[1:]
     halo_x = other_core(edges)
     ctx = call(
         attend_kernel,
@@ -466,10 +465,9 @@
         queries,
         send,
         received,
-        flops=8 * count * step * count * rows * HD,
-    )
-    depth_kernel, pw_mine, pw_part, *_ = barrier((depth_kernel, pw_mine, pw_part, *ctx))
-    pw_pieces = [pw_mine, other_core(pw_mine), pw_part, other_core(pw_part)]
+    )
+    depth_kernel, stack_part, *_ = barrier((depth_kernel, stack_part, *ctx))
+    far = [stack_part, other_core(stack_part)]
     channels = jnp.concatenate([depth_kernel, bn_scale[None], bn_shift[None], jnp.zeros((5, columns), F32)])
     channels_peer = other_core(channels)
     ctx = [ctx[0]] + [lax.ppermute(ctx[k], "seq", xor_pairs(k)) for k in range(1, SEQ)]
@@ -481,14 +479,11 @@
             pltpu.VMEM((SEQ, 2 * columns, columns), BF16),
         ],
         length,
-        *out_pieces,
+        *w_mine,
+        *w_other,
+        *far,
         *ctx,
-        flops=2 * step * width * width,
-    )
-    *pw_others, own_share, sent_share = barrier((*pw_others, own_share, sent_share))
-    for near in pw_others:
-        part = other_part(near)
-        pw_pieces += [near, other_core(near), part, other_core(part)]
+    )
     base, share = call(
         convolve_kernel,
         [shape((rows, width), F32), shape((rows, width), BF16)],
@@ -504,7 +499,7 @@
             pltpu.VMEM((2 * rows, width), F32),
         ],
         length,
-        *pw_pieces,
+        pw_all,
         frames,
         blocks[1],
         halo_x,
@@ -513,7 +508,6 @@
         ln2_gain[None],
         channels,
         channels_peer,
-        flops=6 * step * width * width,
         vmem=14,
     )
     return (base + other_side(share).astype(F32)).astype(BF16)

time: 104 us -> 97.5 us (0.938)
  waiting for transfers between devices: 55.1 us -> 36 us
  between operations: 0.91 us -> 14.2 us
  starting transfers between devices: 36.6 us -> 30.2 us
  local copies, waits for them, and re-layouts: 3.55 us -> 7.2 us
  other arithmetic: 0.78 us -> 2.38 us
    ppermute x9 -> x3, waiting for transfers between devices: 24.7 us -> 0.67 us  [planes(): return [x] + [lax.ppermute(x, 'seq', xor_pairs(k)) for k in range(1, SEQ)]]
    ppermute x5 -> x1, waiting for transfers between devices: 15.2 us -> 4.7 us  [other_part(): return lax.ppermute(x, 'parts', SWAP)]
    ppermute x6, waiting for transfers between devices: 7.46 us -> 15.3 us  [other_side(): return lax.ppermute(x, 'head', SWAP)]
    ppermute x9 -> x3, starting transfers between devices: 12.9 us -> 5.64 us  [planes(): return [x] + [lax.ppermute(x, 'seq', xor_pairs(k)) for k in range(1, SEQ)]]
    ppermute x3, waiting for transfers between devices: 4.55 us -> 9.96 us  [shards_chip_per_head(): lax.ppermute(dealt[k], 'seq', xor_pairs(k))]
    ppermute x5 -> x1, starting transfers between devices: 5.77 us -> 1.58 us  [other_part(): return lax.ppermute(x, 'parts', SWAP)]
    unnamed x26 -> x24, local copies, waits for them, and re-layouts: 3.46 us -> 7.12 us
    ppermute x3, waiting for transfers between devices: 1.01 us -> 4.48 us  [shards_chip_per_head(): lax.ppermute(ctx[k], 'seq', xor_pairs(k))]
  transfers between devices with their start and end apart: 46 -> 28, of which waited for: 17 -> 12; matrix products, arithmetic and copies ran while one was open for 0% -> 0% of each run, Pallas kernels for 3% -> 6%
where the time goes in v4:
time: 97.5 us; the launch traced here: 97.2 us
  waiting for transfers between devices  36 us (37%)
  starting transfers between devices  30.2 us (31%)
  between operations  14.2 us (15%)
  local copies, waits for them, and re-layouts  7.2 us (7%)
  Pallas kernels  7.14 us (7%)
  other arithmetic  2.38 us (2%)
    ppermute x6, waiting for transfers between devices, other_side(): return lax.ppermute(x, 'head', SWAP)  15.3 us
    ppermute x3, waiting for transfers between devices, shards_chip_per_head(): lax.ppermute(dealt[k], 'seq', xor_pairs(k))  9.96 us
    ppermute x6, starting transfers between devices, other_side(): return lax.ppermute(x, 'head', SWAP)  8.09 us
    ppermute x3, starting transfers between devices, shards_chip_per_head(): lax.ppermute(dealt[k], 'seq', xor_pairs(k))  7.49 us
    pallas_call x5, Pallas kernels, call(): pl.pallas_call(kernel, out_shape=outs, in_specs=[pl.BlockSpec(memory_spac...  7.14 us
    unnamed x24, local copies, waits for them, and re-layouts  7.12 us
    ppermute x3, starting transfers between devices, planes(): return [x] + [lax.ppermute(x, 'seq', xor_pairs(k)) for k in range(1, SEQ)]  5.64 us
    ppermute x3, starting transfers between devices, shards_chip_per_head(): lax.ppermute(ctx[k], 'seq', xor_pairs(k))  5.27 us
  transfers between devices with their start and end apart: 28, of which 12 were waited for; matrix products, arithmetic and copies ran while one was open for 0% of the time, Pallas kernels for 6%

profile of v4, /device:TPU:0, one launch (start us, length us, event | category | flops | bytes accessed | tf_op | source)
XLA Modules:
  0.0 97.2 jit_solution(6213632342192710972)
XLA Ops:
  6.5 1.6 %fusion.1 = bf16[3,128,256]{2,1,0:T(8,128)(2,1)} fusion(s32[]{:T(128)S(6)} %select_n.3, bf16[1,256,256]{2,1,0:T(8,128)(2,1)} %bitcast.9, bf16[1,256,256]{2,1,0:T(8,128)(2,1)} %bitcast.10, bf16[1,256,256]{2,1,0:T(8,128)(2,1)} %bitcast.11), kind=kLoop, calls=%fused_computation.5 | loop fusion | flops 589824 | bytes 589828 | tf_op jit(solution)/shard_map/stack | solution.py:421
  9.2 2.7 %collective-permute-start.1 = (bf16[64,1024]{1,0:T(8,128)(2,1)}, bf16[64,1024]{1,0:T(8,128)(2,1)S(1)}, u32[]{:S(2)}, u32[]{:S(2)}) collective-permute-start(bf16[64,1024]{1,0:T(8,128)(2,1)} %refs_1_.3), channel_id=1, source_target_pairs={{0,4},{4,0},{8,12},{12,8},{1,5},{5,1},{9,13},{13,9},{2,6},{6,2},{1... | collective-permute-start | bytes 393224 | tf_op jit(solution)/shard_map/ppermute | solution.py:412
  11.9 2.6 %collective-permute-start.3 = (bf16[64,1024]{1,0:T(8,128)(2,1)}, bf16[64,1024]{1,0:T(8,128)(2,1)S(1)}, u32[]{:S(2)}, u32[]{:S(2)}) collective-permute-start(bf16[64,1024]{1,0:T(8,128)(2,1)} %refs_1_.3), channel_id=1, source_target_pairs={{0,8},{4,12},{8,0},{12,4},{1,9},{5,13},{9,1},{13,5},{2,10},{6,14},... | collective-permute-start | bytes 393224 | tf_op jit(solution)/shard_map/ppermute | solution.py:412
  14.9 1.5 %collective-permute-start = (bf16[64,1024]{1,0:T(8,128)(2,1)}, bf16[64,1024]{1,0:T(8,128)(2,1)S(1)}, u32[]{:S(2)}, u32[]{:S(2)}) collective-permute-start(bf16[64,1024]{1,0:T(8,128)(2,1)} %refs_1_.3), channel_id=1, source_target_pairs={{0,2},{2,0},{1,3},{3,1},{4,6},{6,4},{5,7},{7,5},{8,10},{10,8},{9,1... | collective-permute-start | bytes 393224 | tf_op jit(solution)/shard_map/ppermute | solution.py:406
  17.0 0.9 copy-done.3
  17.9 0.9 copy-done.4
  18.8 0.9 copy-done.5
  19.8 0.9 copy-done.6
  20.7 0.9 shard_map.136
  22.1 3.5 %collective-permute-start.11 = (bf16[5,128,128]{2,1,0:T(8,128)(2,1)S(1)}, bf16[5,128,128]{2,1,0:T(8,128)(2,1)S(1)}, u32[]{:S(2)}, u32[]{:S(2)}) collective-permute-start(bf16[5,128,128]{2,1,0:T(8,128)(2,1)S(1)} %get-tuple-element.25), channel_id=1, source_target_pairs={{0,8},{4,12},{8,0},{12,4},{1,9},{5,13},{9,1},{13,5},{2,10},{6,14},... | collective-permute-start | bytes 491528 | tf_op jit(solution)/shard_map/ppermute | solution.py:435
  26.3 3.4 %collective-permute-start.12 = (bf16[5,128,128]{2,1,0:T(8,128)(2,1)S(1)}, bf16[5,128,128]{2,1,0:T(8,128)(2,1)S(1)}, u32[]{:S(2)}, u32[]{:S(2)}) collective-permute-start(bf16[5,128,128]{2,1,0:T(8,128)(2,1)S(1)} %get-tuple-element.26), channel_id=1, source_target_pairs={{0,12},{4,8},{8,4},{12,0},{1,13},{5,9},{9,5},{13,1},{2,14},{6,10},... | collective-permute-start | bytes 491528 | tf_op jit(solution)/shard_map/ppermute | solution.py:435
  29.7 1.5 %collective-permute-start.2 = (bf16[64,1024]{1,0:T(8,128)(2,1)S(1)}, bf16[64,1024]{1,0:T(8,128)(2,1)S(1)}, u32[]{:S(2)}, u32[]{:S(2)}) collective-permute-start(bf16[64,1024]{1,0:T(8,128)(2,1)S(1)} %collective-permute-done.1.refs_2_), channel_id=1, source_target_pairs={{0,2},{2,0},{1,3},{3,1},{4,6},{6,4},{5,7},{7,5},{8,10},{10,8},{9,1... | collective-permute-start | bytes 393224 | tf_op jit(solution)/shard_map/ppermute | solution.py:406
  31.7 2.9 %collective-permute-done.2.refs_3_ = bf16[64,1024]{1,0:T(8,128)(2,1)S(1)} collective-permute-done((bf16[64,1024]{1,0:T(8,128)(2,1)S(1)}, bf16[64,1024]{1,0:T(8,128)(2,1)S(1)}, u32[]{:S(2)}, u32[]{:S(2)}) %collective-permute-start.2) | collective-permute-done | bytes 131104 | tf_op jit(solution)/shard_map/ppermute | solution.py:406
  35.2 9.4 %collective-permute-done.11.refs_10_.refs_2_ = bf16[5,128,128]{2,1,0:T(8,128)(2,1)S(1)} collective-permute-done((bf16[5,128,128]{2,1,0:T(8,128)(2,1)S(1)}, bf16[5,128,128]{2,1,0:T(8,128)(2,1)S(1)}, u32[]{:S(2)}, u32[]{:S(2)}) %collective-permute-start.11) | collective-permute-done | bytes 163872 | tf_op jit(solution)/shard_map/ppermute | solution.py:435
  45.2 1.5 %collective-permute-start.6 = (bf16[64,1024]{1,0:T(8,128)(2,1)S(1)}, bf16[64,1024]{1,0:T(8,128)(2,1)S(1)}, u32[]{:S(2)}, u32[]{:S(2)}) collective-permute-start(bf16[64,1024]{1,0:T(8,128)(2,1)S(1)} %collective-permute-done.5.refs_6_), channel_id=1, source_target_pairs={{0,2},{2,0},{1,3},{3,1},{4,6},{6,4},{5,7},{7,5},{8,10},{10,8},{9,1... | collective-permute-start | bytes 393224 | tf_op jit(solution)/shard_map/ppermute | solution.py:406
  46.7 4.0 %collective-permute-done.6.refs_7_ = bf16[64,1024]{1,0:T(8,128)(2,1)S(1)} collective-permute-done((bf16[64,1024]{1,0:T(8,128)(2,1)S(1)}, bf16[64,1024]{1,0:T(8,128)(2,1)S(1)}, u32[]{:S(2)}, u32[]{:S(2)}) %collective-permute-start.6) | collective-permute-done | bytes 131104 | tf_op jit(solution)/shard_map/ppermute | solution.py:406
  50.7 0.9 copy-done.1
  52.3 1.6 %shard_map.137 = (bf16[512,128]{1,0:T(8,128)(2,1)S(1)}, bf16[1088,128]{1,0:T(8,128)(2,1)S(1)}, bf16[16,1024]{1,0:T(8,128)(2,1)S(1)}, bf16[4,2,128,128]{3,2,1,0:T(8,128)(2,1)S(1)}) custom-call(s32[1]{0:T(128)S(6)} %copy.15.length, bf16[64,1024]{1,0:T(8,128)(2,1)S(1)} %copy-done.1, bf16[64,1024]{1,0:T(8,128)(2,1)S(1)} %collective-permute-done.refs_1_.refs_2_, ...), custom_call_target="tpu_custom_call" | custom-call | tf_op jit(solution)/shard_map/pallas_call | solution.py:170
  54.0 1.6 %collective-permute-start.18 = (bf16[4,2,128,128]{3,2,1,0:T(8,128)(2,1)S(1)}, bf16[4,2,128,128]{3,2,1,0:T(8,128)(2,1)S(1)}, u32[]{:S(2)}, u32[]{:S(2)}) collective-permute-start(bf16[4,2,128,128]{3,2,1,0:T(8,128)(2,1)S(1)} %get-tuple-element.28), channel_id=1, source_target_pairs={{0,16},{16,0},{1,17},{17,1},{2,18},{18,2},{3,19},{19,3},{4,20},{20... | collective-permute-start | bytes 786440 | tf_op jit(solution)/shard_map/ppermute | solution.py:409
  55.6 2.9 %shard_map.138 = (bf16[144,128]{1,0:T(8,128)(2,1)S(1)}, bf16[144,128]{1,0:T(8,128)(2,1)S(1)}, bf16[144,128]{1,0:T(8,128)(2,1)S(1)}, bf16[144,128]{1,0:T(8,128)(2,1)S(1)}) custom-call(s32[1]{0:T(128)S(6)} %copy.15.length, bf16[512,128]{1,0:T(8,128)(2,1)S(1)} %get-tuple-element.29.q_in, bf16[1088,128]{1,0:T(8,128)(2,1)S(1)} %get-tuple-element.30.own, ...), custom_call_target="tpu_custom_call" | custom-call | tf_op jit(solution)/shard_map/pallas_call | solution.py:170
  58.4 4.7 %collective-permute-done.18.refs_8_ = bf16[4,2,128,128]{3,2,1,0:T(8,128)(2,1)S(1)} collective-permute-done((bf16[4,2,128,128]{3,2,1,0:T(8,128)(2,1)S(1)}, bf16[4,2,128,128]{3,2,1,0:T(8,128)(2,1)S(1)}, u32[]{:S(2)}, u32[]{:S(2)}) %collective-permute-start.18) | collective-permute-done | bytes 262176 | tf_op jit(solution)/shard_map/ppermute | solution.py:409
  63.1 2.8 %collective-permute-start.21 = (bf16[144,128]{1,0:T(8,128)(2,1)S(1)}, bf16[144,128]{1,0:T(8,128)(2,1)S(1)}, u32[]{:S(2)}, u32[]{:S(2)}) collective-permute-start(bf16[144,128]{1,0:T(8,128)(2,1)S(1)} %get-tuple-element.32), channel_id=1, source_target_pairs={{0,4},{4,0},{8,12},{12,8},{1,5},{5,1},{9,13},{13,9},{2,6},{6,2},{1... | collective-permute-start | bytes 110600 | tf_op jit(solution)/shard_map/ppermute | solution.py:473
  66.0 1.1 %collective-permute-start.22 = (bf16[144,128]{1,0:T(8,128)(2,1)S(1)}, bf16[144,128]{1,0:T(8,128)(2,1)S(1)}, u32[]{:S(2)}, u32[]{:S(2)}) collective-permute-start(bf16[144,128]{1,0:T(8,128)(2,1)S(1)} %get-tuple-element.33), channel_id=1, source_target_pairs={{0,8},{4,12},{8,0},{12,4},{1,9},{5,13},{9,1},{13,5},{2,10},{6,14},... | collective-permute-start | bytes 110600 | tf_op jit(solution)/shard_map/ppermute | solution.py:473
  67.1 1.3 %collective-permute-start.23 = (bf16[144,128]{1,0:T(8,128)(2,1)S(1)}, bf16[144,128]{1,0:T(8,128)(2,1)S(1)}, u32[]{:S(2)}, u32[]{:S(2)}) collective-permute-start(bf16[144,128]{1,0:T(8,128)(2,1)S(1)} %get-tuple-element.34), channel_id=1, source_target_pairs={{0,12},{4,8},{8,4},{12,0},{1,13},{5,9},{9,5},{13,1},{2,14},{6,10},... | collective-permute-start | bytes 110600 | tf_op jit(solution)/shard_map/ppermute | solution.py:473
  68.4 3.2 %collective-permute-done.22.refs_12_ = bf16[144,128]{1,0:T(8,128)(2,1)S(1)} collective-permute-done((bf16[144,128]{1,0:T(8,128)(2,1)S(1)}, bf16[144,128]{1,0:T(8,128)(2,1)S(1)}, u32[]{:S(2)}, u32[]{:S(2)}) %collective-permute-start.22) | collective-permute-done | bytes 36896 | tf_op jit(solution)/shard_map/ppermute | solution.py:473
  71.6 1.3 %collective-permute-done.23.refs_13_ = bf16[144,128]{1,0:T(8,128)(2,1)S(1)} collective-permute-done((bf16[144,128]{1,0:T(8,128)(2,1)S(1)}, bf16[144,128]{1,0:T(8,128)(2,1)S(1)}, u32[]{:S(2)}, u32[]{:S(2)}) %collective-permute-start.23) | collective-permute-done | bytes 36896 | tf_op jit(solution)/shard_map/ppermute | solution.py:473
  73.4 1.5 %collective-permute-start.24 = (bf16[144,1024]{1,0:T(8,128)(2,1)S(1)}, bf16[144,1024]{1,0:T(8,128)(2,1)S(1)}, u32[]{:S(2)}, u32[]{:S(2)}) collective-permute-start(bf16[144,1024]{1,0:T(8,128)(2,1)S(1)} %get-tuple-element.37), channel_id=1, source_target_pairs={{0,2},{2,0},{1,3},{3,1},{4,6},{6,4},{5,7},{7,5},{8,10},{10,8},{9,1... | collective-permute-start | bytes 884744 | tf_op jit(solution)/shard_map/ppermute | solution.py:406
  76.5 5.0 %collective-permute-done.24.refs_5_ = bf16[144,1024]{1,0:T(8,128)(2,1)S(1)} collective-permute-done((bf16[144,1024]{1,0:T(8,128)(2,1)S(1)}, bf16[144,1024]{1,0:T(8,128)(2,1)S(1)}, u32[]{:S(2)}, u32[]{:S(2)}) %collective-permute-start.24) | collective-permute-done | bytes 294944 | tf_op jit(solution)/shard_map/ppermute | solution.py:406
  81.4 1.9 %copy-done = bf16[48,128,256]{2,1,0:T(8,128)(2,1)S(1)} copy-done((bf16[48,128,256]{2,1,0:T(8,128)(2,1)S(1)}, bf16[48,128,256]{2,1,0:T(8,128)(2,1)}, u32[]{:S(2)}) %copy-start) | copy-done | bytes 3145752
  83.3 1.3 %shard_map.140 = (f32[64,1024]{1,0:T(8,128)S(1)}, bf16[64,1024]{1,0:T(8,128)(2,1)S(1)}) custom-call(s32[1]{0:T(128)S(6)} %copy.15.length, bf16[48,128,256]{2,1,0:T(8,128)(2,1)S(1)} %copy-done, bf16[64,1024]{1,0:T(8,128)(2,1)S(1)} %copy-done.2, bf16[64,1024]{1,0:T(8,128)(2,1)S(1)} %collective-permute-done.refs_1_.refs_2_, ...), custom_call_target="tpu_custom_call" | custom-call | tf_op jit(solution)/shard_map/pallas_call | solution.py:170
  84.6 1.6 %collective-permute-start.26 = (bf16[64,1024]{1,0:T(8,128)(2,1)S(1)}, bf16[64,1024]{1,0:T(8,128)(2,1)S(1)}, u32[]{:S(2)}, u32[]{:S(2)}) collective-permute-start(bf16[64,1024]{1,0:T(8,128)(2,1)S(1)} %get-tuple-element.40), channel_id=1, source_target_pairs={{0,2},{2,0},{1,3},{3,1},{4,6},{6,4},{5,7},{7,5},{8,10},{10,8},{9,1... | collective-permute-start | bytes 393224 | tf_op jit(solution)/shard_map/ppermute | solution.py:406
  86.2 3.5 %collective-permute-done.26 = bf16[64,1024]{1,0:T(8,128)(2,1)S(1)} collective-permute-done((bf16[64,1024]{1,0:T(8,128)(2,1)S(1)}, bf16[64,1024]{1,0:T(8,128)(2,1)S(1)}, u32[]{:S(2)}, u32[]{:S(2)}) %collective-permute-start.26) | collective-permute-done | bytes 131104 | tf_op jit(solution)/shard_map/ppermute | solution.py:406
  (59 shorter events, 7.8 us)
Async XLA Ops:
  6.5 74.9 %all-gather.2.cloned.1.call-start = ((), (), s32[]{:S(2)}) async-start(), calls=%async_computation | async-start | bytes 3342336 | tf_op jit(solution)/shard_map/all_gather | solution.py:422
  8.2 66.9 %copy-start.10 = (f32[256]{0:T(256)S(1)}, f32[256]{0:T(256)}, u32[]{:S(2)}) copy-start(f32[256]{0:T(256)} %param.26) | copy-start | bytes 3076
  8.2 66.9 %copy-start.11 = (f32[256]{0:T(256)S(1)}, f32[256]{0:T(256)}, u32[]{:S(2)}) copy-start(f32[256]{0:T(256)} %param.25) | copy-start | bytes 3076
  8.2 73.3 %copy-start.2 = (bf16[64,1024]{1,0:T(8,128)(2,1)S(1)}, bf16[64,1024]{1,0:T(8,128)(2,1)}, u32[]{:S(2)}) copy-start(bf16[64,1024]{1,0:T(8,128)(2,1)} %refs_1_.3) | copy-start | bytes 393220
  8.2 73.2 %copy-start.8 = (f32[1024]{0:T(1024)S(1)}, f32[1024]{0:T(1024)}, u32[]{:S(2)}) copy-start(f32[1024]{0:T(1024)} %param.21) | copy-start | bytes 12292
  8.2 6.3 %collective-permute-start.7 = (bf16[256,256]{1,0:T(8,128)(2,1)}, bf16[256,256]{1,0:T(8,128)(2,1)S(1)}, u32[]{:S(2)}, u32[]{:S(2)}) collective-permute-start(bf16[256,256]{1,0:T(8,128)(2,1)} %refs_0_.2), channel_id=1, source_target_pairs={{0,1},{1,0},{2,3},{3,2},{4,5},{5,4},{6,7},{7,6},{8,9},{9,8},{10,11... | collective-permute-start | bytes 393224 | tf_op jit(solution)/shard_map/ppermute | solution.py:403
  8.7 6.2 %collective-permute-start.8 = (bf16[256,256]{1,0:T(8,128)(2,1)}, bf16[256,256]{1,0:T(8,128)(2,1)S(1)}, u32[]{:S(2)}, u32[]{:S(2)}) collective-permute-start(bf16[256,256]{1,0:T(8,128)(2,1)} %refs_1_.2), channel_id=1, source_target_pairs={{0,1},{1,0},{2,3},{3,2},{4,5},{5,4},{6,7},{7,6},{8,9},{9,8},{10,11... | collective-permute-start | bytes 393224 | tf_op jit(solution)/shard_map/ppermute | solution.py:403
  8.8 8.2 %collective-permute-start.9 = (bf16[256,256]{1,0:T(8,128)(2,1)}, bf16[256,256]{1,0:T(8,128)(2,1)S(1)}, u32[]{:S(2)}, u32[]{:S(2)}) collective-permute-start(bf16[256,256]{1,0:T(8,128)(2,1)} %refs_2_.1), channel_id=1, source_target_pairs={{0,1},{1,0},{2,3},{3,2},{4,5},{5,4},{6,7},{7,6},{8,9},{9,8},{10,11... | collective-permute-start | bytes 393224 | tf_op jit(solution)/shard_map/ppermute | solution.py:403
  9.2 12.9 %collective-permute-start.1 = (bf16[64,1024]{1,0:T(8,128)(2,1)}, bf16[64,1024]{1,0:T(8,128)(2,1)S(1)}, u32[]{:S(2)}, u32[]{:S(2)}) collective-permute-start(bf16[64,1024]{1,0:T(8,128)(2,1)} %refs_1_.3), channel_id=1, source_target_pairs={{0,4},{4,0},{8,12},{12,8},{1,5},{5,1},{9,13},{13,9},{2,6},{6,2},{1... | collective-permute-start | bytes 393224 | tf_op jit(solution)/shard_map/ppermute | solution.py:412
  11.9 14.4 %collective-permute-start.3 = (bf16[64,1024]{1,0:T(8,128)(2,1)}, bf16[64,1024]{1,0:T(8,128)(2,1)S(1)}, u32[]{:S(2)}, u32[]{:S(2)}) collective-permute-start(bf16[64,1024]{1,0:T(8,128)(2,1)} %refs_1_.3), channel_id=1, source_target_pairs={{0,8},{4,12},{8,0},{12,4},{1,9},{5,13},{9,1},{13,5},{2,10},{6,14},... | collective-permute-start | bytes 393224 | tf_op jit(solution)/shard_map/ppermute | solution.py:412
  14.5 15.2 %collective-permute-start.5 = (bf16[64,1024]{1,0:T(8,128)(2,1)}, bf16[64,1024]{1,0:T(8,128)(2,1)S(1)}, u32[]{:S(2)}, u32[]{:S(2)}) collective-permute-start(bf16[64,1024]{1,0:T(8,128)(2,1)} %refs_1_.3), channel_id=1, source_target_pairs={{0,12},{4,8},{8,4},{12,0},{1,13},{5,9},{9,5},{13,1},{2,14},{6,10},... | collective-permute-start | bytes 393224 | tf_op jit(solution)/shard_map/ppermute | solution.py:412
  14.9 16.3 %collective-permute-start = (bf16[64,1024]{1,0:T(8,128)(2,1)}, bf16[64,1024]{1,0:T(8,128)(2,1)S(1)}, u32[]{:S(2)}, u32[]{:S(2)}) collective-permute-start(bf16[64,1024]{1,0:T(8,128)(2,1)} %refs_1_.3), channel_id=1, source_target_pairs={{0,2},{2,0},{1,3},{3,1},{4,6},{6,4},{5,7},{7,5},{8,10},{10,8},{9,1... | collective-permute-start | bytes 393224 | tf_op jit(solution)/shard_map/ppermute | solution.py:406
  21.5 13.7 %collective-permute-start.10 = (bf16[5,128,128]{2,1,0:T(8,128)(2,1)S(1)}, bf16[5,128,128]{2,1,0:T(8,128)(2,1)S(1)}, u32[]{:S(2)}, u32[]{:S(2)}) collective-permute-start(bf16[5,128,128]{2,1,0:T(8,128)(2,1)S(1)} %get-tuple-element.24), channel_id=1, source_target_pairs={{0,4},{4,0},{8,12},{12,8},{1,5},{5,1},{9,13},{13,9},{2,6},{6,2},{1... | collective-permute-start | bytes 491528 | tf_op jit(solution)/shard_map/ppermute | solution.py:435
  22.1 22.6 %collective-permute-start.11 = (bf16[5,128,128]{2,1,0:T(8,128)(2,1)S(1)}, bf16[5,128,128]{2,1,0:T(8,128)(2,1)S(1)}, u32[]{:S(2)}, u32[]{:S(2)}) collective-permute-start(bf16[5,128,128]{2,1,0:T(8,128)(2,1)S(1)} %get-tuple-element.25), channel_id=1, source_target_pairs={{0,8},{4,12},{8,0},{12,4},{1,9},{5,13},{9,1},{13,5},{2,10},{6,14},... | collective-permute-start | bytes 491528 | tf_op jit(solution)/shard_map/ppermute | solution.py:435
  26.3 18.4 %collective-permute-start.12 = (bf16[5,128,128]{2,1,0:T(8,128)(2,1)S(1)}, bf16[5,128,128]{2,1,0:T(8,128)(2,1)S(1)}, u32[]{:S(2)}, u32[]{:S(2)}) collective-permute-start(bf16[5,128,128]{2,1,0:T(8,128)(2,1)S(1)} %get-tuple-element.26), channel_id=1, source_target_pairs={{0,12},{4,8},{8,4},{12,0},{1,13},{5,9},{9,5},{13,1},{2,14},{6,10},... | collective-permute-start | bytes 491528 | tf_op jit(solution)/shard_map/ppermute | solution.py:435
  29.7 5.0 %collective-permute-start.2 = (bf16[64,1024]{1,0:T(8,128)(2,1)S(1)}, bf16[64,1024]{1,0:T(8,128)(2,1)S(1)}, u32[]{:S(2)}, u32[]{:S(2)}) collective-permute-start(bf16[64,1024]{1,0:T(8,128)(2,1)S(1)} %collective-permute-done.1.refs_2_), channel_id=1, source_target_pairs={{0,2},{2,0},{1,3},{3,1},{4,6},{6,4},{5,7},{7,5},{8,10},{10,8},{9,1... | collective-permute-start | bytes 393224 | tf_op jit(solution)/shard_map/ppermute | solution.py:406
  31.2 14.0 %collective-permute-start.4 = (bf16[64,1024]{1,0:T(8,128)(2,1)S(1)}, bf16[64,1024]{1,0:T(8,128)(2,1)S(1)}, u32[]{:S(2)}, u32[]{:S(2)}) collective-permute-start(bf16[64,1024]{1,0:T(8,128)(2,1)S(1)} %collective-permute-done.3.refs_4_), channel_id=1, source_target_pairs={{0,2},{2,0},{1,3},{3,1},{4,6},{6,4},{5,7},{7,5},{8,10},{10,8},{9,1... | collective-permute-start | bytes 393224 | tf_op jit(solution)/shard_map/ppermute | solution.py:406
  34.7 16.0 %collective-permute-start.13 = (bf16[5,128,128]{2,1,0:T(8,128)(2,1)S(1)}, bf16[5,128,128]{2,1,0:T(8,128)(2,1)S(1)}, u32[]{:S(2)}, u32[]{:S(2)}) collective-permute-start(bf16[5,128,128]{2,1,0:T(8,128)(2,1)S(1)} %get-tuple-element.23.refs_8_.refs_0_), channel_id=1, source_target_pairs={{0,1},{1,0},{2,3},{3,2},{4,5},{5,4},{6,7},{7,6},{8,9},{9,8},{10,11... | collective-permute-start | bytes 491528 | tf_op jit(solution)/shard_map/ppermute | solution.py:403
  35.2 15.4 %collective-permute-start.14 = (bf16[5,128,128]{2,1,0:T(8,128)(2,1)S(1)}, bf16[5,128,128]{2,1,0:T(8,128)(2,1)S(1)}, u32[]{:S(2)}, u32[]{:S(2)}) collective-permute-start(bf16[5,128,128]{2,1,0:T(8,128)(2,1)S(1)} %collective-permute-done.10.refs_9_.refs_1_), channel_id=1, source_target_pairs={{0,1},{1,0},{2,3},{3,2},{4,5},{5,4},{6,7},{7,6},{8,9},{9,8},{10,11... | collective-permute-start | bytes 491528 | tf_op jit(solution)/shard_map/ppermute | solution.py:403
  44.7 6.0 %collective-permute-start.15 = (bf16[5,128,128]{2,1,0:T(8,128)(2,1)S(1)}, bf16[5,128,128]{2,1,0:T(8,128)(2,1)S(1)}, u32[]{:S(2)}, u32[]{:S(2)}) collective-permute-start(bf16[5,128,128]{2,1,0:T(8,128)(2,1)S(1)} %collective-permute-done.11.refs_10_.refs_2_), channel_id=1, source_target_pairs={{0,1},{1,0},{2,3},{3,2},{4,5},{5,4},{6,7},{7,6},{8,9},{9,8},{10,11... | collective-permute-start | bytes 491528 | tf_op jit(solution)/shard_map/ppermute | solution.py:403
  44.7 6.0 %collective-permute-start.16 = (bf16[5,128,128]{2,1,0:T(8,128)(2,1)S(1)}, bf16[5,128,128]{2,1,0:T(8,128)(2,1)S(1)}, u32[]{:S(2)}, u32[]{:S(2)}) collective-permute-start(bf16[5,128,128]{2,1,0:T(8,128)(2,1)S(1)} %collective-permute-done.12.refs_11_.refs_3_), channel_id=1, source_target_pairs={{0,1},{1,0},{2,3},{3,2},{4,5},{5,4},{6,7},{7,6},{8,9},{9,8},{10,11... | collective-permute-start | bytes 491528 | tf_op jit(solution)/shard_map/ppermute | solution.py:403
  45.2 5.5 %collective-permute-start.6 = (bf16[64,1024]{1,0:T(8,128)(2,1)S(1)}, bf16[64,1024]{1,0:T(8,128)(2,1)S(1)}, u32[]{:S(2)}, u32[]{:S(2)}) collective-permute-start(bf16[64,1024]{1,0:T(8,128)(2,1)S(1)} %collective-permute-done.5.refs_6_), channel_id=1, source_target_pairs={{0,2},{2,0},{1,3},{3,1},{4,6},{6,4},{5,7},{7,5},{8,10},{10,8},{9,1... | collective-permute-start | bytes 393224 | tf_op jit(solution)/shard_map/ppermute | solution.py:406
  53.9 1.7 %collective-permute-start.19 = (bf16[1088,128]{1,0:T(8,128)(2,1)S(1)}, bf16[1088,128]{1,0:T(8,128)(2,1)S(1)}, u32[]{:S(2)}, u32[]{:S(2)}) collective-permute-start(bf16[1088,128]{1,0:T(8,128)(2,1)S(1)} %get-tuple-element.30.own), channel_id=1, source_target_pairs={{0,1},{1,0},{2,3},{3,2},{4,5},{5,4},{6,7},{7,6},{8,9},{9,8},{10,11... | collective-permute-start | bytes 835592 | tf_op jit(solution)/shard_map/ppermute | solution.py:403
  54.0 9.1 %collective-permute-start.18 = (bf16[4,2,128,128]{3,2,1,0:T(8,128)(2,1)S(1)}, bf16[4,2,128,128]{3,2,1,0:T(8,128)(2,1)S(1)}, u32[]{:S(2)}, u32[]{:S(2)}) collective-permute-start(bf16[4,2,128,128]{3,2,1,0:T(8,128)(2,1)S(1)} %get-tuple-element.28), channel_id=1, source_target_pairs={{0,16},{16,0},{1,17},{17,1},{2,18},{18,2},{3,19},{19,3},{4,20},{20... | collective-permute-start | bytes 786440 | tf_op jit(solution)/shard_map/ppermute | solution.py:409
  63.1 9.8 %collective-permute-start.20 = (bf16[4,2,128,128]{3,2,1,0:T(8,128)(2,1)S(1)}, bf16[4,2,128,128]{3,2,1,0:T(8,128)(2,1)S(1)}, u32[]{:S(2)}, u32[]{:S(2)}) collective-permute-start(bf16[4,2,128,128]{3,2,1,0:T(8,128)(2,1)S(1)} %collective-permute-done.18.refs_8_), channel_id=1, source_target_pairs={{0,1},{1,0},{2,3},{3,2},{4,5},{5,4},{6,7},{7,6},{8,9},{9,8},{10,11... | collective-permute-start | bytes 786440 | tf_op jit(solution)/shard_map/ppermute | solution.py:403
  63.1 5.3 %collective-permute-start.21 = (bf16[144,128]{1,0:T(8,128)(2,1)S(1)}, bf16[144,128]{1,0:T(8,128)(2,1)S(1)}, u32[]{:S(2)}, u32[]{:S(2)}) collective-permute-start(bf16[144,128]{1,0:T(8,128)(2,1)S(1)} %get-tuple-element.32), channel_id=1, source_target_pairs={{0,4},{4,0},{8,12},{12,8},{1,5},{5,1},{9,13},{13,9},{2,6},{6,2},{1... | collective-permute-start | bytes 110600 | tf_op jit(solution)/shard_map/ppermute | solution.py:473
  66.0 5.7 %collective-permute-start.22 = (bf16[144,128]{1,0:T(8,128)(2,1)S(1)}, bf16[144,128]{1,0:T(8,128)(2,1)S(1)}, u32[]{:S(2)}, u32[]{:S(2)}) collective-permute-start(bf16[144,128]{1,0:T(8,128)(2,1)S(1)} %get-tuple-element.33), channel_id=1, source_target_pairs={{0,8},{4,12},{8,0},{12,4},{1,9},{5,13},{9,1},{13,5},{2,10},{6,14},... | collective-permute-start | bytes 110600 | tf_op jit(solution)/shard_map/ppermute | solution.py:473
  67.1 5.8 %collective-permute-start.23 = (bf16[144,128]{1,0:T(8,128)(2,1)S(1)}, bf16[144,128]{1,0:T(8,128)(2,1)S(1)}, u32[]{:S(2)}, u32[]{:S(2)}) collective-permute-start(bf16[144,128]{1,0:T(8,128)(2,1)S(1)} %get-tuple-element.34), channel_id=1, source_target_pairs={{0,12},{4,8},{8,4},{12,0},{1,13},{5,9},{9,5},{13,1},{2,14},{6,10},... | collective-permute-start | bytes 110600 | tf_op jit(solution)/shard_map/ppermute | solution.py:473
  73.4 8.0 %collective-permute-start.24 = (bf16[144,1024]{1,0:T(8,128)(2,1)S(1)}, bf16[144,1024]{1,0:T(8,128)(2,1)S(1)}, u32[]{:S(2)}, u32[]{:S(2)}) collective-permute-start(bf16[144,1024]{1,0:T(8,128)(2,1)S(1)} %get-tuple-element.37), channel_id=1, source_target_pairs={{0,2},{2,0},{1,3},{3,1},{4,6},{6,4},{5,7},{7,5},{8,10},{10,8},{9,1... | collective-permute-start | bytes 884744 | tf_op jit(solution)/shard_map/ppermute | solution.py:406
  75.0 1.2 %collective-permute-start.17 = (bf16[16,1024]{1,0:T(8,128)(2,1)S(1)}, bf16[16,1024]{1,0:T(8,128)(2,1)S(1)}, u32[]{:S(2)}, u32[]{:S(2)}) collective-permute-start(bf16[16,1024]{1,0:T(8,128)(2,1)S(1)} %get-tuple-element.27), channel_id=1, source_target_pairs={{0,1},{1,0},{2,3},{3,2},{4,5},{5,4},{6,7},{7,6},{8,9},{9,8},{10,11... | collective-permute-start | bytes 98312 | tf_op jit(solution)/shard_map/ppermute | solution.py:403
  75.1 1.3 %collective-permute-start.25 = (f32[16,256]{1,0:T(8,128)S(1)}, f32[16,256]{1,0:T(8,128)S(1)}, u32[]{:S(2)}, u32[]{:S(2)}) collective-permute-start(f32[16,256]{1,0:T(8,128)S(1)} %maximum_maximum_fusion.refs_7_), channel_id=1, source_target_pairs={{0,1},{1,0},{2,3},{3,2},{4,5},{5,4},{6,7},{7,6},{8,9},{9,8},{10,11... | collective-permute-start | bytes 49160 | tf_op jit(solution)/shard_map/ppermute | solution.py:403
  84.6 5.0 %collective-permute-start.26 = (bf16[64,1024]{1,0:T(8,128)(2,1)S(1)}, bf16[64,1024]{1,0:T(8,128)(2,1)S(1)}, u32[]{:S(2)}, u32[]{:S(2)}) collective-permute-start(bf16[64,1024]{1,0:T(8,128)(2,1)S(1)} %get-tuple-element.40), channel_id=1, source_target_pairs={{0,2},{2,0},{1,3},{3,1},{4,6},{6,4},{5,7},{7,5},{8,10},{10,8},{9,1... | collective-permute-start | bytes 393224 | tf_op jit(solution)/shard_map/ppermute | solution.py:406
  (8 other events, 74.0 us)
Sparse Core Ops, SparseCore 0:
  9.7 56.6 all-gather.1

commit v5 on v4

--- a/solution.py
+++ b/solution.py
@@ -167,17 +167,18 @@
 
 
 def call(kernel, outs, scratch, length, *operands, vmem=8, left=0):
+    fixed = [pltpu.with_memory_space_constraint(a, pltpu.HBM) for a in operands[:left]]
     return pl.pallas_call(
         kernel,
         out_shape=outs,
         in_specs=[pl.BlockSpec(memory_space=pltpu.SMEM)]
-        + [pl.BlockSpec(memory_space=pl.ANY)] * left
+        + [pl.BlockSpec(memory_space=pltpu.HBM)] * left
         + [pl.BlockSpec(memory_space=pltpu.VMEM)] * (len(operands) - left),
         out_specs=[pl.BlockSpec(memory_space=pltpu.VMEM)] * len(outs),
         scratch_shapes=scratch,
         cost_estimate=pl.CostEstimate(flops=0, bytes_accessed=0, transcendentals=0),
         compiler_params=pltpu.CompilerParams(vmem_limit_bytes=vmem << 20),
-    )(length, *operands)
+    )(length, *fixed, *operands[left:])
 
 
 def aligned(value, to):
@@ -193,15 +194,20 @@
 
 
 def deal_kernel(length, *refs):
-    sources, other, outs, (held, sems) = refs[:4], refs[4:7], refs[7:-2], refs[-2:]
+    sources, later, other = refs[:4], refs[4:7], refs[7:10]
+    outs, later_out, held, sems, later_sems = refs[10:14], *refs[14:]
+    s, _, f, p = here()
+    half = outs[0].shape[1]
     copies = [pltpu.make_async_copy(w, held.at[i], sems.at[i]) for i, w in enumerate(sources)]
-    for copy in copies:
+    at = pl.ds(aligned(p * half, half), half)
+    later_copies = [
+        pltpu.make_async_copy(w.at[at], later_out.at[i], later_sems.at[i]) for i, w in enumerate(later)
+    ]
+    for copy in copies + later_copies:
         copy.start()
     mine, w_out = [held.at[m] for m in range(3)], held.at[3]
-    s, _, f, p = here()
     for copy in copies:
         copy.wait()
-    half = outs[0].shape[1]
     rows = pl.ds(aligned(f * half, half), half)
     for k in range(SEQ):
         head = s ^ k
@@ -217,18 +223,35 @@
             for m in range(3):
                 outs[k][m] = other[m][rows, columns]
 
-        for m in range(w_out.shape[1] // HD):
-            outs[k][3 + m] = w_out[pl.ds(aligned(p * half, half), half), m * HD : (m + 1) * HD]
+        for m in range(outs[k].shape[0] - 3):
+            outs[k][3 + m] = w_out[at, m * HD : (m + 1) * HD]
+    for copy in later_copies:
+        copy.wait()
+
+
+def stack_kernel(length, *refs):
+    s = lax.axis_index("seq")
+    for k in range(SEQ):
+        refs[SEQ][s ^ k] = refs[k][...]
 
 
 def project_kernel(length, *refs):
-    blocks = refs[: 2 * SEQ]
-    mine, other = refs[2 * SEQ : 3 * SEQ], refs[3 * SEQ : 4 * SEQ]
-    gain, q_out, send_out, edge_out, stack_out, normed, weights, x_edge, q_edge = refs[4 * SEQ :]
+    frames, gain, *blocks = refs[: 2 * SEQ + 1]
+    mine, other, down = refs[2 * SEQ + 1 : 3 * SEQ + 1], refs[3 * SEQ + 1 : 4 * SEQ + 1], refs[4 * SEQ + 1]
+    q_out, send_out, edge_out, stack_out, normed, weights, x_edge, q_edge, own_x, own_gain, sems = refs[4 * SEQ + 2 :]
+    copies = [
+        pltpu.make_async_copy(frames, own_x, sems.at[0]),
+        pltpu.make_async_copy(gain, own_gain, sems.at[1]),
+    ]
+    for copy in copies:
+        copy.start()
     s, h, f, _ = here()
+    blocks = [own_x, *blocks]
     rows = blocks[0].shape[0]
     half = mine[0].shape[1]
-    gain_row = gain[...]
+    for copy in copies:
+        copy.wait()
+    gain_row = own_gain[...]
     for slot, block in enumerate(blocks):
         at = (s ^ (slot // 2)) * 2 + (h ^ (slot % 2))
         x = block[...].astype(F32)
@@ -240,7 +263,7 @@
             at = pl.ds(aligned((s ^ k) * 2 * half + (f ^ core) * half, half), half)
             for m in range(3):
                 weights[at, m * HD : (m + 1) * HD] = pieces[k][m]
-        stack_out[s ^ k] = mine[k][3:]
+        stack_out[s ^ k] = down[...] if k == 2 else mine[k][3:]
     count = 2 * SEQ
     total = count * rows
     projected = dot(normed[...], weights[...])
@@ -298,20 +321,17 @@
 
 
 def output_kernel(length, *refs):
-    near, far, ctx = refs[: 2 * SEQ], refs[2 * SEQ : 2 * SEQ + 2], refs[2 * SEQ + 2 : 3 * SEQ + 2]
-    share_out, send_out, context, weights = refs[3 * SEQ + 2 :]
+    pieces, ctx = refs[:4], refs[4 : 4 + SEQ]
+    share_out, send_out, context, weights = refs[4 + SEQ :]
     s, h, f, p = here()
-    half = near[0].shape[1]
+    half = pieces[0].shape[2]
     columns = weights.shape[2]
-    for core in range(2):
-        first = (f ^ core) * 2 * half
-        here_at = pl.ds(aligned(first + p * half, half), half)
-        there_at = pl.ds(aligned(first + (1 - p) * half, half), half)
-        for m in range(columns // HD):
-            at = slice(m * HD, (m + 1) * HD)
-            for k in range(SEQ):
-                weights[s ^ k, here_at, at] = near[core * SEQ + k][3 + m]
-                weights[k, there_at, at] = far[core][k, m]
+    for y in range(2):
+        for core in range(2):
+            rows = pl.ds(aligned((f ^ core) * 2 * half + (p ^ y) * half, half), half)
+            for m in range(columns // HD):
+                for j in range(SEQ):
+                    weights[j, rows, m * HD : (m + 1) * HD] = pieces[y * 2 + core][j, m]
     for k in range(SEQ):
         context[:, pl.ds(aligned((s ^ k) * HD, HD), HD)] = ctx[k][...]
     for j in range(SEQ):
@@ -322,22 +342,23 @@
 
 
 def convolve_kernel(length, *refs):
-    pieces, own_x, peer_x, halo_x, own_share, peer_share, gain, own_c, peer_c, base_out, share_out = refs[:11]
-    mid, normed, w_value, w_gate, w_down, channel, padded, active, shares = refs[11:]
+    pieces = refs[:4]
+    own_x, peer_x, halo_x, own_share, peer_share, gain, own_c, peer_c, base_out, share_out = refs[4:14]
+    mid, normed, w_value, w_gate, w_down, channel, padded, active, shares = refs[14:]
     s, h, f, p = here()
     valid_len = length[0]
-    half, columns = pieces.shape[1:]
+    half, columns = pieces[0].shape[2:]
     rows = own_x.shape[0]
     step = rows + HALO
-    for part in range(2):
-        for plane in range(SEQ):
-            for core in range(2):
-                first = ((part * SEQ + plane) * 2 + core) * 3
-                at = slice((2 * plane + part) * half, (2 * plane + part + 1) * half)
-                w_value[core, at, :] = pieces[first]
-                w_gate[core, at, :] = pieces[first + 1]
-                at = slice((2 * core + part) * half, (2 * core + part + 1) * half)
-                w_down[plane, at, :] = pieces[first + 2]
+    for y in range(2):
+        for core in range(2):
+            stack = pieces[y * 2 + core]
+            down = pl.ds(aligned((f ^ core) * 2 * half + (p ^ y) * half, half), half)
+            for plane in range(SEQ):
+                at = pl.ds(aligned(plane * 2 * half + (p ^ y) * half, half), half)
+                w_value[f ^ core, at, :] = stack[plane, 0]
+                w_gate[f ^ core, at, :] = stack[plane, 1]
+                w_down[plane, down, :] = stack[plane, 2]
     channel[f] = own_c[...]
     channel[1 - f] = peer_c[...]
     mid[pl.ds(aligned(h * step, 8), rows), :] = own_x[...].astype(F32)
@@ -408,8 +429,12 @@
     def other_part(x):
         return lax.ppermute(x, "parts", SWAP)
 
+    def across(x, k):
+        return lax.ppermute(x, "seq", xor_pairs(k))
+
     def planes(x):
-        return [x] + [lax.ppermute(x, "seq", xor_pairs(k)) for k in range(1, SEQ)]
+        far = across(x, 3)
+        return [x, across(x, 1), across(far, 1), far]
 
     def part_half(x):
         return lax.dynamic_slice_in_dim(x, p * half, half, axis=x.ndim - 2)
@@ -418,22 +443,34 @@
     blocks = []
     for block in near:
         blocks += [block, other_side(block)]
-    pw_mine = part_half(jnp.stack([pw1_value, pw1_gate, pw2]))
-    pw_all = lax.all_gather(pw_mine, ("parts", "seq", "fsdp"), axis=0, tiled=True)
     given = [w_query, w_key, w_value]
     shape = jax.ShapeDtypeStruct
-    dealt = call(
+    *dealt, pw_mine = call(
         deal_kernel,
-        [shape((3 + columns // HD, half, HD), BF16)] * SEQ,
-        [pltpu.VMEM((4, 2 * half, columns), BF16), pltpu.SemaphoreType.DMA((4,))],
+        [shape((3 if k == 2 else 3 + columns // HD, half, HD), BF16) for k in range(SEQ)]
+        + [shape((3, half, columns), BF16)],
+        [
+            pltpu.VMEM((4, 2 * half, columns), BF16),
+            pltpu.SemaphoreType.DMA((4,)),
+            pltpu.SemaphoreType.DMA((3,)),
+        ],
         length,
         *given,
         w_out,
+        pw1_value,
+        pw1_gate,
+        pw2,
         *[other_core(w) for w in given],
-        left=4,
-    )
-    w_mine = [dealt[0]] + [lax.ppermute(dealt[k], "seq", xor_pairs(k)) for k in range(1, SEQ)]
-    w_other = [other_core(w) for w in w_mine]
+        left=7,
+    )
+    *dealt, _ = barrier((*dealt, near[1]))
+    w_mine = [dealt[0]] + [across(dealt[k], k) for k in range(1, SEQ)]
+    w_other = [other_core(w[:3]) for w in w_mine]
+    down = across(w_mine[3][3:], 1)
+    pw_part = other_part(pw_mine)
+    w_other[0], pw_part = barrier((w_other[0], pw_part))
+    after, *_ = barrier((pw_mine, *w_mine[1:], down))
+    pw_one, pw_three = across(after, 1), across(after, 3)
     queries, send, edges, stack = call(
         project_kernel,
         [
@@ -447,16 +484,21 @@
             pltpu.VMEM((width, 3 * HD), BF16),
             pltpu.VMEM((count, HALO, width), F32),
             pltpu.VMEM((count, HALO, HD), F32),
+            pltpu.VMEM((rows, width), BF16),
+            pltpu.VMEM((1, width), F32),
+            pltpu.SemaphoreType.DMA((2,)),
         ],
         length,
-        *blocks,
+        frames,
+        ln1_gain[None],
+        *blocks[1:],
         *w_mine,
         *w_other,
-        ln1_gain[None],
+        down,
+        left=2,
     )
     received = other_core(send)
     stack_part = other_part(stack)
-    halo_x = other_core(edges)
     ctx = call(
         attend_kernel,
         [shape((2 * step, HD), BF16)] * SEQ,
@@ -466,11 +508,12 @@
         send,
         received,
     )
-    depth_kernel, stack_part, *_ = barrier((depth_kernel, stack_part, *ctx))
-    far = [stack_part, other_core(stack_part)]
-    channels = jnp.concatenate([depth_kernel, bn_scale[None], bn_shift[None], jnp.zeros((5, columns), F32)])
-    channels_peer = other_core(channels)
+    stack, stack_part, *_ = barrier((stack, stack_part, *ctx))
+    out_pieces = [stack, other_core(stack), stack_part, other_core(stack_part)]
     ctx = [ctx[0]] + [lax.ppermute(ctx[k], "seq", xor_pairs(k)) for k in range(1, SEQ)]
+    pw_one, pw_three, *ctx = barrier((pw_one, pw_three, *ctx))
+    pw_two = across(pw_three, 1)
+    one_part, three_part = other_part(pw_one), other_part(pw_three)
     own_share, sent_share = call(
         output_kernel,
         [shape((2 * step, width), F32), shape((2 * step, width), BF16)],
@@ -479,11 +522,22 @@
             pltpu.VMEM((SEQ, 2 * columns, columns), BF16),
         ],
         length,
-        *w_mine,
-        *w_other,
-        *far,
+        *out_pieces,
         *ctx,
     )
+    own_share, edges, depth_kernel = barrier((own_share, edges, depth_kernel))
+    halo_x = other_core(edges)
+    channels = jnp.concatenate([depth_kernel, bn_scale[None], bn_shift[None], jnp.zeros((5, columns), F32)])
+    channels_peer = other_core(channels)
+    peer_share = other_side(sent_share)
+
+    def stacked(*pieces):
+        (stack,) = call(stack_kernel, [shape((SEQ, *pieces[0].shape), BF16)], [], length, *pieces)
+        return [stack, other_core(stack)]
+
+    two_part = other_part(pw_two)
+    pw_mine, _ = barrier((pw_mine, peer_share))
+    pw_pieces = stacked(pw_mine, pw_one, pw_two, pw_three) + stacked(pw_part, one_part, two_part, three_part)
     base, share = call(
         convolve_kernel,
         [shape((rows, width), F32), shape((rows, width), BF16)],
@@ -499,12 +553,12 @@
             pltpu.VMEM((2 * rows, width), F32),
         ],
         length,
-        pw_all,
+        *pw_pieces,
         frames,
         blocks[1],
         halo_x,
         own_share,
-        other_side(sent_share),
+        peer_share,
         ln2_gain[None],
         channels,
         channels_peer,

time: 97.5 us -> 83.4 us (0.86)
  between operations: 14.2 us -> 0.85 us
  local copies, waits for them, and re-layouts: 7.2 us -> 0.8 us
  starting transfers between devices: 30.2 us -> 34.8 us
  Pallas kernels: 7.14 us -> 8.82 us
  other arithmetic: 2.38 us -> 0.76 us
  waiting for transfers between devices: 36 us -> 37.2 us
    ppermute x6, waiting for transfers between devices: 15.3 us -> 4.88 us  [other_side(): return lax.ppermute(x, 'head', SWAP)]
    ppermute x1 -> x5, waiting for transfers between devices: 4.7 us -> 11.5 us  [other_part(): return lax.ppermute(x, 'parts', SWAP)]
    unnamed x24 -> x10, local copies, waits for them, and re-layouts: 7.12 us -> 0.7 us
    ppermute x6 -> x10, waiting for transfers between devices: 10.6 us -> 15.3 us  [across(): return lax.ppermute(x, 'seq', xor_pairs(k))]
    ppermute x1 -> x5, starting transfers between devices: 1.58 us -> 5.63 us  [other_part(): return lax.ppermute(x, 'parts', SWAP)]
    pallas_call x5 -> x7, Pallas kernels: 7.14 us -> 8.82 us  [call(): pl.pallas_call(kernel, out_shape=outs, in_specs=[pl.BlockSpec(memory_spac...]
    another operation x1 -> x0, other arithmetic: 1.61 us -> none  [shards_chip_per_head(): pw_mine = part_half(jnp.stack([pw1_value, pw1_gate, pw2]))]
    ppermute x11 -> x14, starting transfers between devices: 2.12 us -> 3.31 us  [other_core(): return lax.ppermute(x, 'fsdp', SWAP)]
  transfers between devices with their start and end apart: 28 -> 38, of which waited for: 12 -> 16; matrix products, arithmetic and copies ran while one was open for 0% -> 0% of each run, Pallas kernels for 6% -> 6%
where the time goes in v5:
time: 83.4 us; the launch traced here: 83.2 us
  waiting for transfers between devices  37.2 us (45%)
  starting transfers between devices  34.8 us (42%)
  Pallas kernels  8.82 us (11%)
  between operations  0.85 us (1%)
    ppermute x10, waiting for transfers between devices, across(): return lax.ppermute(x, 'seq', xor_pairs(k))  15.3 us
    ppermute x10, starting transfers between devices, across(): return lax.ppermute(x, 'seq', xor_pairs(k))  13.5 us
    ppermute x5, waiting for transfers between devices, other_part(): return lax.ppermute(x, 'parts', SWAP)  11.5 us
    pallas_call x7, Pallas kernels, call(): pl.pallas_call(kernel, out_shape=outs, in_specs=[pl.BlockSpec(memory_spac...  8.82 us
    ppermute x6, starting transfers between devices, other_side(): return lax.ppermute(x, 'head', SWAP)  8.06 us
    ppermute x5, starting transfers between devices, other_part(): return lax.ppermute(x, 'parts', SWAP)  5.63 us
    ppermute x6, waiting for transfers between devices, other_side(): return lax.ppermute(x, 'head', SWAP)  4.88 us
    ppermute x3, starting transfers between devices, shards_chip_per_head(): lax.ppermute(ctx[k], 'seq', xor_pairs(k))  4.27 us
  transfers between devices with their start and end apart: 38, of which 16 were waited for; matrix products, arithmetic and copies ran while one was open for 0% of the time, Pallas kernels for 6%

profile of v5, /device:TPU:0, one launch (start us, length us, event | category | flops | bytes accessed | tf_op | source)
XLA Modules:
  0.0 83.2 jit_solution(17826906935676544300)
XLA Ops:
  1.0 2.6 %collective-permute-start.4 = (bf16[64,1024]{1,0:T(8,128)(2,1)}, bf16[64,1024]{1,0:T(8,128)(2,1)S(1)}, u32[]{:S(2)}, u32[]{:S(2)}) collective-permute-start(bf16[64,1024]{1,0:T(8,128)(2,1)} %refs_4_.3), channel_id=1, source_target_pairs={{0,4},{4,0},{8,12},{12,8},{1,5},{5,1},{9,13},{13,9},{2,6},{6,2},{1... | collective-permute-start | bytes 393224 | tf_op jit(solution)/shard_map/ppermute | solution.py:433
  3.5 2.5 %collective-permute-start.6 = (bf16[64,1024]{1,0:T(8,128)(2,1)}, bf16[64,1024]{1,0:T(8,128)(2,1)S(1)}, u32[]{:S(2)}, u32[]{:S(2)}) collective-permute-start(bf16[64,1024]{1,0:T(8,128)(2,1)} %refs_4_.3), channel_id=1, source_target_pairs={{0,12},{4,8},{8,4},{12,0},{1,13},{5,9},{9,5},{13,1},{2,14},{6,10},... | collective-permute-start | bytes 393224 | tf_op jit(solution)/shard_map/ppermute | solution.py:433
  6.0 1.5 %collective-permute-start.3 = (bf16[64,1024]{1,0:T(8,128)(2,1)}, bf16[64,1024]{1,0:T(8,128)(2,1)S(1)}, u32[]{:S(2)}, u32[]{:S(2)}) collective-permute-start(bf16[64,1024]{1,0:T(8,128)(2,1)} %refs_4_.3), channel_id=1, source_target_pairs={{0,2},{2,0},{1,3},{3,1},{4,6},{6,4},{5,7},{7,5},{8,10},{10,8},{9,1... | collective-permute-start | bytes 393224 | tf_op jit(solution)/shard_map/ppermute | solution.py:427
  8.2 1.3 %shard_map.136 = (bf16[5,128,128]{2,1,0:T(8,128)(2,1)S(1)}, bf16[5,128,128]{2,1,0:T(8,128)(2,1)S(1)}, bf16[3,128,128]{2,1,0:T(8,128)(2,1)S(1)}, bf16[5,128,128]{2,1,0:T(8,128)(2,1)S(1)}, bf16[3,128,256]{2,1,0:T(8,128)(2,1)S(1)}) custom-call(s32[1]{0:T(128)S(6)} %copy.15.length, bf16[256,256]{1,0:T(8,128)(2,1)} %refs_0_.2, bf16[256,256]{1,0:T(8,128)(2,1)} %refs_1_.1, ...), custom_call_target="tpu_custom_call" | custom-call | tf_op jit(solution)/shard_map/pallas_call | solution.py:171
  10.3 3.1 %collective-permute-done.6.refs_7_ = bf16[64,1024]{1,0:T(8,128)(2,1)S(1)} collective-permute-done((bf16[64,1024]{1,0:T(8,128)(2,1)}, bf16[64,1024]{1,0:T(8,128)(2,1)S(1)}, u32[]{:S(2)}, u32[]{:S(2)}) %collective-permute-start.6) | collective-permute-done | bytes 131104 | tf_op jit(solution)/shard_map/ppermute | solution.py:433
  13.4 3.2 %collective-permute-start.12 = (bf16[5,128,128]{2,1,0:T(8,128)(2,1)S(1)}, bf16[5,128,128]{2,1,0:T(8,128)(2,1)S(1)}, u32[]{:S(2)}, u32[]{:S(2)}) collective-permute-start(bf16[5,128,128]{2,1,0:T(8,128)(2,1)S(1)} %get-tuple-element.49), channel_id=1, source_target_pairs={{0,12},{4,8},{8,4},{12,0},{1,13},{5,9},{9,5},{13,1},{2,14},{6,10},... | collective-permute-start | bytes 491528 | tf_op jit(solution)/shard_map/ppermute | solution.py:433
  16.7 1.5 %collective-permute-start.14 = (bf16[3,128,256]{2,1,0:T(8,128)(2,1)S(1)}, bf16[3,128,256]{2,1,0:T(8,128)(2,1)S(1)}, u32[]{:S(2)}, u32[]{:S(2)}) collective-permute-start(bf16[3,128,256]{2,1,0:T(8,128)(2,1)S(1)} %get-tuple-element.66.refs_0_), channel_id=1, source_target_pairs={{0,16},{16,0},{1,17},{17,1},{2,18},{18,2},{3,19},{19,3},{4,20},{20... | collective-permute-start | bytes 589832 | tf_op jit(solution)/shard_map/ppermute | solution.py:430
  18.2 1.3 %collective-permute-start.9 = (bf16[64,1024]{1,0:T(8,128)(2,1)S(1)}, bf16[64,1024]{1,0:T(8,128)(2,1)S(1)}, u32[]{:S(2)}, u32[]{:S(2)}) collective-permute-start(bf16[64,1024]{1,0:T(8,128)(2,1)S(1)} %collective-permute-done.6.refs_7_), channel_id=1, source_target_pairs={{0,2},{2,0},{1,3},{3,1},{4,6},{6,4},{5,7},{7,5},{8,10},{10,8},{9,1... | collective-permute-start | bytes 393224 | tf_op jit(solution)/shard_map/ppermute | solution.py:427
  19.6 1.6 %collective-permute-start.5 = (bf16[64,1024]{1,0:T(8,128)(2,1)S(1)}, bf16[64,1024]{1,0:T(8,128)(2,1)S(1)}, u32[]{:S(2)}, u32[]{:S(2)}) collective-permute-start(bf16[64,1024]{1,0:T(8,128)(2,1)S(1)} %collective-permute-done.4.refs_3_), channel_id=1, source_target_pairs={{0,2},{2,0},{1,3},{3,1},{4,6},{6,4},{5,7},{7,5},{8,10},{10,8},{9,1... | collective-permute-start | bytes 393224 | tf_op jit(solution)/shard_map/ppermute | solution.py:427
  21.2 2.7 %collective-permute-start.11 = (bf16[3,128,128]{2,1,0:T(8,128)(2,1)S(1)}, bf16[3,128,128]{2,1,0:T(8,128)(2,1)S(1)}, u32[]{:S(2)}, u32[]{:S(2)}) collective-permute-start(bf16[3,128,128]{2,1,0:T(8,128)(2,1)S(1)} %get-tuple-element.48), channel_id=1, source_target_pairs={{0,8},{4,12},{8,0},{12,4},{1,9},{5,13},{9,1},{13,5},{2,10},{6,14},... | collective-permute-start | bytes 294920 | tf_op jit(solution)/shard_map/ppermute | solution.py:433
  23.9 1.4 %collective-permute-done.12.refs_12_ = bf16[5,128,128]{2,1,0:T(8,128)(2,1)S(1)} collective-permute-done((bf16[5,128,128]{2,1,0:T(8,128)(2,1)S(1)}, bf16[5,128,128]{2,1,0:T(8,128)(2,1)S(1)}, u32[]{:S(2)}, u32[]{:S(2)}) %collective-permute-start.12) | collective-permute-done | bytes 163872 | tf_op jit(solution)/shard_map/ppermute | solution.py:433
  25.3 1.3 %collective-permute-start.8 = (bf16[64,1024]{1,0:T(8,128)(2,1)S(1)}, bf16[64,1024]{1,0:T(8,128)(2,1)S(1)}, u32[]{:S(2)}, u32[]{:S(2)}) collective-permute-start(bf16[64,1024]{1,0:T(8,128)(2,1)S(1)} %collective-permute-done.7.refs_5_), channel_id=1, source_target_pairs={{0,2},{2,0},{1,3},{3,1},{4,6},{6,4},{5,7},{7,5},{8,10},{10,8},{9,1... | collective-permute-start | bytes 393224 | tf_op jit(solution)/shard_map/ppermute | solution.py:427
  26.6 2.7 %collective-permute-done.11.refs_11_ = bf16[3,128,128]{2,1,0:T(8,128)(2,1)S(1)} collective-permute-done((bf16[3,128,128]{2,1,0:T(8,128)(2,1)S(1)}, bf16[3,128,128]{2,1,0:T(8,128)(2,1)S(1)}, u32[]{:S(2)}, u32[]{:S(2)}) %collective-permute-start.11) | collective-permute-done | bytes 98336 | tf_op jit(solution)/shard_map/ppermute | solution.py:433
  30.5 3.8 %collective-permute-done.18.refs_17_ = bf16[2,128,128]{2,1,0:T(8,128)(2,1)S(1)} collective-permute-done((bf16[2,128,128]{2,1,0:T(8,128)(2,1)S(1)}, bf16[2,128,128]{2,1,0:T(8,128)(2,1)S(1)}, u32[]{:S(2)}, u32[]{:S(2)}) %collective-permute-start.18) | collective-permute-done | bytes 65568 | tf_op jit(solution)/shard_map/ppermute | solution.py:433
  34.3 2.6 %shard_map.137 = (bf16[512,128]{1,0:T(8,128)(2,1)S(1)}, bf16[1088,128]{1,0:T(8,128)(2,1)S(1)}, bf16[16,1024]{1,0:T(8,128)(2,1)S(1)}, bf16[4,2,128,128]{3,2,1,0:T(8,128)(2,1)S(1)}) custom-call(s32[1]{0:T(128)S(6)} %copy.15.length, bf16[64,1024]{1,0:T(8,128)(2,1)} %refs_4_.3, f32[1,1024]{1,0:T(1,128)} %bitcast.5, ...), custom_call_target="tpu_custom_call" | custom-call | tf_op jit(solution)/shard_map/pallas_call | solution.py:171
  37.1 1.6 %collective-permute-start.19 = (bf16[4,2,128,128]{3,2,1,0:T(8,128)(2,1)S(1)}, bf16[4,2,128,128]{3,2,1,0:T(8,128)(2,1)S(1)}, u32[]{:S(2)}, u32[]{:S(2)}) collective-permute-start(bf16[4,2,128,128]{3,2,1,0:T(8,128)(2,1)S(1)} %get-tuple-element.58.refs_0_), channel_id=1, source_target_pairs={{0,16},{16,0},{1,17},{17,1},{2,18},{18,2},{3,19},{19,3},{4,20},{20... | collective-permute-start | bytes 786440 | tf_op jit(solution)/shard_map/ppermute | solution.py:430
  38.7 1.2 %collective-permute-start.24 = (bf16[3,128,256]{2,1,0:T(8,128)(2,1)S(1)}, bf16[3,128,256]{2,1,0:T(8,128)(2,1)S(1)}, u32[]{:S(2)}, u32[]{:S(2)}) collective-permute-start(bf16[3,128,256]{2,1,0:T(8,128)(2,1)S(1)} %get-tuple-element.66.refs_0_), channel_id=1, source_target_pairs={{0,12},{4,8},{8,4},{12,0},{1,13},{5,9},{9,5},{13,1},{2,14},{6,10},... | collective-permute-start | bytes 589832 | tf_op jit(solution)/shard_map/ppermute | solution.py:433
  39.9 2.8 %shard_map.138 = (bf16[144,128]{1,0:T(8,128)(2,1)S(1)}, bf16[144,128]{1,0:T(8,128)(2,1)S(1)}, bf16[144,128]{1,0:T(8,128)(2,1)S(1)}, bf16[144,128]{1,0:T(8,128)(2,1)S(1)}) custom-call(s32[1]{0:T(128)S(6)} %copy.15.length, bf16[512,128]{1,0:T(8,128)(2,1)S(1)} %get-tuple-element.52.q_in, bf16[1088,128]{1,0:T(8,128)(2,1)S(1)} %get-tuple-element.53.own, ...), custom_call_target="tpu_custom_call" | custom-call | tf_op jit(solution)/shard_map/pallas_call | solution.py:171
  42.7 3.1 %collective-permute-done.19.refs_2_ = bf16[4,2,128,128]{3,2,1,0:T(8,128)(2,1)S(1)} collective-permute-done((bf16[4,2,128,128]{3,2,1,0:T(8,128)(2,1)S(1)}, bf16[4,2,128,128]{3,2,1,0:T(8,128)(2,1)S(1)}, u32[]{:S(2)}, u32[]{:S(2)}) %collective-permute-start.19) | collective-permute-done | bytes 262176 | tf_op jit(solution)/shard_map/ppermute | solution.py:430
  46.8 1.4 %collective-permute-done.24.refs_3_ = bf16[3,128,256]{2,1,0:T(8,128)(2,1)S(1)} collective-permute-done((bf16[3,128,256]{2,1,0:T(8,128)(2,1)S(1)}, bf16[3,128,256]{2,1,0:T(8,128)(2,1)S(1)}, u32[]{:S(2)}, u32[]{:S(2)}) %collective-permute-start.24) | collective-permute-done | bytes 196640 | tf_op jit(solution)/shard_map/ppermute | solution.py:433
  48.2 1.9 %collective-permute-start.26 = (bf16[144,128]{1,0:T(8,128)(2,1)S(1)}, bf16[144,128]{1,0:T(8,128)(2,1)S(1)}, u32[]{:S(2)}, u32[]{:S(2)}) collective-permute-start(bf16[144,128]{1,0:T(8,128)(2,1)S(1)} %get-tuple-element.56), channel_id=1, source_target_pairs={{0,8},{4,12},{8,0},{12,4},{1,9},{5,13},{9,1},{13,5},{2,10},{6,14},... | collective-permute-start | bytes 110600 | tf_op jit(solution)/shard_map/ppermute | solution.py:513
  50.1 1.4 %collective-permute-done.23.refs_1_ = bf16[3,128,256]{2,1,0:T(8,128)(2,1)S(1)} collective-permute-done((bf16[3,128,256]{2,1,0:T(8,128)(2,1)S(1)}, bf16[3,128,256]{2,1,0:T(8,128)(2,1)S(1)}, u32[]{:S(2)}, u32[]{:S(2)}) %collective-permute-start.23) | collective-permute-done | bytes 196640 | tf_op jit(solution)/shard_map/ppermute | solution.py:433
  51.5 1.9 %collective-permute-start.27 = (bf16[144,128]{1,0:T(8,128)(2,1)S(1)}, bf16[144,128]{1,0:T(8,128)(2,1)S(1)}, u32[]{:S(2)}, u32[]{:S(2)}) collective-permute-start(bf16[144,128]{1,0:T(8,128)(2,1)S(1)} %get-tuple-element.57), channel_id=1, source_target_pairs={{0,12},{4,8},{8,4},{12,0},{1,13},{5,9},{9,5},{13,1},{2,14},{6,10},... | collective-permute-start | bytes 110600 | tf_op jit(solution)/shard_map/ppermute | solution.py:513
  53.7 3.6 %collective-permute-done.27.refs_7_ = bf16[144,128]{1,0:T(8,128)(2,1)S(1)} collective-permute-done((bf16[144,128]{1,0:T(8,128)(2,1)S(1)}, bf16[144,128]{1,0:T(8,128)(2,1)S(1)}, u32[]{:S(2)}, u32[]{:S(2)}) %collective-permute-start.27) | collective-permute-done | bytes 36896 | tf_op jit(solution)/shard_map/ppermute | solution.py:513
  57.8 1.7 %collective-permute-start.28 = (bf16[144,1024]{1,0:T(8,128)(2,1)S(1)}, bf16[144,1024]{1,0:T(8,128)(2,1)S(1)}, u32[]{:S(2)}, u32[]{:S(2)}) collective-permute-start(bf16[144,1024]{1,0:T(8,128)(2,1)S(1)} %get-tuple-element.65), channel_id=1, source_target_pairs={{0,2},{2,0},{1,3},{3,1},{4,6},{6,4},{5,7},{7,5},{8,10},{10,8},{9,1... | collective-permute-start | bytes 884744 | tf_op jit(solution)/shard_map/ppermute | solution.py:427
  60.1 1.5 %collective-permute-start.31 = (bf16[3,128,256]{2,1,0:T(8,128)(2,1)S(1)}, bf16[3,128,256]{2,1,0:T(8,128)(2,1)S(1)}, u32[]{:S(2)}, u32[]{:S(2)}) collective-permute-start(bf16[3,128,256]{2,1,0:T(8,128)(2,1)S(1)} %collective-permute-done.23.refs_1_), channel_id=1, source_target_pairs={{0,16},{16,0},{1,17},{17,1},{2,18},{18,2},{3,19},{19,3},{4,20},{20... | collective-permute-start | bytes 589832 | tf_op jit(solution)/shard_map/ppermute | solution.py:430
  61.6 1.4 %collective-permute-done.29.refs_2_ = bf16[3,128,256]{2,1,0:T(8,128)(2,1)S(1)} collective-permute-done((bf16[3,128,256]{2,1,0:T(8,128)(2,1)S(1)}, bf16[3,128,256]{2,1,0:T(8,128)(2,1)S(1)}, u32[]{:S(2)}, u32[]{:S(2)}) %collective-permute-start.29) | collective-permute-done | bytes 196640 | tf_op jit(solution)/shard_map/ppermute | solution.py:433
  63.5 6.3 %collective-permute-done.31.refs_1_ = bf16[3,128,256]{2,1,0:T(8,128)(2,1)S(1)} collective-permute-done((bf16[3,128,256]{2,1,0:T(8,128)(2,1)S(1)}, bf16[3,128,256]{2,1,0:T(8,128)(2,1)S(1)}, u32[]{:S(2)}, u32[]{:S(2)}) %collective-permute-start.31) | collective-permute-done | bytes 196640 | tf_op jit(solution)/shard_map/ppermute | solution.py:430
  69.7 2.1 %collective-permute-done.32.refs_2_ = bf16[3,128,256]{2,1,0:T(8,128)(2,1)S(1)} collective-permute-done((bf16[3,128,256]{2,1,0:T(8,128)(2,1)S(1)}, bf16[3,128,256]{2,1,0:T(8,128)(2,1)S(1)}, u32[]{:S(2)}, u32[]{:S(2)}) %collective-permute-start.32) | collective-permute-done | bytes 196640 | tf_op jit(solution)/shard_map/ppermute | solution.py:430
  74.0 1.5 %collective-permute-done.36.refs_11_ = f32[16,256]{1,0:T(8,128)S(1)} collective-permute-done((f32[16,256]{1,0:T(8,128)S(1)}, f32[16,256]{1,0:T(8,128)S(1)}, u32[]{:S(2)}, u32[]{:S(2)}) %collective-permute-start.36) | collective-permute-done | bytes 16416 | tf_op jit(solution)/shard_map/ppermute | solution.py:424
  75.5 1.4 %shard_map.142 = (f32[64,1024]{1,0:T(8,128)S(1)}, bf16[64,1024]{1,0:T(8,128)(2,1)S(1)}) custom-call(s32[1]{0:T(128)S(6)} %copy.15.length, bf16[4,3,128,256]{3,2,1,0:T(8,128)(2,1)S(1)} %shard_map.140.refs_0_, bf16[4,3,128,256]{3,2,1,0:T(8,128)(2,1)S(1)} %collective-permute-done.30.refs_1_, bf16[4,3,128,256]{3,2,1,0:T(8,128)(2,1)S(1)} %shard_map.141.refs_2_, ...), custom_call_target="tpu_custom_call" | custom-call | tf_op jit(solution)/shard_map/pallas_call | solution.py:171
  77.6 4.9 %collective-permute-done.37 = bf16[64,1024]{1,0:T(8,128)(2,1)S(1)} collective-permute-done((bf16[64,1024]{1,0:T(8,128)(2,1)S(1)}, bf16[64,1024]{1,0:T(8,128)(2,1)S(1)}, u32[]{:S(2)}, u32[]{:S(2)}) %collective-permute-start.37) | collective-permute-done | bytes 131104 | tf_op jit(solution)/shard_map/ppermute | solution.py:427
  (69 shorter events, 9.7 us)
Async XLA Ops:
  0.0 6.0 %collective-permute-start = (bf16[256,256]{1,0:T(8,128)(2,1)}, bf16[256,256]{1,0:T(8,128)(2,1)S(1)}, u32[]{:S(2)}, u32[]{:S(2)}) collective-permute-start(bf16[256,256]{1,0:T(8,128)(2,1)} %refs_0_.2), channel_id=1, source_target_pairs={{0,1},{1,0},{2,3},{3,2},{4,5},{5,4},{6,7},{7,6},{8,9},{9,8},{10,11... | collective-permute-start | bytes 393224 | tf_op jit(solution)/shard_map/ppermute | solution.py:424
  0.5 7.7 %collective-permute-start.1 = (bf16[256,256]{1,0:T(8,128)(2,1)}, bf16[256,256]{1,0:T(8,128)(2,1)S(1)}, u32[]{:S(2)}, u32[]{:S(2)}) collective-permute-start(bf16[256,256]{1,0:T(8,128)(2,1)} %refs_1_.1), channel_id=1, source_target_pairs={{0,1},{1,0},{2,3},{3,2},{4,5},{5,4},{6,7},{7,6},{8,9},{9,8},{10,11... | collective-permute-start | bytes 393224 | tf_op jit(solution)/shard_map/ppermute | solution.py:424
  0.5 7.7 %collective-permute-start.2 = (bf16[256,256]{1,0:T(8,128)(2,1)}, bf16[256,256]{1,0:T(8,128)(2,1)S(1)}, u32[]{:S(2)}, u32[]{:S(2)}) collective-permute-start(bf16[256,256]{1,0:T(8,128)(2,1)} %refs_2_.1), channel_id=1, source_target_pairs={{0,1},{1,0},{2,3},{3,2},{4,5},{5,4},{6,7},{7,6},{8,9},{9,8},{10,11... | collective-permute-start | bytes 393224 | tf_op jit(solution)/shard_map/ppermute | solution.py:424
  1.0 8.5 %collective-permute-start.4 = (bf16[64,1024]{1,0:T(8,128)(2,1)}, bf16[64,1024]{1,0:T(8,128)(2,1)S(1)}, u32[]{:S(2)}, u32[]{:S(2)}) collective-permute-start(bf16[64,1024]{1,0:T(8,128)(2,1)} %refs_4_.3), channel_id=1, source_target_pairs={{0,4},{4,0},{8,12},{12,8},{1,5},{5,1},{9,13},{13,9},{2,6},{6,2},{1... | collective-permute-start | bytes 393224 | tf_op jit(solution)/shard_map/ppermute | solution.py:433
  3.5 9.8 %collective-permute-start.6 = (bf16[64,1024]{1,0:T(8,128)(2,1)}, bf16[64,1024]{1,0:T(8,128)(2,1)S(1)}, u32[]{:S(2)}, u32[]{:S(2)}) collective-permute-start(bf16[64,1024]{1,0:T(8,128)(2,1)} %refs_4_.3), channel_id=1, source_target_pairs={{0,12},{4,8},{8,4},{12,0},{1,13},{5,9},{9,5},{13,1},{2,14},{6,10},... | collective-permute-start | bytes 393224 | tf_op jit(solution)/shard_map/ppermute | solution.py:433
  6.0 10.7 %collective-permute-start.3 = (bf16[64,1024]{1,0:T(8,128)(2,1)}, bf16[64,1024]{1,0:T(8,128)(2,1)S(1)}, u32[]{:S(2)}, u32[]{:S(2)}) collective-permute-start(bf16[64,1024]{1,0:T(8,128)(2,1)} %refs_4_.3), channel_id=1, source_target_pairs={{0,2},{2,0},{1,3},{3,1},{4,6},{6,4},{5,7},{7,5},{8,10},{10,8},{9,1... | collective-permute-start | bytes 393224 | tf_op jit(solution)/shard_map/ppermute | solution.py:427
  9.5 11.7 %collective-permute-start.10 = (bf16[5,128,128]{2,1,0:T(8,128)(2,1)S(1)}, bf16[5,128,128]{2,1,0:T(8,128)(2,1)S(1)}, u32[]{:S(2)}, u32[]{:S(2)}) collective-permute-start(bf16[5,128,128]{2,1,0:T(8,128)(2,1)S(1)} %get-tuple-element.47), channel_id=1, source_target_pairs={{0,4},{4,0},{8,12},{12,8},{1,5},{5,1},{9,13},{13,9},{2,6},{6,2},{1... | collective-permute-start | bytes 491528 | tf_op jit(solution)/shard_map/ppermute | solution.py:433
  13.3 6.3 %collective-permute-start.7 = (bf16[64,1024]{1,0:T(8,128)(2,1)S(1)}, bf16[64,1024]{1,0:T(8,128)(2,1)S(1)}, u32[]{:S(2)}, u32[]{:S(2)}) collective-permute-start(bf16[64,1024]{1,0:T(8,128)(2,1)S(1)} %collective-permute-done.6.refs_7_), channel_id=1, source_target_pairs={{0,4},{4,0},{8,12},{12,8},{1,5},{5,1},{9,13},{13,9},{2,6},{6,2},{1... | collective-permute-start | bytes 393224 | tf_op jit(solution)/shard_map/ppermute | solution.py:433
  13.4 4.8 %collective-permute-start.13 = (bf16[3,128,128]{2,1,0:T(8,128)(2,1)S(1)}, bf16[3,128,128]{2,1,0:T(8,128)(2,1)S(1)}, u32[]{:S(2)}, u32[]{:S(2)}) collective-permute-start(bf16[3,128,128]{2,1,0:T(8,128)(2,1)S(1)} %slice.12), channel_id=1, source_target_pairs={{0,1},{1,0},{2,3},{3,2},{4,5},{5,4},{6,7},{7,6},{8,9},{9,8},{10,11... | collective-permute-start | bytes 294920 | tf_op jit(solution)/shard_map/ppermute | solution.py:424
  13.4 11.8 %collective-permute-start.12 = (bf16[5,128,128]{2,1,0:T(8,128)(2,1)S(1)}, bf16[5,128,128]{2,1,0:T(8,128)(2,1)S(1)}, u32[]{:S(2)}, u32[]{:S(2)}) collective-permute-start(bf16[5,128,128]{2,1,0:T(8,128)(2,1)S(1)} %get-tuple-element.49), channel_id=1, source_target_pairs={{0,12},{4,8},{8,4},{12,0},{1,13},{5,9},{9,5},{13,1},{2,14},{6,10},... | collective-permute-start | bytes 491528 | tf_op jit(solution)/shard_map/ppermute | solution.py:433
  16.7 13.1 %collective-permute-start.14 = (bf16[3,128,256]{2,1,0:T(8,128)(2,1)S(1)}, bf16[3,128,256]{2,1,0:T(8,128)(2,1)S(1)}, u32[]{:S(2)}, u32[]{:S(2)}) collective-permute-start(bf16[3,128,256]{2,1,0:T(8,128)(2,1)S(1)} %get-tuple-element.66.refs_0_), channel_id=1, source_target_pairs={{0,16},{16,0},{1,17},{17,1},{2,18},{18,2},{3,19},{19,3},{4,20},{20... | collective-permute-start | bytes 589832 | tf_op jit(solution)/shard_map/ppermute | solution.py:430
  18.2 11.0 %collective-permute-start.9 = (bf16[64,1024]{1,0:T(8,128)(2,1)S(1)}, bf16[64,1024]{1,0:T(8,128)(2,1)S(1)}, u32[]{:S(2)}, u32[]{:S(2)}) collective-permute-start(bf16[64,1024]{1,0:T(8,128)(2,1)S(1)} %collective-permute-done.6.refs_7_), channel_id=1, source_target_pairs={{0,2},{2,0},{1,3},{3,1},{4,6},{6,4},{5,7},{7,5},{8,10},{10,8},{9,1... | collective-permute-start | bytes 393224 | tf_op jit(solution)/shard_map/ppermute | solution.py:427
  19.6 10.1 %collective-permute-start.5 = (bf16[64,1024]{1,0:T(8,128)(2,1)S(1)}, bf16[64,1024]{1,0:T(8,128)(2,1)S(1)}, u32[]{:S(2)}, u32[]{:S(2)}) collective-permute-start(bf16[64,1024]{1,0:T(8,128)(2,1)S(1)} %collective-permute-done.4.refs_3_), channel_id=1, source_target_pairs={{0,2},{2,0},{1,3},{3,1},{4,6},{6,4},{5,7},{7,5},{8,10},{10,8},{9,1... | collective-permute-start | bytes 393224 | tf_op jit(solution)/shard_map/ppermute | solution.py:427
  21.2 8.0 %collective-permute-start.11 = (bf16[3,128,128]{2,1,0:T(8,128)(2,1)S(1)}, bf16[3,128,128]{2,1,0:T(8,128)(2,1)S(1)}, u32[]{:S(2)}, u32[]{:S(2)}) collective-permute-start(bf16[3,128,128]{2,1,0:T(8,128)(2,1)S(1)} %get-tuple-element.48), channel_id=1, source_target_pairs={{0,8},{4,12},{8,0},{12,4},{1,9},{5,13},{9,1},{13,5},{2,10},{6,14},... | collective-permute-start | bytes 294920 | tf_op jit(solution)/shard_map/ppermute | solution.py:433
  25.3 9.1 %collective-permute-start.8 = (bf16[64,1024]{1,0:T(8,128)(2,1)S(1)}, bf16[64,1024]{1,0:T(8,128)(2,1)S(1)}, u32[]{:S(2)}, u32[]{:S(2)}) collective-permute-start(bf16[64,1024]{1,0:T(8,128)(2,1)S(1)} %collective-permute-done.7.refs_5_), channel_id=1, source_target_pairs={{0,2},{2,0},{1,3},{3,1},{4,6},{6,4},{5,7},{7,5},{8,10},{10,8},{9,1... | collective-permute-start | bytes 393224 | tf_op jit(solution)/shard_map/ppermute | solution.py:427
  29.2 5.1 %collective-permute-start.15 = (bf16[3,128,128]{2,1,0:T(8,128)(2,1)S(1)}, bf16[3,128,128]{2,1,0:T(8,128)(2,1)S(1)}, u32[]{:S(2)}, u32[]{:S(2)}) collective-permute-start(bf16[3,128,128]{2,1,0:T(8,128)(2,1)S(1)} %slice.16), channel_id=1, source_target_pairs={{0,1},{1,0},{2,3},{3,2},{4,5},{5,4},{6,7},{7,6},{8,9},{9,8},{10,11... | collective-permute-start | bytes 294920 | tf_op jit(solution)/shard_map/ppermute | solution.py:424
  29.8 4.6 %collective-permute-start.17 = (bf16[3,128,128]{2,1,0:T(8,128)(2,1)S(1)}, bf16[3,128,128]{2,1,0:T(8,128)(2,1)S(1)}, u32[]{:S(2)}, u32[]{:S(2)}) collective-permute-start(bf16[3,128,128]{2,1,0:T(8,128)(2,1)S(1)} %slice.17), channel_id=1, source_target_pairs={{0,1},{1,0},{2,3},{3,2},{4,5},{5,4},{6,7},{7,6},{8,9},{9,8},{10,11... | collective-permute-start | bytes 294920 | tf_op jit(solution)/shard_map/ppermute | solution.py:424
  29.8 4.5 %collective-permute-start.18 = (bf16[2,128,128]{2,1,0:T(8,128)(2,1)S(1)}, bf16[2,128,128]{2,1,0:T(8,128)(2,1)S(1)}, u32[]{:S(2)}, u32[]{:S(2)}) collective-permute-start(bf16[2,128,128]{2,1,0:T(8,128)(2,1)S(1)} %slice.18), channel_id=1, source_target_pairs={{0,4},{4,0},{8,12},{12,8},{1,5},{5,1},{9,13},{13,9},{2,6},{6,2},{1... | collective-permute-start | bytes 196616 | tf_op jit(solution)/shard_map/ppermute | solution.py:433
  37.1 8.7 %collective-permute-start.19 = (bf16[4,2,128,128]{3,2,1,0:T(8,128)(2,1)S(1)}, bf16[4,2,128,128]{3,2,1,0:T(8,128)(2,1)S(1)}, u32[]{:S(2)}, u32[]{:S(2)}) collective-permute-start(bf16[4,2,128,128]{3,2,1,0:T(8,128)(2,1)S(1)} %get-tuple-element.58.refs_0_), channel_id=1, source_target_pairs={{0,16},{16,0},{1,17},{17,1},{2,18},{18,2},{3,19},{19,3},{4,20},{20... | collective-permute-start | bytes 786440 | tf_op jit(solution)/shard_map/ppermute | solution.py:430
  38.7 9.6 %collective-permute-start.24 = (bf16[3,128,256]{2,1,0:T(8,128)(2,1)S(1)}, bf16[3,128,256]{2,1,0:T(8,128)(2,1)S(1)}, u32[]{:S(2)}, u32[]{:S(2)}) collective-permute-start(bf16[3,128,256]{2,1,0:T(8,128)(2,1)S(1)} %get-tuple-element.66.refs_0_), channel_id=1, source_target_pairs={{0,12},{4,8},{8,4},{12,0},{1,13},{5,9},{9,5},{13,1},{2,14},{6,10},... | collective-permute-start | bytes 589832 | tf_op jit(solution)/shard_map/ppermute | solution.py:433
  39.8 11.7 %collective-permute-start.23 = (bf16[3,128,256]{2,1,0:T(8,128)(2,1)S(1)}, bf16[3,128,256]{2,1,0:T(8,128)(2,1)S(1)}, u32[]{:S(2)}, u32[]{:S(2)}) collective-permute-start(bf16[3,128,256]{2,1,0:T(8,128)(2,1)S(1)} %get-tuple-element.66.refs_0_), channel_id=1, source_target_pairs={{0,4},{4,0},{8,12},{12,8},{1,5},{5,1},{9,13},{13,9},{2,6},{6,2},{1... | collective-permute-start | bytes 589832 | tf_op jit(solution)/shard_map/ppermute | solution.py:433
  45.8 11.5 %collective-permute-start.21 = (bf16[4,2,128,128]{3,2,1,0:T(8,128)(2,1)S(1)}, bf16[4,2,128,128]{3,2,1,0:T(8,128)(2,1)S(1)}, u32[]{:S(2)}, u32[]{:S(2)}) collective-permute-start(bf16[4,2,128,128]{3,2,1,0:T(8,128)(2,1)S(1)} %get-tuple-element.58.refs_0_), channel_id=1, source_target_pairs={{0,1},{1,0},{2,3},{3,2},{4,5},{5,4},{6,7},{7,6},{8,9},{9,8},{10,11... | collective-permute-start | bytes 786440 | tf_op jit(solution)/shard_map/ppermute | solution.py:424
  45.8 11.5 %collective-permute-start.22 = (bf16[4,2,128,128]{3,2,1,0:T(8,128)(2,1)S(1)}, bf16[4,2,128,128]{3,2,1,0:T(8,128)(2,1)S(1)}, u32[]{:S(2)}, u32[]{:S(2)}) collective-permute-start(bf16[4,2,128,128]{3,2,1,0:T(8,128)(2,1)S(1)} %collective-permute-done.19.refs_2_), channel_id=1, source_target_pairs={{0,1},{1,0},{2,3},{3,2},{4,5},{5,4},{6,7},{7,6},{8,9},{9,8},{10,11... | collective-permute-start | bytes 786440 | tf_op jit(solution)/shard_map/ppermute | solution.py:424
  46.3 7.1 %collective-permute-start.25 = (bf16[144,128]{1,0:T(8,128)(2,1)S(1)}, bf16[144,128]{1,0:T(8,128)(2,1)S(1)}, u32[]{:S(2)}, u32[]{:S(2)}) collective-permute-start(bf16[144,128]{1,0:T(8,128)(2,1)S(1)} %get-tuple-element.55), channel_id=1, source_target_pairs={{0,4},{4,0},{8,12},{12,8},{1,5},{5,1},{9,13},{13,9},{2,6},{6,2},{1... | collective-permute-start | bytes 110600 | tf_op jit(solution)/shard_map/ppermute | solution.py:513
  48.2 5.4 %collective-permute-start.26 = (bf16[144,128]{1,0:T(8,128)(2,1)S(1)}, bf16[144,128]{1,0:T(8,128)(2,1)S(1)}, u32[]{:S(2)}, u32[]{:S(2)}) collective-permute-start(bf16[144,128]{1,0:T(8,128)(2,1)S(1)} %get-tuple-element.56), channel_id=1, source_target_pairs={{0,8},{4,12},{8,0},{12,4},{1,9},{5,13},{9,1},{13,5},{2,10},{6,14},... | collective-permute-start | bytes 110600 | tf_op jit(solution)/shard_map/ppermute | solution.py:513
  51.5 5.8 %collective-permute-start.27 = (bf16[144,128]{1,0:T(8,128)(2,1)S(1)}, bf16[144,128]{1,0:T(8,128)(2,1)S(1)}, u32[]{:S(2)}, u32[]{:S(2)}) collective-permute-start(bf16[144,128]{1,0:T(8,128)(2,1)S(1)} %get-tuple-element.57), channel_id=1, source_target_pairs={{0,12},{4,8},{8,4},{12,0},{1,13},{5,9},{9,5},{13,1},{2,14},{6,10},... | collective-permute-start | bytes 110600 | tf_op jit(solution)/shard_map/ppermute | solution.py:513
  57.3 5.7 %collective-permute-start.29 = (bf16[3,128,256]{2,1,0:T(8,128)(2,1)S(1)}, bf16[3,128,256]{2,1,0:T(8,128)(2,1)S(1)}, u32[]{:S(2)}, u32[]{:S(2)}) collective-permute-start(bf16[3,128,256]{2,1,0:T(8,128)(2,1)S(1)} %collective-permute-done.24.refs_3_), channel_id=1, source_target_pairs={{0,4},{4,0},{8,12},{12,8},{1,5},{5,1},{9,13},{13,9},{2,6},{6,2},{1... | collective-permute-start | bytes 589832 | tf_op jit(solution)/shard_map/ppermute | solution.py:433
  57.8 14.2 %collective-permute-start.28 = (bf16[144,1024]{1,0:T(8,128)(2,1)S(1)}, bf16[144,1024]{1,0:T(8,128)(2,1)S(1)}, u32[]{:S(2)}, u32[]{:S(2)}) collective-permute-start(bf16[144,1024]{1,0:T(8,128)(2,1)S(1)} %get-tuple-element.65), channel_id=1, source_target_pairs={{0,2},{2,0},{1,3},{3,1},{4,6},{6,4},{5,7},{7,5},{8,10},{10,8},{9,1... | collective-permute-start | bytes 884744 | tf_op jit(solution)/shard_map/ppermute | solution.py:427
  59.6 10.2 %collective-permute-start.33 = (bf16[3,128,256]{2,1,0:T(8,128)(2,1)S(1)}, bf16[3,128,256]{2,1,0:T(8,128)(2,1)S(1)}, u32[]{:S(2)}, u32[]{:S(2)}) collective-permute-start(bf16[3,128,256]{2,1,0:T(8,128)(2,1)S(1)} %collective-permute-done.24.refs_3_), channel_id=1, source_target_pairs={{0,16},{16,0},{1,17},{17,1},{2,18},{18,2},{3,19},{19,3},{4,20},{20... | collective-permute-start | bytes 589832 | tf_op jit(solution)/shard_map/ppermute | solution.py:430
  60.1 9.7 %collective-permute-start.31 = (bf16[3,128,256]{2,1,0:T(8,128)(2,1)S(1)}, bf16[3,128,256]{2,1,0:T(8,128)(2,1)S(1)}, u32[]{:S(2)}, u32[]{:S(2)}) collective-permute-start(bf16[3,128,256]{2,1,0:T(8,128)(2,1)S(1)} %collective-permute-done.23.refs_1_), channel_id=1, source_target_pairs={{0,16},{16,0},{1,17},{17,1},{2,18},{18,2},{3,19},{19,3},{4,20},{20... | collective-permute-start | bytes 589832 | tf_op jit(solution)/shard_map/ppermute | solution.py:430
  63.0 8.9 %collective-permute-start.32 = (bf16[3,128,256]{2,1,0:T(8,128)(2,1)S(1)}, bf16[3,128,256]{2,1,0:T(8,128)(2,1)S(1)}, u32[]{:S(2)}, u32[]{:S(2)}) collective-permute-start(bf16[3,128,256]{2,1,0:T(8,128)(2,1)S(1)} %collective-permute-done.29.refs_2_), channel_id=1, source_target_pairs={{0,16},{16,0},{1,17},{17,1},{2,18},{18,2},{3,19},{19,3},{4,20},{20... | collective-permute-start | bytes 589832 | tf_op jit(solution)/shard_map/ppermute | solution.py:430
  76.9 5.6 %collective-permute-start.37 = (bf16[64,1024]{1,0:T(8,128)(2,1)S(1)}, bf16[64,1024]{1,0:T(8,128)(2,1)S(1)}, u32[]{:S(2)}, u32[]{:S(2)}) collective-permute-start(bf16[64,1024]{1,0:T(8,128)(2,1)S(1)} %get-tuple-element.76), channel_id=1, source_target_pairs={{0,2},{2,0},{1,3},{3,1},{4,6},{6,4},{5,7},{7,5},{8,10},{10,8},{9,1... | collective-permute-start | bytes 393224 | tf_op jit(solution)/shard_map/ppermute | solution.py:427
  (11 other events, 23.4 us)

commit v6 on v5

--- a/solution.py
+++ b/solution.py
@@ -229,6 +229,11 @@
         copy.wait()
 
 
+def join_kernel(length, *refs):
+    for k, ref in enumerate(refs[:-1]):
+        refs[-1][k] = ref[...]
+
+
 def stack_kernel(length, *refs):
     s = lax.axis_index("seq")
     for k in range(SEQ):
@@ -236,9 +241,9 @@
 
 
 def project_kernel(length, *refs):
-    frames, gain, *blocks = refs[: 2 * SEQ + 1]
-    mine, other, down = refs[2 * SEQ + 1 : 3 * SEQ + 1], refs[3 * SEQ + 1 : 4 * SEQ + 1], refs[4 * SEQ + 1]
-    q_out, send_out, edge_out, stack_out, normed, weights, x_edge, q_edge, own_x, own_gain, sems = refs[4 * SEQ + 2 :]
+    frames, gain, own_far, *near = refs[: SEQ + 2]
+    far, mine, other = refs[SEQ + 2], refs[SEQ + 3 : 2 * SEQ + 3], refs[2 * SEQ + 3 : 3 * SEQ + 3]
+    q_out, send_out, edge_out, stack_out, normed, weights, x_edge, q_edge, own_x, own_gain, sems = refs[3 * SEQ + 3 :]
     copies = [
         pltpu.make_async_copy(frames, own_x, sems.at[0]),
         pltpu.make_async_copy(gain, own_gain, sems.at[1]),
@@ -246,7 +251,9 @@
     for copy in copies:
         copy.start()
     s, h, f, _ = here()
-    blocks = [own_x, *blocks]
+    blocks = [own_x, own_far]
+    for k in range(1, SEQ):
+        blocks += [near[k - 1], far.at[k - 1]]
     rows = blocks[0].shape[0]
     half = mine[0].shape[1]
     for copy in copies:
@@ -263,7 +270,7 @@
             at = pl.ds(aligned((s ^ k) * 2 * half + (f ^ core) * half, half), half)
             for m in range(3):
                 weights[at, m * HD : (m + 1) * HD] = pieces[k][m]
-        stack_out[s ^ k] = down[...] if k == 2 else mine[k][3:]
+        stack_out[s ^ k] = mine[k][3:]
     count = 2 * SEQ
     total = count * rows
     projected = dot(normed[...], weights[...])
@@ -440,14 +447,11 @@
         return lax.dynamic_slice_in_dim(x, p * half, half, axis=x.ndim - 2)
 
     near = planes(frames)
-    blocks = []
-    for block in near:
-        blocks += [block, other_side(block)]
     given = [w_query, w_key, w_value]
     shape = jax.ShapeDtypeStruct
     *dealt, pw_mine = call(
         deal_kernel,
-        [shape((3 if k == 2 else 3 + columns // HD, half, HD), BF16) for k in range(SEQ)]
+        [shape((3 + columns // HD, half, HD), BF16)] * SEQ
         + [shape((3, half, columns), BF16)],
         [
             pltpu.VMEM((4, 2 * half, columns), BF16),
@@ -465,12 +469,15 @@
     )
     *dealt, _ = barrier((*dealt, near[1]))
     w_mine = [dealt[0]] + [across(dealt[k], k) for k in range(1, SEQ)]
+    own_far = other_side(frames)
+    *near[1:], own_far, _ = barrier((*near[1:], own_far, w_mine[1]))
+    (joined,) = call(join_kernel, [shape((SEQ - 1, rows, width), BF16)], [], length, *near[1:])
+    far = other_side(joined)
     w_other = [other_core(w[:3]) for w in w_mine]
-    down = across(w_mine[3][3:], 1)
-    pw_part = other_part(pw_mine)
-    w_other[0], pw_part = barrier((w_other[0], pw_part))
-    after, *_ = barrier((pw_mine, *w_mine[1:], down))
-    pw_one, pw_three = across(after, 1), across(after, 3)
+    after, *_ = barrier((pw_mine, joined, w_mine[2], w_mine[3]))
+    pw_part, pw_one, pw_three = other_part(after), across(after, 1), across(after, 3)
+    w_other[0], pw_part, pw_one = barrier((w_other[0], pw_part, pw_one))
+    pw_two, one_part, three_part = across(pw_three, 1), other_part(pw_one), other_part(pw_three)
     queries, send, edges, stack = call(
         project_kernel,
         [
@@ -491,13 +498,15 @@
         length,
         frames,
         ln1_gain[None],
-        *blocks[1:],
+        own_far,
+        *near[1:],
+        far,
         *w_mine,
         *w_other,
-        down,
         left=2,
     )
     received = other_core(send)
+    queries, pw_three = barrier((queries, pw_three))
     stack_part = other_part(stack)
     ctx = call(
         attend_kernel,
@@ -508,12 +517,9 @@
         send,
         received,
     )
-    stack, stack_part, *_ = barrier((stack, stack_part, *ctx))
+    ctx = [ctx[0]] + [lax.ppermute(ctx[k], "seq", xor_pairs(k)) for k in range(1, SEQ)]
+    pw_two, one_part, stack, stack_part, *ctx[2:] = barrier((pw_two, one_part, stack, stack_part, *ctx[2:]))
     out_pieces = [stack, other_core(stack), stack_part, other_core(stack_part)]
-    ctx = [ctx[0]] + [lax.ppermute(ctx[k], "seq", xor_pairs(k)) for k in range(1, SEQ)]
-    pw_one, pw_three, *ctx = barrier((pw_one, pw_three, *ctx))
-    pw_two = across(pw_three, 1)
-    one_part, three_part = other_part(pw_one), other_part(pw_three)
     own_share, sent_share = call(
         output_kernel,
         [shape((2 * step, width), F32), shape((2 * step, width), BF16)],
@@ -555,7 +561,7 @@
         length,
         *pw_pieces,
         frames,
-        blocks[1],
+        own_far,
         halo_x,
         own_share,
         peer_share,

time: 83.4 us -> 85.7 us (1.028)
  starting transfers between devices: 34.8 us -> 37.6 us
    ppermute x10 -> x9, starting transfers between devices: 13.5 us -> 20.5 us  [across(): return lax.ppermute(x, 'seq', xor_pairs(k))]
    ppermute x10 -> x9, waiting for transfers between devices: 15.3 us -> 11.7 us  [across(): return lax.ppermute(x, 'seq', xor_pairs(k))]
    ppermute x3, waiting for transfers between devices: 3.88 us -> 6.91 us  [shards_chip_per_head(): lax.ppermute(ctx[k], 'seq', xor_pairs(k))]
    ppermute x6 -> x4, starting transfers between devices: 8.06 us -> 5.08 us  [other_side(): return lax.ppermute(x, 'head', SWAP)]
    ppermute x3, starting transfers between devices: 4.27 us -> 2.96 us  [shards_chip_per_head(): lax.ppermute(ctx[k], 'seq', xor_pairs(k))]
    ppermute x6 -> x4, waiting for transfers between devices: 4.88 us -> 5.01 us  [other_side(): return lax.ppermute(x, 'head', SWAP)]
    pallas_call x7 -> x8, Pallas kernels: 8.82 us -> 8.87 us  [call(): pl.pallas_call(kernel, out_shape=outs, in_specs=[pl.BlockSpec(memory_spac...]
  transfers between devices with their start and end apart: 38 -> 35, of which waited for: 16 -> 15; matrix products, arithmetic and copies ran while one was open for 0% -> 0% of each run, Pallas kernels for 6% -> 8%
where the time goes in v6:
time: 85.7 us; the launch traced here: 85.4 us
  starting transfers between devices  37.6 us (44%)
  waiting for transfers between devices  36.6 us (43%)
  Pallas kernels  8.87 us (10%)
  between operations  0.87 us (1%)
    ppermute x9, starting transfers between devices, across(): return lax.ppermute(x, 'seq', xor_pairs(k))  20.5 us
    ppermute x9, waiting for transfers between devices, across(): return lax.ppermute(x, 'seq', xor_pairs(k))  11.7 us
    ppermute x5, waiting for transfers between devices, other_part(): return lax.ppermute(x, 'parts', SWAP)  10.7 us
    pallas_call x8, Pallas kernels, call(): pl.pallas_call(kernel, out_shape=outs, in_specs=[pl.BlockSpec(memory_spac...  8.87 us
    ppermute x3, waiting for transfers between devices, shards_chip_per_head(): lax.ppermute(ctx[k], 'seq', xor_pairs(k))  6.91 us
    ppermute x5, starting transfers between devices, other_part(): return lax.ppermute(x, 'parts', SWAP)  5.64 us
    ppermute x4, starting transfers between devices, other_side(): return lax.ppermute(x, 'head', SWAP)  5.08 us
    ppermute x4, waiting for transfers between devices, other_side(): return lax.ppermute(x, 'head', SWAP)  5.01 us
  transfers between devices with their start and end apart: 35, of which 15 were waited for; matrix products, arithmetic and copies ran while one was open for 0% of the time, Pallas kernels for 8%

profile of v6, /device:TPU:0, one launch (start us, length us, event | category | flops | bytes accessed | tf_op | source)
XLA Modules:
  0.0 85.4 jit_solution(5662831372737064574)
XLA Ops:
  1.0 2.6 %collective-permute-start.3 = (bf16[64,1024]{1,0:T(8,128)(2,1)}, bf16[64,1024]{1,0:T(8,128)(2,1)S(1)}, u32[]{:S(2)}, u32[]{:S(2)}) collective-permute-start(bf16[64,1024]{1,0:T(8,128)(2,1)} %refs_4_.3), channel_id=1, source_target_pairs={{0,4},{4,0},{8,12},{12,8},{1,5},{5,1},{9,13},{13,9},{2,6},{6,2},{1... | collective-permute-start | bytes 393224 | tf_op jit(solution)/shard_map/ppermute | solution.py:440
  3.5 2.5 %collective-permute-start.4 = (bf16[64,1024]{1,0:T(8,128)(2,1)}, bf16[64,1024]{1,0:T(8,128)(2,1)S(1)}, u32[]{:S(2)}, u32[]{:S(2)}) collective-permute-start(bf16[64,1024]{1,0:T(8,128)(2,1)} %refs_4_.3), channel_id=1, source_target_pairs={{0,12},{4,8},{8,4},{12,0},{1,13},{5,9},{9,5},{13,1},{2,14},{6,10},... | collective-permute-start | bytes 393224 | tf_op jit(solution)/shard_map/ppermute | solution.py:440
  6.7 1.4 %shard_map.136 = (bf16[5,128,128]{2,1,0:T(8,128)(2,1)S(1)}, bf16[5,128,128]{2,1,0:T(8,128)(2,1)S(1)}, bf16[5,128,128]{2,1,0:T(8,128)(2,1)S(1)}, bf16[5,128,128]{2,1,0:T(8,128)(2,1)S(1)}, bf16[3,128,256]{2,1,0:T(8,128)(2,1)S(1)}) custom-call(s32[1]{0:T(128)S(6)} %copy.15.length, bf16[256,256]{1,0:T(8,128)(2,1)} %refs_0_.2, bf16[256,256]{1,0:T(8,128)(2,1)} %refs_1_.1, ...), custom_call_target="tpu_custom_call" | custom-call | tf_op jit(solution)/shard_map/pallas_call | solution.py:171
  8.1 2.0 %collective-permute-start.7 = (bf16[5,128,128]{2,1,0:T(8,128)(2,1)S(1)}, bf16[5,128,128]{2,1,0:T(8,128)(2,1)S(1)}, u32[]{:S(2)}, u32[]{:S(2)}) collective-permute-start(bf16[5,128,128]{2,1,0:T(8,128)(2,1)S(1)} %get-tuple-element.51), channel_id=1, source_target_pairs={{0,4},{4,0},{8,12},{12,8},{1,5},{5,1},{9,13},{13,9},{2,6},{6,2},{1... | collective-permute-start | bytes 491528 | tf_op jit(solution)/shard_map/ppermute | solution.py:440
  10.0 1.5 %collective-permute-start.6 = (bf16[64,1024]{1,0:T(8,128)(2,1)S(1)}, bf16[64,1024]{1,0:T(8,128)(2,1)S(1)}, u32[]{:S(2)}, u32[]{:S(2)}) collective-permute-start(bf16[64,1024]{1,0:T(8,128)(2,1)S(1)} %copy-done), channel_id=1, source_target_pairs={{0,2},{2,0},{1,3},{3,1},{4,6},{6,4},{5,7},{7,5},{8,10},{10,8},{9,1... | collective-permute-start | bytes 393224 | tf_op jit(solution)/shard_map/ppermute | solution.py:434
  11.5 1.8 %collective-permute-done.4.refs_2_.refs_5_ = bf16[64,1024]{1,0:T(8,128)(2,1)S(1)} collective-permute-done((bf16[64,1024]{1,0:T(8,128)(2,1)}, bf16[64,1024]{1,0:T(8,128)(2,1)S(1)}, u32[]{:S(2)}, u32[]{:S(2)}) %collective-permute-start.4) | collective-permute-done | bytes 131104 | tf_op jit(solution)/shard_map/ppermute | solution.py:440
  13.3 3.0 %collective-permute-start.8 = (bf16[5,128,128]{2,1,0:T(8,128)(2,1)S(1)}, bf16[5,128,128]{2,1,0:T(8,128)(2,1)S(1)}, u32[]{:S(2)}, u32[]{:S(2)}) collective-permute-start(bf16[5,128,128]{2,1,0:T(8,128)(2,1)S(1)} %get-tuple-element.55), channel_id=1, source_target_pairs={{0,8},{4,12},{8,0},{12,4},{1,9},{5,13},{9,1},{13,5},{2,10},{6,14},... | collective-permute-start | bytes 491528 | tf_op jit(solution)/shard_map/ppermute | solution.py:440
  16.4 1.5 %collective-permute-start.9 = (bf16[5,128,128]{2,1,0:T(8,128)(2,1)S(1)}, bf16[5,128,128]{2,1,0:T(8,128)(2,1)S(1)}, u32[]{:S(2)}, u32[]{:S(2)}) collective-permute-start(bf16[5,128,128]{2,1,0:T(8,128)(2,1)S(1)} %get-tuple-element.56), channel_id=1, source_target_pairs={{0,12},{4,8},{8,4},{12,0},{1,13},{5,9},{9,5},{13,1},{2,14},{6,10},... | collective-permute-start | bytes 491528 | tf_op jit(solution)/shard_map/ppermute | solution.py:440
  17.8 4.7 %collective-permute-done.5.refs_1_.refs_4_ = bf16[64,1024]{1,0:T(8,128)(2,1)S(1)} collective-permute-done((bf16[64,1024]{1,0:T(8,128)(2,1)S(1)}, bf16[64,1024]{1,0:T(8,128)(2,1)S(1)}, u32[]{:S(2)}, u32[]{:S(2)}) %collective-permute-start.5) | collective-permute-done | bytes 131104 | tf_op jit(solution)/shard_map/ppermute | solution.py:440
  22.6 1.4 %collective-permute-start.16 = (bf16[3,64,1024]{2,1,0:T(8,128)(2,1)S(1)}, bf16[3,64,1024]{2,1,0:T(8,128)(2,1)S(1)}, u32[]{:S(2)}, u32[]{:S(2)}) collective-permute-start(bf16[3,64,1024]{2,1,0:T(8,128)(2,1)S(1)} %shard_map.137), channel_id=1, source_target_pairs={{0,2},{2,0},{1,3},{3,1},{4,6},{6,4},{5,7},{7,5},{8,10},{10,8},{9,1... | collective-permute-start | bytes 1179656 | tf_op jit(solution)/shard_map/ppermute | solution.py:434
  24.0 4.5 %collective-permute-done.8.refs_9_ = bf16[5,128,128]{2,1,0:T(8,128)(2,1)S(1)} collective-permute-done((bf16[5,128,128]{2,1,0:T(8,128)(2,1)S(1)}, bf16[5,128,128]{2,1,0:T(8,128)(2,1)S(1)}, u32[]{:S(2)}, u32[]{:S(2)}) %collective-permute-start.8) | collective-permute-done | bytes 163872 | tf_op jit(solution)/shard_map/ppermute | solution.py:440
  28.5 2.3 %collective-permute-start.14 = (bf16[3,128,256]{2,1,0:T(8,128)(2,1)S(1)}, bf16[3,128,256]{2,1,0:T(8,128)(2,1)S(1)}, u32[]{:S(2)}, u32[]{:S(2)}) collective-permute-start(bf16[3,128,256]{2,1,0:T(8,128)(2,1)S(1)} %get-tuple-element.75.refs_0_), channel_id=1, source_target_pairs={{0,4},{4,0},{8,12},{12,8},{1,5},{5,1},{9,13},{13,9},{2,6},{6,2},{1... | collective-permute-start | bytes 589832 | tf_op jit(solution)/shard_map/ppermute | solution.py:440
  30.8 1.5 %collective-permute-start.13 = (bf16[3,128,256]{2,1,0:T(8,128)(2,1)S(1)}, bf16[3,128,256]{2,1,0:T(8,128)(2,1)S(1)}, u32[]{:S(2)}, u32[]{:S(2)}) collective-permute-start(bf16[3,128,256]{2,1,0:T(8,128)(2,1)S(1)} %get-tuple-element.75.refs_0_), channel_id=1, source_target_pairs={{0,16},{16,0},{1,17},{17,1},{2,18},{18,2},{3,19},{19,3},{4,20},{20... | collective-permute-start | bytes 589832 | tf_op jit(solution)/shard_map/ppermute | solution.py:437
  34.5 2.0 %collective-permute-done.13.refs_0_ = bf16[3,128,256]{2,1,0:T(8,128)(2,1)S(1)} collective-permute-done((bf16[3,128,256]{2,1,0:T(8,128)(2,1)S(1)}, bf16[3,128,256]{2,1,0:T(8,128)(2,1)S(1)}, u32[]{:S(2)}, u32[]{:S(2)}) %collective-permute-start.13) | collective-permute-done | bytes 196640 | tf_op jit(solution)/shard_map/ppermute | solution.py:437
  36.5 2.6 %collective-permute-start.10 = (bf16[3,128,256]{2,1,0:T(8,128)(2,1)S(1)}, bf16[3,128,256]{2,1,0:T(8,128)(2,1)S(1)}, u32[]{:S(2)}, u32[]{:S(2)}) collective-permute-start(bf16[3,128,256]{2,1,0:T(8,128)(2,1)S(1)} %get-tuple-element.75.refs_0_), channel_id=1, source_target_pairs={{0,12},{4,8},{8,4},{12,0},{1,13},{5,9},{9,5},{13,1},{2,14},{6,10},... | collective-permute-start | bytes 589832 | tf_op jit(solution)/shard_map/ppermute | solution.py:440
  39.2 2.6 %shard_map.138 = (bf16[512,128]{1,0:T(8,128)(2,1)S(1)}, bf16[1088,128]{1,0:T(8,128)(2,1)S(1)}, bf16[16,1024]{1,0:T(8,128)(2,1)S(1)}, bf16[4,2,128,128]{3,2,1,0:T(8,128)(2,1)S(1)}) custom-call(s32[1]{0:T(128)S(6)} %copy.15.length, bf16[64,1024]{1,0:T(8,128)(2,1)} %refs_4_.3, f32[1,1024]{1,0:T(1,128)} %bitcast.5, ...), custom_call_target="tpu_custom_call" | custom-call | tf_op jit(solution)/shard_map/pallas_call | solution.py:171
  41.9 1.6 %collective-permute-start.20 = (bf16[4,2,128,128]{3,2,1,0:T(8,128)(2,1)S(1)}, bf16[4,2,128,128]{3,2,1,0:T(8,128)(2,1)S(1)}, u32[]{:S(2)}, u32[]{:S(2)}) collective-permute-start(bf16[4,2,128,128]{3,2,1,0:T(8,128)(2,1)S(1)} %get-tuple-element.68.refs_0_), channel_id=1, source_target_pairs={{0,16},{16,0},{1,17},{17,1},{2,18},{18,2},{3,19},{19,3},{4,20},{20... | collective-permute-start | bytes 786440 | tf_op jit(solution)/shard_map/ppermute | solution.py:437
  44.0 4.0 %collective-permute-start.11 = (bf16[3,128,256]{2,1,0:T(8,128)(2,1)S(1)}, bf16[3,128,256]{2,1,0:T(8,128)(2,1)S(1)}, u32[]{:S(2)}, u32[]{:S(2)}) collective-permute-start(bf16[3,128,256]{2,1,0:T(8,128)(2,1)S(1)} %collective-permute-done.10.refs_3_), channel_id=1, source_target_pairs={{0,4},{4,0},{8,12},{12,8},{1,5},{5,1},{9,13},{13,9},{2,6},{6,2},{1... | collective-permute-start | bytes 589832 | tf_op jit(solution)/shard_map/ppermute | solution.py:440
  48.0 2.8 %shard_map.139 = (bf16[144,128]{1,0:T(8,128)(2,1)S(1)}, bf16[144,128]{1,0:T(8,128)(2,1)S(1)}, bf16[144,128]{1,0:T(8,128)(2,1)S(1)}, bf16[144,128]{1,0:T(8,128)(2,1)S(1)}) custom-call(s32[1]{0:T(128)S(6)} %copy.15.length, bf16[512,128]{1,0:T(8,128)(2,1)S(1)} %get-tuple-element.64.q_in, bf16[1088,128]{1,0:T(8,128)(2,1)S(1)} %get-tuple-element.65.own, ...), custom_call_target="tpu_custom_call" | custom-call | tf_op jit(solution)/shard_map/pallas_call | solution.py:171
  50.9 1.2 %collective-permute-start.22 = (bf16[144,128]{1,0:T(8,128)(2,1)S(1)}, bf16[144,128]{1,0:T(8,128)(2,1)S(1)}, u32[]{:S(2)}, u32[]{:S(2)}) collective-permute-start(bf16[144,128]{1,0:T(8,128)(2,1)S(1)} %get-tuple-element.66), channel_id=1, source_target_pairs={{0,8},{4,12},{8,0},{12,4},{1,9},{5,13},{9,1},{13,5},{2,10},{6,14},... | collective-permute-start | bytes 110600 | tf_op jit(solution)/shard_map/ppermute | solution.py:520
  52.1 1.6 %collective-permute-start.23 = (bf16[144,128]{1,0:T(8,128)(2,1)S(1)}, bf16[144,128]{1,0:T(8,128)(2,1)S(1)}, u32[]{:S(2)}, u32[]{:S(2)}) collective-permute-start(bf16[144,128]{1,0:T(8,128)(2,1)S(1)} %get-tuple-element.67), channel_id=1, source_target_pairs={{0,12},{4,8},{8,4},{12,0},{1,13},{5,9},{9,5},{13,1},{2,14},{6,10},... | collective-permute-start | bytes 110600 | tf_op jit(solution)/shard_map/ppermute | solution.py:520
  53.7 1.1 %collective-permute-done.15.refs_1_ = bf16[3,128,256]{2,1,0:T(8,128)(2,1)S(1)} collective-permute-done((bf16[3,128,256]{2,1,0:T(8,128)(2,1)S(1)}, bf16[3,128,256]{2,1,0:T(8,128)(2,1)S(1)}, u32[]{:S(2)}, u32[]{:S(2)}) %collective-permute-start.15) | collective-permute-done | bytes 196640 | tf_op jit(solution)/shard_map/ppermute | solution.py:437
  54.8 2.1 %collective-permute-done.22.refs_6_ = bf16[144,128]{1,0:T(8,128)(2,1)S(1)} collective-permute-done((bf16[144,128]{1,0:T(8,128)(2,1)S(1)}, bf16[144,128]{1,0:T(8,128)(2,1)S(1)}, u32[]{:S(2)}, u32[]{:S(2)}) %collective-permute-start.22) | collective-permute-done | bytes 36896 | tf_op jit(solution)/shard_map/ppermute | solution.py:520
  57.0 1.0 %collective-permute-done.23.refs_7_ = bf16[144,128]{1,0:T(8,128)(2,1)S(1)} collective-permute-done((bf16[144,128]{1,0:T(8,128)(2,1)S(1)}, bf16[144,128]{1,0:T(8,128)(2,1)S(1)}, u32[]{:S(2)}, u32[]{:S(2)}) %collective-permute-start.23) | collective-permute-done | bytes 36896 | tf_op jit(solution)/shard_map/ppermute | solution.py:520
  58.6 3.8 %collective-permute-done.26.refs_5_ = bf16[144,128]{1,0:T(8,128)(2,1)S(1)} collective-permute-done((bf16[144,128]{1,0:T(8,128)(2,1)S(1)}, bf16[144,128]{1,0:T(8,128)(2,1)S(1)}, u32[]{:S(2)}, u32[]{:S(2)}) %collective-permute-start.26) | collective-permute-done | bytes 36896 | tf_op jit(solution)/shard_map/ppermute | solution.py:520
  62.9 1.6 %collective-permute-start.27 = (bf16[144,1024]{1,0:T(8,128)(2,1)S(1)}, bf16[144,1024]{1,0:T(8,128)(2,1)S(1)}, u32[]{:S(2)}, u32[]{:S(2)}) collective-permute-start(bf16[144,1024]{1,0:T(8,128)(2,1)S(1)} %get-tuple-element.74), channel_id=1, source_target_pairs={{0,2},{2,0},{1,3},{3,1},{4,6},{6,4},{5,7},{7,5},{8,10},{10,8},{9,1... | collective-permute-start | bytes 884744 | tf_op jit(solution)/shard_map/ppermute | solution.py:434
  64.5 1.5 %collective-permute-start.30 = (bf16[3,128,256]{2,1,0:T(8,128)(2,1)S(1)}, bf16[3,128,256]{2,1,0:T(8,128)(2,1)S(1)}, u32[]{:S(2)}, u32[]{:S(2)}) collective-permute-start(bf16[3,128,256]{2,1,0:T(8,128)(2,1)S(1)} %collective-permute-done.10.refs_3_), channel_id=1, source_target_pairs={{0,16},{16,0},{1,17},{17,1},{2,18},{18,2},{3,19},{19,3},{4,20},{20... | collective-permute-start | bytes 589832 | tf_op jit(solution)/shard_map/ppermute | solution.py:437
  66.5 5.5 %collective-permute-done.30.refs_3_ = bf16[3,128,256]{2,1,0:T(8,128)(2,1)S(1)} collective-permute-done((bf16[3,128,256]{2,1,0:T(8,128)(2,1)S(1)}, bf16[3,128,256]{2,1,0:T(8,128)(2,1)S(1)}, u32[]{:S(2)}, u32[]{:S(2)}) %collective-permute-start.30) | collective-permute-done | bytes 196640 | tf_op jit(solution)/shard_map/ppermute | solution.py:437
  72.0 2.1 %collective-permute-done.29.refs_2_ = bf16[3,128,256]{2,1,0:T(8,128)(2,1)S(1)} collective-permute-done((bf16[3,128,256]{2,1,0:T(8,128)(2,1)S(1)}, bf16[3,128,256]{2,1,0:T(8,128)(2,1)S(1)}, u32[]{:S(2)}, u32[]{:S(2)}) %collective-permute-start.29) | collective-permute-done | bytes 196640 | tf_op jit(solution)/shard_map/ppermute | solution.py:437
  76.2 1.5 %collective-permute-done.33.refs_11_ = f32[16,256]{1,0:T(8,128)S(1)} collective-permute-done((f32[16,256]{1,0:T(8,128)S(1)}, f32[16,256]{1,0:T(8,128)S(1)}, u32[]{:S(2)}, u32[]{:S(2)}) %collective-permute-start.33) | collective-permute-done | bytes 16416 | tf_op jit(solution)/shard_map/ppermute | solution.py:431
  77.7 1.4 %shard_map.143 = (f32[64,1024]{1,0:T(8,128)S(1)}, bf16[64,1024]{1,0:T(8,128)(2,1)S(1)}) custom-call(s32[1]{0:T(128)S(6)} %copy.15.length, bf16[4,3,128,256]{3,2,1,0:T(8,128)(2,1)S(1)} %shard_map.141.refs_0_, bf16[4,3,128,256]{3,2,1,0:T(8,128)(2,1)S(1)} %collective-permute-done.28.refs_1_, bf16[4,3,128,256]{3,2,1,0:T(8,128)(2,1)S(1)} %shard_map.142.refs_2_, ...), custom_call_target="tpu_custom_call" | custom-call | tf_op jit(solution)/shard_map/pallas_call | solution.py:171
  79.7 5.0 %collective-permute-done.34 = bf16[64,1024]{1,0:T(8,128)(2,1)S(1)} collective-permute-done((bf16[64,1024]{1,0:T(8,128)(2,1)S(1)}, bf16[64,1024]{1,0:T(8,128)(2,1)S(1)}, u32[]{:S(2)}, u32[]{:S(2)}) %collective-permute-start.34) | collective-permute-done | bytes 131104 | tf_op jit(solution)/shard_map/ppermute | solution.py:434
  (66 shorter events, 8.9 us)
Async XLA Ops:
  0.0 6.7 %collective-permute-start = (bf16[256,256]{1,0:T(8,128)(2,1)}, bf16[256,256]{1,0:T(8,128)(2,1)S(1)}, u32[]{:S(2)}, u32[]{:S(2)}) collective-permute-start(bf16[256,256]{1,0:T(8,128)(2,1)} %refs_0_.2), channel_id=1, source_target_pairs={{0,1},{1,0},{2,3},{3,2},{4,5},{5,4},{6,7},{7,6},{8,9},{9,8},{10,11... | collective-permute-start | bytes 393224 | tf_op jit(solution)/shard_map/ppermute | solution.py:431
  0.5 6.2 %collective-permute-start.1 = (bf16[256,256]{1,0:T(8,128)(2,1)}, bf16[256,256]{1,0:T(8,128)(2,1)S(1)}, u32[]{:S(2)}, u32[]{:S(2)}) collective-permute-start(bf16[256,256]{1,0:T(8,128)(2,1)} %refs_1_.1), channel_id=1, source_target_pairs={{0,1},{1,0},{2,3},{3,2},{4,5},{5,4},{6,7},{7,6},{8,9},{9,8},{10,11... | collective-permute-start | bytes 393224 | tf_op jit(solution)/shard_map/ppermute | solution.py:431
  0.5 6.2 %collective-permute-start.2 = (bf16[256,256]{1,0:T(8,128)(2,1)}, bf16[256,256]{1,0:T(8,128)(2,1)S(1)}, u32[]{:S(2)}, u32[]{:S(2)}) collective-permute-start(bf16[256,256]{1,0:T(8,128)(2,1)} %refs_2_.1), channel_id=1, source_target_pairs={{0,1},{1,0},{2,3},{3,2},{4,5},{5,4},{6,7},{7,6},{8,9},{9,8},{10,11... | collective-permute-start | bytes 393224 | tf_op jit(solution)/shard_map/ppermute | solution.py:431
  1.0 7.1 %collective-permute-start.3 = (bf16[64,1024]{1,0:T(8,128)(2,1)}, bf16[64,1024]{1,0:T(8,128)(2,1)S(1)}, u32[]{:S(2)}, u32[]{:S(2)}) collective-permute-start(bf16[64,1024]{1,0:T(8,128)(2,1)} %refs_4_.3), channel_id=1, source_target_pairs={{0,4},{4,0},{8,12},{12,8},{1,5},{5,1},{9,13},{13,9},{2,6},{6,2},{1... | collective-permute-start | bytes 393224 | tf_op jit(solution)/shard_map/ppermute | solution.py:440
  3.5 9.8 %collective-permute-start.4 = (bf16[64,1024]{1,0:T(8,128)(2,1)}, bf16[64,1024]{1,0:T(8,128)(2,1)S(1)}, u32[]{:S(2)}, u32[]{:S(2)}) collective-permute-start(bf16[64,1024]{1,0:T(8,128)(2,1)} %refs_4_.3), channel_id=1, source_target_pairs={{0,12},{4,8},{8,4},{12,0},{1,13},{5,9},{9,5},{13,1},{2,14},{6,10},... | collective-permute-start | bytes 393224 | tf_op jit(solution)/shard_map/ppermute | solution.py:440
  8.1 14.5 %collective-permute-start.7 = (bf16[5,128,128]{2,1,0:T(8,128)(2,1)S(1)}, bf16[5,128,128]{2,1,0:T(8,128)(2,1)S(1)}, u32[]{:S(2)}, u32[]{:S(2)}) collective-permute-start(bf16[5,128,128]{2,1,0:T(8,128)(2,1)S(1)} %get-tuple-element.51), channel_id=1, source_target_pairs={{0,4},{4,0},{8,12},{12,8},{1,5},{5,1},{9,13},{13,9},{2,6},{6,2},{1... | collective-permute-start | bytes 491528 | tf_op jit(solution)/shard_map/ppermute | solution.py:440
  10.0 7.8 %collective-permute-start.6 = (bf16[64,1024]{1,0:T(8,128)(2,1)S(1)}, bf16[64,1024]{1,0:T(8,128)(2,1)S(1)}, u32[]{:S(2)}, u32[]{:S(2)}) collective-permute-start(bf16[64,1024]{1,0:T(8,128)(2,1)S(1)} %copy-done), channel_id=1, source_target_pairs={{0,2},{2,0},{1,3},{3,1},{4,6},{6,4},{5,7},{7,5},{8,10},{10,8},{9,1... | collective-permute-start | bytes 393224 | tf_op jit(solution)/shard_map/ppermute | solution.py:434
  13.3 9.2 %collective-permute-start.5 = (bf16[64,1024]{1,0:T(8,128)(2,1)S(1)}, bf16[64,1024]{1,0:T(8,128)(2,1)S(1)}, u32[]{:S(2)}, u32[]{:S(2)}) collective-permute-start(bf16[64,1024]{1,0:T(8,128)(2,1)S(1)} %collective-permute-done.4.refs_2_.refs_5_), channel_id=1, source_target_pairs={{0,4},{4,0},{8,12},{12,8},{1,5},{5,1},{9,13},{13,9},{2,6},{6,2},{1... | collective-permute-start | bytes 393224 | tf_op jit(solution)/shard_map/ppermute | solution.py:440
  13.3 15.1 %collective-permute-start.8 = (bf16[5,128,128]{2,1,0:T(8,128)(2,1)S(1)}, bf16[5,128,128]{2,1,0:T(8,128)(2,1)S(1)}, u32[]{:S(2)}, u32[]{:S(2)}) collective-permute-start(bf16[5,128,128]{2,1,0:T(8,128)(2,1)S(1)} %get-tuple-element.55), channel_id=1, source_target_pairs={{0,8},{4,12},{8,0},{12,4},{1,9},{5,13},{9,1},{13,5},{2,10},{6,14},... | collective-permute-start | bytes 491528 | tf_op jit(solution)/shard_map/ppermute | solution.py:440
  16.4 12.1 %collective-permute-start.9 = (bf16[5,128,128]{2,1,0:T(8,128)(2,1)S(1)}, bf16[5,128,128]{2,1,0:T(8,128)(2,1)S(1)}, u32[]{:S(2)}, u32[]{:S(2)}) collective-permute-start(bf16[5,128,128]{2,1,0:T(8,128)(2,1)S(1)} %get-tuple-element.56), channel_id=1, source_target_pairs={{0,12},{4,8},{8,4},{12,0},{1,13},{5,9},{9,5},{13,1},{2,14},{6,10},... | collective-permute-start | bytes 491528 | tf_op jit(solution)/shard_map/ppermute | solution.py:440
  22.6 16.6 %collective-permute-start.16 = (bf16[3,64,1024]{2,1,0:T(8,128)(2,1)S(1)}, bf16[3,64,1024]{2,1,0:T(8,128)(2,1)S(1)}, u32[]{:S(2)}, u32[]{:S(2)}) collective-permute-start(bf16[3,64,1024]{2,1,0:T(8,128)(2,1)S(1)} %shard_map.137), channel_id=1, source_target_pairs={{0,2},{2,0},{1,3},{3,1},{4,6},{6,4},{5,7},{7,5},{8,10},{10,8},{9,1... | collective-permute-start | bytes 1179656 | tf_op jit(solution)/shard_map/ppermute | solution.py:434
  28.5 6.0 %collective-permute-start.14 = (bf16[3,128,256]{2,1,0:T(8,128)(2,1)S(1)}, bf16[3,128,256]{2,1,0:T(8,128)(2,1)S(1)}, u32[]{:S(2)}, u32[]{:S(2)}) collective-permute-start(bf16[3,128,256]{2,1,0:T(8,128)(2,1)S(1)} %get-tuple-element.75.refs_0_), channel_id=1, source_target_pairs={{0,4},{4,0},{8,12},{12,8},{1,5},{5,1},{9,13},{13,9},{2,6},{6,2},{1... | collective-permute-start | bytes 589832 | tf_op jit(solution)/shard_map/ppermute | solution.py:440
  30.8 5.7 %collective-permute-start.13 = (bf16[3,128,256]{2,1,0:T(8,128)(2,1)S(1)}, bf16[3,128,256]{2,1,0:T(8,128)(2,1)S(1)}, u32[]{:S(2)}, u32[]{:S(2)}) collective-permute-start(bf16[3,128,256]{2,1,0:T(8,128)(2,1)S(1)} %get-tuple-element.75.refs_0_), channel_id=1, source_target_pairs={{0,16},{16,0},{1,17},{17,1},{2,18},{18,2},{3,19},{19,3},{4,20},{20... | collective-permute-start | bytes 589832 | tf_op jit(solution)/shard_map/ppermute | solution.py:437
  32.5 6.7 %collective-permute-start.17 = (bf16[3,128,128]{2,1,0:T(8,128)(2,1)S(1)}, bf16[3,128,128]{2,1,0:T(8,128)(2,1)S(1)}, u32[]{:S(2)}, u32[]{:S(2)}) collective-permute-start(bf16[3,128,128]{2,1,0:T(8,128)(2,1)S(1)} %slice.16), channel_id=1, source_target_pairs={{0,1},{1,0},{2,3},{3,2},{4,5},{5,4},{6,7},{7,6},{8,9},{9,8},{10,11... | collective-permute-start | bytes 294920 | tf_op jit(solution)/shard_map/ppermute | solution.py:431
  33.7 5.4 %collective-permute-start.18 = (bf16[3,128,128]{2,1,0:T(8,128)(2,1)S(1)}, bf16[3,128,128]{2,1,0:T(8,128)(2,1)S(1)}, u32[]{:S(2)}, u32[]{:S(2)}) collective-permute-start(bf16[3,128,128]{2,1,0:T(8,128)(2,1)S(1)} %slice.17), channel_id=1, source_target_pairs={{0,1},{1,0},{2,3},{3,2},{4,5},{5,4},{6,7},{7,6},{8,9},{9,8},{10,11... | collective-permute-start | bytes 294920 | tf_op jit(solution)/shard_map/ppermute | solution.py:431
  34.5 4.7 %collective-permute-start.19 = (bf16[3,128,128]{2,1,0:T(8,128)(2,1)S(1)}, bf16[3,128,128]{2,1,0:T(8,128)(2,1)S(1)}, u32[]{:S(2)}, u32[]{:S(2)}) collective-permute-start(bf16[3,128,128]{2,1,0:T(8,128)(2,1)S(1)} %slice.18), channel_id=1, source_target_pairs={{0,1},{1,0},{2,3},{3,2},{4,5},{5,4},{6,7},{7,6},{8,9},{9,8},{10,11... | collective-permute-start | bytes 294920 | tf_op jit(solution)/shard_map/ppermute | solution.py:431
  36.5 7.5 %collective-permute-start.10 = (bf16[3,128,256]{2,1,0:T(8,128)(2,1)S(1)}, bf16[3,128,256]{2,1,0:T(8,128)(2,1)S(1)}, u32[]{:S(2)}, u32[]{:S(2)}) collective-permute-start(bf16[3,128,256]{2,1,0:T(8,128)(2,1)S(1)} %get-tuple-element.75.refs_0_), channel_id=1, source_target_pairs={{0,12},{4,8},{8,4},{12,0},{1,13},{5,9},{9,5},{13,1},{2,14},{6,10},... | collective-permute-start | bytes 589832 | tf_op jit(solution)/shard_map/ppermute | solution.py:440
  41.8 6.3 %collective-permute-start.21 = (bf16[1088,128]{1,0:T(8,128)(2,1)S(1)}, bf16[1088,128]{1,0:T(8,128)(2,1)S(1)}, u32[]{:S(2)}, u32[]{:S(2)}) collective-permute-start(bf16[1088,128]{1,0:T(8,128)(2,1)S(1)} %get-tuple-element.65.own), channel_id=1, source_target_pairs={{0,1},{1,0},{2,3},{3,2},{4,5},{5,4},{6,7},{7,6},{8,9},{9,8},{10,11... | collective-permute-start | bytes 835592 | tf_op jit(solution)/shard_map/ppermute | solution.py:431
  41.9 12.9 %collective-permute-start.20 = (bf16[4,2,128,128]{3,2,1,0:T(8,128)(2,1)S(1)}, bf16[4,2,128,128]{3,2,1,0:T(8,128)(2,1)S(1)}, u32[]{:S(2)}, u32[]{:S(2)}) collective-permute-start(bf16[4,2,128,128]{3,2,1,0:T(8,128)(2,1)S(1)} %get-tuple-element.68.refs_0_), channel_id=1, source_target_pairs={{0,16},{16,0},{1,17},{17,1},{2,18},{18,2},{3,19},{19,3},{4,20},{20... | collective-permute-start | bytes 786440 | tf_op jit(solution)/shard_map/ppermute | solution.py:437
  43.5 11.4 %collective-permute-start.15 = (bf16[3,128,256]{2,1,0:T(8,128)(2,1)S(1)}, bf16[3,128,256]{2,1,0:T(8,128)(2,1)S(1)}, u32[]{:S(2)}, u32[]{:S(2)}) collective-permute-start(bf16[3,128,256]{2,1,0:T(8,128)(2,1)S(1)} %collective-permute-done.14.refs_1_), channel_id=1, source_target_pairs={{0,16},{16,0},{1,17},{17,1},{2,18},{18,2},{3,19},{19,3},{4,20},{20... | collective-permute-start | bytes 589832 | tf_op jit(solution)/shard_map/ppermute | solution.py:437
  44.0 10.8 %collective-permute-start.11 = (bf16[3,128,256]{2,1,0:T(8,128)(2,1)S(1)}, bf16[3,128,256]{2,1,0:T(8,128)(2,1)S(1)}, u32[]{:S(2)}, u32[]{:S(2)}) collective-permute-start(bf16[3,128,256]{2,1,0:T(8,128)(2,1)S(1)} %collective-permute-done.10.refs_3_), channel_id=1, source_target_pairs={{0,4},{4,0},{8,12},{12,8},{1,5},{5,1},{9,13},{13,9},{2,6},{6,2},{1... | collective-permute-start | bytes 589832 | tf_op jit(solution)/shard_map/ppermute | solution.py:440
  50.9 6.1 %collective-permute-start.22 = (bf16[144,128]{1,0:T(8,128)(2,1)S(1)}, bf16[144,128]{1,0:T(8,128)(2,1)S(1)}, u32[]{:S(2)}, u32[]{:S(2)}) collective-permute-start(bf16[144,128]{1,0:T(8,128)(2,1)S(1)} %get-tuple-element.66), channel_id=1, source_target_pairs={{0,8},{4,12},{8,0},{12,4},{1,9},{5,13},{9,1},{13,5},{2,10},{6,14},... | collective-permute-start | bytes 110600 | tf_op jit(solution)/shard_map/ppermute | solution.py:520
  52.1 5.8 %collective-permute-start.23 = (bf16[144,128]{1,0:T(8,128)(2,1)S(1)}, bf16[144,128]{1,0:T(8,128)(2,1)S(1)}, u32[]{:S(2)}, u32[]{:S(2)}) collective-permute-start(bf16[144,128]{1,0:T(8,128)(2,1)S(1)} %get-tuple-element.67), channel_id=1, source_target_pairs={{0,12},{4,8},{8,4},{12,0},{1,13},{5,9},{9,5},{13,1},{2,14},{6,10},... | collective-permute-start | bytes 110600 | tf_op jit(solution)/shard_map/ppermute | solution.py:520
  57.9 4.5 %collective-permute-start.24 = (bf16[4,2,128,128]{3,2,1,0:T(8,128)(2,1)S(1)}, bf16[4,2,128,128]{3,2,1,0:T(8,128)(2,1)S(1)}, u32[]{:S(2)}, u32[]{:S(2)}) collective-permute-start(bf16[4,2,128,128]{3,2,1,0:T(8,128)(2,1)S(1)} %get-tuple-element.68.refs_0_), channel_id=1, source_target_pairs={{0,1},{1,0},{2,3},{3,2},{4,5},{5,4},{6,7},{7,6},{8,9},{9,8},{10,11... | collective-permute-start | bytes 786440 | tf_op jit(solution)/shard_map/ppermute | solution.py:431
  57.9 4.5 %collective-permute-start.25 = (bf16[4,2,128,128]{3,2,1,0:T(8,128)(2,1)S(1)}, bf16[4,2,128,128]{3,2,1,0:T(8,128)(2,1)S(1)}, u32[]{:S(2)}, u32[]{:S(2)}) collective-permute-start(bf16[4,2,128,128]{3,2,1,0:T(8,128)(2,1)S(1)} %collective-permute-done.20.refs_2_), channel_id=1, source_target_pairs={{0,1},{1,0},{2,3},{3,2},{4,5},{5,4},{6,7},{7,6},{8,9},{9,8},{10,11... | collective-permute-start | bytes 786440 | tf_op jit(solution)/shard_map/ppermute | solution.py:431
  58.5 4.0 %collective-permute-start.26 = (bf16[144,128]{1,0:T(8,128)(2,1)S(1)}, bf16[144,128]{1,0:T(8,128)(2,1)S(1)}, u32[]{:S(2)}, u32[]{:S(2)}) collective-permute-start(bf16[144,128]{1,0:T(8,128)(2,1)S(1)} %get-tuple-element.71), channel_id=1, source_target_pairs={{0,4},{4,0},{8,12},{12,8},{1,5},{5,1},{9,13},{13,9},{2,6},{6,2},{1... | collective-permute-start | bytes 110600 | tf_op jit(solution)/shard_map/ppermute | solution.py:520
  62.9 11.3 %collective-permute-start.27 = (bf16[144,1024]{1,0:T(8,128)(2,1)S(1)}, bf16[144,1024]{1,0:T(8,128)(2,1)S(1)}, u32[]{:S(2)}, u32[]{:S(2)}) collective-permute-start(bf16[144,1024]{1,0:T(8,128)(2,1)S(1)} %get-tuple-element.74), channel_id=1, source_target_pairs={{0,2},{2,0},{1,3},{3,1},{4,6},{6,4},{5,7},{7,5},{8,10},{10,8},{9,1... | collective-permute-start | bytes 884744 | tf_op jit(solution)/shard_map/ppermute | solution.py:434
  64.5 7.5 %collective-permute-start.30 = (bf16[3,128,256]{2,1,0:T(8,128)(2,1)S(1)}, bf16[3,128,256]{2,1,0:T(8,128)(2,1)S(1)}, u32[]{:S(2)}, u32[]{:S(2)}) collective-permute-start(bf16[3,128,256]{2,1,0:T(8,128)(2,1)S(1)} %collective-permute-done.10.refs_3_), channel_id=1, source_target_pairs={{0,16},{16,0},{1,17},{17,1},{2,18},{18,2},{3,19},{19,3},{4,20},{20... | collective-permute-start | bytes 589832 | tf_op jit(solution)/shard_map/ppermute | solution.py:437
  66.0 8.1 %collective-permute-start.29 = (bf16[3,128,256]{2,1,0:T(8,128)(2,1)S(1)}, bf16[3,128,256]{2,1,0:T(8,128)(2,1)S(1)}, u32[]{:S(2)}, u32[]{:S(2)}) collective-permute-start(bf16[3,128,256]{2,1,0:T(8,128)(2,1)S(1)} %collective-permute-done.11.refs_2_), channel_id=1, source_target_pairs={{0,16},{16,0},{1,17},{17,1},{2,18},{18,2},{3,19},{19,3},{4,20},{20... | collective-permute-start | bytes 589832 | tf_op jit(solution)/shard_map/ppermute | solution.py:437
  74.2 3.6 %collective-permute-start.31 = (bf16[4,3,128,256]{3,2,1,0:T(8,128)(2,1)S(1)}, bf16[4,3,128,256]{3,2,1,0:T(8,128)(2,1)S(1)}, u32[]{:S(2)}, u32[]{:S(2)}) collective-permute-start(bf16[4,3,128,256]{3,2,1,0:T(8,128)(2,1)S(1)} %shard_map.142.refs_2_), channel_id=1, source_target_pairs={{0,1},{1,0},{2,3},{3,2},{4,5},{5,4},{6,7},{7,6},{8,9},{9,8},{10,11... | collective-permute-start | bytes 2359304 | tf_op jit(solution)/shard_map/ppermute | solution.py:431
  74.4 3.4 %collective-permute-start.28 = (bf16[4,3,128,256]{3,2,1,0:T(8,128)(2,1)S(1)}, bf16[4,3,128,256]{3,2,1,0:T(8,128)(2,1)S(1)}, u32[]{:S(2)}, u32[]{:S(2)}) collective-permute-start(bf16[4,3,128,256]{3,2,1,0:T(8,128)(2,1)S(1)} %shard_map.141.refs_0_), channel_id=1, source_target_pairs={{0,1},{1,0},{2,3},{3,2},{4,5},{5,4},{6,7},{7,6},{8,9},{9,8},{10,11... | collective-permute-start | bytes 2359304 | tf_op jit(solution)/shard_map/ppermute | solution.py:431
  79.1 5.6 %collective-permute-start.34 = (bf16[64,1024]{1,0:T(8,128)(2,1)S(1)}, bf16[64,1024]{1,0:T(8,128)(2,1)S(1)}, u32[]{:S(2)}, u32[]{:S(2)}) collective-permute-start(bf16[64,1024]{1,0:T(8,128)(2,1)S(1)} %get-tuple-element.86), channel_id=1, source_target_pairs={{0,2},{2,0},{1,3},{3,1},{4,6},{6,4},{5,7},{7,5},{8,10},{10,8},{9,1... | collective-permute-start | bytes 393224 | tf_op jit(solution)/shard_map/ppermute | solution.py:434
  (9 other events, 17.1 us)

commit v7 on v6

--- a/solution.py
+++ b/solution.py
@@ -166,7 +166,7 @@
     return [(i, i ^ k) for i in range(SEQ)]
 
 
-def call(kernel, outs, scratch, length, *operands, vmem=8, left=0):
+def call(kernel, outs, scratch, length, *operands, vmem=8, left=0, flops=0):
     fixed = [pltpu.with_memory_space_constraint(a, pltpu.HBM) for a in operands[:left]]
     return pl.pallas_call(
         kernel,
@@ -176,7 +176,7 @@
         + [pl.BlockSpec(memory_space=pltpu.VMEM)] * (len(operands) - left),
         out_specs=[pl.BlockSpec(memory_space=pltpu.VMEM)] * len(outs),
         scratch_shapes=scratch,
-        cost_estimate=pl.CostEstimate(flops=0, bytes_accessed=0, transcendentals=0),
+        cost_estimate=pl.CostEstimate(flops=flops, bytes_accessed=0, transcendentals=0),
         compiler_params=pltpu.CompilerParams(vmem_limit_bytes=vmem << 20),
     )(length, *fixed, *operands[left:])
 
@@ -194,18 +194,16 @@
 
 
 def deal_kernel(length, *refs):
-    sources, later, other = refs[:4], refs[4:7], refs[7:10]
-    outs, later_out, held, sems, later_sems = refs[10:14], *refs[14:]
+    sources, later, other = refs[:3], refs[3:6], refs[6:9]
+    outs, whole, part, held, sems, later_sems = refs[9:13], *refs[13:]
     s, _, f, p = here()
     half = outs[0].shape[1]
     copies = [pltpu.make_async_copy(w, held.at[i], sems.at[i]) for i, w in enumerate(sources)]
     at = pl.ds(aligned(p * half, half), half)
-    later_copies = [
-        pltpu.make_async_copy(w.at[at], later_out.at[i], later_sems.at[i]) for i, w in enumerate(later)
-    ]
+    later_copies = [pltpu.make_async_copy(w, whole.at[i], later_sems.at[0, i]) for i, w in enumerate(later)]
+    later_copies += [pltpu.make_async_copy(w.at[at], part.at[i], later_sems.at[1, i]) for i, w in enumerate(later)]
     for copy in copies + later_copies:
         copy.start()
-    mine, w_out = [held.at[m] for m in range(3)], held.at[3]
     for copy in copies:
         copy.wait()
     rows = pl.ds(aligned(f * half, half), half)
@@ -216,15 +214,13 @@
         @pl.when(head // 2 == f)
         def _():
             for m in range(3):
-                outs[k][m] = mine[m][rows, columns]
+                outs[k][m] = held[m, rows, columns]
 
         @pl.when(head // 2 != f)
         def _():
             for m in range(3):
                 outs[k][m] = other[m][rows, columns]
 
-        for m in range(outs[k].shape[0] - 3):
-            outs[k][3 + m] = w_out[at, m * HD : (m + 1) * HD]
     for copy in later_copies:
         copy.wait()
 
@@ -234,16 +230,10 @@
         refs[-1][k] = ref[...]
 
 
-def stack_kernel(length, *refs):
-    s = lax.axis_index("seq")
-    for k in range(SEQ):
-        refs[SEQ][s ^ k] = refs[k][...]
-
-
 def project_kernel(length, *refs):
     frames, gain, own_far, *near = refs[: SEQ + 2]
     far, mine, other = refs[SEQ + 2], refs[SEQ + 3 : 2 * SEQ + 3], refs[2 * SEQ + 3 : 3 * SEQ + 3]
-    q_out, send_out, edge_out, stack_out, normed, weights, x_edge, q_edge, own_x, own_gain, sems = refs[3 * SEQ + 3 :]
+    q_out, send_out, edge_out, normed, weights, x_edge, q_edge, own_x, own_gain, sems = refs[3 * SEQ + 3 :]
     copies = [
         pltpu.make_async_copy(frames, own_x, sems.at[0]),
         pltpu.make_async_copy(gain, own_gain, sems.at[1]),
@@ -270,7 +260,6 @@
             at = pl.ds(aligned((s ^ k) * 2 * half + (f ^ core) * half, half), half)
             for m in range(3):
                 weights[at, m * HD : (m + 1) * HD] = pieces[k][m]
-        stack_out[s ^ k] = mine[k][3:]
     count = 2 * SEQ
     total = count * rows
     projected = dot(normed[...], weights[...])
@@ -328,17 +317,15 @@
 
 
 def output_kernel(length, *refs):
-    pieces, ctx = refs[:4], refs[4 : 4 + SEQ]
-    share_out, send_out, context, weights = refs[4 + SEQ :]
+    pieces, ctx = refs[:2], refs[2 : 2 + SEQ]
+    share_out, send_out, context, weights = refs[2 + SEQ :]
     s, h, f, p = here()
-    half = pieces[0].shape[2]
     columns = weights.shape[2]
-    for y in range(2):
-        for core in range(2):
-            rows = pl.ds(aligned((f ^ core) * 2 * half + (p ^ y) * half, half), half)
-            for m in range(columns // HD):
-                for j in range(SEQ):
-                    weights[j, rows, m * HD : (m + 1) * HD] = pieces[y * 2 + core][j, m]
+    depth = columns
+    for core in range(2):
+        rows = pl.ds(aligned((f ^ core) * depth, depth), depth)
+        for k in range(SEQ):
+            weights[s ^ k, rows, :] = pieces[core][k]
     for k in range(SEQ):
         context[:, pl.ds(aligned((s ^ k) * HD, HD), HD)] = ctx[k][...]
     for j in range(SEQ):
@@ -349,23 +336,27 @@
 
 
 def convolve_kernel(length, *refs):
-    pieces = refs[:4]
-    own_x, peer_x, halo_x, own_share, peer_share, gain, own_c, peer_c, base_out, share_out = refs[4:14]
-    mid, normed, w_value, w_gate, w_down, channel, padded, active, shares = refs[14:]
+    near, far = refs[:4], refs[4:6]
+    own_x, peer_x, halo_x, own_share, peer_share, gain, own_c, peer_c, base_out, share_out = refs[6:16]
+    mid, normed, w_value, w_gate, w_down, channel, padded, active, shares = refs[16:]
     s, h, f, p = here()
     valid_len = length[0]
-    half, columns = pieces[0].shape[2:]
+    half, columns = far[0].shape[2:]
     rows = own_x.shape[0]
     step = rows + HALO
-    for y in range(2):
-        for core in range(2):
-            stack = pieces[y * 2 + core]
-            down = pl.ds(aligned((f ^ core) * 2 * half + (p ^ y) * half, half), half)
-            for plane in range(SEQ):
-                at = pl.ds(aligned(plane * 2 * half + (p ^ y) * half, half), half)
-                w_value[f ^ core, at, :] = stack[plane, 0]
-                w_gate[f ^ core, at, :] = stack[plane, 1]
-                w_down[plane, down, :] = stack[plane, 2]
+
+    def put(core, plane, first, count, block):
+        at = pl.ds(aligned(plane * 2 * half + first, half), count)
+        w_value[f ^ core, at, :] = block[0]
+        w_gate[f ^ core, at, :] = block[1]
+        w_down[plane, pl.ds(aligned((f ^ core) * 2 * half + first, half), count), :] = block[2]
+
+    for core in range(2):
+        for k in range(2):
+            put(core, s ^ k, 0, 2 * half, near[2 * k + core])
+        for y in range(2):
+            for i, k in enumerate((3, 2)):
+                put(core, s ^ k, (p ^ y) * half, half, far[core].at[2 * y + i])
     channel[f] = own_c[...]
     channel[1 - f] = peer_c[...]
     mid[pl.ds(aligned(h * step, 8), rows), :] = own_x[...].astype(F32)
@@ -440,51 +431,48 @@
         return lax.ppermute(x, "seq", xor_pairs(k))
 
     def planes(x):
-        far = across(x, 3)
-        return [x, across(x, 1), across(far, 1), far]
-
-    def part_half(x):
-        return lax.dynamic_slice_in_dim(x, p * half, half, axis=x.ndim - 2)
+        return [x] + [across(x, k) for k in range(1, SEQ)]
 
     near = planes(frames)
+    own_far = other_side(frames)
     given = [w_query, w_key, w_value]
     shape = jax.ShapeDtypeStruct
-    *dealt, pw_mine = call(
+    *dealt, pw_whole, pw_half = call(
         deal_kernel,
-        [shape((3 + columns // HD, half, HD), BF16)] * SEQ
-        + [shape((3, half, columns), BF16)],
+        [shape((3, half, HD), BF16)] * SEQ
+        + [shape((3, 2 * half, columns), BF16), shape((3, half, columns), BF16)],
         [
-            pltpu.VMEM((4, 2 * half, columns), BF16),
-            pltpu.SemaphoreType.DMA((4,)),
+            pltpu.VMEM((3, 2 * half, columns), BF16),
             pltpu.SemaphoreType.DMA((3,)),
+            pltpu.SemaphoreType.DMA((2, 3)),
         ],
         length,
         *given,
-        w_out,
         pw1_value,
         pw1_gate,
         pw2,
         *[other_core(w) for w in given],
-        left=7,
+        left=6,
     )
     *dealt, _ = barrier((*dealt, near[1]))
     w_mine = [dealt[0]] + [across(dealt[k], k) for k in range(1, SEQ)]
-    own_far = other_side(frames)
-    *near[1:], own_far, _ = barrier((*near[1:], own_far, w_mine[1]))
-    (joined,) = call(join_kernel, [shape((SEQ - 1, rows, width), BF16)], [], length, *near[1:])
-    far = other_side(joined)
-    w_other = [other_core(w[:3]) for w in w_mine]
-    after, *_ = barrier((pw_mine, joined, w_mine[2], w_mine[3]))
-    pw_part, pw_one, pw_three = other_part(after), across(after, 1), across(after, 3)
-    w_other[0], pw_part, pw_one = barrier((w_other[0], pw_part, pw_one))
-    pw_two, one_part, three_part = across(pw_three, 1), other_part(pw_one), other_part(pw_three)
-    queries, send, edges, stack = call(
+    *near[1:], own_far, _ = barrier((*near[1:], own_far, w_mine[3]))
+
+    def joined(*pieces, flops=0):
+        (stack,) = call(join_kernel, [shape((len(pieces), *pieces[0].shape), BF16)], [], length, *pieces, flops=flops)
+        return stack
+
+    far = other_side(joined(*near[1:]))
+    w_other = [other_core(w) for w in w_mine]
+    out_whole, *_ = barrier((w_out, *w_mine[1:]))
+    out_one, out_three = across(out_whole, 1), across(out_whole, 3)
+    out_two = across(out_three, 1)
+    queries, send, edges = call(
         project_kernel,
         [
             shape((count * rows, HD), BF16),
             shape((2 * count * rows + count * HALO, HD), BF16),
             shape((2 * HALO, width), BF16),
-            shape((SEQ, columns // HD, half, HD), BF16),
         ],
         [
             pltpu.VMEM((count * rows, width), BF16),
@@ -506,8 +494,8 @@
         left=2,
     )
     received = other_core(send)
-    queries, pw_three = barrier((queries, pw_three))
-    stack_part = other_part(stack)
+    later_whole, later_half, *_ = barrier((pw_whole, pw_half, send, out_one, out_three))
+    pw_one, pw_three = across(later_whole, 1), across(later_half, 3)
     ctx = call(
         attend_kernel,
         [shape((2 * step, HD), BF16)] * SEQ,
@@ -517,9 +505,13 @@
         send,
         received,
     )
+    out_two, *ctx = barrier((out_two, *ctx))
+    stack = joined(w_out, out_one, out_two, out_three)
+    stack, *ctx = barrier((stack, *ctx))
+    out_pieces = [stack, other_core(stack)]
     ctx = [ctx[0]] + [lax.ppermute(ctx[k], "seq", xor_pairs(k)) for k in range(1, SEQ)]
-    pw_two, one_part, stack, stack_part, *ctx[2:] = barrier((pw_two, one_part, stack, stack_part, *ctx[2:]))
-    out_pieces = [stack, other_core(stack), stack_part, other_core(stack_part)]
+    pw_one, pw_three, *ctx[1:] = barrier((pw_one, pw_three, *ctx[1:]))
+    pw_two, three_part = across(pw_three, 1), other_part(pw_three)
     own_share, sent_share = call(
         output_kernel,
         [shape((2 * step, width), F32), shape((2 * step, width), BF16)],
@@ -531,19 +523,14 @@
         *out_pieces,
         *ctx,
     )
-    own_share, edges, depth_kernel = barrier((own_share, edges, depth_kernel))
+    late = (own_share, edges, depth_kernel, pw_whole, pw_one, pw_two)
+    own_share, edges, depth_kernel, pw_whole, pw_one, pw_two = barrier(late)
     halo_x = other_core(edges)
     channels = jnp.concatenate([depth_kernel, bn_scale[None], bn_shift[None], jnp.zeros((5, columns), F32)])
     channels_peer = other_core(channels)
     peer_share = other_side(sent_share)
-
-    def stacked(*pieces):
-        (stack,) = call(stack_kernel, [shape((SEQ, *pieces[0].shape), BF16)], [], length, *pieces)
-        return [stack, other_core(stack)]
-
-    two_part = other_part(pw_two)
-    pw_mine, _ = barrier((pw_mine, peer_share))
-    pw_pieces = stacked(pw_mine, pw_one, pw_two, pw_three) + stacked(pw_part, one_part, two_part, three_part)
+    far_pieces = joined(pw_three, pw_two, three_part, other_part(pw_two), flops=10**10)
+    pw_pieces = [pw_whole, other_core(pw_whole), pw_one, other_core(pw_one), far_pieces, other_core(far_pieces)]
     base, share = call(
         convolve_kernel,
         [shape((rows, width), F32), shape((rows, width), BF16)],

time: 85.7 us -> 101 us (1.18)
  waiting for transfers between devices: 36.6 us -> 57.8 us
  starting transfers between devices: 37.6 us -> 31.5 us
    ppermute x9 -> x12, waiting for transfers between devices: 11.7 us -> 35.4 us  [across(): return lax.ppermute(x, 'seq', xor_pairs(k))]
    ppermute x5 -> x2, waiting for transfers between devices: 10.7 us -> 4.15 us  [other_part(): return lax.ppermute(x, 'parts', SWAP)]
    ppermute x4, waiting for transfers between devices: 5.01 us -> 9.98 us  [other_side(): return lax.ppermute(x, 'head', SWAP)]
    ppermute x5 -> x2, starting transfers between devices: 5.64 us -> 3.04 us  [other_part(): return lax.ppermute(x, 'parts', SWAP)]
    ppermute x4, starting transfers between devices: 5.08 us -> 2.72 us  [other_side(): return lax.ppermute(x, 'head', SWAP)]
    ppermute x3, waiting for transfers between devices: 6.91 us -> 4.77 us  [shards_chip_per_head(): lax.ppermute(ctx[k], 'seq', xor_pairs(k))]
    ppermute x14, waiting for transfers between devices: 2.2 us -> 3.48 us  [other_core(): return lax.ppermute(x, 'fsdp', SWAP)]
    ppermute x9 -> x12, starting transfers between devices: 20.5 us -> 19.9 us  [across(): return lax.ppermute(x, 'seq', xor_pairs(k))]
  transfers between devices with their start and end apart: 35 -> 35, of which waited for: 15 -> 18; matrix products, arithmetic and copies ran while one was open for 0% -> 0% of each run, Pallas kernels for 8% -> 5%
where the time goes in v7:
time: 101 us; the launch traced here: 100 us
  waiting for transfers between devices  57.8 us (57%)
  starting transfers between devices  31.5 us (31%)
  Pallas kernels  8.79 us (9%)
    ppermute x12, waiting for transfers between devices, across(): return lax.ppermute(x, 'seq', xor_pairs(k))  35.4 us
    ppermute x12, starting transfers between devices, across(): return lax.ppermute(x, 'seq', xor_pairs(k))  19.9 us
    ppermute x4, waiting for transfers between devices, other_side(): return lax.ppermute(x, 'head', SWAP)  9.98 us
    pallas_call x8, Pallas kernels, call(): pl.pallas_call(kernel, out_shape=outs, in_specs=[pl.BlockSpec(memory_spac...  8.79 us
    ppermute x3, waiting for transfers between devices, shards_chip_per_head(): lax.ppermute(ctx[k], 'seq', xor_pairs(k))  4.77 us
    ppermute x2, waiting for transfers between devices, other_part(): return lax.ppermute(x, 'parts', SWAP)  4.15 us
    ppermute x14, waiting for transfers between devices, other_core(): return lax.ppermute(x, 'fsdp', SWAP)  3.48 us
    ppermute x2, starting transfers between devices, other_part(): return lax.ppermute(x, 'parts', SWAP)  3.04 us
  transfers between devices with their start and end apart: 35, of which 18 were waited for; matrix products, arithmetic and copies ran while one was open for 0% of the time, Pallas kernels for 5%

profile of v7, /device:TPU:0, one launch (start us, length us, event | category | flops | bytes accessed | tf_op | source)
XLA Modules:
  0.0 100.4 jit_solution(8966825676371662907)
XLA Ops:
  1.0 2.6 %collective-permute-start.3 = (bf16[64,1024]{1,0:T(8,128)(2,1)}, bf16[64,1024]{1,0:T(8,128)(2,1)S(1)}, u32[]{:S(2)}, u32[]{:S(2)}) collective-permute-start(bf16[64,1024]{1,0:T(8,128)(2,1)} %refs_6_.1), channel_id=1, source_target_pairs={{0,4},{4,0},{8,12},{12,8},{1,5},{5,1},{9,13},{13,9},{2,6},{6,2},{1... | collective-permute-start | bytes 393224 | tf_op jit(solution)/shard_map/ppermute | solution.py:431
  3.5 1.5 %collective-permute-start.12 = (bf16[64,1024]{1,0:T(8,128)(2,1)}, bf16[64,1024]{1,0:T(8,128)(2,1)S(1)}, u32[]{:S(2)}, u32[]{:S(2)}) collective-permute-start(bf16[64,1024]{1,0:T(8,128)(2,1)} %refs_6_.1), channel_id=1, source_target_pairs={{0,2},{2,0},{1,3},{3,1},{4,6},{6,4},{5,7},{7,5},{8,10},{10,8},{9,1... | collective-permute-start | bytes 393224 | tf_op jit(solution)/shard_map/ppermute | solution.py:425
  5.0 2.5 %collective-permute-start.11 = (bf16[64,1024]{1,0:T(8,128)(2,1)}, bf16[64,1024]{1,0:T(8,128)(2,1)S(1)}, u32[]{:S(2)}, u32[]{:S(2)}) collective-permute-start(bf16[64,1024]{1,0:T(8,128)(2,1)} %refs_6_.1), channel_id=1, source_target_pairs={{0,12},{4,8},{8,4},{12,0},{1,13},{5,9},{9,5},{13,1},{2,14},{6,10},... | collective-permute-start | bytes 393224 | tf_op jit(solution)/shard_map/ppermute | solution.py:431
  8.4 1.5 %shard_map.136 = (bf16[3,128,128]{2,1,0:T(8,128)(2,1)S(1)}, bf16[3,128,128]{2,1,0:T(8,128)(2,1)S(1)}, bf16[3,128,128]{2,1,0:T(8,128)(2,1)S(1)}, bf16[3,128,128]{...) custom-call(s32[1]{0:T(128)S(6)} %copy.15.length, bf16[256,256]{1,0:T(8,128)(2,1)} %refs_0_.3, ...), custom_call_target="tpu_custom_call" | custom-call | tf_op jit(solution)/shard_map/pallas_call | solution.py:171
  9.8 2.9 %collective-permute-start.6 = (bf16[3,128,128]{2,1,0:T(8,128)(2,1)S(1)}, bf16[3,128,128]{2,1,0:T(8,128)(2,1)S(1)}, u32[]{:S(2)}, u32[]{:S(2)}) collective-permute-start(bf16[3,128,128]{2,1,0:T(8,128)(2,1)S(1)} %get-tuple-element.60), channel_id=1, source_target_pairs={{0,12},{4,8},{8,4},{12,0},{1,13},{5,9},{9,5},{13,1},{2,14},{6,10},... | collective-permute-start | bytes 294920 | tf_op jit(solution)/shard_map/ppermute | solution.py:431
  12.8 0.8 collective-permute-done.11.refs_2_.refs_5_
  13.6 9.1 %collective-permute-done.10.refs_1_.refs_4_ = bf16[64,1024]{1,0:T(8,128)(2,1)S(1)} collective-permute-done((bf16[64,1024]{1,0:T(8,128)(2,1)}, bf16[64,1024]{1,0:T(8,128)(2,1)S(1)}, u32[]{:S(2)}, u32[]{:S(2)}) %collective-permute-start.10) | collective-permute-done | bytes 131104 | tf_op jit(solution)/shard_map/ppermute | solution.py:431
  23.1 2.2 %collective-permute-start.4 = (bf16[3,128,128]{2,1,0:T(8,128)(2,1)S(1)}, bf16[3,128,128]{2,1,0:T(8,128)(2,1)S(1)}, u32[]{:S(2)}, u32[]{:S(2)}) collective-permute-start(bf16[3,128,128]{2,1,0:T(8,128)(2,1)S(1)} %get-tuple-element.58), channel_id=1, source_target_pairs={{0,4},{4,0},{8,12},{12,8},{1,5},{5,1},{9,13},{13,9},{2,6},{6,2},{1... | collective-permute-start | bytes 294920 | tf_op jit(solution)/shard_map/ppermute | solution.py:431
  25.3 1.5 %collective-permute-start.5 = (bf16[3,128,128]{2,1,0:T(8,128)(2,1)S(1)}, bf16[3,128,128]{2,1,0:T(8,128)(2,1)S(1)}, u32[]{:S(2)}, u32[]{:S(2)}) collective-permute-start(bf16[3,128,128]{2,1,0:T(8,128)(2,1)S(1)} %get-tuple-element.59), channel_id=1, source_target_pairs={{0,8},{4,12},{8,0},{12,4},{1,9},{5,13},{9,1},{13,5},{2,10},{6,14},... | collective-permute-start | bytes 294920 | tf_op jit(solution)/shard_map/ppermute | solution.py:431
  26.8 1.1 %collective-permute-done.4.refs_8_ = bf16[3,128,128]{2,1,0:T(8,128)(2,1)S(1)} collective-permute-done((bf16[3,128,128]{2,1,0:T(8,128)(2,1)S(1)}, bf16[3,128,128]{2,1,0:T(8,128)(2,1)S(1)}, u32[]{:S(2)}, u32[]{:S(2)}) %collective-permute-start.4) | collective-permute-done | bytes 98336 | tf_op jit(solution)/shard_map/ppermute | solution.py:431
  27.9 4.2 %collective-permute-done.5.refs_9_ = bf16[3,128,128]{2,1,0:T(8,128)(2,1)S(1)} collective-permute-done((bf16[3,128,128]{2,1,0:T(8,128)(2,1)S(1)}, bf16[3,128,128]{2,1,0:T(8,128)(2,1)S(1)}, u32[]{:S(2)}, u32[]{:S(2)}) %collective-permute-start.5) | collective-permute-done | bytes 98336 | tf_op jit(solution)/shard_map/ppermute | solution.py:431
  32.6 0.8 collective-permute-done.16.refs_13_
  33.5 2.6 %shard_map.138 = (bf16[512,128]{1,0:T(8,128)(2,1)S(1)}, bf16[1088,128]{1,0:T(8,128)(2,1)S(1)}, bf16[16,1024]{1,0:T(8,128)(2,1)S(1)}) custom-call(s32[1]{0:T(128)S(6)} %copy.15.length, bf16[64,1024]{1,0:T(8,128)(2,1)} %refs_6_.1, f32[1,1024]{1,0:T(1,128)} %bitcast.5, bf16[64,1024]{1,0:T(8,128)(2,1)S(1)} %collective-permute-done.12.refs_2_.refs_7_, ...), custom_call_target="tpu_custom_call" | custom-call | tf_op jit(solution)/shard_map/pallas_call | solution.py:171
  36.6 2.2 %collective-permute-start.8 = (bf16[256,256]{1,0:T(8,128)(2,1)S(1)}, bf16[256,256]{1,0:T(8,128)(2,1)S(1)}, u32[]{:S(2)}, u32[]{:S(2)}) collective-permute-start(bf16[256,256]{1,0:T(8,128)(2,1)S(1)} %copy-done.1), channel_id=1, source_target_pairs={{0,12},{4,8},{8,4},{12,0},{1,13},{5,9},{9,5},{13,1},{2,14},{6,10},... | collective-permute-start | bytes 393224 | tf_op jit(solution)/shard_map/ppermute | solution.py:431
  38.8 0.7 collective-permute-start.7
  39.5 5.3 %collective-permute-done.8.refs_3_ = bf16[256,256]{1,0:T(8,128)(2,1)S(1)} collective-permute-done((bf16[256,256]{1,0:T(8,128)(2,1)S(1)}, bf16[256,256]{1,0:T(8,128)(2,1)S(1)}, u32[]{:S(2)}, u32[]{:S(2)}) %collective-permute-start.8) | collective-permute-done | bytes 131104 | tf_op jit(solution)/shard_map/ppermute | solution.py:431
  44.8 1.9 %collective-permute-start.9 = (bf16[256,256]{1,0:T(8,128)(2,1)S(1)}, bf16[256,256]{1,0:T(8,128)(2,1)S(1)}, u32[]{:S(2)}, u32[]{:S(2)}) collective-permute-start(bf16[256,256]{1,0:T(8,128)(2,1)S(1)} %collective-permute-done.8.refs_3_), channel_id=1, source_target_pairs={{0,4},{4,0},{8,12},{12,8},{1,5},{5,1},{9,13},{13,9},{2,6},{6,2},{1... | collective-permute-start | bytes 393224 | tf_op jit(solution)/shard_map/ppermute | solution.py:431
  47.2 2.8 %shard_map.139 = (bf16[144,128]{1,0:T(8,128)(2,1)S(1)}, bf16[144,128]{1,0:T(8,128)(2,1)S(1)}, bf16[144,128]{1,0:T(8,128)(2,1)S(1)}, bf16[144,128]{1,0:T(8,128)(2,1)S(1)}) custom-call(s32[1]{0:T(128)S(6)} %copy.15.length, bf16[512,128]{1,0:T(8,128)(2,1)S(1)} %get-tuple-element.67.q_in, bf16[1088,128]{1,0:T(8,128)(2,1)S(1)} %get-tuple-element.68.own, ...), custom_call_target="tpu_custom_call" | custom-call | tf_op jit(solution)/shard_map/pallas_call | solution.py:171
  50.7 2.9 %collective-permute-start.21 = (bf16[3,128,256]{2,1,0:T(8,128)(2,1)S(1)}, bf16[3,128,256]{2,1,0:T(8,128)(2,1)S(1)}, u32[]{:S(2)}, u32[]{:S(2)}) collective-permute-start(bf16[3,128,256]{2,1,0:T(8,128)(2,1)S(1)} %get-tuple-element.83), channel_id=1, source_target_pairs={{0,12},{4,8},{8,4},{12,0},{1,13},{5,9},{9,5},{13,1},{2,14},{6,10},... | collective-permute-start | bytes 589832 | tf_op jit(solution)/shard_map/ppermute | solution.py:431
  53.6 1.2 %collective-permute-start.22 = (bf16[144,128]{1,0:T(8,128)(2,1)S(1)}, bf16[144,128]{1,0:T(8,128)(2,1)S(1)}, u32[]{:S(2)}, u32[]{:S(2)}) collective-permute-start(bf16[144,128]{1,0:T(8,128)(2,1)S(1)} %get-tuple-element.84), channel_id=1, source_target_pairs={{0,4},{4,0},{8,12},{12,8},{1,5},{5,1},{9,13},{13,9},{2,6},{6,2},{1... | collective-permute-start | bytes 110600 | tf_op jit(solution)/shard_map/ppermute | solution.py:512
  55.1 10.5 %collective-permute-done.21.refs_0_ = bf16[3,128,256]{2,1,0:T(8,128)(2,1)S(1)} collective-permute-done((bf16[3,128,256]{2,1,0:T(8,128)(2,1)S(1)}, bf16[3,128,256]{2,1,0:T(8,128)(2,1)S(1)}, u32[]{:S(2)}, u32[]{:S(2)}) %collective-permute-start.21) | collective-permute-done | bytes 196640 | tf_op jit(solution)/shard_map/ppermute | solution.py:431
  65.6 1.3 %collective-permute-start.24 = (bf16[144,128]{1,0:T(8,128)(2,1)S(1)}, bf16[144,128]{1,0:T(8,128)(2,1)S(1)}, u32[]{:S(2)}, u32[]{:S(2)}) collective-permute-start(bf16[144,128]{1,0:T(8,128)(2,1)S(1)} %get-tuple-element.86), channel_id=1, source_target_pairs={{0,12},{4,8},{8,4},{12,0},{1,13},{5,9},{9,5},{13,1},{2,14},{6,10},... | collective-permute-start | bytes 110600 | tf_op jit(solution)/shard_map/ppermute | solution.py:512
  67.0 4.8 %collective-permute-done.24.refs_5_ = bf16[144,128]{1,0:T(8,128)(2,1)S(1)} collective-permute-done((bf16[144,128]{1,0:T(8,128)(2,1)S(1)}, bf16[144,128]{1,0:T(8,128)(2,1)S(1)}, u32[]{:S(2)}, u32[]{:S(2)}) %collective-permute-start.24) | collective-permute-done | bytes 36896 | tf_op jit(solution)/shard_map/ppermute | solution.py:512
  71.7 1.5 %collective-permute-start.28 = (bf16[3,128,256]{2,1,0:T(8,128)(2,1)S(1)}, bf16[3,128,256]{2,1,0:T(8,128)(2,1)S(1)}, u32[]{:S(2)}, u32[]{:S(2)}) collective-permute-start(bf16[3,128,256]{2,1,0:T(8,128)(2,1)S(1)} %collective-permute-done.21.refs_0_), channel_id=1, source_target_pairs={{0,16},{16,0},{1,17},{17,1},{2,18},{18,2},{3,19},{19,3},{4,20},{20... | collective-permute-start | bytes 589832 | tf_op jit(solution)/shard_map/ppermute | solution.py:428
  73.7 3.7 %collective-permute-done.25.refs_1_ = bf16[3,128,256]{2,1,0:T(8,128)(2,1)S(1)} collective-permute-done((bf16[3,128,256]{2,1,0:T(8,128)(2,1)S(1)}, bf16[3,128,256]{2,1,0:T(8,128)(2,1)S(1)}, u32[]{:S(2)}, u32[]{:S(2)}) %collective-permute-start.25) | collective-permute-done | bytes 196640 | tf_op jit(solution)/shard_map/ppermute | solution.py:431
  77.4 1.5 %collective-permute-start.29 = (bf16[3,128,256]{2,1,0:T(8,128)(2,1)S(1)}, bf16[3,128,256]{2,1,0:T(8,128)(2,1)S(1)}, u32[]{:S(2)}, u32[]{:S(2)}) collective-permute-start(bf16[3,128,256]{2,1,0:T(8,128)(2,1)S(1)} %collective-permute-done.25.refs_1_), channel_id=1, source_target_pairs={{0,16},{16,0},{1,17},{17,1},{2,18},{18,2},{3,19},{19,3},{4,20},{20... | collective-permute-start | bytes 589832 | tf_op jit(solution)/shard_map/ppermute | solution.py:428
  79.2 3.9 %collective-permute-done.29.refs_3_ = bf16[3,128,256]{2,1,0:T(8,128)(2,1)S(1)} collective-permute-done((bf16[3,128,256]{2,1,0:T(8,128)(2,1)S(1)}, bf16[3,128,256]{2,1,0:T(8,128)(2,1)S(1)}, u32[]{:S(2)}, u32[]{:S(2)}) %collective-permute-start.29) | collective-permute-done | bytes 196640 | tf_op jit(solution)/shard_map/ppermute | solution.py:428
  85.2 1.4 %collective-permute-done.33.refs_13_ = f32[16,256]{1,0:T(8,128)S(1)} collective-permute-done((f32[16,256]{1,0:T(8,128)S(1)}, f32[16,256]{1,0:T(8,128)S(1)}, u32[]{:S(2)}, u32[]{:S(2)}) %collective-permute-start.33) | collective-permute-done | bytes 16416 | tf_op jit(solution)/shard_map/ppermute | solution.py:422
  86.8 1.1 %collective-permute-done.31.refs_8_ = bf16[16,1024]{1,0:T(8,128)(2,1)S(1)} collective-permute-done((bf16[16,1024]{1,0:T(8,128)(2,1)S(1)}, bf16[16,1024]{1,0:T(8,128)(2,1)S(1)}, u32[]{:S(2)}, u32[]{:S(2)}) %collective-permute-start.31) | collective-permute-done | bytes 32800 | tf_op jit(solution)/shard_map/ppermute | solution.py:422
  87.8 5.3 %collective-permute-done.32.refs_10_ = bf16[144,1024]{1,0:T(8,128)(2,1)S(1)} collective-permute-done((bf16[144,1024]{1,0:T(8,128)(2,1)S(1)}, bf16[144,1024]{1,0:T(8,128)(2,1)S(1)}, u32[]{:S(2)}, u32[]{:S(2)}) %collective-permute-start.32) | collective-permute-done | bytes 294944 | tf_op jit(solution)/shard_map/ppermute | solution.py:425
  93.2 1.4 %shard_map.143 = (f32[64,1024]{1,0:T(8,128)S(1)}, bf16[64,1024]{1,0:T(8,128)(2,1)S(1)}) custom-call(s32[1]{0:T(128)S(6)} %copy.15.length, bf16[3,256,256]{2,1,0:T(8,128)(2,1)S(1)} %get-tuple-element.94.refs_0_, bf16[3,256,256]{2,1,0:T(8,128)(2,1)S(1)} %collective-permute-done.26.refs_1_, bf16[3,256,256]{2,1,0:T(8,128)(2,1)S(1)} %collective-permute-done.20.refs_2_, ...), custom_call_target="tpu_custom_call" | custom-call | tf_op jit(solution)/shard_map/pallas_call | solution.py:171
  95.0 4.7 %collective-permute-done.34 = bf16[64,1024]{1,0:T(8,128)(2,1)S(1)} collective-permute-done((bf16[64,1024]{1,0:T(8,128)(2,1)S(1)}, bf16[64,1024]{1,0:T(8,128)(2,1)S(1)}, u32[]{:S(2)}, u32[]{:S(2)}) %collective-permute-start.34) | collective-permute-done | bytes 131104 | tf_op jit(solution)/shard_map/ppermute | solution.py:425
  (62 shorter events, 8.4 us)
Async XLA Ops:
  0.0 5.0 %collective-permute-start = (bf16[256,256]{1,0:T(8,128)(2,1)}, bf16[256,256]{1,0:T(8,128)(2,1)S(1)}, u32[]{:S(2)}, u32[]{:S(2)}) collective-permute-start(bf16[256,256]{1,0:T(8,128)(2,1)} %refs_0_.3), channel_id=1, source_target_pairs={{0,1},{1,0},{2,3},{3,2},{4,5},{5,4},{6,7},{7,6},{8,9},{9,8},{10,11... | collective-permute-start | bytes 393224 | tf_op jit(solution)/shard_map/ppermute | solution.py:422
  0.5 7.1 %collective-permute-start.1 = (bf16[256,256]{1,0:T(8,128)(2,1)}, bf16[256,256]{1,0:T(8,128)(2,1)S(1)}, u32[]{:S(2)}, u32[]{:S(2)}) collective-permute-start(bf16[256,256]{1,0:T(8,128)(2,1)} %refs_1_.1), channel_id=1, source_target_pairs={{0,1},{1,0},{2,3},{3,2},{4,5},{5,4},{6,7},{7,6},{8,9},{9,8},{10,11... | collective-permute-start | bytes 393224 | tf_op jit(solution)/shard_map/ppermute | solution.py:422
  0.5 7.8 %collective-permute-start.2 = (bf16[256,256]{1,0:T(8,128)(2,1)}, bf16[256,256]{1,0:T(8,128)(2,1)S(1)}, u32[]{:S(2)}, u32[]{:S(2)}) collective-permute-start(bf16[256,256]{1,0:T(8,128)(2,1)} %refs_2_.1), channel_id=1, source_target_pairs={{0,1},{1,0},{2,3},{3,2},{4,5},{5,4},{6,7},{7,6},{8,9},{9,8},{10,11... | collective-permute-start | bytes 393224 | tf_op jit(solution)/shard_map/ppermute | solution.py:422
  1.0 8.9 %collective-permute-start.3 = (bf16[64,1024]{1,0:T(8,128)(2,1)}, bf16[64,1024]{1,0:T(8,128)(2,1)S(1)}, u32[]{:S(2)}, u32[]{:S(2)}) collective-permute-start(bf16[64,1024]{1,0:T(8,128)(2,1)} %refs_6_.1), channel_id=1, source_target_pairs={{0,4},{4,0},{8,12},{12,8},{1,5},{5,1},{9,13},{13,9},{2,6},{6,2},{1... | collective-permute-start | bytes 393224 | tf_op jit(solution)/shard_map/ppermute | solution.py:431
  3.5 9.2 %collective-permute-start.12 = (bf16[64,1024]{1,0:T(8,128)(2,1)}, bf16[64,1024]{1,0:T(8,128)(2,1)S(1)}, u32[]{:S(2)}, u32[]{:S(2)}) collective-permute-start(bf16[64,1024]{1,0:T(8,128)(2,1)} %refs_6_.1), channel_id=1, source_target_pairs={{0,2},{2,0},{1,3},{3,1},{4,6},{6,4},{5,7},{7,5},{8,10},{10,8},{9,1... | collective-permute-start | bytes 393224 | tf_op jit(solution)/shard_map/ppermute | solution.py:425
  5.0 8.5 %collective-permute-start.11 = (bf16[64,1024]{1,0:T(8,128)(2,1)}, bf16[64,1024]{1,0:T(8,128)(2,1)S(1)}, u32[]{:S(2)}, u32[]{:S(2)}) collective-permute-start(bf16[64,1024]{1,0:T(8,128)(2,1)} %refs_6_.1), channel_id=1, source_target_pairs={{0,12},{4,8},{8,4},{12,0},{1,13},{5,9},{9,5},{13,1},{2,14},{6,10},... | collective-permute-start | bytes 393224 | tf_op jit(solution)/shard_map/ppermute | solution.py:431
  7.5 15.2 %collective-permute-start.10 = (bf16[64,1024]{1,0:T(8,128)(2,1)}, bf16[64,1024]{1,0:T(8,128)(2,1)S(1)}, u32[]{:S(2)}, u32[]{:S(2)}) collective-permute-start(bf16[64,1024]{1,0:T(8,128)(2,1)} %refs_6_.1), channel_id=1, source_target_pairs={{0,8},{4,12},{8,0},{12,4},{1,9},{5,13},{9,1},{13,5},{2,10},{6,14},... | collective-permute-start | bytes 393224 | tf_op jit(solution)/shard_map/ppermute | solution.py:431
  9.8 12.9 %collective-permute-start.6 = (bf16[3,128,128]{2,1,0:T(8,128)(2,1)S(1)}, bf16[3,128,128]{2,1,0:T(8,128)(2,1)S(1)}, u32[]{:S(2)}, u32[]{:S(2)}) collective-permute-start(bf16[3,128,128]{2,1,0:T(8,128)(2,1)S(1)} %get-tuple-element.60), channel_id=1, source_target_pairs={{0,12},{4,8},{8,4},{12,0},{1,13},{5,9},{9,5},{13,1},{2,14},{6,10},... | collective-permute-start | bytes 294920 | tf_op jit(solution)/shard_map/ppermute | solution.py:431
  22.7 10.8 %collective-permute-start.13 = (bf16[3,64,1024]{2,1,0:T(8,128)(2,1)S(1)}, bf16[3,64,1024]{2,1,0:T(8,128)(2,1)S(1)}, u32[]{:S(2)}, u32[]{:S(2)}) collective-permute-start(bf16[3,64,1024]{2,1,0:T(8,128)(2,1)S(1)} %shard_map.137), channel_id=1, source_target_pairs={{0,2},{2,0},{1,3},{3,1},{4,6},{6,4},{5,7},{7,5},{8,10},{10,8},{9,1... | collective-permute-start | bytes 1179656 | tf_op jit(solution)/shard_map/ppermute | solution.py:425
  23.1 4.8 %collective-permute-start.4 = (bf16[3,128,128]{2,1,0:T(8,128)(2,1)S(1)}, bf16[3,128,128]{2,1,0:T(8,128)(2,1)S(1)}, u32[]{:S(2)}, u32[]{:S(2)}) collective-permute-start(bf16[3,128,128]{2,1,0:T(8,128)(2,1)S(1)} %get-tuple-element.58), channel_id=1, source_target_pairs={{0,4},{4,0},{8,12},{12,8},{1,5},{5,1},{9,13},{13,9},{2,6},{6,2},{1... | collective-permute-start | bytes 294920 | tf_op jit(solution)/shard_map/ppermute | solution.py:431
  25.3 6.8 %collective-permute-start.5 = (bf16[3,128,128]{2,1,0:T(8,128)(2,1)S(1)}, bf16[3,128,128]{2,1,0:T(8,128)(2,1)S(1)}, u32[]{:S(2)}, u32[]{:S(2)}) collective-permute-start(bf16[3,128,128]{2,1,0:T(8,128)(2,1)S(1)} %get-tuple-element.59), channel_id=1, source_target_pairs={{0,8},{4,12},{8,0},{12,4},{1,9},{5,13},{9,1},{13,5},{2,10},{6,14},... | collective-permute-start | bytes 294920 | tf_op jit(solution)/shard_map/ppermute | solution.py:431
  26.8 5.8 %collective-permute-start.14 = (bf16[3,128,128]{2,1,0:T(8,128)(2,1)S(1)}, bf16[3,128,128]{2,1,0:T(8,128)(2,1)S(1)}, u32[]{:S(2)}, u32[]{:S(2)}) collective-permute-start(bf16[3,128,128]{2,1,0:T(8,128)(2,1)S(1)} %get-tuple-element.66.refs_7_), channel_id=1, source_target_pairs={{0,1},{1,0},{2,3},{3,2},{4,5},{5,4},{6,7},{7,6},{8,9},{9,8},{10,11... | collective-permute-start | bytes 294920 | tf_op jit(solution)/shard_map/ppermute | solution.py:422
  27.9 4.7 %collective-permute-start.15 = (bf16[3,128,128]{2,1,0:T(8,128)(2,1)S(1)}, bf16[3,128,128]{2,1,0:T(8,128)(2,1)S(1)}, u32[]{:S(2)}, u32[]{:S(2)}) collective-permute-start(bf16[3,128,128]{2,1,0:T(8,128)(2,1)S(1)} %collective-permute-done.4.refs_8_), channel_id=1, source_target_pairs={{0,1},{1,0},{2,3},{3,2},{4,5},{5,4},{6,7},{7,6},{8,9},{9,8},{10,11... | collective-permute-start | bytes 294920 | tf_op jit(solution)/shard_map/ppermute | solution.py:422
  36.2 11.1 %collective-permute-start.18 = (bf16[1088,128]{1,0:T(8,128)(2,1)S(1)}, bf16[1088,128]{1,0:T(8,128)(2,1)S(1)}, u32[]{:S(2)}, u32[]{:S(2)}) collective-permute-start(bf16[1088,128]{1,0:T(8,128)(2,1)S(1)} %get-tuple-element.68.own), channel_id=1, source_target_pairs={{0,1},{1,0},{2,3},{3,2},{4,5},{5,4},{6,7},{7,6},{8,9},{9,8},{10,11... | collective-permute-start | bytes 835592 | tf_op jit(solution)/shard_map/ppermute | solution.py:422
  36.6 8.2 %collective-permute-start.8 = (bf16[256,256]{1,0:T(8,128)(2,1)S(1)}, bf16[256,256]{1,0:T(8,128)(2,1)S(1)}, u32[]{:S(2)}, u32[]{:S(2)}) collective-permute-start(bf16[256,256]{1,0:T(8,128)(2,1)S(1)} %copy-done.1), channel_id=1, source_target_pairs={{0,12},{4,8},{8,4},{12,0},{1,13},{5,9},{9,5},{13,1},{2,14},{6,10},... | collective-permute-start | bytes 393224 | tf_op jit(solution)/shard_map/ppermute | solution.py:431
  38.8 8.0 %collective-permute-start.7 = (bf16[256,256]{1,0:T(8,128)(2,1)S(1)}, bf16[256,256]{1,0:T(8,128)(2,1)S(1)}, u32[]{:S(2)}, u32[]{:S(2)}) collective-permute-start(bf16[256,256]{1,0:T(8,128)(2,1)S(1)} %copy-done.1), channel_id=1, source_target_pairs={{0,4},{4,0},{8,12},{12,8},{1,5},{5,1},{9,13},{13,9},{2,6},{6,2},{1... | collective-permute-start | bytes 393224 | tf_op jit(solution)/shard_map/ppermute | solution.py:431
  44.8 5.8 %collective-permute-start.9 = (bf16[256,256]{1,0:T(8,128)(2,1)S(1)}, bf16[256,256]{1,0:T(8,128)(2,1)S(1)}, u32[]{:S(2)}, u32[]{:S(2)}) collective-permute-start(bf16[256,256]{1,0:T(8,128)(2,1)S(1)} %collective-permute-done.8.refs_3_), channel_id=1, source_target_pairs={{0,4},{4,0},{8,12},{12,8},{1,5},{5,1},{9,13},{13,9},{2,6},{6,2},{1... | collective-permute-start | bytes 393224 | tf_op jit(solution)/shard_map/ppermute | solution.py:431
  46.8 24.9 %collective-permute-start.20 = (bf16[3,256,256]{2,1,0:T(8,128)(2,1)S(1)}, bf16[3,256,256]{2,1,0:T(8,128)(2,1)S(1)}, u32[]{:S(2)}, u32[]{:S(2)}) collective-permute-start(bf16[3,256,256]{2,1,0:T(8,128)(2,1)S(1)} %get-tuple-element.94.refs_0_), channel_id=1, source_target_pairs={{0,4},{4,0},{8,12},{12,8},{1,5},{5,1},{9,13},{13,9},{2,6},{6,2},{1... | collective-permute-start | bytes 1179656 | tf_op jit(solution)/shard_map/ppermute | solution.py:431
  50.6 22.7 %collective-permute-start.19 = (bf16[4,256,256]{2,1,0:T(8,128)(2,1)S(1)}, bf16[4,256,256]{2,1,0:T(8,128)(2,1)S(1)}, u32[]{:S(2)}, u32[]{:S(2)}) collective-permute-start(bf16[4,256,256]{2,1,0:T(8,128)(2,1)S(1)} %shard_map.140.refs_0_), channel_id=1, source_target_pairs={{0,1},{1,0},{2,3},{3,2},{4,5},{5,4},{6,7},{7,6},{8,9},{9,8},{10,11... | collective-permute-start | bytes 1572872 | tf_op jit(solution)/shard_map/ppermute | solution.py:422
  50.7 15.0 %collective-permute-start.21 = (bf16[3,128,256]{2,1,0:T(8,128)(2,1)S(1)}, bf16[3,128,256]{2,1,0:T(8,128)(2,1)S(1)}, u32[]{:S(2)}, u32[]{:S(2)}) collective-permute-start(bf16[3,128,256]{2,1,0:T(8,128)(2,1)S(1)} %get-tuple-element.83), channel_id=1, source_target_pairs={{0,12},{4,8},{8,4},{12,0},{1,13},{5,9},{9,5},{13,1},{2,14},{6,10},... | collective-permute-start | bytes 589832 | tf_op jit(solution)/shard_map/ppermute | solution.py:431
  53.6 13.4 %collective-permute-start.22 = (bf16[144,128]{1,0:T(8,128)(2,1)S(1)}, bf16[144,128]{1,0:T(8,128)(2,1)S(1)}, u32[]{:S(2)}, u32[]{:S(2)}) collective-permute-start(bf16[144,128]{1,0:T(8,128)(2,1)S(1)} %get-tuple-element.84), channel_id=1, source_target_pairs={{0,4},{4,0},{8,12},{12,8},{1,5},{5,1},{9,13},{13,9},{2,6},{6,2},{1... | collective-permute-start | bytes 110600 | tf_op jit(solution)/shard_map/ppermute | solution.py:512
  54.7 12.2 %collective-permute-start.23 = (bf16[144,128]{1,0:T(8,128)(2,1)S(1)}, bf16[144,128]{1,0:T(8,128)(2,1)S(1)}, u32[]{:S(2)}, u32[]{:S(2)}) collective-permute-start(bf16[144,128]{1,0:T(8,128)(2,1)S(1)} %get-tuple-element.85), channel_id=1, source_target_pairs={{0,8},{4,12},{8,0},{12,4},{1,9},{5,13},{9,1},{13,5},{2,10},{6,14},... | collective-permute-start | bytes 110600 | tf_op jit(solution)/shard_map/ppermute | solution.py:512
  65.6 6.1 %collective-permute-start.24 = (bf16[144,128]{1,0:T(8,128)(2,1)S(1)}, bf16[144,128]{1,0:T(8,128)(2,1)S(1)}, u32[]{:S(2)}, u32[]{:S(2)}) collective-permute-start(bf16[144,128]{1,0:T(8,128)(2,1)S(1)} %get-tuple-element.86), channel_id=1, source_target_pairs={{0,12},{4,8},{8,4},{12,0},{1,13},{5,9},{9,5},{13,1},{2,14},{6,10},... | collective-permute-start | bytes 110600 | tf_op jit(solution)/shard_map/ppermute | solution.py:512
  71.7 5.7 %collective-permute-start.25 = (bf16[3,128,256]{2,1,0:T(8,128)(2,1)S(1)}, bf16[3,128,256]{2,1,0:T(8,128)(2,1)S(1)}, u32[]{:S(2)}, u32[]{:S(2)}) collective-permute-start(bf16[3,128,256]{2,1,0:T(8,128)(2,1)S(1)} %collective-permute-done.21.refs_0_), channel_id=1, source_target_pairs={{0,4},{4,0},{8,12},{12,8},{1,5},{5,1},{9,13},{13,9},{2,6},{6,2},{1... | collective-permute-start | bytes 589832 | tf_op jit(solution)/shard_map/ppermute | solution.py:431
  71.7 7.5 %collective-permute-start.28 = (bf16[3,128,256]{2,1,0:T(8,128)(2,1)S(1)}, bf16[3,128,256]{2,1,0:T(8,128)(2,1)S(1)}, u32[]{:S(2)}, u32[]{:S(2)}) collective-permute-start(bf16[3,128,256]{2,1,0:T(8,128)(2,1)S(1)} %collective-permute-done.21.refs_0_), channel_id=1, source_target_pairs={{0,16},{16,0},{1,17},{17,1},{2,18},{18,2},{3,19},{19,3},{4,20},{20... | collective-permute-start | bytes 589832 | tf_op jit(solution)/shard_map/ppermute | solution.py:428
  77.4 5.7 %collective-permute-start.29 = (bf16[3,128,256]{2,1,0:T(8,128)(2,1)S(1)}, bf16[3,128,256]{2,1,0:T(8,128)(2,1)S(1)}, u32[]{:S(2)}, u32[]{:S(2)}) collective-permute-start(bf16[3,128,256]{2,1,0:T(8,128)(2,1)S(1)} %collective-permute-done.25.refs_1_), channel_id=1, source_target_pairs={{0,16},{16,0},{1,17},{17,1},{2,18},{18,2},{3,19},{19,3},{4,20},{20... | collective-permute-start | bytes 589832 | tf_op jit(solution)/shard_map/ppermute | solution.py:428
  83.1 10.0 %collective-permute-start.30 = (bf16[4,3,128,256]{3,2,1,0:T(8,128)(2,1)S(1)}, bf16[4,3,128,256]{3,2,1,0:T(8,128)(2,1)S(1)}, u32[]{:S(2)}, u32[]{:S(2)}) collective-permute-start(bf16[4,3,128,256]{3,2,1,0:T(8,128)(2,1)S(1)} %shard_map.142.refs_4_), channel_id=1, source_target_pairs={{0,1},{1,0},{2,3},{3,2},{4,5},{5,4},{6,7},{7,6},{8,9},{9,8},{10,11... | collective-permute-start | bytes 2359304 | tf_op jit(solution)/shard_map/ppermute | solution.py:422
  83.2 9.9 %collective-permute-start.26 = (bf16[3,256,256]{2,1,0:T(8,128)(2,1)S(1)}, bf16[3,256,256]{2,1,0:T(8,128)(2,1)S(1)}, u32[]{:S(2)}, u32[]{:S(2)}) collective-permute-start(bf16[3,256,256]{2,1,0:T(8,128)(2,1)S(1)} %get-tuple-element.94.refs_0_), channel_id=1, source_target_pairs={{0,1},{1,0},{2,3},{3,2},{4,5},{5,4},{6,7},{7,6},{8,9},{9,8},{10,11... | collective-permute-start | bytes 1179656 | tf_op jit(solution)/shard_map/ppermute | solution.py:422
  83.7 9.4 %collective-permute-start.27 = (bf16[3,256,256]{2,1,0:T(8,128)(2,1)S(1)}, bf16[3,256,256]{2,1,0:T(8,128)(2,1)S(1)}, u32[]{:S(2)}, u32[]{:S(2)}) collective-permute-start(bf16[3,256,256]{2,1,0:T(8,128)(2,1)S(1)} %collective-permute-done.20.refs_2_), channel_id=1, source_target_pairs={{0,1},{1,0},{2,3},{3,2},{4,5},{5,4},{6,7},{7,6},{8,9},{9,8},{10,11... | collective-permute-start | bytes 1179656 | tf_op jit(solution)/shard_map/ppermute | solution.py:422
  83.8 9.4 %collective-permute-start.32 = (bf16[144,1024]{1,0:T(8,128)(2,1)S(1)}, bf16[144,1024]{1,0:T(8,128)(2,1)S(1)}, u32[]{:S(2)}, u32[]{:S(2)}) collective-permute-start(bf16[144,1024]{1,0:T(8,128)(2,1)S(1)} %get-tuple-element.99), channel_id=1, source_target_pairs={{0,2},{2,0},{1,3},{3,1},{4,6},{6,4},{5,7},{7,5},{8,10},{10,8},{9,1... | collective-permute-start | bytes 884744 | tf_op jit(solution)/shard_map/ppermute | solution.py:425
  85.0 1.6 %collective-permute-start.33 = (f32[16,256]{1,0:T(8,128)S(1)}, f32[16,256]{1,0:T(8,128)S(1)}, u32[]{:S(2)}, u32[]{:S(2)}) collective-permute-start(f32[16,256]{1,0:T(8,128)S(1)} %maximum_maximum_fusion.refs_12_), channel_id=1, source_target_pairs={{0,1},{1,0},{2,3},{3,2},{4,5},{5,4},{6,7},{7,6},{8,9},{9,8},{10,11... | collective-permute-start | bytes 49160 | tf_op jit(solution)/shard_map/ppermute | solution.py:422
  94.6 5.1 %collective-permute-start.34 = (bf16[64,1024]{1,0:T(8,128)(2,1)S(1)}, bf16[64,1024]{1,0:T(8,128)(2,1)S(1)}, u32[]{:S(2)}, u32[]{:S(2)}) collective-permute-start(bf16[64,1024]{1,0:T(8,128)(2,1)S(1)} %get-tuple-element.102), channel_id=1, source_target_pairs={{0,2},{2,0},{1,3},{3,1},{4,6},{6,4},{5,7},{7,5},{8,10},{10,8},{9,1... | collective-permute-start | bytes 393224 | tf_op jit(solution)/shard_map/ppermute | solution.py:425
  (9 other events, 28.4 us)

commit v8 on v5

--- a/solution.py
+++ b/solution.py
@@ -342,8 +342,8 @@
 
 
 def convolve_kernel(length, *refs):
-    pieces = refs[:4]
-    own_x, peer_x, halo_x, own_share, peer_share, gain, own_c, peer_c, base_out, share_out = refs[4:14]
+    own_x, gain, pieces = refs[0], refs[1], refs[2:6]
+    peer_x, halo_x, own_share, peer_share, own_c, peer_c, base_out, share_out = refs[6:14]
     mid, normed, w_value, w_gate, w_down, channel, padded, active, shares = refs[14:]
     s, h, f, p = here()
     valid_len = length[0]
@@ -420,6 +420,9 @@
     columns = w_query.shape[1]
     barrier = lax.optimization_barrier
 
+    def after(x, *others):
+        return barrier((x, *others))[0]
+
     def other_core(x):
         return lax.ppermute(x, "fsdp", SWAP)
 
@@ -469,8 +472,8 @@
     down = across(w_mine[3][3:], 1)
     pw_part = other_part(pw_mine)
     w_other[0], pw_part = barrier((w_other[0], pw_part))
-    after, *_ = barrier((pw_mine, *w_mine[1:], down))
-    pw_one, pw_three = across(after, 1), across(after, 3)
+    pw_later = after(pw_mine, *w_mine[1:], down)
+    pw_one, pw_three = across(pw_later, 1), across(pw_later, 3)
     queries, send, edges, stack = call(
         project_kernel,
         [
@@ -511,9 +514,10 @@
     stack, stack_part, *_ = barrier((stack, stack_part, *ctx))
     out_pieces = [stack, other_core(stack), stack_part, other_core(stack_part)]
     ctx = [ctx[0]] + [lax.ppermute(ctx[k], "seq", xor_pairs(k)) for k in range(1, SEQ)]
-    pw_one, pw_three, *ctx = barrier((pw_one, pw_three, *ctx))
-    pw_two = across(pw_three, 1)
-    one_part, three_part = other_part(pw_one), other_part(pw_three)
+    one_part = other_part(pw_one)
+    ctx[0] = after(ctx[0], one_part)
+    pw_far = after(pw_three, *ctx[1:])
+    pw_two, three_part = across(pw_far, 1), other_part(pw_far)
     own_share, sent_share = call(
         output_kernel,
         [shape((2 * step, width), F32), shape((2 * step, width), BF16)],
@@ -525,7 +529,7 @@
         *out_pieces,
         *ctx,
     )
-    own_share, edges, depth_kernel = barrier((own_share, edges, depth_kernel))
+    edges, depth_kernel = after(edges, own_share), after(depth_kernel, own_share)
     halo_x = other_core(edges)
     channels = jnp.concatenate([depth_kernel, bn_scale[None], bn_shift[None], jnp.zeros((5, columns), F32)])
     channels_peer = other_core(channels)
@@ -536,8 +540,8 @@
         return [stack, other_core(stack)]
 
     two_part = other_part(pw_two)
-    pw_mine, _ = barrier((pw_mine, peer_share))
-    pw_pieces = stacked(pw_mine, pw_one, pw_two, pw_three) + stacked(pw_part, one_part, two_part, three_part)
+    pw_mine = after(pw_mine, own_share)
+    pw_pieces = stacked(pw_mine, pw_one, pw_two, pw_three) + stacked(after(pw_part, channels_peer, halo_x, peer_share), one_part, two_part, three_part)
     base, share = call(
         convolve_kernel,
         [shape((rows, width), F32), shape((rows, width), BF16)],
@@ -553,13 +557,13 @@
             pltpu.VMEM((2 * rows, width), F32),
         ],
         length,
+        frames,
+        ln2_gain[None],
         *pw_pieces,
-        frames,
         blocks[1],
         halo_x,
         own_share,
         peer_share,
-        ln2_gain[None],
         channels,
         channels_peer,
         vmem=14,

time: 83.4 us -> 79 us (0.947)
  waiting for transfers between devices: 37.2 us -> 31.2 us
  starting transfers between devices: 34.8 us -> 36.4 us
    ppermute x5, waiting for transfers between devices: 11.5 us -> 5.59 us  [other_part(): return lax.ppermute(x, 'parts', SWAP)]
    ppermute x14, waiting for transfers between devices: 1.62 us -> 3.18 us  [other_core(): return lax.ppermute(x, 'fsdp', SWAP)]
    ppermute x10, starting transfers between devices: 13.5 us -> 15 us  [across(): return lax.ppermute(x, 'seq', xor_pairs(k))]
    ppermute x3, waiting for transfers between devices: 3.88 us -> 2.5 us  [shards_chip_per_head(): lax.ppermute(ctx[k], 'seq', xor_pairs(k))]
where the time goes in v8:
time: 79 us; the launch traced here: 78.8 us
  starting transfers between devices  36.4 us (46%)
  waiting for transfers between devices  31.2 us (39%)
  Pallas kernels  8.81 us (11%)
  between operations  0.83 us (1%)
  local copies, waits for them, and re-layouts  0.8 us (1%)
    ppermute x10, waiting for transfers between devices, across(): return lax.ppermute(x, 'seq', xor_pairs(k))  15.7 us
    ppermute x10, starting transfers between devices, across(): return lax.ppermute(x, 'seq', xor_pairs(k))  15 us
    pallas_call x7, Pallas kernels, call(): pl.pallas_call(kernel, out_shape=outs, in_specs=[pl.BlockSpec(memory_spac...  8.81 us
    ppermute x6, starting transfers between devices, other_side(): return lax.ppermute(x, 'head', SWAP)  8.12 us
    ppermute x5, starting transfers between devices, other_part(): return lax.ppermute(x, 'parts', SWAP)  6.11 us
    ppermute x5, waiting for transfers between devices, other_part(): return lax.ppermute(x, 'parts', SWAP)  5.59 us
    ppermute x6, waiting for transfers between devices, other_side(): return lax.ppermute(x, 'head', SWAP)  4.27 us
    ppermute x3, starting transfers between devices, shards_chip_per_head(): lax.ppermute(ctx[k], 'seq', xor_pairs(k))  4.05 us
  transfers between devices with their start and end apart: 38, of which 16 were waited for; matrix products, arithmetic and copies ran while one was open for 0% of the time, Pallas kernels for 6%

profile of v8, /device:TPU:0, one launch (start us, length us, event | category | flops | bytes accessed | tf_op | source)
XLA Modules:
  0.0 78.8 jit_solution(11448477101594663964)
XLA Ops:
  1.0 2.6 %collective-permute-start.4 = (bf16[64,1024]{1,0:T(8,128)(2,1)}, bf16[64,1024]{1,0:T(8,128)(2,1)S(1)}, u32[]{:S(2)}, u32[]{:S(2)}) collective-permute-start(bf16[64,1024]{1,0:T(8,128)(2,1)} %refs_0_.5), channel_id=1, source_target_pairs={{0,4},{4,0},{8,12},{12,8},{1,5},{5,1},{9,13},{13,9},{2,6},{6,2},{1... | collective-permute-start | bytes 393224 | tf_op jit(solution)/shard_map/ppermute | solution.py:436
  3.5 2.5 %collective-permute-start.6 = (bf16[64,1024]{1,0:T(8,128)(2,1)}, bf16[64,1024]{1,0:T(8,128)(2,1)S(1)}, u32[]{:S(2)}, u32[]{:S(2)}) collective-permute-start(bf16[64,1024]{1,0:T(8,128)(2,1)} %refs_0_.5), channel_id=1, source_target_pairs={{0,12},{4,8},{8,4},{12,0},{1,13},{5,9},{9,5},{13,1},{2,14},{6,10},... | collective-permute-start | bytes 393224 | tf_op jit(solution)/shard_map/ppermute | solution.py:436
  6.0 1.5 %collective-permute-start.3 = (bf16[64,1024]{1,0:T(8,128)(2,1)}, bf16[64,1024]{1,0:T(8,128)(2,1)S(1)}, u32[]{:S(2)}, u32[]{:S(2)}) collective-permute-start(bf16[64,1024]{1,0:T(8,128)(2,1)} %refs_0_.5), channel_id=1, source_target_pairs={{0,2},{2,0},{1,3},{3,1},{4,6},{6,4},{5,7},{7,5},{8,10},{10,8},{9,1... | collective-permute-start | bytes 393224 | tf_op jit(solution)/shard_map/ppermute | solution.py:430
  8.2 1.3 %shard_map.136 = (bf16[5,128,128]{2,1,0:T(8,128)(2,1)S(1)}, bf16[5,128,128]{2,1,0:T(8,128)(2,1)S(1)}, bf16[3,128,128]{2,1,0:T(8,128)(2,1)S(1)}, bf16[5,128,128]{2,1,0:T(8,128)(2,1)S(1)}, bf16[3,128,256]{2,1,0:T(8,128)(2,1)S(1)}) custom-call(s32[1]{0:T(128)S(6)} %copy.15.length, bf16[256,256]{1,0:T(8,128)(2,1)} %refs_0_.3, bf16[256,256]{1,0:T(8,128)(2,1)} %refs_1_.1, ...), custom_call_target="tpu_custom_call" | custom-call | tf_op jit(solution)/shard_map/pallas_call | solution.py:171
  10.3 3.1 %collective-permute-done.6.refs_7_ = bf16[64,1024]{1,0:T(8,128)(2,1)S(1)} collective-permute-done((bf16[64,1024]{1,0:T(8,128)(2,1)}, bf16[64,1024]{1,0:T(8,128)(2,1)S(1)}, u32[]{:S(2)}, u32[]{:S(2)}) %collective-permute-start.6) | collective-permute-done | bytes 131104 | tf_op jit(solution)/shard_map/ppermute | solution.py:436
  13.4 3.2 %collective-permute-start.12 = (bf16[5,128,128]{2,1,0:T(8,128)(2,1)S(1)}, bf16[5,128,128]{2,1,0:T(8,128)(2,1)S(1)}, u32[]{:S(2)}, u32[]{:S(2)}) collective-permute-start(bf16[5,128,128]{2,1,0:T(8,128)(2,1)S(1)} %get-tuple-element.45), channel_id=1, source_target_pairs={{0,12},{4,8},{8,4},{12,0},{1,13},{5,9},{9,5},{13,1},{2,14},{6,10},... | collective-permute-start | bytes 491528 | tf_op jit(solution)/shard_map/ppermute | solution.py:436
  16.7 1.5 %collective-permute-start.14 = (bf16[3,128,256]{2,1,0:T(8,128)(2,1)S(1)}, bf16[3,128,256]{2,1,0:T(8,128)(2,1)S(1)}, u32[]{:S(2)}, u32[]{:S(2)}) collective-permute-start(bf16[3,128,256]{2,1,0:T(8,128)(2,1)S(1)} %get-tuple-element.59.refs_0_), channel_id=1, source_target_pairs={{0,16},{16,0},{1,17},{17,1},{2,18},{18,2},{3,19},{19,3},{4,20},{20... | collective-permute-start | bytes 589832 | tf_op jit(solution)/shard_map/ppermute | solution.py:433
  18.2 1.3 %collective-permute-start.9 = (bf16[64,1024]{1,0:T(8,128)(2,1)S(1)}, bf16[64,1024]{1,0:T(8,128)(2,1)S(1)}, u32[]{:S(2)}, u32[]{:S(2)}) collective-permute-start(bf16[64,1024]{1,0:T(8,128)(2,1)S(1)} %collective-permute-done.6.refs_7_), channel_id=1, source_target_pairs={{0,2},{2,0},{1,3},{3,1},{4,6},{6,4},{5,7},{7,5},{8,10},{10,8},{9,1... | collective-permute-start | bytes 393224 | tf_op jit(solution)/shard_map/ppermute | solution.py:430
  19.6 1.6 %collective-permute-start.5 = (bf16[64,1024]{1,0:T(8,128)(2,1)S(1)}, bf16[64,1024]{1,0:T(8,128)(2,1)S(1)}, u32[]{:S(2)}, u32[]{:S(2)}) collective-permute-start(bf16[64,1024]{1,0:T(8,128)(2,1)S(1)} %collective-permute-done.4.refs_3_), channel_id=1, source_target_pairs={{0,2},{2,0},{1,3},{3,1},{4,6},{6,4},{5,7},{7,5},{8,10},{10,8},{9,1... | collective-permute-start | bytes 393224 | tf_op jit(solution)/shard_map/ppermute | solution.py:430
  21.2 2.7 %collective-permute-start.11 = (bf16[3,128,128]{2,1,0:T(8,128)(2,1)S(1)}, bf16[3,128,128]{2,1,0:T(8,128)(2,1)S(1)}, u32[]{:S(2)}, u32[]{:S(2)}) collective-permute-start(bf16[3,128,128]{2,1,0:T(8,128)(2,1)S(1)} %get-tuple-element.44), channel_id=1, source_target_pairs={{0,8},{4,12},{8,0},{12,4},{1,9},{5,13},{9,1},{13,5},{2,10},{6,14},... | collective-permute-start | bytes 294920 | tf_op jit(solution)/shard_map/ppermute | solution.py:436
  23.9 1.4 %collective-permute-done.12.refs_12_ = bf16[5,128,128]{2,1,0:T(8,128)(2,1)S(1)} collective-permute-done((bf16[5,128,128]{2,1,0:T(8,128)(2,1)S(1)}, bf16[5,128,128]{2,1,0:T(8,128)(2,1)S(1)}, u32[]{:S(2)}, u32[]{:S(2)}) %collective-permute-start.12) | collective-permute-done | bytes 163872 | tf_op jit(solution)/shard_map/ppermute | solution.py:436
  25.3 1.3 %collective-permute-start.8 = (bf16[64,1024]{1,0:T(8,128)(2,1)S(1)}, bf16[64,1024]{1,0:T(8,128)(2,1)S(1)}, u32[]{:S(2)}, u32[]{:S(2)}) collective-permute-start(bf16[64,1024]{1,0:T(8,128)(2,1)S(1)} %collective-permute-done.7.refs_5_), channel_id=1, source_target_pairs={{0,2},{2,0},{1,3},{3,1},{4,6},{6,4},{5,7},{7,5},{8,10},{10,8},{9,1... | collective-permute-start | bytes 393224 | tf_op jit(solution)/shard_map/ppermute | solution.py:430
  26.6 2.7 %collective-permute-done.11.refs_11_ = bf16[3,128,128]{2,1,0:T(8,128)(2,1)S(1)} collective-permute-done((bf16[3,128,128]{2,1,0:T(8,128)(2,1)S(1)}, bf16[3,128,128]{2,1,0:T(8,128)(2,1)S(1)}, u32[]{:S(2)}, u32[]{:S(2)}) %collective-permute-start.11) | collective-permute-done | bytes 98336 | tf_op jit(solution)/shard_map/ppermute | solution.py:436
  30.5 3.8 %collective-permute-done.18.refs_17_ = bf16[2,128,128]{2,1,0:T(8,128)(2,1)S(1)} collective-permute-done((bf16[2,128,128]{2,1,0:T(8,128)(2,1)S(1)}, bf16[2,128,128]{2,1,0:T(8,128)(2,1)S(1)}, u32[]{:S(2)}, u32[]{:S(2)}) %collective-permute-start.18) | collective-permute-done | bytes 65568 | tf_op jit(solution)/shard_map/ppermute | solution.py:436
  34.3 2.6 %shard_map.137 = (bf16[512,128]{1,0:T(8,128)(2,1)S(1)}, bf16[1088,128]{1,0:T(8,128)(2,1)S(1)}, bf16[16,1024]{1,0:T(8,128)(2,1)S(1)}, bf16[4,2,128,128]{3,2,1,0:T(8,128)(2,1)S(1)}) custom-call(s32[1]{0:T(128)S(6)} %copy.15.length, bf16[64,1024]{1,0:T(8,128)(2,1)} %refs_0_.5, f32[1,1024]{1,0:T(1,128)} %bitcast.5, ...), custom_call_target="tpu_custom_call" | custom-call | tf_op jit(solution)/shard_map/pallas_call | solution.py:171
  37.1 1.6 %collective-permute-start.19 = (bf16[4,2,128,128]{3,2,1,0:T(8,128)(2,1)S(1)}, bf16[4,2,128,128]{3,2,1,0:T(8,128)(2,1)S(1)}, u32[]{:S(2)}, u32[]{:S(2)}) collective-permute-start(bf16[4,2,128,128]{3,2,1,0:T(8,128)(2,1)S(1)} %get-tuple-element.54.refs_0_), channel_id=1, source_target_pairs={{0,16},{16,0},{1,17},{17,1},{2,18},{18,2},{3,19},{19,3},{4,20},{20... | collective-permute-start | bytes 786440 | tf_op jit(solution)/shard_map/ppermute | solution.py:433
  39.2 1.2 %collective-permute-start.28 = (bf16[3,128,256]{2,1,0:T(8,128)(2,1)S(1)}, bf16[3,128,256]{2,1,0:T(8,128)(2,1)S(1)}, u32[]{:S(2)}, u32[]{:S(2)}) collective-permute-start(bf16[3,128,256]{2,1,0:T(8,128)(2,1)S(1)} %get-tuple-element.59.refs_0_), channel_id=1, source_target_pairs={{0,12},{4,8},{8,4},{12,0},{1,13},{5,9},{9,5},{13,1},{2,14},{6,10},... | collective-permute-start | bytes 589832 | tf_op jit(solution)/shard_map/ppermute | solution.py:436
  40.4 2.8 %shard_map.138 = (bf16[144,128]{1,0:T(8,128)(2,1)S(1)}, bf16[144,128]{1,0:T(8,128)(2,1)S(1)}, bf16[144,128]{1,0:T(8,128)(2,1)S(1)}, bf16[144,128]{1,0:T(8,128)(2,1)S(1)}) custom-call(s32[1]{0:T(128)S(6)} %copy.15.length, bf16[512,128]{1,0:T(8,128)(2,1)S(1)} %get-tuple-element.48.q_in, bf16[1088,128]{1,0:T(8,128)(2,1)S(1)} %get-tuple-element.49.own, ...), custom_call_target="tpu_custom_call" | custom-call | tf_op jit(solution)/shard_map/pallas_call | solution.py:171
  43.2 2.6 %collective-permute-done.19.refs_2_ = bf16[4,2,128,128]{3,2,1,0:T(8,128)(2,1)S(1)} collective-permute-done((bf16[4,2,128,128]{3,2,1,0:T(8,128)(2,1)S(1)}, bf16[4,2,128,128]{3,2,1,0:T(8,128)(2,1)S(1)}, u32[]{:S(2)}, u32[]{:S(2)}) %collective-permute-start.19) | collective-permute-done | bytes 262176 | tf_op jit(solution)/shard_map/ppermute | solution.py:433
  46.8 2.6 %collective-permute-done.23.refs_1_ = bf16[3,128,256]{2,1,0:T(8,128)(2,1)S(1)} collective-permute-done((bf16[3,128,256]{2,1,0:T(8,128)(2,1)S(1)}, bf16[3,128,256]{2,1,0:T(8,128)(2,1)S(1)}, u32[]{:S(2)}, u32[]{:S(2)}) %collective-permute-start.23) | collective-permute-done | bytes 196640 | tf_op jit(solution)/shard_map/ppermute | solution.py:436
  49.4 1.0 %collective-permute-start.24 = (bf16[3,128,256]{2,1,0:T(8,128)(2,1)S(1)}, bf16[3,128,256]{2,1,0:T(8,128)(2,1)S(1)}, u32[]{:S(2)}, u32[]{:S(2)}) collective-permute-start(bf16[3,128,256]{2,1,0:T(8,128)(2,1)S(1)} %collective-permute-done.23.refs_1_), channel_id=1, source_target_pairs={{0,16},{16,0},{1,17},{17,1},{2,18},{18,2},{3,19},{19,3},{4,20},{20... | collective-permute-start | bytes 589832 | tf_op jit(solution)/shard_map/ppermute | solution.py:433
  50.6 3.3 %collective-permute-start.27 = (bf16[144,128]{1,0:T(8,128)(2,1)S(1)}, bf16[144,128]{1,0:T(8,128)(2,1)S(1)}, u32[]{:S(2)}, u32[]{:S(2)}) collective-permute-start(bf16[144,128]{1,0:T(8,128)(2,1)S(1)} %get-tuple-element.53), channel_id=1, source_target_pairs={{0,12},{4,8},{8,4},{12,0},{1,13},{5,9},{9,5},{13,1},{2,14},{6,10},... | collective-permute-start | bytes 110600 | tf_op jit(solution)/shard_map/ppermute | solution.py:516
  54.0 2.4 %collective-permute-done.26.refs_6_ = bf16[144,128]{1,0:T(8,128)(2,1)S(1)} collective-permute-done((bf16[144,128]{1,0:T(8,128)(2,1)S(1)}, bf16[144,128]{1,0:T(8,128)(2,1)S(1)}, u32[]{:S(2)}, u32[]{:S(2)}) %collective-permute-start.26) | collective-permute-done | bytes 36896 | tf_op jit(solution)/shard_map/ppermute | solution.py:516
  56.4 1.0 %collective-permute-start.29 = (bf16[3,128,256]{2,1,0:T(8,128)(2,1)S(1)}, bf16[3,128,256]{2,1,0:T(8,128)(2,1)S(1)}, u32[]{:S(2)}, u32[]{:S(2)}) collective-permute-start(bf16[3,128,256]{2,1,0:T(8,128)(2,1)S(1)} %collective-permute-done.28.refs_3_), channel_id=1, source_target_pairs={{0,4},{4,0},{8,12},{12,8},{1,5},{5,1},{9,13},{13,9},{2,6},{6,2},{1... | collective-permute-start | bytes 589832 | tf_op jit(solution)/shard_map/ppermute | solution.py:436
  57.9 1.2 %collective-permute-start.33 = (bf16[144,1024]{1,0:T(8,128)(2,1)S(1)}, bf16[144,1024]{1,0:T(8,128)(2,1)S(1)}, u32[]{:S(2)}, u32[]{:S(2)}) collective-permute-start(bf16[144,1024]{1,0:T(8,128)(2,1)S(1)} %get-tuple-element.65), channel_id=1, source_target_pairs={{0,2},{2,0},{1,3},{3,1},{4,6},{6,4},{5,7},{7,5},{8,10},{10,8},{9,1... | collective-permute-start | bytes 884744 | tf_op jit(solution)/shard_map/ppermute | solution.py:430
  60.1 2.0 %collective-permute-done.29.refs_2_ = bf16[3,128,256]{2,1,0:T(8,128)(2,1)S(1)} collective-permute-done((bf16[3,128,256]{2,1,0:T(8,128)(2,1)S(1)}, bf16[3,128,256]{2,1,0:T(8,128)(2,1)S(1)}, u32[]{:S(2)}, u32[]{:S(2)}) %collective-permute-start.29) | collective-permute-done | bytes 196640 | tf_op jit(solution)/shard_map/ppermute | solution.py:436
  62.1 1.1 %collective-permute-start.34 = (bf16[3,128,256]{2,1,0:T(8,128)(2,1)S(1)}, bf16[3,128,256]{2,1,0:T(8,128)(2,1)S(1)}, u32[]{:S(2)}, u32[]{:S(2)}) collective-permute-start(bf16[3,128,256]{2,1,0:T(8,128)(2,1)S(1)} %collective-permute-done.29.refs_2_), channel_id=1, source_target_pairs={{0,16},{16,0},{1,17},{17,1},{2,18},{18,2},{3,19},{19,3},{4,20},{20... | collective-permute-start | bytes 589832 | tf_op jit(solution)/shard_map/ppermute | solution.py:433
  66.6 2.1 %collective-permute-done.34.refs_2_ = bf16[3,128,256]{2,1,0:T(8,128)(2,1)S(1)} collective-permute-done((bf16[3,128,256]{2,1,0:T(8,128)(2,1)S(1)}, bf16[3,128,256]{2,1,0:T(8,128)(2,1)S(1)}, u32[]{:S(2)}, u32[]{:S(2)}) %collective-permute-start.34) | collective-permute-done | bytes 196640 | tf_op jit(solution)/shard_map/ppermute | solution.py:433
  68.9 2.3 %collective-permute-done.36.refs_5_ = bf16[4,3,128,256]{3,2,1,0:T(8,128)(2,1)S(1)} collective-permute-done((bf16[4,3,128,256]{3,2,1,0:T(8,128)(2,1)S(1)}, bf16[4,3,128,256]{3,2,1,0:T(8,128)(2,1)S(1)}, u32[]{:S(2)}, u32[]{:S(2)}) %collective-permute-start.36) | collective-permute-done | bytes 786464 | tf_op jit(solution)/shard_map/ppermute | solution.py:427
  71.1 1.4 %shard_map.142 = (f32[64,1024]{1,0:T(8,128)S(1)}, bf16[64,1024]{1,0:T(8,128)(2,1)S(1)}) custom-call(s32[1]{0:T(128)S(6)} %copy.15.length, bf16[64,1024]{1,0:T(8,128)(2,1)S(1)} %copy-done, f32[1,1024]{1,0:T(1,128)S(1)} %bitcast.4, bf16[4,3,128,256]{3,2,1,0:T(8,128)(2,1)S(1)} %shard_map.140.refs_2_, ...), custom_call_target="tpu_custom_call" | custom-call | tf_op jit(solution)/shard_map/pallas_call | solution.py:171
  72.5 1.3 %collective-permute-start.37 = (bf16[64,1024]{1,0:T(8,128)(2,1)S(1)}, bf16[64,1024]{1,0:T(8,128)(2,1)S(1)}, u32[]{:S(2)}, u32[]{:S(2)}) collective-permute-start(bf16[64,1024]{1,0:T(8,128)(2,1)S(1)} %get-tuple-element.68), channel_id=1, source_target_pairs={{0,2},{2,0},{1,3},{3,1},{4,6},{6,4},{5,7},{7,5},{8,10},{10,8},{9,1... | collective-permute-start | bytes 393224 | tf_op jit(solution)/shard_map/ppermute | solution.py:430
  73.9 4.3 %collective-permute-done.37 = bf16[64,1024]{1,0:T(8,128)(2,1)S(1)} collective-permute-done((bf16[64,1024]{1,0:T(8,128)(2,1)S(1)}, bf16[64,1024]{1,0:T(8,128)(2,1)S(1)}, u32[]{:S(2)}, u32[]{:S(2)}) %collective-permute-start.37) | collective-permute-done | bytes 131104 | tf_op jit(solution)/shard_map/ppermute | solution.py:430
  (69 shorter events, 10.9 us)
Async XLA Ops:
  0.0 6.0 %collective-permute-start = (bf16[256,256]{1,0:T(8,128)(2,1)}, bf16[256,256]{1,0:T(8,128)(2,1)S(1)}, u32[]{:S(2)}, u32[]{:S(2)}) collective-permute-start(bf16[256,256]{1,0:T(8,128)(2,1)} %refs_0_.3), channel_id=1, source_target_pairs={{0,1},{1,0},{2,3},{3,2},{4,5},{5,4},{6,7},{7,6},{8,9},{9,8},{10,11... | collective-permute-start | bytes 393224 | tf_op jit(solution)/shard_map/ppermute | solution.py:427
  0.5 7.7 %collective-permute-start.1 = (bf16[256,256]{1,0:T(8,128)(2,1)}, bf16[256,256]{1,0:T(8,128)(2,1)S(1)}, u32[]{:S(2)}, u32[]{:S(2)}) collective-permute-start(bf16[256,256]{1,0:T(8,128)(2,1)} %refs_1_.1), channel_id=1, source_target_pairs={{0,1},{1,0},{2,3},{3,2},{4,5},{5,4},{6,7},{7,6},{8,9},{9,8},{10,11... | collective-permute-start | bytes 393224 | tf_op jit(solution)/shard_map/ppermute | solution.py:427
  0.5 7.7 %collective-permute-start.2 = (bf16[256,256]{1,0:T(8,128)(2,1)}, bf16[256,256]{1,0:T(8,128)(2,1)S(1)}, u32[]{:S(2)}, u32[]{:S(2)}) collective-permute-start(bf16[256,256]{1,0:T(8,128)(2,1)} %refs_2_.1), channel_id=1, source_target_pairs={{0,1},{1,0},{2,3},{3,2},{4,5},{5,4},{6,7},{7,6},{8,9},{9,8},{10,11... | collective-permute-start | bytes 393224 | tf_op jit(solution)/shard_map/ppermute | solution.py:427
  1.0 8.5 %collective-permute-start.4 = (bf16[64,1024]{1,0:T(8,128)(2,1)}, bf16[64,1024]{1,0:T(8,128)(2,1)S(1)}, u32[]{:S(2)}, u32[]{:S(2)}) collective-permute-start(bf16[64,1024]{1,0:T(8,128)(2,1)} %refs_0_.5), channel_id=1, source_target_pairs={{0,4},{4,0},{8,12},{12,8},{1,5},{5,1},{9,13},{13,9},{2,6},{6,2},{1... | collective-permute-start | bytes 393224 | tf_op jit(solution)/shard_map/ppermute | solution.py:436
  3.5 9.8 %collective-permute-start.6 = (bf16[64,1024]{1,0:T(8,128)(2,1)}, bf16[64,1024]{1,0:T(8,128)(2,1)S(1)}, u32[]{:S(2)}, u32[]{:S(2)}) collective-permute-start(bf16[64,1024]{1,0:T(8,128)(2,1)} %refs_0_.5), channel_id=1, source_target_pairs={{0,12},{4,8},{8,4},{12,0},{1,13},{5,9},{9,5},{13,1},{2,14},{6,10},... | collective-permute-start | bytes 393224 | tf_op jit(solution)/shard_map/ppermute | solution.py:436
  6.0 10.7 %collective-permute-start.3 = (bf16[64,1024]{1,0:T(8,128)(2,1)}, bf16[64,1024]{1,0:T(8,128)(2,1)S(1)}, u32[]{:S(2)}, u32[]{:S(2)}) collective-permute-start(bf16[64,1024]{1,0:T(8,128)(2,1)} %refs_0_.5), channel_id=1, source_target_pairs={{0,2},{2,0},{1,3},{3,1},{4,6},{6,4},{5,7},{7,5},{8,10},{10,8},{9,1... | collective-permute-start | bytes 393224 | tf_op jit(solution)/shard_map/ppermute | solution.py:430
  9.5 11.7 %collective-permute-start.10 = (bf16[5,128,128]{2,1,0:T(8,128)(2,1)S(1)}, bf16[5,128,128]{2,1,0:T(8,128)(2,1)S(1)}, u32[]{:S(2)}, u32[]{:S(2)}) collective-permute-start(bf16[5,128,128]{2,1,0:T(8,128)(2,1)S(1)} %get-tuple-element.43), channel_id=1, source_target_pairs={{0,4},{4,0},{8,12},{12,8},{1,5},{5,1},{9,13},{13,9},{2,6},{6,2},{1... | collective-permute-start | bytes 491528 | tf_op jit(solution)/shard_map/ppermute | solution.py:436
  13.3 6.3 %collective-permute-start.7 = (bf16[64,1024]{1,0:T(8,128)(2,1)S(1)}, bf16[64,1024]{1,0:T(8,128)(2,1)S(1)}, u32[]{:S(2)}, u32[]{:S(2)}) collective-permute-start(bf16[64,1024]{1,0:T(8,128)(2,1)S(1)} %collective-permute-done.6.refs_7_), channel_id=1, source_target_pairs={{0,4},{4,0},{8,12},{12,8},{1,5},{5,1},{9,13},{13,9},{2,6},{6,2},{1... | collective-permute-start | bytes 393224 | tf_op jit(solution)/shard_map/ppermute | solution.py:436
  13.4 4.8 %collective-permute-start.13 = (bf16[3,128,128]{2,1,0:T(8,128)(2,1)S(1)}, bf16[3,128,128]{2,1,0:T(8,128)(2,1)S(1)}, u32[]{:S(2)}, u32[]{:S(2)}) collective-permute-start(bf16[3,128,128]{2,1,0:T(8,128)(2,1)S(1)} %slice.12), channel_id=1, source_target_pairs={{0,1},{1,0},{2,3},{3,2},{4,5},{5,4},{6,7},{7,6},{8,9},{9,8},{10,11... | collective-permute-start | bytes 294920 | tf_op jit(solution)/shard_map/ppermute | solution.py:427
  13.4 11.8 %collective-permute-start.12 = (bf16[5,128,128]{2,1,0:T(8,128)(2,1)S(1)}, bf16[5,128,128]{2,1,0:T(8,128)(2,1)S(1)}, u32[]{:S(2)}, u32[]{:S(2)}) collective-permute-start(bf16[5,128,128]{2,1,0:T(8,128)(2,1)S(1)} %get-tuple-element.45), channel_id=1, source_target_pairs={{0,12},{4,8},{8,4},{12,0},{1,13},{5,9},{9,5},{13,1},{2,14},{6,10},... | collective-permute-start | bytes 491528 | tf_op jit(solution)/shard_map/ppermute | solution.py:436
  16.7 13.1 %collective-permute-start.14 = (bf16[3,128,256]{2,1,0:T(8,128)(2,1)S(1)}, bf16[3,128,256]{2,1,0:T(8,128)(2,1)S(1)}, u32[]{:S(2)}, u32[]{:S(2)}) collective-permute-start(bf16[3,128,256]{2,1,0:T(8,128)(2,1)S(1)} %get-tuple-element.59.refs_0_), channel_id=1, source_target_pairs={{0,16},{16,0},{1,17},{17,1},{2,18},{18,2},{3,19},{19,3},{4,20},{20... | collective-permute-start | bytes 589832 | tf_op jit(solution)/shard_map/ppermute | solution.py:433
  18.2 11.0 %collective-permute-start.9 = (bf16[64,1024]{1,0:T(8,128)(2,1)S(1)}, bf16[64,1024]{1,0:T(8,128)(2,1)S(1)}, u32[]{:S(2)}, u32[]{:S(2)}) collective-permute-start(bf16[64,1024]{1,0:T(8,128)(2,1)S(1)} %collective-permute-done.6.refs_7_), channel_id=1, source_target_pairs={{0,2},{2,0},{1,3},{3,1},{4,6},{6,4},{5,7},{7,5},{8,10},{10,8},{9,1... | collective-permute-start | bytes 393224 | tf_op jit(solution)/shard_map/ppermute | solution.py:430
  19.6 10.1 %collective-permute-start.5 = (bf16[64,1024]{1,0:T(8,128)(2,1)S(1)}, bf16[64,1024]{1,0:T(8,128)(2,1)S(1)}, u32[]{:S(2)}, u32[]{:S(2)}) collective-permute-start(bf16[64,1024]{1,0:T(8,128)(2,1)S(1)} %collective-permute-done.4.refs_3_), channel_id=1, source_target_pairs={{0,2},{2,0},{1,3},{3,1},{4,6},{6,4},{5,7},{7,5},{8,10},{10,8},{9,1... | collective-permute-start | bytes 393224 | tf_op jit(solution)/shard_map/ppermute | solution.py:430
  21.2 8.0 %collective-permute-start.11 = (bf16[3,128,128]{2,1,0:T(8,128)(2,1)S(1)}, bf16[3,128,128]{2,1,0:T(8,128)(2,1)S(1)}, u32[]{:S(2)}, u32[]{:S(2)}) collective-permute-start(bf16[3,128,128]{2,1,0:T(8,128)(2,1)S(1)} %get-tuple-element.44), channel_id=1, source_target_pairs={{0,8},{4,12},{8,0},{12,4},{1,9},{5,13},{9,1},{13,5},{2,10},{6,14},... | collective-permute-start | bytes 294920 | tf_op jit(solution)/shard_map/ppermute | solution.py:436
  25.3 9.1 %collective-permute-start.8 = (bf16[64,1024]{1,0:T(8,128)(2,1)S(1)}, bf16[64,1024]{1,0:T(8,128)(2,1)S(1)}, u32[]{:S(2)}, u32[]{:S(2)}) collective-permute-start(bf16[64,1024]{1,0:T(8,128)(2,1)S(1)} %collective-permute-done.7.refs_5_), channel_id=1, source_target_pairs={{0,2},{2,0},{1,3},{3,1},{4,6},{6,4},{5,7},{7,5},{8,10},{10,8},{9,1... | collective-permute-start | bytes 393224 | tf_op jit(solution)/shard_map/ppermute | solution.py:430
  29.2 5.1 %collective-permute-start.15 = (bf16[3,128,128]{2,1,0:T(8,128)(2,1)S(1)}, bf16[3,128,128]{2,1,0:T(8,128)(2,1)S(1)}, u32[]{:S(2)}, u32[]{:S(2)}) collective-permute-start(bf16[3,128,128]{2,1,0:T(8,128)(2,1)S(1)} %slice.16), channel_id=1, source_target_pairs={{0,1},{1,0},{2,3},{3,2},{4,5},{5,4},{6,7},{7,6},{8,9},{9,8},{10,11... | collective-permute-start | bytes 294920 | tf_op jit(solution)/shard_map/ppermute | solution.py:427
  29.8 4.6 %collective-permute-start.17 = (bf16[3,128,128]{2,1,0:T(8,128)(2,1)S(1)}, bf16[3,128,128]{2,1,0:T(8,128)(2,1)S(1)}, u32[]{:S(2)}, u32[]{:S(2)}) collective-permute-start(bf16[3,128,128]{2,1,0:T(8,128)(2,1)S(1)} %slice.17), channel_id=1, source_target_pairs={{0,1},{1,0},{2,3},{3,2},{4,5},{5,4},{6,7},{7,6},{8,9},{9,8},{10,11... | collective-permute-start | bytes 294920 | tf_op jit(solution)/shard_map/ppermute | solution.py:427
  29.8 4.5 %collective-permute-start.18 = (bf16[2,128,128]{2,1,0:T(8,128)(2,1)S(1)}, bf16[2,128,128]{2,1,0:T(8,128)(2,1)S(1)}, u32[]{:S(2)}, u32[]{:S(2)}) collective-permute-start(bf16[2,128,128]{2,1,0:T(8,128)(2,1)S(1)} %slice.18), channel_id=1, source_target_pairs={{0,4},{4,0},{8,12},{12,8},{1,5},{5,1},{9,13},{13,9},{2,6},{6,2},{1... | collective-permute-start | bytes 196616 | tf_op jit(solution)/shard_map/ppermute | solution.py:436
  37.1 8.7 %collective-permute-start.19 = (bf16[4,2,128,128]{3,2,1,0:T(8,128)(2,1)S(1)}, bf16[4,2,128,128]{3,2,1,0:T(8,128)(2,1)S(1)}, u32[]{:S(2)}, u32[]{:S(2)}) collective-permute-start(bf16[4,2,128,128]{3,2,1,0:T(8,128)(2,1)S(1)} %get-tuple-element.54.refs_0_), channel_id=1, source_target_pairs={{0,16},{16,0},{1,17},{17,1},{2,18},{18,2},{3,19},{19,3},{4,20},{20... | collective-permute-start | bytes 786440 | tf_op jit(solution)/shard_map/ppermute | solution.py:433
  38.7 10.7 %collective-permute-start.23 = (bf16[3,128,256]{2,1,0:T(8,128)(2,1)S(1)}, bf16[3,128,256]{2,1,0:T(8,128)(2,1)S(1)}, u32[]{:S(2)}, u32[]{:S(2)}) collective-permute-start(bf16[3,128,256]{2,1,0:T(8,128)(2,1)S(1)} %get-tuple-element.59.refs_0_), channel_id=1, source_target_pairs={{0,4},{4,0},{8,12},{12,8},{1,5},{5,1},{9,13},{13,9},{2,6},{6,2},{1... | collective-permute-start | bytes 589832 | tf_op jit(solution)/shard_map/ppermute | solution.py:436
  39.2 11.2 %collective-permute-start.28 = (bf16[3,128,256]{2,1,0:T(8,128)(2,1)S(1)}, bf16[3,128,256]{2,1,0:T(8,128)(2,1)S(1)}, u32[]{:S(2)}, u32[]{:S(2)}) collective-permute-start(bf16[3,128,256]{2,1,0:T(8,128)(2,1)S(1)} %get-tuple-element.59.refs_0_), channel_id=1, source_target_pairs={{0,12},{4,8},{8,4},{12,0},{1,13},{5,9},{9,5},{13,1},{2,14},{6,10},... | collective-permute-start | bytes 589832 | tf_op jit(solution)/shard_map/ppermute | solution.py:436
  45.8 11.6 %collective-permute-start.21 = (bf16[4,2,128,128]{3,2,1,0:T(8,128)(2,1)S(1)}, bf16[4,2,128,128]{3,2,1,0:T(8,128)(2,1)S(1)}, u32[]{:S(2)}, u32[]{:S(2)}) collective-permute-start(bf16[4,2,128,128]{3,2,1,0:T(8,128)(2,1)S(1)} %get-tuple-element.54.refs_0_), channel_id=1, source_target_pairs={{0,1},{1,0},{2,3},{3,2},{4,5},{5,4},{6,7},{7,6},{8,9},{9,8},{10,11... | collective-permute-start | bytes 786440 | tf_op jit(solution)/shard_map/ppermute | solution.py:427
  45.8 11.6 %collective-permute-start.22 = (bf16[4,2,128,128]{3,2,1,0:T(8,128)(2,1)S(1)}, bf16[4,2,128,128]{3,2,1,0:T(8,128)(2,1)S(1)}, u32[]{:S(2)}, u32[]{:S(2)}) collective-permute-start(bf16[4,2,128,128]{3,2,1,0:T(8,128)(2,1)S(1)} %collective-permute-done.19.refs_2_), channel_id=1, source_target_pairs={{0,1},{1,0},{2,3},{3,2},{4,5},{5,4},{6,7},{7,6},{8,9},{9,8},{10,11... | collective-permute-start | bytes 786440 | tf_op jit(solution)/shard_map/ppermute | solution.py:427
  46.3 4.3 %collective-permute-start.25 = (bf16[144,128]{1,0:T(8,128)(2,1)S(1)}, bf16[144,128]{1,0:T(8,128)(2,1)S(1)}, u32[]{:S(2)}, u32[]{:S(2)}) collective-permute-start(bf16[144,128]{1,0:T(8,128)(2,1)S(1)} %get-tuple-element.51), channel_id=1, source_target_pairs={{0,4},{4,0},{8,12},{12,8},{1,5},{5,1},{9,13},{13,9},{2,6},{6,2},{1... | collective-permute-start | bytes 110600 | tf_op jit(solution)/shard_map/ppermute | solution.py:516
  49.4 8.0 %collective-permute-start.24 = (bf16[3,128,256]{2,1,0:T(8,128)(2,1)S(1)}, bf16[3,128,256]{2,1,0:T(8,128)(2,1)S(1)}, u32[]{:S(2)}, u32[]{:S(2)}) collective-permute-start(bf16[3,128,256]{2,1,0:T(8,128)(2,1)S(1)} %collective-permute-done.23.refs_1_), channel_id=1, source_target_pairs={{0,16},{16,0},{1,17},{17,1},{2,18},{18,2},{3,19},{19,3},{4,20},{20... | collective-permute-start | bytes 589832 | tf_op jit(solution)/shard_map/ppermute | solution.py:433
  50.4 6.0 %collective-permute-start.26 = (bf16[144,128]{1,0:T(8,128)(2,1)S(1)}, bf16[144,128]{1,0:T(8,128)(2,1)S(1)}, u32[]{:S(2)}, u32[]{:S(2)}) collective-permute-start(bf16[144,128]{1,0:T(8,128)(2,1)S(1)} %get-tuple-element.52), channel_id=1, source_target_pairs={{0,8},{4,12},{8,0},{12,4},{1,9},{5,13},{9,1},{13,5},{2,10},{6,14},... | collective-permute-start | bytes 110600 | tf_op jit(solution)/shard_map/ppermute | solution.py:516
  50.6 5.8 %collective-permute-start.27 = (bf16[144,128]{1,0:T(8,128)(2,1)S(1)}, bf16[144,128]{1,0:T(8,128)(2,1)S(1)}, u32[]{:S(2)}, u32[]{:S(2)}) collective-permute-start(bf16[144,128]{1,0:T(8,128)(2,1)S(1)} %get-tuple-element.53), channel_id=1, source_target_pairs={{0,12},{4,8},{8,4},{12,0},{1,13},{5,9},{9,5},{13,1},{2,14},{6,10},... | collective-permute-start | bytes 110600 | tf_op jit(solution)/shard_map/ppermute | solution.py:516
  56.4 5.7 %collective-permute-start.29 = (bf16[3,128,256]{2,1,0:T(8,128)(2,1)S(1)}, bf16[3,128,256]{2,1,0:T(8,128)(2,1)S(1)}, u32[]{:S(2)}, u32[]{:S(2)}) collective-permute-start(bf16[3,128,256]{2,1,0:T(8,128)(2,1)S(1)} %collective-permute-done.28.refs_3_), channel_id=1, source_target_pairs={{0,4},{4,0},{8,12},{12,8},{1,5},{5,1},{9,13},{13,9},{2,6},{6,2},{1... | collective-permute-start | bytes 589832 | tf_op jit(solution)/shard_map/ppermute | solution.py:436
  57.9 7.8 %collective-permute-start.33 = (bf16[144,1024]{1,0:T(8,128)(2,1)S(1)}, bf16[144,1024]{1,0:T(8,128)(2,1)S(1)}, u32[]{:S(2)}, u32[]{:S(2)}) collective-permute-start(bf16[144,1024]{1,0:T(8,128)(2,1)S(1)} %get-tuple-element.65), channel_id=1, source_target_pairs={{0,2},{2,0},{1,3},{3,1},{4,6},{6,4},{5,7},{7,5},{8,10},{10,8},{9,1... | collective-permute-start | bytes 884744 | tf_op jit(solution)/shard_map/ppermute | solution.py:430
  59.2 7.4 %collective-permute-start.35 = (bf16[3,128,256]{2,1,0:T(8,128)(2,1)S(1)}, bf16[3,128,256]{2,1,0:T(8,128)(2,1)S(1)}, u32[]{:S(2)}, u32[]{:S(2)}) collective-permute-start(bf16[3,128,256]{2,1,0:T(8,128)(2,1)S(1)} %collective-permute-done.28.refs_3_), channel_id=1, source_target_pairs={{0,16},{16,0},{1,17},{17,1},{2,18},{18,2},{3,19},{19,3},{4,20},{20... | collective-permute-start | bytes 589832 | tf_op jit(solution)/shard_map/ppermute | solution.py:433
  62.1 6.6 %collective-permute-start.34 = (bf16[3,128,256]{2,1,0:T(8,128)(2,1)S(1)}, bf16[3,128,256]{2,1,0:T(8,128)(2,1)S(1)}, u32[]{:S(2)}, u32[]{:S(2)}) collective-permute-start(bf16[3,128,256]{2,1,0:T(8,128)(2,1)S(1)} %collective-permute-done.29.refs_2_), channel_id=1, source_target_pairs={{0,16},{16,0},{1,17},{17,1},{2,18},{18,2},{3,19},{19,3},{4,20},{20... | collective-permute-start | bytes 589832 | tf_op jit(solution)/shard_map/ppermute | solution.py:433
  72.5 5.6 %collective-permute-start.37 = (bf16[64,1024]{1,0:T(8,128)(2,1)S(1)}, bf16[64,1024]{1,0:T(8,128)(2,1)S(1)}, u32[]{:S(2)}, u32[]{:S(2)}) collective-permute-start(bf16[64,1024]{1,0:T(8,128)(2,1)S(1)} %get-tuple-element.68), channel_id=1, source_target_pairs={{0,2},{2,0},{1,3},{3,1},{4,6},{6,4},{5,7},{7,5},{8,10},{10,8},{9,1... | collective-permute-start | bytes 393224 | tf_op jit(solution)/shard_map/ppermute | solution.py:430
  (11 other events, 35.8 us)

commit v9 on v8

--- a/solution.py
+++ b/solution.py
@@ -292,7 +292,7 @@
     total = q_in.shape[0]
     rows = total // count
     step = q_rows.shape[1]
-    local = lax.broadcasted_iota(jnp.int32, (step, total), 1)
+    local = lax.broadcasted_iota(jnp.int32, (1, total), 1)
     base = (local // rows) * (2 * rows) + local % rows
     keep_own = base + f * rows < valid_len
     keep_peer = base + (1 - f) * rows < valid_len
@@ -301,9 +301,8 @@
     for b in range(count):
         q_rows[b, 0:rows, :] = q_in[b * rows : (b + 1) * rows, :].astype(F32)
         q_rows[b, rows:step, :] = peer[2 * total + b * HALO : 2 * total + (b + 1) * HALO, :].astype(F32)
-    for b in range(count):
-        k, side = b // 2, b % 2
-        q = q_rows[(s ^ k) * 2 + side].astype(BF16)
+    for k in range(SEQ):
+        q = jnp.concatenate([q_rows[(s ^ k) * 2 + side] for side in range(2)], axis=0).astype(BF16)
         first = lax.dot_general(q, own[0:total, :], keys_t, preferred_element_type=F32) * scale
         second = lax.dot_general(q, peer[0:total, :], keys_t, preferred_element_type=F32) * scale
         first = jnp.where(keep_own, first, -jnp.inf)
@@ -317,7 +316,7 @@
         weighted = dot(first.astype(BF16), own[total : 2 * total, :]) + dot(
             second.astype(BF16), peer[total : 2 * total, :]
         )
-        ctx_outs[k][side * step : (side + 1) * step, :] = (weighted / weight_sum).astype(BF16)
+        ctx_outs[k][...] = (weighted / weight_sum).astype(BF16)
 
 
 def output_kernel(length, *refs):

time: 79 us -> 79 us (level)
  Pallas kernels: 8.81 us -> 7.59 us
  waiting for transfers between devices: 31.2 us -> 32.4 us
    pallas_call x7, Pallas kernels: 8.81 us -> 7.59 us  [call(): pl.pallas_call(kernel, out_shape=outs, in_specs=[pl.BlockSpec(memory_spac...]
    ppermute x5, waiting for transfers between devices: 5.59 us -> 6.81 us  [other_part(): return lax.ppermute(x, 'parts', SWAP)]
  transfers between devices with their start and end apart: 38 -> 38, of which waited for: 16 -> 16; matrix products, arithmetic and copies ran while one was open for 0% -> 0% of each run, Pallas kernels for 6% -> 5%
where the time goes in v9:
time: 79 us; the launch traced here: 78.8 us
  starting transfers between devices  36.4 us (46%)
  waiting for transfers between devices  32.4 us (41%)
  Pallas kernels  7.59 us (10%)
  between operations  0.83 us (1%)
  local copies, waits for them, and re-layouts  0.8 us (1%)
    ppermute x10, waiting for transfers between devices, across(): return lax.ppermute(x, 'seq', xor_pairs(k))  15.7 us
    ppermute x10, starting transfers between devices, across(): return lax.ppermute(x, 'seq', xor_pairs(k))  15 us
    ppermute x6, starting transfers between devices, other_side(): return lax.ppermute(x, 'head', SWAP)  8.12 us
    pallas_call x7, Pallas kernels, call(): pl.pallas_call(kernel, out_shape=outs, in_specs=[pl.BlockSpec(memory_spac...  7.59 us
    ppermute x5, waiting for transfers between devices, other_part(): return lax.ppermute(x, 'parts', SWAP)  6.81 us
    ppermute x5, starting transfers between devices, other_part(): return lax.ppermute(x, 'parts', SWAP)  6.11 us
    ppermute x6, waiting for transfers between devices, other_side(): return lax.ppermute(x, 'head', SWAP)  4.27 us
    ppermute x3, starting transfers between devices, shards_chip_per_head(): lax.ppermute(ctx[k], 'seq', xor_pairs(k))  4.05 us
  transfers between devices with their start and end apart: 38, of which 16 were waited for; matrix products, arithmetic and copies ran while one was open for 0% of the time, Pallas kernels for 5%

profile of v9, /device:TPU:0, one launch (start us, length us, event | category | flops | bytes accessed | tf_op | source)
XLA Modules:
  0.0 78.8 jit_solution(2487487551709572443)
XLA Ops:
  1.0 2.6 %collective-permute-start.4 = (bf16[64,1024]{1,0:T(8,128)(2,1)}, bf16[64,1024]{1,0:T(8,128)(2,1)S(1)}, u32[]{:S(2)}, u32[]{:S(2)}) collective-permute-start(bf16[64,1024]{1,0:T(8,128)(2,1)} %refs_0_.5), channel_id=1, source_target_pairs={{0,4},{4,0},{8,12},{12,8},{1,5},{5,1},{9,13},{13,9},{2,6},{6,2},{1... | collective-permute-start | bytes 393224 | tf_op jit(solution)/shard_map/ppermute | solution.py:435
  3.5 2.5 %collective-permute-start.6 = (bf16[64,1024]{1,0:T(8,128)(2,1)}, bf16[64,1024]{1,0:T(8,128)(2,1)S(1)}, u32[]{:S(2)}, u32[]{:S(2)}) collective-permute-start(bf16[64,1024]{1,0:T(8,128)(2,1)} %refs_0_.5), channel_id=1, source_target_pairs={{0,12},{4,8},{8,4},{12,0},{1,13},{5,9},{9,5},{13,1},{2,14},{6,10},... | collective-permute-start | bytes 393224 | tf_op jit(solution)/shard_map/ppermute | solution.py:435
  6.0 1.5 %collective-permute-start.3 = (bf16[64,1024]{1,0:T(8,128)(2,1)}, bf16[64,1024]{1,0:T(8,128)(2,1)S(1)}, u32[]{:S(2)}, u32[]{:S(2)}) collective-permute-start(bf16[64,1024]{1,0:T(8,128)(2,1)} %refs_0_.5), channel_id=1, source_target_pairs={{0,2},{2,0},{1,3},{3,1},{4,6},{6,4},{5,7},{7,5},{8,10},{10,8},{9,1... | collective-permute-start | bytes 393224 | tf_op jit(solution)/shard_map/ppermute | solution.py:429
  8.2 1.3 %shard_map.136 = (bf16[5,128,128]{2,1,0:T(8,128)(2,1)S(1)}, bf16[5,128,128]{2,1,0:T(8,128)(2,1)S(1)}, bf16[3,128,128]{2,1,0:T(8,128)(2,1)S(1)}, bf16[5,128,128]{2,1,0:T(8,128)(2,1)S(1)}, bf16[3,128,256]{2,1,0:T(8,128)(2,1)S(1)}) custom-call(s32[1]{0:T(128)S(6)} %copy.15.length, bf16[256,256]{1,0:T(8,128)(2,1)} %refs_0_.3, bf16[256,256]{1,0:T(8,128)(2,1)} %refs_1_.1, ...), custom_call_target="tpu_custom_call" | custom-call | tf_op jit(solution)/shard_map/pallas_call | solution.py:171
  10.3 3.1 %collective-permute-done.6.refs_7_ = bf16[64,1024]{1,0:T(8,128)(2,1)S(1)} collective-permute-done((bf16[64,1024]{1,0:T(8,128)(2,1)}, bf16[64,1024]{1,0:T(8,128)(2,1)S(1)}, u32[]{:S(2)}, u32[]{:S(2)}) %collective-permute-start.6) | collective-permute-done | bytes 131104 | tf_op jit(solution)/shard_map/ppermute | solution.py:435
  13.4 3.2 %collective-permute-start.12 = (bf16[5,128,128]{2,1,0:T(8,128)(2,1)S(1)}, bf16[5,128,128]{2,1,0:T(8,128)(2,1)S(1)}, u32[]{:S(2)}, u32[]{:S(2)}) collective-permute-start(bf16[5,128,128]{2,1,0:T(8,128)(2,1)S(1)} %get-tuple-element.45), channel_id=1, source_target_pairs={{0,12},{4,8},{8,4},{12,0},{1,13},{5,9},{9,5},{13,1},{2,14},{6,10},... | collective-permute-start | bytes 491528 | tf_op jit(solution)/shard_map/ppermute | solution.py:435
  16.7 1.5 %collective-permute-start.14 = (bf16[3,128,256]{2,1,0:T(8,128)(2,1)S(1)}, bf16[3,128,256]{2,1,0:T(8,128)(2,1)S(1)}, u32[]{:S(2)}, u32[]{:S(2)}) collective-permute-start(bf16[3,128,256]{2,1,0:T(8,128)(2,1)S(1)} %get-tuple-element.59.refs_0_), channel_id=1, source_target_pairs={{0,16},{16,0},{1,17},{17,1},{2,18},{18,2},{3,19},{19,3},{4,20},{20... | collective-permute-start | bytes 589832 | tf_op jit(solution)/shard_map/ppermute | solution.py:432
  18.2 1.3 %collective-permute-start.9 = (bf16[64,1024]{1,0:T(8,128)(2,1)S(1)}, bf16[64,1024]{1,0:T(8,128)(2,1)S(1)}, u32[]{:S(2)}, u32[]{:S(2)}) collective-permute-start(bf16[64,1024]{1,0:T(8,128)(2,1)S(1)} %collective-permute-done.6.refs_7_), channel_id=1, source_target_pairs={{0,2},{2,0},{1,3},{3,1},{4,6},{6,4},{5,7},{7,5},{8,10},{10,8},{9,1... | collective-permute-start | bytes 393224 | tf_op jit(solution)/shard_map/ppermute | solution.py:429
  19.6 1.6 %collective-permute-start.5 = (bf16[64,1024]{1,0:T(8,128)(2,1)S(1)}, bf16[64,1024]{1,0:T(8,128)(2,1)S(1)}, u32[]{:S(2)}, u32[]{:S(2)}) collective-permute-start(bf16[64,1024]{1,0:T(8,128)(2,1)S(1)} %collective-permute-done.4.refs_3_), channel_id=1, source_target_pairs={{0,2},{2,0},{1,3},{3,1},{4,6},{6,4},{5,7},{7,5},{8,10},{10,8},{9,1... | collective-permute-start | bytes 393224 | tf_op jit(solution)/shard_map/ppermute | solution.py:429
  21.2 2.7 %collective-permute-start.11 = (bf16[3,128,128]{2,1,0:T(8,128)(2,1)S(1)}, bf16[3,128,128]{2,1,0:T(8,128)(2,1)S(1)}, u32[]{:S(2)}, u32[]{:S(2)}) collective-permute-start(bf16[3,128,128]{2,1,0:T(8,128)(2,1)S(1)} %get-tuple-element.44), channel_id=1, source_target_pairs={{0,8},{4,12},{8,0},{12,4},{1,9},{5,13},{9,1},{13,5},{2,10},{6,14},... | collective-permute-start | bytes 294920 | tf_op jit(solution)/shard_map/ppermute | solution.py:435
  23.9 1.4 %collective-permute-done.12.refs_12_ = bf16[5,128,128]{2,1,0:T(8,128)(2,1)S(1)} collective-permute-done((bf16[5,128,128]{2,1,0:T(8,128)(2,1)S(1)}, bf16[5,128,128]{2,1,0:T(8,128)(2,1)S(1)}, u32[]{:S(2)}, u32[]{:S(2)}) %collective-permute-start.12) | collective-permute-done | bytes 163872 | tf_op jit(solution)/shard_map/ppermute | solution.py:435
  25.3 1.3 %collective-permute-start.8 = (bf16[64,1024]{1,0:T(8,128)(2,1)S(1)}, bf16[64,1024]{1,0:T(8,128)(2,1)S(1)}, u32[]{:S(2)}, u32[]{:S(2)}) collective-permute-start(bf16[64,1024]{1,0:T(8,128)(2,1)S(1)} %collective-permute-done.7.refs_5_), channel_id=1, source_target_pairs={{0,2},{2,0},{1,3},{3,1},{4,6},{6,4},{5,7},{7,5},{8,10},{10,8},{9,1... | collective-permute-start | bytes 393224 | tf_op jit(solution)/shard_map/ppermute | solution.py:429
  26.6 2.7 %collective-permute-done.11.refs_11_ = bf16[3,128,128]{2,1,0:T(8,128)(2,1)S(1)} collective-permute-done((bf16[3,128,128]{2,1,0:T(8,128)(2,1)S(1)}, bf16[3,128,128]{2,1,0:T(8,128)(2,1)S(1)}, u32[]{:S(2)}, u32[]{:S(2)}) %collective-permute-start.11) | collective-permute-done | bytes 98336 | tf_op jit(solution)/shard_map/ppermute | solution.py:435
  30.5 3.8 %collective-permute-done.18.refs_17_ = bf16[2,128,128]{2,1,0:T(8,128)(2,1)S(1)} collective-permute-done((bf16[2,128,128]{2,1,0:T(8,128)(2,1)S(1)}, bf16[2,128,128]{2,1,0:T(8,128)(2,1)S(1)}, u32[]{:S(2)}, u32[]{:S(2)}) %collective-permute-start.18) | collective-permute-done | bytes 65568 | tf_op jit(solution)/shard_map/ppermute | solution.py:435
  34.3 2.6 %shard_map.137 = (bf16[512,128]{1,0:T(8,128)(2,1)S(1)}, bf16[1088,128]{1,0:T(8,128)(2,1)S(1)}, bf16[16,1024]{1,0:T(8,128)(2,1)S(1)}, bf16[4,2,128,128]{3,2,1,0:T(8,128)(2,1)S(1)}) custom-call(s32[1]{0:T(128)S(6)} %copy.15.length, bf16[64,1024]{1,0:T(8,128)(2,1)} %refs_0_.5, f32[1,1024]{1,0:T(1,128)} %bitcast.5, ...), custom_call_target="tpu_custom_call" | custom-call | tf_op jit(solution)/shard_map/pallas_call | solution.py:171
  37.1 1.6 %collective-permute-start.19 = (bf16[4,2,128,128]{3,2,1,0:T(8,128)(2,1)S(1)}, bf16[4,2,128,128]{3,2,1,0:T(8,128)(2,1)S(1)}, u32[]{:S(2)}, u32[]{:S(2)}) collective-permute-start(bf16[4,2,128,128]{3,2,1,0:T(8,128)(2,1)S(1)} %get-tuple-element.54.refs_0_), channel_id=1, source_target_pairs={{0,16},{16,0},{1,17},{17,1},{2,18},{18,2},{3,19},{19,3},{4,20},{20... | collective-permute-start | bytes 786440 | tf_op jit(solution)/shard_map/ppermute | solution.py:432
  39.2 1.2 %collective-permute-start.28 = (bf16[3,128,256]{2,1,0:T(8,128)(2,1)S(1)}, bf16[3,128,256]{2,1,0:T(8,128)(2,1)S(1)}, u32[]{:S(2)}, u32[]{:S(2)}) collective-permute-start(bf16[3,128,256]{2,1,0:T(8,128)(2,1)S(1)} %get-tuple-element.59.refs_0_), channel_id=1, source_target_pairs={{0,12},{4,8},{8,4},{12,0},{1,13},{5,9},{9,5},{13,1},{2,14},{6,10},... | collective-permute-start | bytes 589832 | tf_op jit(solution)/shard_map/ppermute | solution.py:435
  40.4 1.6 %shard_map.138 = (bf16[144,128]{1,0:T(8,128)(2,1)S(1)}, bf16[144,128]{1,0:T(8,128)(2,1)S(1)}, bf16[144,128]{1,0:T(8,128)(2,1)S(1)}, bf16[144,128]{1,0:T(8,128)(2,1)S(1)}) custom-call(s32[1]{0:T(128)S(6)} %copy.15.length, bf16[512,128]{1,0:T(8,128)(2,1)S(1)} %get-tuple-element.48.q_in, bf16[1088,128]{1,0:T(8,128)(2,1)S(1)} %get-tuple-element.49.own, ...), custom_call_target="tpu_custom_call" | custom-call | tf_op jit(solution)/shard_map/pallas_call | solution.py:171
  42.0 3.8 %collective-permute-done.19.refs_2_ = bf16[4,2,128,128]{3,2,1,0:T(8,128)(2,1)S(1)} collective-permute-done((bf16[4,2,128,128]{3,2,1,0:T(8,128)(2,1)S(1)}, bf16[4,2,128,128]{3,2,1,0:T(8,128)(2,1)S(1)}, u32[]{:S(2)}, u32[]{:S(2)}) %collective-permute-start.19) | collective-permute-done | bytes 262176 | tf_op jit(solution)/shard_map/ppermute | solution.py:432
  46.8 2.6 %collective-permute-done.23.refs_1_ = bf16[3,128,256]{2,1,0:T(8,128)(2,1)S(1)} collective-permute-done((bf16[3,128,256]{2,1,0:T(8,128)(2,1)S(1)}, bf16[3,128,256]{2,1,0:T(8,128)(2,1)S(1)}, u32[]{:S(2)}, u32[]{:S(2)}) %collective-permute-start.23) | collective-permute-done | bytes 196640 | tf_op jit(solution)/shard_map/ppermute | solution.py:435
  49.4 1.0 %collective-permute-start.24 = (bf16[3,128,256]{2,1,0:T(8,128)(2,1)S(1)}, bf16[3,128,256]{2,1,0:T(8,128)(2,1)S(1)}, u32[]{:S(2)}, u32[]{:S(2)}) collective-permute-start(bf16[3,128,256]{2,1,0:T(8,128)(2,1)S(1)} %collective-permute-done.23.refs_1_), channel_id=1, source_target_pairs={{0,16},{16,0},{1,17},{17,1},{2,18},{18,2},{3,19},{19,3},{4,20},{20... | collective-permute-start | bytes 589832 | tf_op jit(solution)/shard_map/ppermute | solution.py:432
  50.6 3.3 %collective-permute-start.27 = (bf16[144,128]{1,0:T(8,128)(2,1)S(1)}, bf16[144,128]{1,0:T(8,128)(2,1)S(1)}, u32[]{:S(2)}, u32[]{:S(2)}) collective-permute-start(bf16[144,128]{1,0:T(8,128)(2,1)S(1)} %get-tuple-element.53), channel_id=1, source_target_pairs={{0,12},{4,8},{8,4},{12,0},{1,13},{5,9},{9,5},{13,1},{2,14},{6,10},... | collective-permute-start | bytes 110600 | tf_op jit(solution)/shard_map/ppermute | solution.py:515
  54.0 2.4 %collective-permute-done.26.refs_6_ = bf16[144,128]{1,0:T(8,128)(2,1)S(1)} collective-permute-done((bf16[144,128]{1,0:T(8,128)(2,1)S(1)}, bf16[144,128]{1,0:T(8,128)(2,1)S(1)}, u32[]{:S(2)}, u32[]{:S(2)}) %collective-permute-start.26) | collective-permute-done | bytes 36896 | tf_op jit(solution)/shard_map/ppermute | solution.py:515
  56.4 1.0 %collective-permute-start.29 = (bf16[3,128,256]{2,1,0:T(8,128)(2,1)S(1)}, bf16[3,128,256]{2,1,0:T(8,128)(2,1)S(1)}, u32[]{:S(2)}, u32[]{:S(2)}) collective-permute-start(bf16[3,128,256]{2,1,0:T(8,128)(2,1)S(1)} %collective-permute-done.28.refs_3_), channel_id=1, source_target_pairs={{0,4},{4,0},{8,12},{12,8},{1,5},{5,1},{9,13},{13,9},{2,6},{6,2},{1... | collective-permute-start | bytes 589832 | tf_op jit(solution)/shard_map/ppermute | solution.py:435
  57.9 1.2 %collective-permute-start.33 = (bf16[144,1024]{1,0:T(8,128)(2,1)S(1)}, bf16[144,1024]{1,0:T(8,128)(2,1)S(1)}, u32[]{:S(2)}, u32[]{:S(2)}) collective-permute-start(bf16[144,1024]{1,0:T(8,128)(2,1)S(1)} %get-tuple-element.65), channel_id=1, source_target_pairs={{0,2},{2,0},{1,3},{3,1},{4,6},{6,4},{5,7},{7,5},{8,10},{10,8},{9,1... | collective-permute-start | bytes 884744 | tf_op jit(solution)/shard_map/ppermute | solution.py:429
  60.1 2.0 %collective-permute-done.29.refs_2_ = bf16[3,128,256]{2,1,0:T(8,128)(2,1)S(1)} collective-permute-done((bf16[3,128,256]{2,1,0:T(8,128)(2,1)S(1)}, bf16[3,128,256]{2,1,0:T(8,128)(2,1)S(1)}, u32[]{:S(2)}, u32[]{:S(2)}) %collective-permute-start.29) | collective-permute-done | bytes 196640 | tf_op jit(solution)/shard_map/ppermute | solution.py:435
  62.1 1.1 %collective-permute-start.34 = (bf16[3,128,256]{2,1,0:T(8,128)(2,1)S(1)}, bf16[3,128,256]{2,1,0:T(8,128)(2,1)S(1)}, u32[]{:S(2)}, u32[]{:S(2)}) collective-permute-start(bf16[3,128,256]{2,1,0:T(8,128)(2,1)S(1)} %collective-permute-done.29.refs_2_), channel_id=1, source_target_pairs={{0,16},{16,0},{1,17},{17,1},{2,18},{18,2},{3,19},{19,3},{4,20},{20... | collective-permute-start | bytes 589832 | tf_op jit(solution)/shard_map/ppermute | solution.py:432
  66.6 2.1 %collective-permute-done.34.refs_2_ = bf16[3,128,256]{2,1,0:T(8,128)(2,1)S(1)} collective-permute-done((bf16[3,128,256]{2,1,0:T(8,128)(2,1)S(1)}, bf16[3,128,256]{2,1,0:T(8,128)(2,1)S(1)}, u32[]{:S(2)}, u32[]{:S(2)}) %collective-permute-start.34) | collective-permute-done | bytes 196640 | tf_op jit(solution)/shard_map/ppermute | solution.py:432
  68.9 2.3 %collective-permute-done.36.refs_5_ = bf16[4,3,128,256]{3,2,1,0:T(8,128)(2,1)S(1)} collective-permute-done((bf16[4,3,128,256]{3,2,1,0:T(8,128)(2,1)S(1)}, bf16[4,3,128,256]{3,2,1,0:T(8,128)(2,1)S(1)}, u32[]{:S(2)}, u32[]{:S(2)}) %collective-permute-start.36) | collective-permute-done | bytes 786464 | tf_op jit(solution)/shard_map/ppermute | solution.py:426
  71.1 1.4 %shard_map.142 = (f32[64,1024]{1,0:T(8,128)S(1)}, bf16[64,1024]{1,0:T(8,128)(2,1)S(1)}) custom-call(s32[1]{0:T(128)S(6)} %copy.15.length, bf16[64,1024]{1,0:T(8,128)(2,1)S(1)} %copy-done, f32[1,1024]{1,0:T(1,128)S(1)} %bitcast.4, bf16[4,3,128,256]{3,2,1,0:T(8,128)(2,1)S(1)} %shard_map.140.refs_2_, ...), custom_call_target="tpu_custom_call" | custom-call | tf_op jit(solution)/shard_map/pallas_call | solution.py:171
  72.5 1.3 %collective-permute-start.37 = (bf16[64,1024]{1,0:T(8,128)(2,1)S(1)}, bf16[64,1024]{1,0:T(8,128)(2,1)S(1)}, u32[]{:S(2)}, u32[]{:S(2)}) collective-permute-start(bf16[64,1024]{1,0:T(8,128)(2,1)S(1)} %get-tuple-element.68), channel_id=1, source_target_pairs={{0,2},{2,0},{1,3},{3,1},{4,6},{6,4},{5,7},{7,5},{8,10},{10,8},{9,1... | collective-permute-start | bytes 393224 | tf_op jit(solution)/shard_map/ppermute | solution.py:429
  73.9 4.3 %collective-permute-done.37 = bf16[64,1024]{1,0:T(8,128)(2,1)S(1)} collective-permute-done((bf16[64,1024]{1,0:T(8,128)(2,1)S(1)}, bf16[64,1024]{1,0:T(8,128)(2,1)S(1)}, u32[]{:S(2)}, u32[]{:S(2)}) %collective-permute-start.37) | collective-permute-done | bytes 131104 | tf_op jit(solution)/shard_map/ppermute | solution.py:429
  (69 shorter events, 10.9 us)
Async XLA Ops:
  0.0 6.0 %collective-permute-start = (bf16[256,256]{1,0:T(8,128)(2,1)}, bf16[256,256]{1,0:T(8,128)(2,1)S(1)}, u32[]{:S(2)}, u32[]{:S(2)}) collective-permute-start(bf16[256,256]{1,0:T(8,128)(2,1)} %refs_0_.3), channel_id=1, source_target_pairs={{0,1},{1,0},{2,3},{3,2},{4,5},{5,4},{6,7},{7,6},{8,9},{9,8},{10,11... | collective-permute-start | bytes 393224 | tf_op jit(solution)/shard_map/ppermute | solution.py:426
  0.5 7.7 %collective-permute-start.1 = (bf16[256,256]{1,0:T(8,128)(2,1)}, bf16[256,256]{1,0:T(8,128)(2,1)S(1)}, u32[]{:S(2)}, u32[]{:S(2)}) collective-permute-start(bf16[256,256]{1,0:T(8,128)(2,1)} %refs_1_.1), channel_id=1, source_target_pairs={{0,1},{1,0},{2,3},{3,2},{4,5},{5,4},{6,7},{7,6},{8,9},{9,8},{10,11... | collective-permute-start | bytes 393224 | tf_op jit(solution)/shard_map/ppermute | solution.py:426
  0.5 7.7 %collective-permute-start.2 = (bf16[256,256]{1,0:T(8,128)(2,1)}, bf16[256,256]{1,0:T(8,128)(2,1)S(1)}, u32[]{:S(2)}, u32[]{:S(2)}) collective-permute-start(bf16[256,256]{1,0:T(8,128)(2,1)} %refs_2_.1), channel_id=1, source_target_pairs={{0,1},{1,0},{2,3},{3,2},{4,5},{5,4},{6,7},{7,6},{8,9},{9,8},{10,11... | collective-permute-start | bytes 393224 | tf_op jit(solution)/shard_map/ppermute | solution.py:426
  1.0 8.5 %collective-permute-start.4 = (bf16[64,1024]{1,0:T(8,128)(2,1)}, bf16[64,1024]{1,0:T(8,128)(2,1)S(1)}, u32[]{:S(2)}, u32[]{:S(2)}) collective-permute-start(bf16[64,1024]{1,0:T(8,128)(2,1)} %refs_0_.5), channel_id=1, source_target_pairs={{0,4},{4,0},{8,12},{12,8},{1,5},{5,1},{9,13},{13,9},{2,6},{6,2},{1... | collective-permute-start | bytes 393224 | tf_op jit(solution)/shard_map/ppermute | solution.py:435
  3.5 9.8 %collective-permute-start.6 = (bf16[64,1024]{1,0:T(8,128)(2,1)}, bf16[64,1024]{1,0:T(8,128)(2,1)S(1)}, u32[]{:S(2)}, u32[]{:S(2)}) collective-permute-start(bf16[64,1024]{1,0:T(8,128)(2,1)} %refs_0_.5), channel_id=1, source_target_pairs={{0,12},{4,8},{8,4},{12,0},{1,13},{5,9},{9,5},{13,1},{2,14},{6,10},... | collective-permute-start | bytes 393224 | tf_op jit(solution)/shard_map/ppermute | solution.py:435
  6.0 10.7 %collective-permute-start.3 = (bf16[64,1024]{1,0:T(8,128)(2,1)}, bf16[64,1024]{1,0:T(8,128)(2,1)S(1)}, u32[]{:S(2)}, u32[]{:S(2)}) collective-permute-start(bf16[64,1024]{1,0:T(8,128)(2,1)} %refs_0_.5), channel_id=1, source_target_pairs={{0,2},{2,0},{1,3},{3,1},{4,6},{6,4},{5,7},{7,5},{8,10},{10,8},{9,1... | collective-permute-start | bytes 393224 | tf_op jit(solution)/shard_map/ppermute | solution.py:429
  9.5 11.7 %collective-permute-start.10 = (bf16[5,128,128]{2,1,0:T(8,128)(2,1)S(1)}, bf16[5,128,128]{2,1,0:T(8,128)(2,1)S(1)}, u32[]{:S(2)}, u32[]{:S(2)}) collective-permute-start(bf16[5,128,128]{2,1,0:T(8,128)(2,1)S(1)} %get-tuple-element.43), channel_id=1, source_target_pairs={{0,4},{4,0},{8,12},{12,8},{1,5},{5,1},{9,13},{13,9},{2,6},{6,2},{1... | collective-permute-start | bytes 491528 | tf_op jit(solution)/shard_map/ppermute | solution.py:435
  13.3 6.3 %collective-permute-start.7 = (bf16[64,1024]{1,0:T(8,128)(2,1)S(1)}, bf16[64,1024]{1,0:T(8,128)(2,1)S(1)}, u32[]{:S(2)}, u32[]{:S(2)}) collective-permute-start(bf16[64,1024]{1,0:T(8,128)(2,1)S(1)} %collective-permute-done.6.refs_7_), channel_id=1, source_target_pairs={{0,4},{4,0},{8,12},{12,8},{1,5},{5,1},{9,13},{13,9},{2,6},{6,2},{1... | collective-permute-start | bytes 393224 | tf_op jit(solution)/shard_map/ppermute | solution.py:435
  13.4 4.8 %collective-permute-start.13 = (bf16[3,128,128]{2,1,0:T(8,128)(2,1)S(1)}, bf16[3,128,128]{2,1,0:T(8,128)(2,1)S(1)}, u32[]{:S(2)}, u32[]{:S(2)}) collective-permute-start(bf16[3,128,128]{2,1,0:T(8,128)(2,1)S(1)} %slice.12), channel_id=1, source_target_pairs={{0,1},{1,0},{2,3},{3,2},{4,5},{5,4},{6,7},{7,6},{8,9},{9,8},{10,11... | collective-permute-start | bytes 294920 | tf_op jit(solution)/shard_map/ppermute | solution.py:426
  13.4 11.8 %collective-permute-start.12 = (bf16[5,128,128]{2,1,0:T(8,128)(2,1)S(1)}, bf16[5,128,128]{2,1,0:T(8,128)(2,1)S(1)}, u32[]{:S(2)}, u32[]{:S(2)}) collective-permute-start(bf16[5,128,128]{2,1,0:T(8,128)(2,1)S(1)} %get-tuple-element.45), channel_id=1, source_target_pairs={{0,12},{4,8},{8,4},{12,0},{1,13},{5,9},{9,5},{13,1},{2,14},{6,10},... | collective-permute-start | bytes 491528 | tf_op jit(solution)/shard_map/ppermute | solution.py:435
  16.7 13.1 %collective-permute-start.14 = (bf16[3,128,256]{2,1,0:T(8,128)(2,1)S(1)}, bf16[3,128,256]{2,1,0:T(8,128)(2,1)S(1)}, u32[]{:S(2)}, u32[]{:S(2)}) collective-permute-start(bf16[3,128,256]{2,1,0:T(8,128)(2,1)S(1)} %get-tuple-element.59.refs_0_), channel_id=1, source_target_pairs={{0,16},{16,0},{1,17},{17,1},{2,18},{18,2},{3,19},{19,3},{4,20},{20... | collective-permute-start | bytes 589832 | tf_op jit(solution)/shard_map/ppermute | solution.py:432
  18.2 11.0 %collective-permute-start.9 = (bf16[64,1024]{1,0:T(8,128)(2,1)S(1)}, bf16[64,1024]{1,0:T(8,128)(2,1)S(1)}, u32[]{:S(2)}, u32[]{:S(2)}) collective-permute-start(bf16[64,1024]{1,0:T(8,128)(2,1)S(1)} %collective-permute-done.6.refs_7_), channel_id=1, source_target_pairs={{0,2},{2,0},{1,3},{3,1},{4,6},{6,4},{5,7},{7,5},{8,10},{10,8},{9,1... | collective-permute-start | bytes 393224 | tf_op jit(solution)/shard_map/ppermute | solution.py:429
  19.6 10.1 %collective-permute-start.5 = (bf16[64,1024]{1,0:T(8,128)(2,1)S(1)}, bf16[64,1024]{1,0:T(8,128)(2,1)S(1)}, u32[]{:S(2)}, u32[]{:S(2)}) collective-permute-start(bf16[64,1024]{1,0:T(8,128)(2,1)S(1)} %collective-permute-done.4.refs_3_), channel_id=1, source_target_pairs={{0,2},{2,0},{1,3},{3,1},{4,6},{6,4},{5,7},{7,5},{8,10},{10,8},{9,1... | collective-permute-start | bytes 393224 | tf_op jit(solution)/shard_map/ppermute | solution.py:429
  21.2 8.0 %collective-permute-start.11 = (bf16[3,128,128]{2,1,0:T(8,128)(2,1)S(1)}, bf16[3,128,128]{2,1,0:T(8,128)(2,1)S(1)}, u32[]{:S(2)}, u32[]{:S(2)}) collective-permute-start(bf16[3,128,128]{2,1,0:T(8,128)(2,1)S(1)} %get-tuple-element.44), channel_id=1, source_target_pairs={{0,8},{4,12},{8,0},{12,4},{1,9},{5,13},{9,1},{13,5},{2,10},{6,14},... | collective-permute-start | bytes 294920 | tf_op jit(solution)/shard_map/ppermute | solution.py:435
  25.3 9.1 %collective-permute-start.8 = (bf16[64,1024]{1,0:T(8,128)(2,1)S(1)}, bf16[64,1024]{1,0:T(8,128)(2,1)S(1)}, u32[]{:S(2)}, u32[]{:S(2)}) collective-permute-start(bf16[64,1024]{1,0:T(8,128)(2,1)S(1)} %collective-permute-done.7.refs_5_), channel_id=1, source_target_pairs={{0,2},{2,0},{1,3},{3,1},{4,6},{6,4},{5,7},{7,5},{8,10},{10,8},{9,1... | collective-permute-start | bytes 393224 | tf_op jit(solution)/shard_map/ppermute | solution.py:429
  29.2 5.1 %collective-permute-start.15 = (bf16[3,128,128]{2,1,0:T(8,128)(2,1)S(1)}, bf16[3,128,128]{2,1,0:T(8,128)(2,1)S(1)}, u32[]{:S(2)}, u32[]{:S(2)}) collective-permute-start(bf16[3,128,128]{2,1,0:T(8,128)(2,1)S(1)} %slice.16), channel_id=1, source_target_pairs={{0,1},{1,0},{2,3},{3,2},{4,5},{5,4},{6,7},{7,6},{8,9},{9,8},{10,11... | collective-permute-start | bytes 294920 | tf_op jit(solution)/shard_map/ppermute | solution.py:426
  29.8 4.6 %collective-permute-start.17 = (bf16[3,128,128]{2,1,0:T(8,128)(2,1)S(1)}, bf16[3,128,128]{2,1,0:T(8,128)(2,1)S(1)}, u32[]{:S(2)}, u32[]{:S(2)}) collective-permute-start(bf16[3,128,128]{2,1,0:T(8,128)(2,1)S(1)} %slice.17), channel_id=1, source_target_pairs={{0,1},{1,0},{2,3},{3,2},{4,5},{5,4},{6,7},{7,6},{8,9},{9,8},{10,11... | collective-permute-start | bytes 294920 | tf_op jit(solution)/shard_map/ppermute | solution.py:426
  29.8 4.5 %collective-permute-start.18 = (bf16[2,128,128]{2,1,0:T(8,128)(2,1)S(1)}, bf16[2,128,128]{2,1,0:T(8,128)(2,1)S(1)}, u32[]{:S(2)}, u32[]{:S(2)}) collective-permute-start(bf16[2,128,128]{2,1,0:T(8,128)(2,1)S(1)} %slice.18), channel_id=1, source_target_pairs={{0,4},{4,0},{8,12},{12,8},{1,5},{5,1},{9,13},{13,9},{2,6},{6,2},{1... | collective-permute-start | bytes 196616 | tf_op jit(solution)/shard_map/ppermute | solution.py:435
  37.1 8.7 %collective-permute-start.19 = (bf16[4,2,128,128]{3,2,1,0:T(8,128)(2,1)S(1)}, bf16[4,2,128,128]{3,2,1,0:T(8,128)(2,1)S(1)}, u32[]{:S(2)}, u32[]{:S(2)}) collective-permute-start(bf16[4,2,128,128]{3,2,1,0:T(8,128)(2,1)S(1)} %get-tuple-element.54.refs_0_), channel_id=1, source_target_pairs={{0,16},{16,0},{1,17},{17,1},{2,18},{18,2},{3,19},{19,3},{4,20},{20... | collective-permute-start | bytes 786440 | tf_op jit(solution)/shard_map/ppermute | solution.py:432
  38.7 10.7 %collective-permute-start.23 = (bf16[3,128,256]{2,1,0:T(8,128)(2,1)S(1)}, bf16[3,128,256]{2,1,0:T(8,128)(2,1)S(1)}, u32[]{:S(2)}, u32[]{:S(2)}) collective-permute-start(bf16[3,128,256]{2,1,0:T(8,128)(2,1)S(1)} %get-tuple-element.59.refs_0_), channel_id=1, source_target_pairs={{0,4},{4,0},{8,12},{12,8},{1,5},{5,1},{9,13},{13,9},{2,6},{6,2},{1... | collective-permute-start | bytes 589832 | tf_op jit(solution)/shard_map/ppermute | solution.py:435
  39.2 11.2 %collective-permute-start.28 = (bf16[3,128,256]{2,1,0:T(8,128)(2,1)S(1)}, bf16[3,128,256]{2,1,0:T(8,128)(2,1)S(1)}, u32[]{:S(2)}, u32[]{:S(2)}) collective-permute-start(bf16[3,128,256]{2,1,0:T(8,128)(2,1)S(1)} %get-tuple-element.59.refs_0_), channel_id=1, source_target_pairs={{0,12},{4,8},{8,4},{12,0},{1,13},{5,9},{9,5},{13,1},{2,14},{6,10},... | collective-permute-start | bytes 589832 | tf_op jit(solution)/shard_map/ppermute | solution.py:435
  45.8 11.6 %collective-permute-start.21 = (bf16[4,2,128,128]{3,2,1,0:T(8,128)(2,1)S(1)}, bf16[4,2,128,128]{3,2,1,0:T(8,128)(2,1)S(1)}, u32[]{:S(2)}, u32[]{:S(2)}) collective-permute-start(bf16[4,2,128,128]{3,2,1,0:T(8,128)(2,1)S(1)} %get-tuple-element.54.refs_0_), channel_id=1, source_target_pairs={{0,1},{1,0},{2,3},{3,2},{4,5},{5,4},{6,7},{7,6},{8,9},{9,8},{10,11... | collective-permute-start | bytes 786440 | tf_op jit(solution)/shard_map/ppermute | solution.py:426
  45.8 11.6 %collective-permute-start.22 = (bf16[4,2,128,128]{3,2,1,0:T(8,128)(2,1)S(1)}, bf16[4,2,128,128]{3,2,1,0:T(8,128)(2,1)S(1)}, u32[]{:S(2)}, u32[]{:S(2)}) collective-permute-start(bf16[4,2,128,128]{3,2,1,0:T(8,128)(2,1)S(1)} %collective-permute-done.19.refs_2_), channel_id=1, source_target_pairs={{0,1},{1,0},{2,3},{3,2},{4,5},{5,4},{6,7},{7,6},{8,9},{9,8},{10,11... | collective-permute-start | bytes 786440 | tf_op jit(solution)/shard_map/ppermute | solution.py:426
  46.3 4.3 %collective-permute-start.25 = (bf16[144,128]{1,0:T(8,128)(2,1)S(1)}, bf16[144,128]{1,0:T(8,128)(2,1)S(1)}, u32[]{:S(2)}, u32[]{:S(2)}) collective-permute-start(bf16[144,128]{1,0:T(8,128)(2,1)S(1)} %get-tuple-element.51), channel_id=1, source_target_pairs={{0,4},{4,0},{8,12},{12,8},{1,5},{5,1},{9,13},{13,9},{2,6},{6,2},{1... | collective-permute-start | bytes 110600 | tf_op jit(solution)/shard_map/ppermute | solution.py:515
  49.4 8.0 %collective-permute-start.24 = (bf16[3,128,256]{2,1,0:T(8,128)(2,1)S(1)}, bf16[3,128,256]{2,1,0:T(8,128)(2,1)S(1)}, u32[]{:S(2)}, u32[]{:S(2)}) collective-permute-start(bf16[3,128,256]{2,1,0:T(8,128)(2,1)S(1)} %collective-permute-done.23.refs_1_), channel_id=1, source_target_pairs={{0,16},{16,0},{1,17},{17,1},{2,18},{18,2},{3,19},{19,3},{4,20},{20... | collective-permute-start | bytes 589832 | tf_op jit(solution)/shard_map/ppermute | solution.py:432
  50.4 6.0 %collective-permute-start.26 = (bf16[144,128]{1,0:T(8,128)(2,1)S(1)}, bf16[144,128]{1,0:T(8,128)(2,1)S(1)}, u32[]{:S(2)}, u32[]{:S(2)}) collective-permute-start(bf16[144,128]{1,0:T(8,128)(2,1)S(1)} %get-tuple-element.52), channel_id=1, source_target_pairs={{0,8},{4,12},{8,0},{12,4},{1,9},{5,13},{9,1},{13,5},{2,10},{6,14},... | collective-permute-start | bytes 110600 | tf_op jit(solution)/shard_map/ppermute | solution.py:515
  50.6 5.8 %collective-permute-start.27 = (bf16[144,128]{1,0:T(8,128)(2,1)S(1)}, bf16[144,128]{1,0:T(8,128)(2,1)S(1)}, u32[]{:S(2)}, u32[]{:S(2)}) collective-permute-start(bf16[144,128]{1,0:T(8,128)(2,1)S(1)} %get-tuple-element.53), channel_id=1, source_target_pairs={{0,12},{4,8},{8,4},{12,0},{1,13},{5,9},{9,5},{13,1},{2,14},{6,10},... | collective-permute-start | bytes 110600 | tf_op jit(solution)/shard_map/ppermute | solution.py:515
  56.4 5.7 %collective-permute-start.29 = (bf16[3,128,256]{2,1,0:T(8,128)(2,1)S(1)}, bf16[3,128,256]{2,1,0:T(8,128)(2,1)S(1)}, u32[]{:S(2)}, u32[]{:S(2)}) collective-permute-start(bf16[3,128,256]{2,1,0:T(8,128)(2,1)S(1)} %collective-permute-done.28.refs_3_), channel_id=1, source_target_pairs={{0,4},{4,0},{8,12},{12,8},{1,5},{5,1},{9,13},{13,9},{2,6},{6,2},{1... | collective-permute-start | bytes 589832 | tf_op jit(solution)/shard_map/ppermute | solution.py:435
  57.9 7.8 %collective-permute-start.33 = (bf16[144,1024]{1,0:T(8,128)(2,1)S(1)}, bf16[144,1024]{1,0:T(8,128)(2,1)S(1)}, u32[]{:S(2)}, u32[]{:S(2)}) collective-permute-start(bf16[144,1024]{1,0:T(8,128)(2,1)S(1)} %get-tuple-element.65), channel_id=1, source_target_pairs={{0,2},{2,0},{1,3},{3,1},{4,6},{6,4},{5,7},{7,5},{8,10},{10,8},{9,1... | collective-permute-start | bytes 884744 | tf_op jit(solution)/shard_map/ppermute | solution.py:429
  59.2 7.4 %collective-permute-start.35 = (bf16[3,128,256]{2,1,0:T(8,128)(2,1)S(1)}, bf16[3,128,256]{2,1,0:T(8,128)(2,1)S(1)}, u32[]{:S(2)}, u32[]{:S(2)}) collective-permute-start(bf16[3,128,256]{2,1,0:T(8,128)(2,1)S(1)} %collective-permute-done.28.refs_3_), channel_id=1, source_target_pairs={{0,16},{16,0},{1,17},{17,1},{2,18},{18,2},{3,19},{19,3},{4,20},{20... | collective-permute-start | bytes 589832 | tf_op jit(solution)/shard_map/ppermute | solution.py:432
  62.1 6.6 %collective-permute-start.34 = (bf16[3,128,256]{2,1,0:T(8,128)(2,1)S(1)}, bf16[3,128,256]{2,1,0:T(8,128)(2,1)S(1)}, u32[]{:S(2)}, u32[]{:S(2)}) collective-permute-start(bf16[3,128,256]{2,1,0:T(8,128)(2,1)S(1)} %collective-permute-done.29.refs_2_), channel_id=1, source_target_pairs={{0,16},{16,0},{1,17},{17,1},{2,18},{18,2},{3,19},{19,3},{4,20},{20... | collective-permute-start | bytes 589832 | tf_op jit(solution)/shard_map/ppermute | solution.py:432
  72.5 5.6 %collective-permute-start.37 = (bf16[64,1024]{1,0:T(8,128)(2,1)S(1)}, bf16[64,1024]{1,0:T(8,128)(2,1)S(1)}, u32[]{:S(2)}, u32[]{:S(2)}) collective-permute-start(bf16[64,1024]{1,0:T(8,128)(2,1)S(1)} %get-tuple-element.68), channel_id=1, source_target_pairs={{0,2},{2,0},{1,3},{3,1},{4,6},{6,4},{5,7},{7,5},{8,10},{10,8},{9,1... | collective-permute-start | bytes 393224 | tf_op jit(solution)/shard_map/ppermute | solution.py:429
  (11 other events, 35.8 us)

commit v10 on v9

--- a/solution.py
+++ b/solution.py
@@ -252,12 +252,6 @@
     for copy in copies:
         copy.wait()
     gain_row = own_gain[...]
-    for slot, block in enumerate(blocks):
-        at = (s ^ (slot // 2)) * 2 + (h ^ (slot % 2))
-        x = block[...].astype(F32)
-        normed[pl.ds(aligned(at * rows, rows), rows), :] = layer_norm(x, gain_row).astype(BF16)
-        x_edge[at, 0:EDGE, :] = x[:EDGE]
-        x_edge[at, EDGE:HALO, :] = x[rows - EDGE :]
     for k in range(SEQ):
         for core, pieces in enumerate((mine, other)):
             at = pl.ds(aligned((s ^ k) * 2 * half + (f ^ core) * half, half), half)
@@ -266,13 +260,23 @@
         stack_out[s ^ k] = down[...] if k == 2 else mine[k][3:]
     count = 2 * SEQ
     total = count * rows
-    projected = dot(normed[...], weights[...])
-    q_out[...] = projected[:, :HD].astype(BF16)
-    send_out[0:total, :] = projected[:, HD : 2 * HD].astype(BF16)
-    send_out[total : 2 * total, :] = projected[:, 2 * HD :].astype(BF16)
-    for b in range(count):
-        q_edge[b, 0:EDGE, :] = projected[b * rows : b * rows + EDGE, :HD]
-        q_edge[b, EDGE:HALO, :] = projected[(b + 1) * rows - EDGE : (b + 1) * rows, :HD]
+    for k in range(SEQ):
+        for side in range(2):
+            at = (s ^ k) * 2 + (h ^ side)
+            x = blocks[2 * k + side][...].astype(F32)
+            normed[k, side * rows : (side + 1) * rows, :] = layer_norm(x, gain_row).astype(BF16)
+            x_edge[at, 0:EDGE, :] = x[:EDGE]
+            x_edge[at, EDGE:HALO, :] = x[rows - EDGE :]
+        both = dot(normed[k], weights[...])
+        for side in range(2):
+            at = (s ^ k) * 2 + (h ^ side)
+            start = aligned(at * rows, rows)
+            part = both[side * rows : (side + 1) * rows]
+            q_out[pl.ds(start, rows), :] = part[:, :HD].astype(BF16)
+            send_out[pl.ds(start, rows), :] = part[:, HD : 2 * HD].astype(BF16)
+            send_out[pl.ds(aligned(start + total, rows), rows), :] = part[:, 2 * HD :].astype(BF16)
+            q_edge[at, 0:EDGE, :] = part[:EDGE, :HD]
+            q_edge[at, EDGE:HALO, :] = part[rows - EDGE :, :HD]
 
     def around(edge, b):
         low = jnp.maximum(b - f, 0)
@@ -482,7 +486,7 @@
             shape((SEQ, columns // HD, half, HD), BF16),
         ],
         [
-            pltpu.VMEM((count * rows, width), BF16),
+            pltpu.VMEM((SEQ, 2 * rows, width), BF16),
             pltpu.VMEM((width, 3 * HD), BF16),
             pltpu.VMEM((count, HALO, width), F32),
             pltpu.VMEM((count, HALO, HD), F32),

time: 79 us -> 78.5 us (level)
  transfers between devices with their start and end apart: 38 -> 38, of which waited for: 16 -> 17; matrix products, arithmetic and copies ran while one was open for 0% -> 0% of each run, Pallas kernels for 5% -> 5%
where the time goes in v10:
time: 78.5 us; the launch traced here: 78.4 us
  starting transfers between devices  36.4 us (46%)
  waiting for transfers between devices  32.5 us (41%)
  Pallas kernels  7.17 us (9%)
  between operations  0.83 us (1%)
  local copies, waits for them, and re-layouts  0.8 us (1%)
    ppermute x10, waiting for transfers between devices, across(): return lax.ppermute(x, 'seq', xor_pairs(k))  15.7 us
    ppermute x10, starting transfers between devices, across(): return lax.ppermute(x, 'seq', xor_pairs(k))  15 us
    ppermute x6, starting transfers between devices, other_side(): return lax.ppermute(x, 'head', SWAP)  8.11 us
    pallas_call x7, Pallas kernels, call(): pl.pallas_call(kernel, out_shape=outs, in_specs=[pl.BlockSpec(memory_spac...  7.17 us
    ppermute x5, waiting for transfers between devices, other_part(): return lax.ppermute(x, 'parts', SWAP)  6.8 us
    ppermute x5, starting transfers between devices, other_part(): return lax.ppermute(x, 'parts', SWAP)  6.1 us
    ppermute x6, waiting for transfers between devices, other_side(): return lax.ppermute(x, 'head', SWAP)  4.27 us
    ppermute x3, starting transfers between devices, shards_chip_per_head(): lax.ppermute(ctx[k], 'seq', xor_pairs(k))  4.05 us
  transfers between devices with their start and end apart: 38, of which 17 were waited for; matrix products, arithmetic and copies ran while one was open for 0% of the time, Pallas kernels for 5%

profile of v10, /device:TPU:0, one launch (start us, length us, event | category | flops | bytes accessed | tf_op | source)
XLA Modules:
  0.0 78.4 jit_solution(12400632411620541366)
XLA Ops:
  1.0 2.6 %collective-permute-start.4 = (bf16[64,1024]{1,0:T(8,128)(2,1)}, bf16[64,1024]{1,0:T(8,128)(2,1)S(1)}, u32[]{:S(2)}, u32[]{:S(2)}) collective-permute-start(bf16[64,1024]{1,0:T(8,128)(2,1)} %refs_0_.5), channel_id=1, source_target_pairs={{0,4},{4,0},{8,12},{12,8},{1,5},{5,1},{9,13},{13,9},{2,6},{6,2},{1... | collective-permute-start | bytes 393224 | tf_op jit(solution)/shard_map/ppermute | solution.py:439
  3.5 2.5 %collective-permute-start.6 = (bf16[64,1024]{1,0:T(8,128)(2,1)}, bf16[64,1024]{1,0:T(8,128)(2,1)S(1)}, u32[]{:S(2)}, u32[]{:S(2)}) collective-permute-start(bf16[64,1024]{1,0:T(8,128)(2,1)} %refs_0_.5), channel_id=1, source_target_pairs={{0,12},{4,8},{8,4},{12,0},{1,13},{5,9},{9,5},{13,1},{2,14},{6,10},... | collective-permute-start | bytes 393224 | tf_op jit(solution)/shard_map/ppermute | solution.py:439
  6.0 1.5 %collective-permute-start.3 = (bf16[64,1024]{1,0:T(8,128)(2,1)}, bf16[64,1024]{1,0:T(8,128)(2,1)S(1)}, u32[]{:S(2)}, u32[]{:S(2)}) collective-permute-start(bf16[64,1024]{1,0:T(8,128)(2,1)} %refs_0_.5), channel_id=1, source_target_pairs={{0,2},{2,0},{1,3},{3,1},{4,6},{6,4},{5,7},{7,5},{8,10},{10,8},{9,1... | collective-permute-start | bytes 393224 | tf_op jit(solution)/shard_map/ppermute | solution.py:433
  8.2 1.3 %shard_map.136 = (bf16[5,128,128]{2,1,0:T(8,128)(2,1)S(1)}, bf16[5,128,128]{2,1,0:T(8,128)(2,1)S(1)}, bf16[3,128,128]{2,1,0:T(8,128)(2,1)S(1)}, bf16[5,128,128]{2,1,0:T(8,128)(2,1)S(1)}, bf16[3,128,256]{2,1,0:T(8,128)(2,1)S(1)}) custom-call(s32[1]{0:T(128)S(6)} %copy.15.length, bf16[256,256]{1,0:T(8,128)(2,1)} %refs_0_.3, bf16[256,256]{1,0:T(8,128)(2,1)} %refs_1_.1, ...), custom_call_target="tpu_custom_call" | custom-call | tf_op jit(solution)/shard_map/pallas_call | solution.py:171
  10.3 3.1 %collective-permute-done.6.refs_7_ = bf16[64,1024]{1,0:T(8,128)(2,1)S(1)} collective-permute-done((bf16[64,1024]{1,0:T(8,128)(2,1)}, bf16[64,1024]{1,0:T(8,128)(2,1)S(1)}, u32[]{:S(2)}, u32[]{:S(2)}) %collective-permute-start.6) | collective-permute-done | bytes 131104 | tf_op jit(solution)/shard_map/ppermute | solution.py:439
  13.4 3.2 %collective-permute-start.12 = (bf16[5,128,128]{2,1,0:T(8,128)(2,1)S(1)}, bf16[5,128,128]{2,1,0:T(8,128)(2,1)S(1)}, u32[]{:S(2)}, u32[]{:S(2)}) collective-permute-start(bf16[5,128,128]{2,1,0:T(8,128)(2,1)S(1)} %get-tuple-element.45), channel_id=1, source_target_pairs={{0,12},{4,8},{8,4},{12,0},{1,13},{5,9},{9,5},{13,1},{2,14},{6,10},... | collective-permute-start | bytes 491528 | tf_op jit(solution)/shard_map/ppermute | solution.py:439
  16.7 1.5 %collective-permute-start.14 = (bf16[3,128,256]{2,1,0:T(8,128)(2,1)S(1)}, bf16[3,128,256]{2,1,0:T(8,128)(2,1)S(1)}, u32[]{:S(2)}, u32[]{:S(2)}) collective-permute-start(bf16[3,128,256]{2,1,0:T(8,128)(2,1)S(1)} %get-tuple-element.59.refs_0_), channel_id=1, source_target_pairs={{0,16},{16,0},{1,17},{17,1},{2,18},{18,2},{3,19},{19,3},{4,20},{20... | collective-permute-start | bytes 589832 | tf_op jit(solution)/shard_map/ppermute | solution.py:436
  18.2 1.3 %collective-permute-start.9 = (bf16[64,1024]{1,0:T(8,128)(2,1)S(1)}, bf16[64,1024]{1,0:T(8,128)(2,1)S(1)}, u32[]{:S(2)}, u32[]{:S(2)}) collective-permute-start(bf16[64,1024]{1,0:T(8,128)(2,1)S(1)} %collective-permute-done.6.refs_7_), channel_id=1, source_target_pairs={{0,2},{2,0},{1,3},{3,1},{4,6},{6,4},{5,7},{7,5},{8,10},{10,8},{9,1... | collective-permute-start | bytes 393224 | tf_op jit(solution)/shard_map/ppermute | solution.py:433
  19.6 1.6 %collective-permute-start.5 = (bf16[64,1024]{1,0:T(8,128)(2,1)S(1)}, bf16[64,1024]{1,0:T(8,128)(2,1)S(1)}, u32[]{:S(2)}, u32[]{:S(2)}) collective-permute-start(bf16[64,1024]{1,0:T(8,128)(2,1)S(1)} %collective-permute-done.4.refs_3_), channel_id=1, source_target_pairs={{0,2},{2,0},{1,3},{3,1},{4,6},{6,4},{5,7},{7,5},{8,10},{10,8},{9,1... | collective-permute-start | bytes 393224 | tf_op jit(solution)/shard_map/ppermute | solution.py:433
  21.2 2.7 %collective-permute-start.11 = (bf16[3,128,128]{2,1,0:T(8,128)(2,1)S(1)}, bf16[3,128,128]{2,1,0:T(8,128)(2,1)S(1)}, u32[]{:S(2)}, u32[]{:S(2)}) collective-permute-start(bf16[3,128,128]{2,1,0:T(8,128)(2,1)S(1)} %get-tuple-element.44), channel_id=1, source_target_pairs={{0,8},{4,12},{8,0},{12,4},{1,9},{5,13},{9,1},{13,5},{2,10},{6,14},... | collective-permute-start | bytes 294920 | tf_op jit(solution)/shard_map/ppermute | solution.py:439
  23.9 1.4 %collective-permute-done.12.refs_12_ = bf16[5,128,128]{2,1,0:T(8,128)(2,1)S(1)} collective-permute-done((bf16[5,128,128]{2,1,0:T(8,128)(2,1)S(1)}, bf16[5,128,128]{2,1,0:T(8,128)(2,1)S(1)}, u32[]{:S(2)}, u32[]{:S(2)}) %collective-permute-start.12) | collective-permute-done | bytes 163872 | tf_op jit(solution)/shard_map/ppermute | solution.py:439
  25.3 1.3 %collective-permute-start.8 = (bf16[64,1024]{1,0:T(8,128)(2,1)S(1)}, bf16[64,1024]{1,0:T(8,128)(2,1)S(1)}, u32[]{:S(2)}, u32[]{:S(2)}) collective-permute-start(bf16[64,1024]{1,0:T(8,128)(2,1)S(1)} %collective-permute-done.7.refs_5_), channel_id=1, source_target_pairs={{0,2},{2,0},{1,3},{3,1},{4,6},{6,4},{5,7},{7,5},{8,10},{10,8},{9,1... | collective-permute-start | bytes 393224 | tf_op jit(solution)/shard_map/ppermute | solution.py:433
  26.6 2.7 %collective-permute-done.11.refs_11_ = bf16[3,128,128]{2,1,0:T(8,128)(2,1)S(1)} collective-permute-done((bf16[3,128,128]{2,1,0:T(8,128)(2,1)S(1)}, bf16[3,128,128]{2,1,0:T(8,128)(2,1)S(1)}, u32[]{:S(2)}, u32[]{:S(2)}) %collective-permute-start.11) | collective-permute-done | bytes 98336 | tf_op jit(solution)/shard_map/ppermute | solution.py:439
  30.5 3.8 %collective-permute-done.18.refs_17_ = bf16[2,128,128]{2,1,0:T(8,128)(2,1)S(1)} collective-permute-done((bf16[2,128,128]{2,1,0:T(8,128)(2,1)S(1)}, bf16[2,128,128]{2,1,0:T(8,128)(2,1)S(1)}, u32[]{:S(2)}, u32[]{:S(2)}) %collective-permute-start.18) | collective-permute-done | bytes 65568 | tf_op jit(solution)/shard_map/ppermute | solution.py:439
  34.3 2.2 %shard_map.137 = (bf16[512,128]{1,0:T(8,128)(2,1)S(1)}, bf16[1088,128]{1,0:T(8,128)(2,1)S(1)}, bf16[16,1024]{1,0:T(8,128)(2,1)S(1)}, bf16[4,2,128,128]{3,2,1,0:T(8,128)(2,1)S(1)}) custom-call(s32[1]{0:T(128)S(6)} %copy.15.length, bf16[64,1024]{1,0:T(8,128)(2,1)} %refs_0_.5, f32[1,1024]{1,0:T(1,128)} %bitcast.5, ...), custom_call_target="tpu_custom_call" | custom-call | tf_op jit(solution)/shard_map/pallas_call | solution.py:171
  36.6 1.6 %collective-permute-start.19 = (bf16[4,2,128,128]{3,2,1,0:T(8,128)(2,1)S(1)}, bf16[4,2,128,128]{3,2,1,0:T(8,128)(2,1)S(1)}, u32[]{:S(2)}, u32[]{:S(2)}) collective-permute-start(bf16[4,2,128,128]{3,2,1,0:T(8,128)(2,1)S(1)} %get-tuple-element.54.refs_0_), channel_id=1, source_target_pairs={{0,16},{16,0},{1,17},{17,1},{2,18},{18,2},{3,19},{19,3},{4,20},{20... | collective-permute-start | bytes 786440 | tf_op jit(solution)/shard_map/ppermute | solution.py:436
  38.7 1.2 %collective-permute-start.28 = (bf16[3,128,256]{2,1,0:T(8,128)(2,1)S(1)}, bf16[3,128,256]{2,1,0:T(8,128)(2,1)S(1)}, u32[]{:S(2)}, u32[]{:S(2)}) collective-permute-start(bf16[3,128,256]{2,1,0:T(8,128)(2,1)S(1)} %get-tuple-element.59.refs_0_), channel_id=1, source_target_pairs={{0,12},{4,8},{8,4},{12,0},{1,13},{5,9},{9,5},{13,1},{2,14},{6,10},... | collective-permute-start | bytes 589832 | tf_op jit(solution)/shard_map/ppermute | solution.py:439
  40.0 1.6 %shard_map.138 = (bf16[144,128]{1,0:T(8,128)(2,1)S(1)}, bf16[144,128]{1,0:T(8,128)(2,1)S(1)}, bf16[144,128]{1,0:T(8,128)(2,1)S(1)}, bf16[144,128]{1,0:T(8,128)(2,1)S(1)}) custom-call(s32[1]{0:T(128)S(6)} %copy.15.length, bf16[512,128]{1,0:T(8,128)(2,1)S(1)} %get-tuple-element.48.q_in, bf16[1088,128]{1,0:T(8,128)(2,1)S(1)} %get-tuple-element.49.own, ...), custom_call_target="tpu_custom_call" | custom-call | tf_op jit(solution)/shard_map/pallas_call | solution.py:171
  41.6 3.8 %collective-permute-done.19.refs_2_ = bf16[4,2,128,128]{3,2,1,0:T(8,128)(2,1)S(1)} collective-permute-done((bf16[4,2,128,128]{3,2,1,0:T(8,128)(2,1)S(1)}, bf16[4,2,128,128]{3,2,1,0:T(8,128)(2,1)S(1)}, u32[]{:S(2)}, u32[]{:S(2)}) %collective-permute-start.19) | collective-permute-done | bytes 262176 | tf_op jit(solution)/shard_map/ppermute | solution.py:436
  46.4 2.6 %collective-permute-done.23.refs_1_ = bf16[3,128,256]{2,1,0:T(8,128)(2,1)S(1)} collective-permute-done((bf16[3,128,256]{2,1,0:T(8,128)(2,1)S(1)}, bf16[3,128,256]{2,1,0:T(8,128)(2,1)S(1)}, u32[]{:S(2)}, u32[]{:S(2)}) %collective-permute-start.23) | collective-permute-done | bytes 196640 | tf_op jit(solution)/shard_map/ppermute | solution.py:439
  49.0 0.9 %collective-permute-start.24 = (bf16[3,128,256]{2,1,0:T(8,128)(2,1)S(1)}, bf16[3,128,256]{2,1,0:T(8,128)(2,1)S(1)}, u32[]{:S(2)}, u32[]{:S(2)}) collective-permute-start(bf16[3,128,256]{2,1,0:T(8,128)(2,1)S(1)} %collective-permute-done.23.refs_1_), channel_id=1, source_target_pairs={{0,16},{16,0},{1,17},{17,1},{2,18},{18,2},{3,19},{19,3},{4,20},{20... | collective-permute-start | bytes 589832 | tf_op jit(solution)/shard_map/ppermute | solution.py:436
  50.2 3.3 %collective-permute-start.27 = (bf16[144,128]{1,0:T(8,128)(2,1)S(1)}, bf16[144,128]{1,0:T(8,128)(2,1)S(1)}, u32[]{:S(2)}, u32[]{:S(2)}) collective-permute-start(bf16[144,128]{1,0:T(8,128)(2,1)S(1)} %get-tuple-element.53), channel_id=1, source_target_pairs={{0,12},{4,8},{8,4},{12,0},{1,13},{5,9},{9,5},{13,1},{2,14},{6,10},... | collective-permute-start | bytes 110600 | tf_op jit(solution)/shard_map/ppermute | solution.py:519
  53.5 2.0 %collective-permute-done.26.refs_6_ = bf16[144,128]{1,0:T(8,128)(2,1)S(1)} collective-permute-done((bf16[144,128]{1,0:T(8,128)(2,1)S(1)}, bf16[144,128]{1,0:T(8,128)(2,1)S(1)}, u32[]{:S(2)}, u32[]{:S(2)}) %collective-permute-start.26) | collective-permute-done | bytes 36896 | tf_op jit(solution)/shard_map/ppermute | solution.py:519
  56.0 0.9 %collective-permute-start.29 = (bf16[3,128,256]{2,1,0:T(8,128)(2,1)S(1)}, bf16[3,128,256]{2,1,0:T(8,128)(2,1)S(1)}, u32[]{:S(2)}, u32[]{:S(2)}) collective-permute-start(bf16[3,128,256]{2,1,0:T(8,128)(2,1)S(1)} %collective-permute-done.28.refs_3_), channel_id=1, source_target_pairs={{0,4},{4,0},{8,12},{12,8},{1,5},{5,1},{9,13},{13,9},{2,6},{6,2},{1... | collective-permute-start | bytes 589832 | tf_op jit(solution)/shard_map/ppermute | solution.py:439
  57.5 1.2 %collective-permute-start.33 = (bf16[144,1024]{1,0:T(8,128)(2,1)S(1)}, bf16[144,1024]{1,0:T(8,128)(2,1)S(1)}, u32[]{:S(2)}, u32[]{:S(2)}) collective-permute-start(bf16[144,1024]{1,0:T(8,128)(2,1)S(1)} %get-tuple-element.65), channel_id=1, source_target_pairs={{0,2},{2,0},{1,3},{3,1},{4,6},{6,4},{5,7},{7,5},{8,10},{10,8},{9,1... | collective-permute-start | bytes 884744 | tf_op jit(solution)/shard_map/ppermute | solution.py:433
  59.6 2.0 %collective-permute-done.29.refs_2_ = bf16[3,128,256]{2,1,0:T(8,128)(2,1)S(1)} collective-permute-done((bf16[3,128,256]{2,1,0:T(8,128)(2,1)S(1)}, bf16[3,128,256]{2,1,0:T(8,128)(2,1)S(1)}, u32[]{:S(2)}, u32[]{:S(2)}) %collective-permute-start.29) | collective-permute-done | bytes 196640 | tf_op jit(solution)/shard_map/ppermute | solution.py:439
  61.6 1.1 %collective-permute-start.34 = (bf16[3,128,256]{2,1,0:T(8,128)(2,1)S(1)}, bf16[3,128,256]{2,1,0:T(8,128)(2,1)S(1)}, u32[]{:S(2)}, u32[]{:S(2)}) collective-permute-start(bf16[3,128,256]{2,1,0:T(8,128)(2,1)S(1)} %collective-permute-done.29.refs_2_), channel_id=1, source_target_pairs={{0,16},{16,0},{1,17},{17,1},{2,18},{18,2},{3,19},{19,3},{4,20},{20... | collective-permute-start | bytes 589832 | tf_op jit(solution)/shard_map/ppermute | solution.py:436
  66.2 2.1 %collective-permute-done.34.refs_2_ = bf16[3,128,256]{2,1,0:T(8,128)(2,1)S(1)} collective-permute-done((bf16[3,128,256]{2,1,0:T(8,128)(2,1)S(1)}, bf16[3,128,256]{2,1,0:T(8,128)(2,1)S(1)}, u32[]{:S(2)}, u32[]{:S(2)}) %collective-permute-start.34) | collective-permute-done | bytes 196640 | tf_op jit(solution)/shard_map/ppermute | solution.py:436
  68.4 2.3 %collective-permute-done.36.refs_5_ = bf16[4,3,128,256]{3,2,1,0:T(8,128)(2,1)S(1)} collective-permute-done((bf16[4,3,128,256]{3,2,1,0:T(8,128)(2,1)S(1)}, bf16[4,3,128,256]{3,2,1,0:T(8,128)(2,1)S(1)}, u32[]{:S(2)}, u32[]{:S(2)}) %collective-permute-start.36) | collective-permute-done | bytes 786464 | tf_op jit(solution)/shard_map/ppermute | solution.py:430
  70.7 1.4 %shard_map.142 = (f32[64,1024]{1,0:T(8,128)S(1)}, bf16[64,1024]{1,0:T(8,128)(2,1)S(1)}) custom-call(s32[1]{0:T(128)S(6)} %copy.15.length, bf16[64,1024]{1,0:T(8,128)(2,1)S(1)} %copy-done, f32[1,1024]{1,0:T(1,128)S(1)} %bitcast.4, bf16[4,3,128,256]{3,2,1,0:T(8,128)(2,1)S(1)} %shard_map.140.refs_2_, ...), custom_call_target="tpu_custom_call" | custom-call | tf_op jit(solution)/shard_map/pallas_call | solution.py:171
  72.1 1.3 %collective-permute-start.37 = (bf16[64,1024]{1,0:T(8,128)(2,1)S(1)}, bf16[64,1024]{1,0:T(8,128)(2,1)S(1)}, u32[]{:S(2)}, u32[]{:S(2)}) collective-permute-start(bf16[64,1024]{1,0:T(8,128)(2,1)S(1)} %get-tuple-element.68), channel_id=1, source_target_pairs={{0,2},{2,0},{1,3},{3,1},{4,6},{6,4},{5,7},{7,5},{8,10},{10,8},{9,1... | collective-permute-start | bytes 393224 | tf_op jit(solution)/shard_map/ppermute | solution.py:433
  73.4 4.3 %collective-permute-done.37 = bf16[64,1024]{1,0:T(8,128)(2,1)S(1)} collective-permute-done((bf16[64,1024]{1,0:T(8,128)(2,1)S(1)}, bf16[64,1024]{1,0:T(8,128)(2,1)S(1)}, u32[]{:S(2)}, u32[]{:S(2)}) %collective-permute-start.37) | collective-permute-done | bytes 131104 | tf_op jit(solution)/shard_map/ppermute | solution.py:433
  (69 shorter events, 11.3 us)
Async XLA Ops:
  0.0 6.0 %collective-permute-start = (bf16[256,256]{1,0:T(8,128)(2,1)}, bf16[256,256]{1,0:T(8,128)(2,1)S(1)}, u32[]{:S(2)}, u32[]{:S(2)}) collective-permute-start(bf16[256,256]{1,0:T(8,128)(2,1)} %refs_0_.3), channel_id=1, source_target_pairs={{0,1},{1,0},{2,3},{3,2},{4,5},{5,4},{6,7},{7,6},{8,9},{9,8},{10,11... | collective-permute-start | bytes 393224 | tf_op jit(solution)/shard_map/ppermute | solution.py:430
  0.5 7.7 %collective-permute-start.1 = (bf16[256,256]{1,0:T(8,128)(2,1)}, bf16[256,256]{1,0:T(8,128)(2,1)S(1)}, u32[]{:S(2)}, u32[]{:S(2)}) collective-permute-start(bf16[256,256]{1,0:T(8,128)(2,1)} %refs_1_.1), channel_id=1, source_target_pairs={{0,1},{1,0},{2,3},{3,2},{4,5},{5,4},{6,7},{7,6},{8,9},{9,8},{10,11... | collective-permute-start | bytes 393224 | tf_op jit(solution)/shard_map/ppermute | solution.py:430
  0.5 7.7 %collective-permute-start.2 = (bf16[256,256]{1,0:T(8,128)(2,1)}, bf16[256,256]{1,0:T(8,128)(2,1)S(1)}, u32[]{:S(2)}, u32[]{:S(2)}) collective-permute-start(bf16[256,256]{1,0:T(8,128)(2,1)} %refs_2_.1), channel_id=1, source_target_pairs={{0,1},{1,0},{2,3},{3,2},{4,5},{5,4},{6,7},{7,6},{8,9},{9,8},{10,11... | collective-permute-start | bytes 393224 | tf_op jit(solution)/shard_map/ppermute | solution.py:430
  1.0 8.5 %collective-permute-start.4 = (bf16[64,1024]{1,0:T(8,128)(2,1)}, bf16[64,1024]{1,0:T(8,128)(2,1)S(1)}, u32[]{:S(2)}, u32[]{:S(2)}) collective-permute-start(bf16[64,1024]{1,0:T(8,128)(2,1)} %refs_0_.5), channel_id=1, source_target_pairs={{0,4},{4,0},{8,12},{12,8},{1,5},{5,1},{9,13},{13,9},{2,6},{6,2},{1... | collective-permute-start | bytes 393224 | tf_op jit(solution)/shard_map/ppermute | solution.py:439
  3.5 9.8 %collective-permute-start.6 = (bf16[64,1024]{1,0:T(8,128)(2,1)}, bf16[64,1024]{1,0:T(8,128)(2,1)S(1)}, u32[]{:S(2)}, u32[]{:S(2)}) collective-permute-start(bf16[64,1024]{1,0:T(8,128)(2,1)} %refs_0_.5), channel_id=1, source_target_pairs={{0,12},{4,8},{8,4},{12,0},{1,13},{5,9},{9,5},{13,1},{2,14},{6,10},... | collective-permute-start | bytes 393224 | tf_op jit(solution)/shard_map/ppermute | solution.py:439
  6.0 10.7 %collective-permute-start.3 = (bf16[64,1024]{1,0:T(8,128)(2,1)}, bf16[64,1024]{1,0:T(8,128)(2,1)S(1)}, u32[]{:S(2)}, u32[]{:S(2)}) collective-permute-start(bf16[64,1024]{1,0:T(8,128)(2,1)} %refs_0_.5), channel_id=1, source_target_pairs={{0,2},{2,0},{1,3},{3,1},{4,6},{6,4},{5,7},{7,5},{8,10},{10,8},{9,1... | collective-permute-start | bytes 393224 | tf_op jit(solution)/shard_map/ppermute | solution.py:433
  9.5 11.7 %collective-permute-start.10 = (bf16[5,128,128]{2,1,0:T(8,128)(2,1)S(1)}, bf16[5,128,128]{2,1,0:T(8,128)(2,1)S(1)}, u32[]{:S(2)}, u32[]{:S(2)}) collective-permute-start(bf16[5,128,128]{2,1,0:T(8,128)(2,1)S(1)} %get-tuple-element.43), channel_id=1, source_target_pairs={{0,4},{4,0},{8,12},{12,8},{1,5},{5,1},{9,13},{13,9},{2,6},{6,2},{1... | collective-permute-start | bytes 491528 | tf_op jit(solution)/shard_map/ppermute | solution.py:439
  13.3 6.3 %collective-permute-start.7 = (bf16[64,1024]{1,0:T(8,128)(2,1)S(1)}, bf16[64,1024]{1,0:T(8,128)(2,1)S(1)}, u32[]{:S(2)}, u32[]{:S(2)}) collective-permute-start(bf16[64,1024]{1,0:T(8,128)(2,1)S(1)} %collective-permute-done.6.refs_7_), channel_id=1, source_target_pairs={{0,4},{4,0},{8,12},{12,8},{1,5},{5,1},{9,13},{13,9},{2,6},{6,2},{1... | collective-permute-start | bytes 393224 | tf_op jit(solution)/shard_map/ppermute | solution.py:439
  13.4 4.8 %collective-permute-start.13 = (bf16[3,128,128]{2,1,0:T(8,128)(2,1)S(1)}, bf16[3,128,128]{2,1,0:T(8,128)(2,1)S(1)}, u32[]{:S(2)}, u32[]{:S(2)}) collective-permute-start(bf16[3,128,128]{2,1,0:T(8,128)(2,1)S(1)} %slice.12), channel_id=1, source_target_pairs={{0,1},{1,0},{2,3},{3,2},{4,5},{5,4},{6,7},{7,6},{8,9},{9,8},{10,11... | collective-permute-start | bytes 294920 | tf_op jit(solution)/shard_map/ppermute | solution.py:430
  13.4 11.8 %collective-permute-start.12 = (bf16[5,128,128]{2,1,0:T(8,128)(2,1)S(1)}, bf16[5,128,128]{2,1,0:T(8,128)(2,1)S(1)}, u32[]{:S(2)}, u32[]{:S(2)}) collective-permute-start(bf16[5,128,128]{2,1,0:T(8,128)(2,1)S(1)} %get-tuple-element.45), channel_id=1, source_target_pairs={{0,12},{4,8},{8,4},{12,0},{1,13},{5,9},{9,5},{13,1},{2,14},{6,10},... | collective-permute-start | bytes 491528 | tf_op jit(solution)/shard_map/ppermute | solution.py:439
  16.7 13.1 %collective-permute-start.14 = (bf16[3,128,256]{2,1,0:T(8,128)(2,1)S(1)}, bf16[3,128,256]{2,1,0:T(8,128)(2,1)S(1)}, u32[]{:S(2)}, u32[]{:S(2)}) collective-permute-start(bf16[3,128,256]{2,1,0:T(8,128)(2,1)S(1)} %get-tuple-element.59.refs_0_), channel_id=1, source_target_pairs={{0,16},{16,0},{1,17},{17,1},{2,18},{18,2},{3,19},{19,3},{4,20},{20... | collective-permute-start | bytes 589832 | tf_op jit(solution)/shard_map/ppermute | solution.py:436
  18.2 11.0 %collective-permute-start.9 = (bf16[64,1024]{1,0:T(8,128)(2,1)S(1)}, bf16[64,1024]{1,0:T(8,128)(2,1)S(1)}, u32[]{:S(2)}, u32[]{:S(2)}) collective-permute-start(bf16[64,1024]{1,0:T(8,128)(2,1)S(1)} %collective-permute-done.6.refs_7_), channel_id=1, source_target_pairs={{0,2},{2,0},{1,3},{3,1},{4,6},{6,4},{5,7},{7,5},{8,10},{10,8},{9,1... | collective-permute-start | bytes 393224 | tf_op jit(solution)/shard_map/ppermute | solution.py:433
  19.6 10.1 %collective-permute-start.5 = (bf16[64,1024]{1,0:T(8,128)(2,1)S(1)}, bf16[64,1024]{1,0:T(8,128)(2,1)S(1)}, u32[]{:S(2)}, u32[]{:S(2)}) collective-permute-start(bf16[64,1024]{1,0:T(8,128)(2,1)S(1)} %collective-permute-done.4.refs_3_), channel_id=1, source_target_pairs={{0,2},{2,0},{1,3},{3,1},{4,6},{6,4},{5,7},{7,5},{8,10},{10,8},{9,1... | collective-permute-start | bytes 393224 | tf_op jit(solution)/shard_map/ppermute | solution.py:433
  21.2 8.0 %collective-permute-start.11 = (bf16[3,128,128]{2,1,0:T(8,128)(2,1)S(1)}, bf16[3,128,128]{2,1,0:T(8,128)(2,1)S(1)}, u32[]{:S(2)}, u32[]{:S(2)}) collective-permute-start(bf16[3,128,128]{2,1,0:T(8,128)(2,1)S(1)} %get-tuple-element.44), channel_id=1, source_target_pairs={{0,8},{4,12},{8,0},{12,4},{1,9},{5,13},{9,1},{13,5},{2,10},{6,14},... | collective-permute-start | bytes 294920 | tf_op jit(solution)/shard_map/ppermute | solution.py:439
  25.3 9.1 %collective-permute-start.8 = (bf16[64,1024]{1,0:T(8,128)(2,1)S(1)}, bf16[64,1024]{1,0:T(8,128)(2,1)S(1)}, u32[]{:S(2)}, u32[]{:S(2)}) collective-permute-start(bf16[64,1024]{1,0:T(8,128)(2,1)S(1)} %collective-permute-done.7.refs_5_), channel_id=1, source_target_pairs={{0,2},{2,0},{1,3},{3,1},{4,6},{6,4},{5,7},{7,5},{8,10},{10,8},{9,1... | collective-permute-start | bytes 393224 | tf_op jit(solution)/shard_map/ppermute | solution.py:433
  29.2 5.1 %collective-permute-start.15 = (bf16[3,128,128]{2,1,0:T(8,128)(2,1)S(1)}, bf16[3,128,128]{2,1,0:T(8,128)(2,1)S(1)}, u32[]{:S(2)}, u32[]{:S(2)}) collective-permute-start(bf16[3,128,128]{2,1,0:T(8,128)(2,1)S(1)} %slice.16), channel_id=1, source_target_pairs={{0,1},{1,0},{2,3},{3,2},{4,5},{5,4},{6,7},{7,6},{8,9},{9,8},{10,11... | collective-permute-start | bytes 294920 | tf_op jit(solution)/shard_map/ppermute | solution.py:430
  29.8 4.6 %collective-permute-start.17 = (bf16[3,128,128]{2,1,0:T(8,128)(2,1)S(1)}, bf16[3,128,128]{2,1,0:T(8,128)(2,1)S(1)}, u32[]{:S(2)}, u32[]{:S(2)}) collective-permute-start(bf16[3,128,128]{2,1,0:T(8,128)(2,1)S(1)} %slice.17), channel_id=1, source_target_pairs={{0,1},{1,0},{2,3},{3,2},{4,5},{5,4},{6,7},{7,6},{8,9},{9,8},{10,11... | collective-permute-start | bytes 294920 | tf_op jit(solution)/shard_map/ppermute | solution.py:430
  29.8 4.5 %collective-permute-start.18 = (bf16[2,128,128]{2,1,0:T(8,128)(2,1)S(1)}, bf16[2,128,128]{2,1,0:T(8,128)(2,1)S(1)}, u32[]{:S(2)}, u32[]{:S(2)}) collective-permute-start(bf16[2,128,128]{2,1,0:T(8,128)(2,1)S(1)} %slice.18), channel_id=1, source_target_pairs={{0,4},{4,0},{8,12},{12,8},{1,5},{5,1},{9,13},{13,9},{2,6},{6,2},{1... | collective-permute-start | bytes 196616 | tf_op jit(solution)/shard_map/ppermute | solution.py:439
  36.6 8.7 %collective-permute-start.19 = (bf16[4,2,128,128]{3,2,1,0:T(8,128)(2,1)S(1)}, bf16[4,2,128,128]{3,2,1,0:T(8,128)(2,1)S(1)}, u32[]{:S(2)}, u32[]{:S(2)}) collective-permute-start(bf16[4,2,128,128]{3,2,1,0:T(8,128)(2,1)S(1)} %get-tuple-element.54.refs_0_), channel_id=1, source_target_pairs={{0,16},{16,0},{1,17},{17,1},{2,18},{18,2},{3,19},{19,3},{4,20},{20... | collective-permute-start | bytes 786440 | tf_op jit(solution)/shard_map/ppermute | solution.py:436
  38.2 10.7 %collective-permute-start.23 = (bf16[3,128,256]{2,1,0:T(8,128)(2,1)S(1)}, bf16[3,128,256]{2,1,0:T(8,128)(2,1)S(1)}, u32[]{:S(2)}, u32[]{:S(2)}) collective-permute-start(bf16[3,128,256]{2,1,0:T(8,128)(2,1)S(1)} %get-tuple-element.59.refs_0_), channel_id=1, source_target_pairs={{0,4},{4,0},{8,12},{12,8},{1,5},{5,1},{9,13},{13,9},{2,6},{6,2},{1... | collective-permute-start | bytes 589832 | tf_op jit(solution)/shard_map/ppermute | solution.py:439
  38.7 11.2 %collective-permute-start.28 = (bf16[3,128,256]{2,1,0:T(8,128)(2,1)S(1)}, bf16[3,128,256]{2,1,0:T(8,128)(2,1)S(1)}, u32[]{:S(2)}, u32[]{:S(2)}) collective-permute-start(bf16[3,128,256]{2,1,0:T(8,128)(2,1)S(1)} %get-tuple-element.59.refs_0_), channel_id=1, source_target_pairs={{0,12},{4,8},{8,4},{12,0},{1,13},{5,9},{9,5},{13,1},{2,14},{6,10},... | collective-permute-start | bytes 589832 | tf_op jit(solution)/shard_map/ppermute | solution.py:439
  45.4 11.6 %collective-permute-start.21 = (bf16[4,2,128,128]{3,2,1,0:T(8,128)(2,1)S(1)}, bf16[4,2,128,128]{3,2,1,0:T(8,128)(2,1)S(1)}, u32[]{:S(2)}, u32[]{:S(2)}) collective-permute-start(bf16[4,2,128,128]{3,2,1,0:T(8,128)(2,1)S(1)} %get-tuple-element.54.refs_0_), channel_id=1, source_target_pairs={{0,1},{1,0},{2,3},{3,2},{4,5},{5,4},{6,7},{7,6},{8,9},{9,8},{10,11... | collective-permute-start | bytes 786440 | tf_op jit(solution)/shard_map/ppermute | solution.py:430
  45.4 11.6 %collective-permute-start.22 = (bf16[4,2,128,128]{3,2,1,0:T(8,128)(2,1)S(1)}, bf16[4,2,128,128]{3,2,1,0:T(8,128)(2,1)S(1)}, u32[]{:S(2)}, u32[]{:S(2)}) collective-permute-start(bf16[4,2,128,128]{3,2,1,0:T(8,128)(2,1)S(1)} %collective-permute-done.19.refs_2_), channel_id=1, source_target_pairs={{0,1},{1,0},{2,3},{3,2},{4,5},{5,4},{6,7},{7,6},{8,9},{9,8},{10,11... | collective-permute-start | bytes 786440 | tf_op jit(solution)/shard_map/ppermute | solution.py:430
  45.9 4.3 %collective-permute-start.25 = (bf16[144,128]{1,0:T(8,128)(2,1)S(1)}, bf16[144,128]{1,0:T(8,128)(2,1)S(1)}, u32[]{:S(2)}, u32[]{:S(2)}) collective-permute-start(bf16[144,128]{1,0:T(8,128)(2,1)S(1)} %get-tuple-element.51), channel_id=1, source_target_pairs={{0,4},{4,0},{8,12},{12,8},{1,5},{5,1},{9,13},{13,9},{2,6},{6,2},{1... | collective-permute-start | bytes 110600 | tf_op jit(solution)/shard_map/ppermute | solution.py:519
  49.0 8.0 %collective-permute-start.24 = (bf16[3,128,256]{2,1,0:T(8,128)(2,1)S(1)}, bf16[3,128,256]{2,1,0:T(8,128)(2,1)S(1)}, u32[]{:S(2)}, u32[]{:S(2)}) collective-permute-start(bf16[3,128,256]{2,1,0:T(8,128)(2,1)S(1)} %collective-permute-done.23.refs_1_), channel_id=1, source_target_pairs={{0,16},{16,0},{1,17},{17,1},{2,18},{18,2},{3,19},{19,3},{4,20},{20... | collective-permute-start | bytes 589832 | tf_op jit(solution)/shard_map/ppermute | solution.py:436
  49.9 5.6 %collective-permute-start.26 = (bf16[144,128]{1,0:T(8,128)(2,1)S(1)}, bf16[144,128]{1,0:T(8,128)(2,1)S(1)}, u32[]{:S(2)}, u32[]{:S(2)}) collective-permute-start(bf16[144,128]{1,0:T(8,128)(2,1)S(1)} %get-tuple-element.52), channel_id=1, source_target_pairs={{0,8},{4,12},{8,0},{12,4},{1,9},{5,13},{9,1},{13,5},{2,10},{6,14},... | collective-permute-start | bytes 110600 | tf_op jit(solution)/shard_map/ppermute | solution.py:519
  50.2 5.8 %collective-permute-start.27 = (bf16[144,128]{1,0:T(8,128)(2,1)S(1)}, bf16[144,128]{1,0:T(8,128)(2,1)S(1)}, u32[]{:S(2)}, u32[]{:S(2)}) collective-permute-start(bf16[144,128]{1,0:T(8,128)(2,1)S(1)} %get-tuple-element.53), channel_id=1, source_target_pairs={{0,12},{4,8},{8,4},{12,0},{1,13},{5,9},{9,5},{13,1},{2,14},{6,10},... | collective-permute-start | bytes 110600 | tf_op jit(solution)/shard_map/ppermute | solution.py:519
  56.0 5.7 %collective-permute-start.29 = (bf16[3,128,256]{2,1,0:T(8,128)(2,1)S(1)}, bf16[3,128,256]{2,1,0:T(8,128)(2,1)S(1)}, u32[]{:S(2)}, u32[]{:S(2)}) collective-permute-start(bf16[3,128,256]{2,1,0:T(8,128)(2,1)S(1)} %collective-permute-done.28.refs_3_), channel_id=1, source_target_pairs={{0,4},{4,0},{8,12},{12,8},{1,5},{5,1},{9,13},{13,9},{2,6},{6,2},{1... | collective-permute-start | bytes 589832 | tf_op jit(solution)/shard_map/ppermute | solution.py:439
  57.5 7.8 %collective-permute-start.33 = (bf16[144,1024]{1,0:T(8,128)(2,1)S(1)}, bf16[144,1024]{1,0:T(8,128)(2,1)S(1)}, u32[]{:S(2)}, u32[]{:S(2)}) collective-permute-start(bf16[144,1024]{1,0:T(8,128)(2,1)S(1)} %get-tuple-element.65), channel_id=1, source_target_pairs={{0,2},{2,0},{1,3},{3,1},{4,6},{6,4},{5,7},{7,5},{8,10},{10,8},{9,1... | collective-permute-start | bytes 884744 | tf_op jit(solution)/shard_map/ppermute | solution.py:433
  58.7 7.4 %collective-permute-start.35 = (bf16[3,128,256]{2,1,0:T(8,128)(2,1)S(1)}, bf16[3,128,256]{2,1,0:T(8,128)(2,1)S(1)}, u32[]{:S(2)}, u32[]{:S(2)}) collective-permute-start(bf16[3,128,256]{2,1,0:T(8,128)(2,1)S(1)} %collective-permute-done.28.refs_3_), channel_id=1, source_target_pairs={{0,16},{16,0},{1,17},{17,1},{2,18},{18,2},{3,19},{19,3},{4,20},{20... | collective-permute-start | bytes 589832 | tf_op jit(solution)/shard_map/ppermute | solution.py:436
  61.6 6.6 %collective-permute-start.34 = (bf16[3,128,256]{2,1,0:T(8,128)(2,1)S(1)}, bf16[3,128,256]{2,1,0:T(8,128)(2,1)S(1)}, u32[]{:S(2)}, u32[]{:S(2)}) collective-permute-start(bf16[3,128,256]{2,1,0:T(8,128)(2,1)S(1)} %collective-permute-done.29.refs_2_), channel_id=1, source_target_pairs={{0,16},{16,0},{1,17},{17,1},{2,18},{18,2},{3,19},{19,3},{4,20},{20... | collective-permute-start | bytes 589832 | tf_op jit(solution)/shard_map/ppermute | solution.py:436
  72.1 5.6 %collective-permute-start.37 = (bf16[64,1024]{1,0:T(8,128)(2,1)S(1)}, bf16[64,1024]{1,0:T(8,128)(2,1)S(1)}, u32[]{:S(2)}, u32[]{:S(2)}) collective-permute-start(bf16[64,1024]{1,0:T(8,128)(2,1)S(1)} %get-tuple-element.68), channel_id=1, source_target_pairs={{0,2},{2,0},{1,3},{3,1},{4,6},{6,4},{5,7},{7,5},{8,10},{10,8},{9,1... | collective-permute-start | bytes 393224 | tf_op jit(solution)/shard_map/ppermute | solution.py:433
  (11 other events, 35.8 us)
